TPU v7x, 32 devices: a whole 2x2x4 slice. The times are simulated.
32 devices in a mesh: bag: 8 (over z, x), head: 4 (over y, core).
Axes of the slice: x: 2, y: 2, z: 4, core: 2. Of those that a mesh axis runs over, the one named last changes fastest.
Arguments:
- latents: bfloat16 [8, 8, 16, 16, 512], P('bag', 'head'), may hold values from -6 to 6
- frame_counts: int32 [8], P('bag'), may hold values from 4 to 8
- routes: int32 [4096, 1], P('bag'), may hold values from 0 to 7; in each aligned block of 128 rows (0 to 127, 128 to 255, ...) at most 24 rows name the same one
- samples: int32 [4096], P('bag'), may hold values from 0 to 3, as said below
- conv_weight: bfloat16 [27, 512, 128], replicated, may hold values from -0.0546875 to 0.0546875
- embed_weight: bfloat16 [512, 2048], replicated, may hold values from -0.25 to 0.25
- qkv_weight: bfloat16 [3, 2048, 2048], P(None, None, 'head')
Outputs:
- attended: bfloat16 [4096, 2048], P(('bag', 'head'))
Inputs may be any that keep to these rules, and one draw needn't show every extreme that they name: `routes`: in each aligned block of 128 rows (the tokens of one device) no bag is named by more than 24 rows, a bound that some block reaches. `samples`: all tokens of one clip carry the same sample id, and every id occurs in some clip.
All inputs are finite; a program needn't handle non-finite values.
Results may differ from a plain program's by a relative error of at most 0.013.
Values may be sent and summed in bfloat16 or wider, within the bound.
No kernel may reach another device: no remote copies, remote signals or barrier semaphores. Data moves between devices by JAX's collectives and lax.ppermute only.
A program may use at most 128 MiB of HBM per device.

v0:
```python
import jax
import jax.numpy as jnp
from jax import lax
from jax.sharding import PartitionSpec as P

HDIM = 64


epsilon = 1e-06
far_below = -1e30


def padded_2(cells, sides, width):
    for axis, dim in sides:
        count = lax.axis_size(axis)
        ends = count - 1
        head = lax.slice_in_dim(cells, 0, width, axis=dim)
        tail = lax.slice_in_dim(cells, cells.shape[dim] - width, cells.shape[dim], axis=dim)
        cells = jnp.concatenate(
            [
                lax.ppermute(tail, axis, [(i, (i + 1) % count) for i in range(ends)]),
                cells,
                lax.ppermute(head, axis, [((i + 1) % count, i) for i in range(ends)]),
            ],
            axis=dim,
        )
    return cells


def patchify(latent_grid):
    frames_in, rows_in, cols_in, chans = latent_grid.shape
    shaped = latent_grid.reshape(frames_in, rows_in // 2, 2, cols_in // 2, 2, chans)
    return shaped.transpose(0, 1, 3, 2, 4, 5).reshape(
        frames_in * (rows_in // 2) * (cols_in // 2), 4 * chans
    )


def project(embedded, qkv_weight):
    widened = embedded.astype(jnp.float32)
    normed = (
        widened * lax.rsqrt(jnp.mean(widened * widened, axis=-1, keepdims=True) + epsilon)
    ).astype(jnp.bfloat16)
    return jnp.einsum("rd,mdc->rmc", normed, qkv_weight, preferred_element_type=jnp.float32).astype(
        jnp.bfloat16
    )


def convolve(padded, conv_weight, frame_live, frames_dev, side_rows, side_cols):
    depth_in = padded.shape[3]
    accumulated = jnp.zeros((frames_dev * side_rows * side_cols, conv_weight.shape[2]), jnp.float32)
    for offset_t in range(3):
        for offset_h in range(3):
            for offset_w in range(3):
                window = padded[
                    offset_t : offset_t + frames_dev,
                    offset_h : offset_h + side_rows,
                    offset_w : offset_w + side_cols,
                ]
                accumulated = accumulated + jnp.dot(
                    window.reshape(-1, depth_in),
                    conv_weight[9 * offset_t + 3 * offset_h + offset_w],
                    preferred_element_type=jnp.float32,
                )
    shaped = accumulated.reshape(frames_dev, side_rows, side_cols, -1)
    shaped = shaped * frame_live[:, None, None, None].astype(jnp.float32)
    return patchify(shaped.astype(jnp.bfloat16))


def shards(latents, frame_counts, routes, samples, conv_weight, embed_weight, qkv_weight):
    frames_dev = latents.shape[1]
    side_rows = latents.shape[2]
    side_cols = latents.shape[3]
    heads_dev = lax.axis_size("head")
    bags = lax.axis_size("bag")
    place = lax.axis_index("head")
    frame_count = frame_counts[0]
    frame_ids = place * frames_dev + jnp.arange(frames_dev, dtype=jnp.int32)
    frame_live = frame_ids < frame_count
    masked = latents[0] * frame_live[:, None, None, None].astype(jnp.bfloat16)
    padded = padded_2(masked, (("head", 0),), 1)
    padded = jnp.pad(padded, ((0, 0), (1, 1), (1, 1), (0, 0)))
    patches = convolve(padded, conv_weight, frame_live, frames_dev, side_rows, side_cols)
    tok_dev = patches.shape[0]
    embedded_rows = jnp.dot(
        lax.all_gather(patches, "head", axis=0, tiled=True),
        embed_weight,
        preferred_element_type=jnp.float32,
    ).astype(jnp.bfloat16)
    qkv_all = project(embedded_rows, qkv_weight)
    local_width = qkv_all.shape[2]
    route_rows = routes[:, 0].reshape(heads_dev, tok_dev)
    per_frame = tok_dev // frames_dev
    token_frame = (
        jnp.arange(heads_dev, dtype=jnp.int32)[:, None] * frames_dev
        + (jnp.arange(tok_dev, dtype=jnp.int32) // per_frame)[None, :]
    )
    token_live = token_frame < frame_count
    bag_ids = jnp.arange(bags, dtype=jnp.int32)
    onehot = (route_rows[:, :, None] == bag_ids[None, None, :]).astype(jnp.int32)
    slot_rank = jnp.sum((jnp.cumsum(onehot, axis=1) - onehot) * onehot, axis=2)
    capacity = 3 * tok_dev // (2 * bags)
    matches = (route_rows[None, :, None, :] == bag_ids[:, None, None, None]) & (
        slot_rank[None, :, None, :] == jnp.arange(capacity, dtype=jnp.int32)[None, None, :, None]
    )
    positions = jnp.arange(tok_dev, dtype=jnp.int32)
    slot_token = jnp.sum(jnp.where(matches, positions[None, None, None, :], 0), axis=3)
    filled = jnp.any(matches, axis=3)
    flat_index = jnp.arange(heads_dev, dtype=jnp.int32)[None, :, None] * tok_dev + slot_token
    slot_live = filled & token_live.reshape(-1)[flat_index]
    slot_labels = jnp.where(slot_live, samples[flat_index], -1).reshape(bags, heads_dev * capacity)
    outgoing = jnp.take(qkv_all, flat_index.reshape(-1), axis=0).reshape(
        bags, heads_dev * capacity, 3, local_width
    )
    incoming, incoming_labels = (
        lax.all_to_all(outgoing, "bag", split_axis=0, concat_axis=0, tiled=True),
        lax.all_to_all(slot_labels, "bag", split_axis=0, concat_axis=0, tiled=True),
    )
    count_slots = bags * heads_dev * capacity
    heads_here = local_width // HDIM
    slot_rows = incoming.reshape(count_slots, 3, local_width)
    labels_all = incoming_labels.reshape(count_slots)
    key_rows = slot_rows[:, 1].reshape(count_slots, heads_here, HDIM)
    value_rows = slot_rows[:, 2].reshape(count_slots, heads_here, HDIM)
    block_count = max(1, count_slots // 512)
    block_size = count_slots // block_count
    key_ok = labels_all >= 0

    def attend(operands):
        query_block, label_block = operands
        scores = jnp.einsum(
            "qhd,khd->hqk", query_block, key_rows, preferred_element_type=jnp.float32
        ) * HDIM ** (-0.5)
        admissible = (labels_all[None, :] == label_block[:, None]) & key_ok[None, :]
        scores = jnp.where(admissible[None, :, :], scores, far_below)
        shifted = jnp.exp(scores - jnp.max(scores, axis=-1, keepdims=True))
        weights = (shifted / jnp.sum(shifted, axis=-1, keepdims=True)).astype(jnp.bfloat16)
        mixed = jnp.einsum("hqk,khd->qhd", weights, value_rows, preferred_element_type=jnp.float32)
        return mixed.astype(jnp.bfloat16).reshape(block_size, local_width)

    query_blocks = slot_rows[:, 0].reshape(block_count, block_size, heads_here, HDIM)
    outputs = lax.map(attend, (query_blocks, labels_all.reshape(block_count, block_size)))
    outputs = outputs.reshape(bags, heads_dev, capacity, local_width)
    own_live = jnp.take(token_live, place, axis=0)
    returned = lax.all_to_all(outputs, "bag", split_axis=0, concat_axis=0, tiled=True)
    flattened = returned.reshape(bags * heads_dev * capacity, local_width)
    row_index = (
        route_rows * heads_dev + jnp.arange(heads_dev, dtype=jnp.int32)[:, None]
    ) * capacity + slot_rank
    chosen = jnp.take(flattened, row_index.reshape(-1), axis=0).reshape(
        heads_dev, tok_dev, local_width
    )
    own_rows = lax.all_to_all(chosen, "head", split_axis=0, concat_axis=2, tiled=True)
    picked = own_rows[0]
    return jnp.where(own_live[:, None], picked, jnp.zeros((), jnp.bfloat16))


def solution(mesh):
    placed = (
        P("bag", "head", None, None, None),
        P("bag"),
        P("bag", None),
        P("bag"),
        P(),
        P(),
        P(None, None, "head"),
    )
    return jax.shard_map(
        shards, mesh=mesh, in_specs=placed, out_specs=P(("bag", "head"), None), check_vma=False
    )
```

profile of v0, /device:TPU:0, one launch (start us, length us, event | category | flops | bytes accessed | tf_op | source)
XLA Modules:
  0.0 195.3 jit_solution(16876934549669467401)
XLA Ops:
  0.8 1.1 bitcast_multiply_fusion
  2.0 0.8 fusion.137
  2.8 1.3 collective-permute-start.1
  4.1 3.7 %collective-permute-start = (bf16[1,16,16,512]{3,2,1,0:T(8,128)(2,1)}, bf16[1,16,16,512]{3,2,1,0:T(8,128)(2,1)}, u32[]{:S(2)}, u32[]{:S(2)}) collective-permute-start(bf16[1,16,16,512]{3,2,1,0:T(8,128)(2,1)} %get-tuple-element.71), channel_id=1, source_target_pairs={{0,1},{1,2},{2,3},{4,5},{5,6},{6,7},{8,9},{9,10},{10,11},{12,13},{... | collective-permute-start | bytes 786440 | tf_op jit(solution)/shard_map/ppermute | solution.py:21
  7.8 0.8 fusion.51
  8.6 0.7 iota_compare_fusion.6
  9.6 0.9 select_reduce_fusion
  10.6 0.6 fusion.49
  11.2 0.6 and_reduce_fusion
  12.1 5.0 %gather_fusion.2 = s32[768]{0:T(1024)S(1)} fusion(s32[512]{0:T(512)S(1)} %copy-done.2, s32[1024]{0:T(1024)S(1)} %pad_clamp_fusion.1), kind=kCustom, calls=%fused_computation.2 | custom fusion | bytes 9216 | tf_op jit(solution)/shard_map/gather | solution.py:110
  17.2 4.8 %gather_fusion.1 = pred[768]{0:T(1024)(128)(4,1)S(1)} fusion(pred[512]{0:T(512)(128)(4,1)S(1)} %fusion.174, s32[1024]{0:T(1024)S(1)} %pad_clamp_fusion.1), kind=kCustom, calls=%fused_computation.1 | custom fusion | bytes 4608 | tf_op jit(solution)/shard_map/gather | solution.py:109
  22.1 0.7 select_n.105
  22.8 7.3 %all-to-all-start.1 = ((s32[8,1,96]{2,1,0:T(1,128)}), s32[8,1,96]{2,1,0:T(1,128)S(1)}, u32[]{:S(2)}, u32[]{:S(2)}) async-start(s32[8,1,96]{2,1,0:T(1,128)} %bitcast.69), calls=%async_computation.1 | async-start | bytes 8192 | tf_op jit(solution)/shard_map/all_to_all | solution.py:116
  30.1 1.1 broadcast_multiply_fusion
  31.7 1.2 fusion.77
  32.9 1.7 select_maximum_fusion
  34.6 0.6 fusion.136
  35.2 2.7 %fusion.135 = (bf16[2,16,16,512]{3,2,1,0:T(8,128)(2,1)S(1)}, bf16[2,16,16,512]{3,2,1,0:T(8,128)(2,1)S(1)}, bf16[2,16,16,512]{3,2,1,0:T(8,128)(2,1)S(1)}, bf16[2,...) fusion(bf16[4,18,18,512]{3,2,1,0:T(8,128)(2,1)S(1)} %select_max, ...), kind=kLoop, calls=%fused_computation.189 | loop fusion | bytes 19922944 | tf_op jit(solution)/shard_map/slice | solution.py:54
  38.8 0.3 fusion.58
  39.1 1.1 pad_maximum_fusion.1
  41.4 0.3 fusion.68
  46.2 0.3 fusion.48
  46.5 0.3 fusion.37
  46.9 7.4 %all_gather.3 = bf16[512,512]{1,0:T(8,128)(2,1)S(1)} all-gather(bf16[128,512]{1,0:T(8,128)(2,1)S(1)} %bitcast.227), channel_id=1, replica_groups=mesh['bag'=8,'head'=4] {'head'}, dimensions={0}, use_global_device_ids=true | all-gather | bytes 655360 | tf_op jit(solution)/shard_map/all_gather | solution.py:85
  54.3 1.3 fusion.8
  55.9 3.4 %fusion.20 = bf16[512,3,512]{2,0,1:T(8,128)(2,1)S(1)} fusion(bf16[3,2048,512]{2,1,0:T(8,128)(2,1)S(1)} %bitcast.236, bf16[512,2048]{1,0:T(8,128)(2,1)S(1)} %get-tuple-element.74, f32[512]{0:T(512)S(1)} %add_rsqrt_fusion), kind=kOutput, calls=%fused_computation.36 | convolution fusion | flops 3225157632 | bytes 9963520 | tf_op jit(solution)/shard_map/rd,mdc->rmc/dot_general | solution.py:43
  59.3 1.4 copy.40
  60.7 4.9 %gather_fusion = bf16[768,3,512]{2,1,0:T(4,128)(2,1)} fusion(bf16[512,3,512]{2,1,0:T(4,128)(2,1)S(1)} %copy.40, s32[1024]{0:T(1024)S(1)} %pad_clamp_fusion.2), kind=kCustom, calls=%fused_computation | custom fusion | bytes 4721664 | tf_op jit(solution)/shard_map/jit(_take)/gather | solution.py:111
  65.6 4.0 %copy_select_fusion = bf16[8,96,3,512]{3,1,2,0:T(8,128)(2,1)} fusion(bf16[8,96,3,512]{3,2,1,0:T(4,128)(2,1)} %bitcast.190, pred[8,96]{1,0:T(8,128)(4,1)S(1)} %compare_and_fusion.1), kind=kLoop, calls=%fused_computation.26 | loop fusion | flops 1179648 | bytes 4719360 | tf_op jit(solution)/shard_map/jit(_take)/select_n | solution.py:111
  69.6 5.7 %all-to-all-start = ((bf16[8,96,3,512]{3,1,2,0:T(8,128)(2,1)}), bf16[8,96,3,512]{3,1,2,0:T(8,128)(2,1)}, u32[]{:S(2)}, u32[]{:S(2)}) async-start(bf16[8,96,3,512]{3,1,2,0:T(8,128)(2,1)} %copy_select_fusion), calls=%async_computation | async-start | bytes 4718592 | tf_op jit(solution)/shard_map/all_to_all | solution.py:115
  75.3 0.5 broadcast.316
  75.8 0.7 reduce.7
  76.6 0.5 compare_and_fusion
  77.1 52.8 %all-to-all-done = bf16[8,96,3,512]{3,1,2,0:T(8,128)(2,1)} async-done(((bf16[8,96,3,512]{3,1,2,0:T(8,128)(2,1)}), bf16[8,96,3,512]{3,1,2,0:T(8,128)(2,1)}, u32[]{:S(2)}, u32[]{:S(2)}) %all-to-all-start) | async-done | bytes 2359328 | tf_op jit(solution)/shard_map/all_to_all | solution.py:115
  129.8 1.8 copy.42
  131.8 1.2 copy.43
  133.5 10.2 %fusion.138 = (f32[8,768]{1,0:T(8,128)S(1)}, f32[8,768,768]{1,2,0:T(8,128)}) fusion(pred[768,768]{0,1:T(8,128)(4,1)S(1)} %compare_and_fusion, bf16[768,8,64]{0,2,1:T(8,128)(2,1)S(1)} %bitcast.225, bf16[768,8,64]{0,2,1:T(8,128)(2,1)S(1)} %bitcast.226), kind=kOutput, calls=%fused_computation.192 | convolution fusion | flops 622854912 | bytes 21061632 | tf_op jit(solution)/shard_map/while/body/eval_jaxpr/sub | solution.py:135
  143.8 8.1 %fusion.24 = bf16[768,8,64]{0,2,1:T(8,128)(2,1)S(1)} fusion(bf16[768,8,64]{0,2,1:T(8,128)(2,1)S(1)} %bitcast.224, f32[8,768,768]{1,2,0:T(8,128)} %get-tuple-element.76, f32[8,768]{1,0:T(8,128)S(1)} %get-tuple-element.75), kind=kOutput, calls=%fused_computation.38 | convolution fusion | flops 613810176 | bytes 20471808 | tf_op jit(solution)/shard_map/while/body/eval_jaxpr/hqk,khd->qhd/dot_general | solution.py:137
  151.9 1.1 copy.48
  153.0 1.7 reshape.384
  154.7 3.6 %all-to-all-start.2 = ((bf16[8,4,24,512]{3,2,1,0:T(8,128)(2,1)}), bf16[8,4,24,512]{3,2,1,0:T(8,128)(2,1)S(1)}, u32[]{:S(2)}, u32[]{:S(2)}) async-start(bf16[8,4,24,512]{3,2,1,0:T(8,128)(2,1)} %reshape.384), calls=%async_computation.2 | async-start | bytes 1572864 | tf_op jit(solution)/shard_map/all_to_all | solution.py:144
  158.4 20.3 %all-to-all-done.2 = bf16[8,4,24,512]{3,2,1,0:T(8,128)(2,1)S(1)} async-done(((bf16[8,4,24,512]{3,2,1,0:T(8,128)(2,1)}), bf16[8,4,24,512]{3,2,1,0:T(8,128)(2,1)S(1)}, u32[]{:S(2)}, u32[]{:S(2)}) %all-to-all-start.2) | async-done | bytes 786464 | tf_op jit(solution)/shard_map/all_to_all | solution.py:144
  178.8 2.0 %gather_fusion.3 = bf16[512,512]{1,0:T(8,128)(2,1)S(1)} fusion(bf16[768,512]{1,0:T(8,128)(2,1)S(1)} %bitcast.189, s32[1024]{0:T(1024)S(1)} %pad_clamp_fusion), kind=kCustom, calls=%fused_computation.3 | custom fusion | bytes 1050624 | tf_op jit(solution)/shard_map/jit(_take)/gather | solution.py:149
  180.7 0.9 broadcast_select_fusion.1
  181.7 3.5 %all-to-all-start.3 = ((bf16[4,128,512]{2,1,0:T(8,128)(2,1)}), bf16[4,128,512]{2,1,0:T(8,128)(2,1)S(1)}, u32[]{:S(2)}, u32[]{:S(2)}) async-start(bf16[4,128,512]{2,1,0:T(8,128)(2,1)} %broadcast_select_fusion.1), calls=%async_computation.3 | async-start | bytes 1048576 | tf_op jit(solution)/shard_map/all_to_all | solution.py:152
  185.2 8.7 %all-to-all-done.3 = bf16[4,128,512]{2,1,0:T(8,128)(2,1)S(1)} async-done(((bf16[4,128,512]{2,1,0:T(8,128)(2,1)}), bf16[4,128,512]{2,1,0:T(8,128)(2,1)S(1)}, u32[]{:S(2)}, u32[]{:S(2)}) %all-to-all-start.3) | async-done | bytes 524320 | tf_op jit(solution)/shard_map/all_to_all | solution.py:152
  193.9 0.4 copy.49
  194.4 0.9 broadcast_select_fusion
  (76 shorter events, 9.0 us)
Async XLA Ops:
  0.0 54.3 %copy-start = (bf16[512,2048]{1,0:T(8,128)(2,1)S(1)}, bf16[512,2048]{1,0:T(8,128)(2,1)}, u32[]{:S(2)}) copy-start(bf16[512,2048]{1,0:T(8,128)(2,1)} %param.12) | copy-start | bytes 6291460
  0.0 12.0 %copy-start.2 = (s32[512]{0:T(512)S(1)}, s32[512]{0:T(512)}, u32[]{:S(2)}) copy-start(s32[512]{0:T(512)} %param.10) | copy-start | bytes 6148
  2.8 30.1 %collective-permute-start.1 = (bf16[1,16,16,512]{3,2,1,0:T(8,128)(2,1)}, bf16[1,16,16,512]{3,2,1,0:T(8,128)(2,1)S(1)}, u32[]{:S(2)}, u32[]{:S(2)}) collective-permute-start(bf16[1,16,16,512]{3,2,1,0:T(8,128)(2,1)} %get-tuple-element.72), channel_id=1, source_target_pairs={{1,0},{2,1},{3,2},{5,4},{6,5},{7,6},{9,8},{10,9},{11,10},{13,12},{... | collective-permute-start | bytes 786440 | tf_op jit(solution)/shard_map/ppermute | solution.py:23
  4.1 28.8 %collective-permute-start = (bf16[1,16,16,512]{3,2,1,0:T(8,128)(2,1)}, bf16[1,16,16,512]{3,2,1,0:T(8,128)(2,1)}, u32[]{:S(2)}, u32[]{:S(2)}) collective-permute-start(bf16[1,16,16,512]{3,2,1,0:T(8,128)(2,1)} %get-tuple-element.71), channel_id=1, source_target_pairs={{0,1},{1,2},{2,3},{4,5},{5,6},{6,7},{8,9},{9,10},{10,11},{12,13},{... | collective-permute-start | bytes 786440 | tf_op jit(solution)/shard_map/ppermute | solution.py:21
  22.8 46.8 %all-to-all-start.1 = ((s32[8,1,96]{2,1,0:T(1,128)}), s32[8,1,96]{2,1,0:T(1,128)S(1)}, u32[]{:S(2)}, u32[]{:S(2)}) async-start(s32[8,1,96]{2,1,0:T(1,128)} %bitcast.69), calls=%async_computation.1 | async-start | bytes 8192 | tf_op jit(solution)/shard_map/all_to_all | solution.py:116
  35.2 2.7 %copy-start.3 = (bf16[27,512,128]{2,1,0:T(8,128)(2,1)S(1)}, bf16[27,512,128]{2,1,0:T(8,128)(2,1)}, u32[]{:S(2)}) copy-start(bf16[27,512,128]{2,1,0:T(8,128)(2,1)} %param.11) | copy-start | bytes 10616836
  46.5 9.2 %slice-start = ((s8[6291456]{0:T(1024)(128)(4,1)}), s8[4194304]{0:T(1024)(128)(4,1)S(1)}, s32[]{:S(2)}) async-start(s8[6291456]{0:T(1024)(128)(4,1)} %bitcast.235), calls=%async_computation.4 | async-start | bytes 8388608
  54.3 1.6 slice-start.1
  69.6 60.2 %all-to-all-start = ((bf16[8,96,3,512]{3,1,2,0:T(8,128)(2,1)}), bf16[8,96,3,512]{3,1,2,0:T(8,128)(2,1)}, u32[]{:S(2)}, u32[]{:S(2)}) async-start(bf16[8,96,3,512]{3,1,2,0:T(8,128)(2,1)} %copy_select_fusion), calls=%async_computation | async-start | bytes 4718592 | tf_op jit(solution)/shard_map/all_to_all | solution.py:115
  133.5 10.2 %copy-start.4 = (bf16[768,1,512]{0,2,1:T(8,128)(2,1)S(1)}, bf16[768,1,512]{0,2,1:T(8,128)(2,1)}, u32[]{:S(2)}) copy-start(bf16[768,1,512]{0,2,1:T(8,128)(2,1)} %copy.43) | copy-start | bytes 2359300
  151.9 6.5 %copy-start.5 = (s32[512,1]{0,1:T(1,128)S(1)}, s32[512,1]{0,1:T(1,128)}, u32[]{:S(2)}) copy-start(s32[512,1]{0,1:T(1,128)} %param.9) | copy-start | bytes 6148
  154.7 24.0 %all-to-all-start.2 = ((bf16[8,4,24,512]{3,2,1,0:T(8,128)(2,1)}), bf16[8,4,24,512]{3,2,1,0:T(8,128)(2,1)S(1)}, u32[]{:S(2)}, u32[]{:S(2)}) async-start(bf16[8,4,24,512]{3,2,1,0:T(8,128)(2,1)} %reshape.384), calls=%async_computation.2 | async-start | bytes 1572864 | tf_op jit(solution)/shard_map/all_to_all | solution.py:144
  178.8 16.6 %copy-start.1 = (bf16[512,2048]{1,0:T(8,128)(2,1)S(1)}, bf16[512,2048]{1,0:T(8,128)(2,1)}, u32[]{:S(2)}) copy-start(bf16[512,2048]{1,0:T(8,128)(2,1)} %param.12) | copy-start | bytes 6291460
  181.7 12.3 %all-to-all-start.3 = ((bf16[4,128,512]{2,1,0:T(8,128)(2,1)}), bf16[4,128,512]{2,1,0:T(8,128)(2,1)S(1)}, u32[]{:S(2)}, u32[]{:S(2)}) async-start(bf16[4,128,512]{2,1,0:T(8,128)(2,1)} %broadcast_select_fusion.1), calls=%async_computation.3 | async-start | bytes 1048576 | tf_op jit(solution)/shard_map/all_to_all | solution.py:152
where the time goes:
time: 196 us; the launch traced here: 195 us
  waiting for transfers between devices  81.8 us (42%)
  matrix products  32 us (16%)
  local copies, waits for them, and re-layouts  31.2 us (16%)
  starting transfers between devices  25.1 us (13%)
  other arithmetic  16.5 us (8%)
  blocking collectives  7.39 us (4%)
    all_to_all x1, waiting for transfers between devices, shards(): lax.all_to_all(outgoing, 'bag', split_axis=0, concat_axis=0, tiled=True)  52.8 us
    all_to_all x1, waiting for transfers between devices, shards(): lax.all_to_all(outputs, 'bag', split_axis=0, concat_axis=0, tiled=True)  20.3 us
    sub x1, matrix products, attend(): shifted = jnp.exp(scores - jnp.max(scores, axis=-1, keepdims=True))  10.2 us
    dot_general x27, matrix products, convolve(): jnp.dot(window.reshape(-1, depth_in), conv_weight[9 * offset_t + 3 * offs...  8.87 us
    all_to_all x1, waiting for transfers between devices, shards(): lax.all_to_all(chosen, 'head', split_axis=0, concat_axis=2, tiled=True)  8.69 us
    dot_general x1, matrix products, attend(): jnp.einsum('hqk,khd->qhd', weights, value_rows, preferred_element_type=jn...  8.12 us
    all_gather x1, blocking collectives, shards(): lax.all_gather(patches, 'head', axis=0, tiled=True)  7.39 us
    all_to_all x1, starting transfers between devices, shards(): lax.all_to_all(slot_labels, 'bag', split_axis=0, concat_axis=0, tiled=True)  7.28 us
  transfers between devices with their start and end apart: 6, of which 3 were waited for; matrix products, arithmetic and copies ran while one was open for 25% of the time, Pallas kernels for 0%

commit v1 on v0

v1 whole, which is shorter than its diff:
```python
import functools
import jax
import jax.numpy as jnp
from jax import lax
from jax.experimental import pallas as pl
from jax.experimental.pallas import tpu as pltpu
from jax.sharding import PartitionSpec as P

HDIM = 64
TAPS = 3

epsilon = 1e-06
far_below = -1e30

SMEM = pl.BlockSpec(memory_space=pltpu.SMEM)
VMEM = pl.BlockSpec(memory_space=pltpu.VMEM)


def slot_onehot(route_row, bags, cap, keep):
    tokens = route_row.shape[1]
    bag_ids = lax.broadcasted_iota(jnp.int32, (bags, tokens), 0)
    onehot = (bag_ids == route_row).astype(jnp.float32)
    before = (
        lax.broadcasted_iota(jnp.int32, (tokens, tokens), 0)
        < lax.broadcasted_iota(jnp.int32, (tokens, tokens), 1)
    )
    earlier = jnp.dot(
        onehot.astype(jnp.bfloat16),
        before.astype(jnp.float32).astype(jnp.bfloat16),
        preferred_element_type=jnp.float32,
    )
    rank = jnp.sum(earlier * onehot, axis=0, keepdims=True).astype(jnp.int32)
    slot = route_row * cap + rank
    if keep is not None:
        slot = jnp.where(keep, slot, -1)
    slot_ids = lax.broadcasted_iota(jnp.int32, (bags * cap, tokens), 0)
    return (slot_ids == slot).astype(jnp.float32).astype(jnp.bfloat16)


def conv_kernel(
    bags, cap, rows, cols, frames, scal_ref, x_ref, prev_ref, next_ref, w_ref, route_ref, out_ref, grid_ref
):
    count, place = scal_ref[0], scal_ref[1]
    area = rows * cols
    first = place * frames

    def live(frame):
        return jnp.logical_and(frame >= 0, frame < count)

    def masked(value, frame):
        return jnp.where(live(frame), value, jnp.zeros_like(value))

    inputs = [masked(prev_ref[...], first - 1)]
    for f in range(frames):
        inputs.append(masked(x_ref[f * area : (f + 1) * area, :], first + f))
    inputs.append(masked(next_ref[...], first + frames))
    stacked = jnp.concatenate(
        [jnp.concatenate(inputs[t : t + frames], axis=0) for t in range(TAPS)], axis=1
    )
    plane = TAPS * TAPS
    products = []
    for p in range(0, plane, 2):
        pair = [
            jnp.concatenate([w_ref[plane * t + q] for t in range(TAPS)], axis=0)
            for q in range(p, min(p + 2, plane))
        ]
        weight = pair[0] if len(pair) == 1 else jnp.concatenate(pair, axis=1)
        value = jnp.dot(stacked, weight, preferred_element_type=jnp.float32)
        chans = w_ref.shape[2]
        for q in range(len(pair)):
            products.append(value[:, q * chans : (q + 1) * chans].reshape(frames, rows, cols, chans))
    chans = w_ref.shape[2]
    blank = jnp.zeros((frames, 1, cols, chans), jnp.float32)
    column = lax.broadcasted_iota(jnp.int32, (frames * area, chans), 0) % cols
    total = None
    for e in range(TAPS):
        up, mid, down = products[e], products[TAPS + e], products[2 * TAPS + e]
        merged = (
            mid
            + jnp.concatenate([blank, up[:, : rows - 1]], axis=1)
            + jnp.concatenate([down[:, 1:], blank], axis=1)
        ).reshape(frames * area, chans)
        if e == 0:
            merged = jnp.where(column == 0, 0.0, pltpu.roll(merged, 1, axis=0))
        elif e == 2:
            merged = jnp.where(column == cols - 1, 0.0, pltpu.roll(merged, frames * area - 1, axis=0))
        total = merged if total is None else total + merged
    for f in range(frames):
        part = total[f * area : (f + 1) * area]
        grid_ref[f * area : (f + 1) * area, :] = jnp.where(live(first + f), part, 0.0)
    pieces = [[None] * 2 for _ in range(2)]
    for odd in range(2):
        half = grid_ref[pl.ds(odd, frames * area // 2, stride=2), :]
        half = half.reshape(frames * rows // 2, 2, cols // 2, chans)
        for i in range(2):
            pieces[i][odd] = half[:, i].reshape(frames * area // 4, chans)
    patches = jnp.concatenate(
        [pieces[0][0], pieces[0][1], pieces[1][0], pieces[1][1]], axis=1
    ).astype(jnp.bfloat16)
    route_row = route_ref[pl.ds(place, 1), :]
    onehot = slot_onehot(route_row, bags, cap, None)
    out_ref[...] = jnp.dot(onehot, patches, preferred_element_type=jnp.float32).astype(jnp.bfloat16)


def attention_kernel(heads, q_ref, k_ref, v_ref, lab_col_ref, lab_row_ref, out_ref, bias_ref):
    @pl.when(pl.program_id(1) == 0)
    def _():
        same = jnp.logical_and(lab_col_ref[...] == lab_row_ref[...], lab_row_ref[...] >= 0)
        bias_ref[...] = jnp.where(same, 0.0, far_below)

    outs = []
    for h in range(heads):
        cols = slice(h * HDIM, (h + 1) * HDIM)
        scores = lax.dot_general(
            q_ref[:, cols], k_ref[:, cols], (((1,), (1,)), ((), ())), preferred_element_type=jnp.float32
        )
        scores = scores * HDIM ** (-0.5) + bias_ref[...]
        top = jnp.max(scores, axis=-1, keepdims=True)
        shifted = jnp.exp(scores - top)
        norm = jnp.sum(shifted, axis=-1, keepdims=True)
        mixed = jnp.dot(shifted.astype(jnp.bfloat16), v_ref[:, cols], preferred_element_type=jnp.float32)
        outs.append(mixed / norm)
    out_ref[...] = jnp.concatenate(outs, axis=1).astype(jnp.bfloat16)


def collect_kernel(bags, cap, frames, heads, scal_ref, recv_ref, route_ref, out_ref):
    count, place = scal_ref[0], scal_ref[1]
    route_row = route_ref[pl.ds(place, 1), :]
    tokens = route_row.shape[1]
    per_frame = tokens // frames
    frame = place * frames + lax.broadcasted_iota(jnp.int32, (1, tokens), 1) // per_frame
    onehot = slot_onehot(route_row, bags, cap, frame < count)
    slots = bags * cap
    width = recv_ref.shape[1]
    for h in range(heads):
        picked = lax.dot_general(
            onehot,
            recv_ref[h * slots : (h + 1) * slots, :],
            (((0,), (0,)), ((), ())),
            preferred_element_type=jnp.float32,
        )
        out_ref[:, h * width : (h + 1) * width] = picked.astype(jnp.bfloat16)


def shards(latents, frame_counts, routes, samples, conv_weight, embed_weight, qkv_weight):
    frames_dev, rows, cols, depth = latents.shape[1:]
    heads_dev = lax.axis_size("head")
    bags = lax.axis_size("bag")
    place = lax.axis_index("head")
    frame_count = frame_counts[0]
    area = rows * cols
    tok_dev = frames_dev * area // 4
    cap = 3 * tok_dev // (2 * bags)
    slots = bags * cap
    local_width = qkv_weight.shape[2]
    chans = conv_weight.shape[2]

    tile = latents.reshape(frames_dev, area, depth)
    ends = heads_dev - 1
    prev_frame = lax.ppermute(tile[frames_dev - 1], "head", [(i, i + 1) for i in range(ends)])
    next_frame = lax.ppermute(tile[0], "head", [(i + 1, i) for i in range(ends)])

    route_rows = routes[:, 0].reshape(heads_dev, tok_dev)
    per_frame = tok_dev // frames_dev
    token_frame = (
        jnp.arange(heads_dev, dtype=jnp.int32)[:, None] * frames_dev
        + (jnp.arange(tok_dev, dtype=jnp.int32) // per_frame)[None, :]
    )
    token_live = token_frame < frame_count
    bag_ids = jnp.arange(bags, dtype=jnp.int32)
    counts = jnp.sum(
        ((route_rows[None] == bag_ids[:, None, None]) & token_live[None]).astype(jnp.int32), axis=2
    )
    notes = jnp.concatenate(
        [counts, jnp.broadcast_to(samples[:1][None, :], (bags, heads_dev))], axis=1
    )
    notes = lax.all_to_all(notes, "bag", split_axis=0, concat_axis=0, tiled=True)

    scal = jnp.stack([frame_count, place.astype(jnp.int32)])
    outgoing = pl.pallas_call(
        functools.partial(conv_kernel, bags, cap, rows, cols, frames_dev),
        out_shape=jax.ShapeDtypeStruct((slots, 4 * chans), jnp.bfloat16),
        in_specs=[SMEM, VMEM, VMEM, VMEM, VMEM, VMEM],
        out_specs=VMEM,
        scratch_shapes=[pltpu.VMEM((frames_dev * area, chans), jnp.float32)],
        name="conv",
    )(scal, tile.reshape(frames_dev * area, depth), prev_frame, next_frame, conv_weight, route_rows)

    arrived = lax.all_to_all(
        outgoing.reshape(bags, cap, 4 * chans), "bag", split_axis=0, concat_axis=0, tiled=True
    ).reshape(slots, 4 * chans)
    patches = lax.all_gather(arrived, "head", axis=0, tiled=True)

    embedded = jnp.dot(patches, embed_weight, preferred_element_type=jnp.float32).astype(jnp.bfloat16)
    widened = embedded.astype(jnp.float32)
    normed = (
        widened * lax.rsqrt(jnp.mean(widened * widened, axis=-1, keepdims=True) + epsilon)
    ).astype(jnp.bfloat16)
    count_slots = heads_dev * slots
    query, key, value = [
        jnp.dot(normed, qkv_weight[m], preferred_element_type=jnp.float32).astype(jnp.bfloat16)
        for m in range(3)
    ]

    live_count = notes[:, :heads_dev].T
    labels = jnp.where(
        jnp.arange(cap, dtype=jnp.int32)[None, None, :] < live_count[:, :, None],
        notes[:, heads_dev][None, :, None],
        -1,
    ).reshape(count_slots)

    pair = 2
    wide = pair * HDIM
    q_tile = 256
    attended = pl.pallas_call(
        functools.partial(attention_kernel, pair),
        out_shape=jax.ShapeDtypeStruct((count_slots, local_width), jnp.bfloat16),
        grid=(count_slots // q_tile, local_width // wide),
        in_specs=[
            pl.BlockSpec((q_tile, wide), lambda i, h: (i, h)),
            pl.BlockSpec((count_slots, wide), lambda i, h: (0, h)),
            pl.BlockSpec((count_slots, wide), lambda i, h: (0, h)),
            pl.BlockSpec((q_tile, 1), lambda i, h: (i, 0)),
            pl.BlockSpec((1, count_slots), lambda i, h: (0, 0)),
        ],
        out_specs=pl.BlockSpec((q_tile, wide), lambda i, h: (i, h)),
        scratch_shapes=[pltpu.VMEM((q_tile, count_slots), jnp.float32)],
        name="attention",
    )(query, key, value, labels.reshape(count_slots, 1), labels.reshape(1, count_slots))

    returned = lax.all_to_all(
        attended.reshape(heads_dev * bags, cap, local_width),
        ("head", "bag"),
        split_axis=0,
        concat_axis=0,
        tiled=True,
    ).reshape(count_slots, local_width)
    return pl.pallas_call(
        functools.partial(collect_kernel, bags, cap, frames_dev, heads_dev),
        out_shape=jax.ShapeDtypeStruct((tok_dev, heads_dev * local_width), jnp.bfloat16),
        in_specs=[SMEM, VMEM, VMEM],
        out_specs=VMEM,
        name="collect",
    )(scal, returned, route_rows)


def solution(mesh):
    placed = (
        P("bag", "head", None, None, None),
        P("bag"),
        P("bag", None),
        P("bag"),
        P(),
        P(),
        P(None, None, "head"),
    )
    return jax.shard_map(
        shards, mesh=mesh, in_specs=placed, out_specs=P(("bag", "head"), None), check_vma=False
    )
```

time: 196 us -> 104 us (0.53)
  waiting for transfers between devices: 81.8 us -> 6.57 us
  blocking collectives: 7.39 us -> 35.6 us
  local copies, waits for them, and re-layouts: 31.2 us -> 6.36 us
  Pallas kernels: 0 us -> 24.3 us
  matrix products: 32 us -> 11.8 us
  other arithmetic: 16.5 us -> 1.58 us
  starting transfers between devices: 25.1 us -> 16.3 us
    all_to_all x4 -> x2, waiting for transfers between devices: 81.8 us -> 6.57 us  [the longest x1 6.56 us: shards(): lax.all_to_all(outgoing.reshape(bags, cap, 4 * chans), 'bag', split_axis=...]
    all_to_all x0 -> x1, blocking collectives: none -> 25.2 us  [shards(): lax.all_to_all(attended.reshape(heads_dev * bags, cap, local_width), ('he...]
    pallas_call x0 -> x3, Pallas kernels: none -> 24.3 us  [the longest x1 16.4 us: shards(): pl.pallas_call(functools.partial(attention_kernel, pair), out_shape=jax.S...]
    gather x6 -> x0, local copies, waits for them, and re-layouts: 16.8 us -> none  [the longest x2 5.1 us: shards(): samples[flat_index]]
    sub x1 -> x0, matrix products: 10.2 us -> none  [attend(): shifted = jnp.exp(scores - jnp.max(scores, axis=-1, keepdims=True))]
    dot_general x30 -> x4, matrix products: 21.8 us -> 11.8 us  [the longest x3 9.93 us: shards(): jnp.dot(normed, qkv_weight[m], preferred_element_type=jnp.float32)]
    all_to_all x4 -> x2, starting transfers between devices: 20.1 us -> 12.6 us  [the longest x1 6.62 us: shards(): lax.all_to_all(notes, 'bag', split_axis=0, concat_axis=0, tiled=True)]
    select_n x7 -> x1, other arithmetic: 5.95 us -> 0.07 us  [shards(): jnp.where(jnp.arange(cap, dtype=jnp.int32)[None, None, :] < live_count[:,...]
  transfers between devices with their start and end apart: 6 -> 4, of which waited for: 3 -> 1; matrix products, arithmetic and copies ran while one was open for 25% -> 6% of each run, Pallas kernels for 0% -> 5%
where the time goes in v1:
time: 104 us; the launch traced here: 103 us
  blocking collectives  35.6 us (34%)
  Pallas kernels  24.3 us (23%)
  starting transfers between devices  16.3 us (16%)
  matrix products  11.8 us (11%)
  waiting for transfers between devices  6.57 us (6%)
  local copies, waits for them, and re-layouts  6.36 us (6%)
  other arithmetic  1.58 us (2%)
    all_to_all x1, blocking collectives, shards(): lax.all_to_all(attended.reshape(heads_dev * bags, cap, local_width), ('he...  25.2 us
    pallas_call x1, Pallas kernels, shards(): pl.pallas_call(functools.partial(attention_kernel, pair), out_shape=jax.S...  16.4 us
    all_gather x1, blocking collectives, shards(): patches = lax.all_gather(arrived, 'head', axis=0, tiled=True)  10.4 us
    dot_general x3, matrix products, shards(): jnp.dot(normed, qkv_weight[m], preferred_element_type=jnp.float32)  9.93 us
    all_to_all x1, starting transfers between devices, shards(): lax.all_to_all(notes, 'bag', split_axis=0, concat_axis=0, tiled=True)  6.62 us
    all_to_all x1, waiting for transfers between devices, shards(): lax.all_to_all(outgoing.reshape(bags, cap, 4 * chans), 'bag', split_axis=...  6.56 us
    all_to_all x1, starting transfers between devices, shards(): lax.all_to_all(outgoing.reshape(bags, cap, 4 * chans), 'bag', split_axis=...  6 us
    pallas_call x1, Pallas kernels, shards(): pl.pallas_call(functools.partial(conv_kernel, bags, cap, rows, cols, fram...  5.49 us
  transfers between devices with their start and end apart: 4, of which 1 were waited for; matrix products, arithmetic and copies ran while one was open for 6% of the time, Pallas kernels for 5%

profile of v1, /device:TPU:0, one launch (start us, length us, event | category | flops | bytes accessed | tf_op | source)
XLA Modules:
  0.0 103.3 jit_solution(13267446567602754042)
XLA Ops:
  0.0 0.0 copy-start
  0.0 1.2 %fusion.25 = (bf16[1,1,16,16,512]{4,3,2,1,0:T(8,128)(2,1)S(1)}, bf16[1,1,16,16,512]{4,3,2,1,0:T(8,128)(2,1)S(1)}) fusion(bf16[1,2,16,16,512]{4,3,2,1,0:T(8,128)(2,1)} %param.7), kind=kLoop, calls=%fused_computation.33 | loop fusion | bytes 1048576 | tf_op jit(solution)/shard_map/slice | solution.py:161
  1.2 2.4 %collective-permute-start = (bf16[256,512]{1,0:T(8,128)(2,1)S(1)}, bf16[256,512]{1,0:T(8,128)(2,1)S(1)}, u32[]{:S(2)}, u32[]{:S(2)}) collective-permute-start(bf16[256,512]{1,0:T(8,128)(2,1)S(1)} %bitcast.40), channel_id=1, source_target_pairs={{0,1},{1,2},{2,3},{4,5},{5,6},{6,7},{8,9},{9,10},{10,11},{12,13},{... | collective-permute-start | bytes 786440 | tf_op jit(solution)/shard_map/ppermute | solution.py:160
  3.6 1.3 %collective-permute-start.1 = (bf16[256,512]{1,0:T(8,128)(2,1)S(1)}, bf16[256,512]{1,0:T(8,128)(2,1)S(1)}, u32[]{:S(2)}, u32[]{:S(2)}) collective-permute-start(bf16[256,512]{1,0:T(8,128)(2,1)S(1)} %bitcast.39), channel_id=1, source_target_pairs={{1,0},{2,1},{3,2},{5,4},{6,5},{7,6},{9,8},{10,9},{11,10},{13,12},{... | collective-permute-start | bytes 786440 | tf_op jit(solution)/shard_map/ppermute | solution.py:161
  5.6 0.1 add_compare_fusion
  5.7 0.8 convert_reduce_fusion
  6.5 1.2 %slice.31 = s32[1]{0:T(128)} slice(s32[512]{0:T(512)} %param.10), slice={[0:1]} | slice | bytes 8 | tf_op jit(solution)/shard_map/slice | solution.py:175
  7.7 0.6 pad_bitcast_fusion
  8.4 0.7 copy.15
  9.0 6.6 %all-to-all-start.1 = ((s32[8,1,8]{2,1,0:T(1,128)}), s32[8,1,8]{2,1,0:T(1,128)S(1)}, u32[]{:S(2)}, u32[]{:S(2)}) async-start(s32[8,1,8]{2,1,0:T(1,128)} %copy.15), calls=%async_computation.1 | async-start | bytes 8192 | tf_op jit(solution)/shard_map/all_to_all | solution.py:177
  15.6 0.6 pad_add_fusion.scal_ref
  16.2 0.0 collective-permute-done.prev_ref
  16.2 0.0 copy-start.1
  16.2 0.0 collective-permute-done.1.next_ref
  16.2 0.0 copy-start.2
  16.3 0.7 copy-done.1
  16.9 0.1 copy-done.2
  17.0 5.5 %conv.1 = bf16[192,512]{1,0:T(8,128)(2,1)} custom-call(s32[2]{0:T(128)} %pad_add_fusion.scal_ref, bf16[512,512]{1,0:T(8,128)(2,1)} %bitcast.36, bf16[256,512]{1,0:T(8,128)(2,1)} %copy-done.1, bf16[256,512]{1,0:T(8,128)(2,1)} %copy-done.2, bf16[27,512,128]{2,1,0:T(8,128)(2,1)} %w_ref.1, s32[4,128]{1,0:T(4,128)} %bitcast.44), custom_call_target="tpu_custom_call" | custom-call | tf_op jit(solution)/shard_map/conv/pallas_call | solution.py:180
  22.5 0.0 all-to-all-done.1
  22.5 6.0 %all-to-all-start = ((bf16[8,24,512]{2,1,0:T(8,128)(2,1)}), bf16[8,24,512]{2,1,0:T(8,128)(2,1)S(1)}, u32[]{:S(2)}, u32[]{:S(2)}) async-start(bf16[8,24,512]{2,1,0:T(8,128)(2,1)} %bitcast.37), calls=%async_computation | async-start | bytes 393216 | tf_op jit(solution)/shard_map/all_to_all | solution.py:189
  28.5 0.1 copy.16
  28.6 0.2 slice_reduce_fusion
  28.8 0.1 fusion.20
  28.9 0.9 select_n.37.lab_col_ref
  29.8 0.7 select_n.36.lab_row_ref
  30.5 6.6 %all-to-all-done = bf16[8,24,512]{2,1,0:T(8,128)(2,1)S(1)} async-done(((bf16[8,24,512]{2,1,0:T(8,128)(2,1)}), bf16[8,24,512]{2,1,0:T(8,128)(2,1)S(1)}, u32[]{:S(2)}, u32[]{:S(2)}) %all-to-all-start) | async-done | bytes 196640 | tf_op jit(solution)/shard_map/all_to_all | solution.py:189
  37.0 10.4 %all_gather.3 = bf16[768,512]{1,0:T(8,128)(2,1)S(1)} all-gather(bf16[192,512]{1,0:T(8,128)(2,1)S(1)} %bitcast.38), channel_id=1, replica_groups=mesh['bag'=8,'head'=4] {'head'}, dimensions={0}, use_global_device_ids=true | all-gather | bytes 983040 | tf_op jit(solution)/shard_map/all_gather | solution.py:192
  47.4 0.0 copy-done
  47.4 0.0 slice-start
  47.4 1.9 %fusion = (f32[768]{0:T(1024)S(1)}, bf16[768,2048]{1,0:T(8,128)(2,1)S(1)}) fusion(bf16[768,512]{1,0:T(8,128)(2,1)S(1)} %all_gather.3, bf16[512,2048]{1,0:T(8,128)(2,1)S(1)} %copy-done), kind=kOutput, calls=%fused_computation.2 | convolution fusion | flops 1616903424 | bytes 6032384 | tf_op jit(solution)/shard_map/dot_general | solution.py:194
  49.4 0.0 slice-start.1
  49.4 4.5 %fusion.17.v_ref = bf16[768,512]{1,0:T(8,128)(2,1)} fusion(bf16[3,2048,512]{2,1,0:T(8,128)(2,1)} %param.13, bf16[768,2048]{1,0:T(8,128)(2,1)S(1)} %get-tuple-element.8, f32[768]{0:T(1024)S(1)} %add_rsqrt_fusion), kind=kOutput, calls=%fused_computation.16 | convolution fusion | flops 1615724544 | bytes 6032384 | tf_op jit(solution)/shard_map/dot_general | solution.py:201
  53.8 0.0 slice-done
  53.8 0.0 slice-done.1
  53.8 2.7 %fusion.14.k_ref = bf16[768,512]{1,0:T(8,128)(2,1)} fusion(bf16[3,2048,512]{2,1,0:T(8,128)(2,1)S(1)} %bitcast.47, bf16[768,2048]{1,0:T(8,128)(2,1)S(1)} %get-tuple-element.8, f32[768]{0:T(1024)S(1)} %add_rsqrt_fusion), kind=kOutput, calls=%fused_computation.15 | convolution fusion | flops 1615724544 | bytes 6033408 | tf_op jit(solution)/shard_map/dot_general | solution.py:201
  56.6 2.7 %fusion.11.q_ref = bf16[768,512]{1,0:T(8,128)(2,1)} fusion(bf16[3,2048,512]{2,1,0:T(8,128)(2,1)S(1)} %bitcast.47, bf16[768,2048]{1,0:T(8,128)(2,1)S(1)} %get-tuple-element.8, f32[768]{0:T(1024)S(1)} %add_rsqrt_fusion), kind=kOutput, calls=%fused_computation.14 | convolution fusion | flops 1615724544 | bytes 6033408 | tf_op jit(solution)/shard_map/dot_general | solution.py:201
  59.3 16.4 %attention.1 = bf16[768,512]{1,0:T(8,128)(2,1)} custom-call(bf16[768,512]{1,0:T(8,128)(2,1)} %fusion.11.q_ref, bf16[768,512]{1,0:T(8,128)(2,1)} %fusion.14.k_ref, bf16[768,512]{1,0:T(8,128)(2,1)} %fusion.17.v_ref, s32[768,1]{1,0:T(8,128)} %select_n.37.lab_col_ref, s32[1,768]{1,0:T(1,128)} %select_n.36.lab_row_ref), custom_call_target="tpu_custom_call" | custom-call | tf_op jit(solution)/shard_map/attention/pallas_call | solution.py:215
  75.7 25.2 %all_to_all.22 = bf16[32,24,512]{2,1,0:T(8,128)(2,1)} all-to-all(bf16[32,24,512]{2,1,0:T(8,128)(2,1)} %bitcast.34), channel_id=1, replica_groups=mesh['bag'=8,'head'=4] {'head','bag'}, dimensions={0} | all-to-all | bytes 1572864 | tf_op jit(solution)/shard_map/all_to_all | solution.py:231
  100.9 2.4 %collect.1 = bf16[128,2048]{1,0:T(8,128)(2,1)} custom-call(s32[2]{0:T(128)} %pad_add_fusion.scal_ref, bf16[768,512]{1,0:T(8,128)(2,1)} %bitcast.35, s32[4,128]{1,0:T(4,128)} %bitcast.45), custom_call_target="tpu_custom_call" | custom-call | tf_op jit(solution)/shard_map/collect/pallas_call | solution.py:238
  (5 shorter events, 0.0 us)
Async XLA Ops:
  0.0 47.4 %copy-start = (bf16[512,2048]{1,0:T(8,128)(2,1)S(1)}, bf16[512,2048]{1,0:T(8,128)(2,1)}, u32[]{:S(2)}) copy-start(bf16[512,2048]{1,0:T(8,128)(2,1)} %param.12) | copy-start | bytes 6291460
  1.2 15.0 %collective-permute-start = (bf16[256,512]{1,0:T(8,128)(2,1)S(1)}, bf16[256,512]{1,0:T(8,128)(2,1)S(1)}, u32[]{:S(2)}, u32[]{:S(2)}) collective-permute-start(bf16[256,512]{1,0:T(8,128)(2,1)S(1)} %bitcast.40), channel_id=1, source_target_pairs={{0,1},{1,2},{2,3},{4,5},{5,6},{6,7},{8,9},{9,10},{10,11},{12,13},{... | collective-permute-start | bytes 786440 | tf_op jit(solution)/shard_map/ppermute | solution.py:160
  3.6 12.6 %collective-permute-start.1 = (bf16[256,512]{1,0:T(8,128)(2,1)S(1)}, bf16[256,512]{1,0:T(8,128)(2,1)S(1)}, u32[]{:S(2)}, u32[]{:S(2)}) collective-permute-start(bf16[256,512]{1,0:T(8,128)(2,1)S(1)} %bitcast.39), channel_id=1, source_target_pairs={{1,0},{2,1},{3,2},{5,4},{6,5},{7,6},{9,8},{10,9},{11,10},{13,12},{... | collective-permute-start | bytes 786440 | tf_op jit(solution)/shard_map/ppermute | solution.py:161
  9.0 13.5 %all-to-all-start.1 = ((s32[8,1,8]{2,1,0:T(1,128)}), s32[8,1,8]{2,1,0:T(1,128)S(1)}, u32[]{:S(2)}, u32[]{:S(2)}) async-start(s32[8,1,8]{2,1,0:T(1,128)} %copy.15), calls=%async_computation.1 | async-start | bytes 8192 | tf_op jit(solution)/shard_map/all_to_all | solution.py:177
  16.2 0.7 copy-start.1
  16.2 0.8 copy-start.2
  22.5 14.5 %all-to-all-start = ((bf16[8,24,512]{2,1,0:T(8,128)(2,1)}), bf16[8,24,512]{2,1,0:T(8,128)(2,1)S(1)}, u32[]{:S(2)}, u32[]{:S(2)}) async-start(bf16[8,24,512]{2,1,0:T(8,128)(2,1)} %bitcast.37), calls=%async_computation | async-start | bytes 393216 | tf_op jit(solution)/shard_map/all_to_all | solution.py:189
  47.4 6.4 %slice-start = ((s8[6291456]{0:T(1024)(128)(4,1)}), s8[2097152]{0:T(1024)(128)(4,1)S(1)}, s32[]{:S(2)}) async-start(s8[6291456]{0:T(1024)(128)(4,1)} %bitcast.46), calls=%async_computation.3 | async-start | bytes 4194304
  49.4 4.5 %slice-start.1 = ((s8[6291456]{0:T(1024)(128)(4,1)}), s8[4194304]{0:T(1024)(128)(4,1)S(1)}, s32[]{:S(2)}) async-start(s8[6291456]{0:T(1024)(128)(4,1)} %bitcast.46), calls=%async_computation.4 | async-start | bytes 8388608

commit v2 on v1

v2 whole, which is shorter than its diff:
```python
import functools
import jax
import jax.numpy as jnp
from jax import lax
from jax.experimental import pallas as pl
from jax.experimental.pallas import tpu as pltpu
from jax.sharding import PartitionSpec as P

HDIM = 64
TAPS = 3
SAMPLES = 4
LANES = 128

epsilon = 1e-06
far_below = -1e30

SMEM = pl.BlockSpec(memory_space=pltpu.SMEM)
VMEM = pl.BlockSpec(memory_space=pltpu.VMEM)


def slot_of(route_row, bags, cap, stride):
    tokens = route_row.shape[1]
    bag_ids = lax.broadcasted_iota(jnp.int32, (bags, tokens), 0)
    onehot = (bag_ids == route_row).astype(jnp.float32)
    before = (
        lax.broadcasted_iota(jnp.int32, (tokens, tokens), 0)
        < lax.broadcasted_iota(jnp.int32, (tokens, tokens), 1)
    )
    earlier = jnp.dot(
        onehot.astype(jnp.bfloat16),
        before.astype(jnp.float32).astype(jnp.bfloat16),
        preferred_element_type=jnp.float32,
    )
    rank = jnp.sum(earlier * onehot, axis=0, keepdims=True).astype(jnp.int32)
    return route_row * stride + rank


def onehot_of(slot, slots):
    slot_ids = lax.broadcasted_iota(jnp.int32, (slots, slot.shape[1]), 0)
    return (slot_ids == slot).astype(jnp.float32).astype(jnp.bfloat16)


def conv_kernel(
    bags, cap, rows, cols, frames, scal_ref, x_ref, prev_ref, next_ref, w_ref, route_ref, out_ref, grid_ref
):
    count, place, sample = scal_ref[0], scal_ref[1], scal_ref[2]
    area = rows * cols
    first = place * frames

    def live(frame):
        return jnp.logical_and(frame >= 0, frame < count)

    def masked(value, frame):
        return jnp.where(live(frame), value, jnp.zeros_like(value))

    inputs = [masked(prev_ref[...], first - 1)]
    for f in range(frames):
        inputs.append(masked(x_ref[f * area : (f + 1) * area, :], first + f))
    inputs.append(masked(next_ref[...], first + frames))
    stacked = jnp.concatenate(
        [jnp.concatenate(inputs[t : t + frames], axis=0) for t in range(TAPS)], axis=1
    )
    plane = TAPS * TAPS
    products = []
    for p in range(0, plane, 2):
        pair = [
            jnp.concatenate([w_ref[plane * t + q] for t in range(TAPS)], axis=0)
            for q in range(p, min(p + 2, plane))
        ]
        weight = pair[0] if len(pair) == 1 else jnp.concatenate(pair, axis=1)
        value = jnp.dot(stacked, weight, preferred_element_type=jnp.float32)
        chans = w_ref.shape[2]
        for q in range(len(pair)):
            products.append(value[:, q * chans : (q + 1) * chans].reshape(frames, rows, cols, chans))
    chans = w_ref.shape[2]
    blank = jnp.zeros((frames, 1, cols, chans), jnp.float32)
    column = lax.broadcasted_iota(jnp.int32, (frames * area, chans), 0) % cols
    total = None
    for e in range(TAPS):
        up, mid, down = products[e], products[TAPS + e], products[2 * TAPS + e]
        merged = (
            mid
            + jnp.concatenate([blank, up[:, : rows - 1]], axis=1)
            + jnp.concatenate([down[:, 1:], blank], axis=1)
        ).reshape(frames * area, chans)
        if e == 0:
            merged = jnp.where(column == 0, 0.0, pltpu.roll(merged, 1, axis=0))
        elif e == 2:
            merged = jnp.where(column == cols - 1, 0.0, pltpu.roll(merged, frames * area - 1, axis=0))
        total = merged if total is None else total + merged
    for f in range(frames):
        part = total[f * area : (f + 1) * area]
        grid_ref[f * area : (f + 1) * area, :] = jnp.where(live(first + f), part, 0.0)
    pieces = [[None] * 2 for _ in range(2)]
    for odd in range(2):
        half = grid_ref[pl.ds(odd, frames * area // 2, stride=2), :]
        half = half.reshape(frames * rows // 2, 2, cols // 2, chans)
        for i in range(2):
            pieces[i][odd] = half[:, i].reshape(frames * area // 4, chans)
    tokens = frames * area // 4
    frame = first + lax.broadcasted_iota(jnp.int32, (tokens, LANES), 0) // (area // 4)
    label = jnp.where(frame < count, sample + 1, 0).astype(jnp.float32)
    patches = jnp.concatenate(
        [pieces[0][0], pieces[0][1], pieces[1][0], pieces[1][1], label], axis=1
    ).astype(jnp.bfloat16)
    route_row = route_ref[pl.ds(place, 1), :]
    onehot = onehot_of(slot_of(route_row, bags, cap, cap), bags * cap)
    out_ref[...] = jnp.dot(onehot, patches, preferred_element_type=jnp.float32).astype(jnp.bfloat16)


def bag_kernel(
    clips, x_ref, e_hbm, w_hbm, out_ref, e_ref, w_ref, normed_ref, qkv_ref, m_ref, r_ref, order_ref, sems
):
    count_slots = x_ref.shape[0]
    feats = e_ref.shape[0]
    model = e_ref.shape[1]
    width = w_ref.shape[2]
    clip_rows = count_slots // clips
    copies = [pltpu.make_async_copy(e_hbm, e_ref, sems.at[0])]
    for m in range(3):
        copies.append(pltpu.make_async_copy(w_hbm.at[m], w_ref.at[m], sems.at[1 + m]))
    for copy in copies:
        copy.start()

    for c in range(clips):
        note = x_ref[c * clip_rows : (c + 1) * clip_rows, feats : feats + LANES].astype(jnp.float32)
        order_ref[clips + c] = jnp.max(note).astype(jnp.int32)
    starts = [jnp.int32(0)]
    for s in range(SAMPLES):

        def keep_clip(c, at):
            hit = order_ref[clips + c] == s + 1

            @pl.when(hit)
            def _():
                order_ref[at] = c

            return at + hit.astype(jnp.int32)

        starts.append(lax.fori_loop(0, clips, keep_clip, starts[-1]))

    row_tile = 256
    copies[0].wait()

    def embed(i, carry):
        at = pl.multiple_of(i * row_tile, row_tile)
        rows = pl.ds(at, row_tile)
        patch = x_ref[rows, :feats]
        total = jnp.zeros((row_tile, 1), jnp.float32)
        step = 512
        for n in range(0, model, step):
            part = jnp.dot(patch, e_ref[:, n : n + step], preferred_element_type=jnp.float32).astype(
                jnp.bfloat16
            )
            normed_ref[rows, n : n + step] = part
            wide = part.astype(jnp.float32)
            total = total + jnp.sum(wide * wide, axis=-1, keepdims=True)
        scale = lax.rsqrt(total * (1.0 / model) + epsilon)
        for n in range(0, model, step):
            wide = normed_ref[rows, n : n + step].astype(jnp.float32)
            normed_ref[rows, n : n + step] = (wide * scale).astype(jnp.bfloat16)
        return carry

    lax.fori_loop(0, count_slots // row_tile, embed, 0)

    col_tile = 256
    for m in range(3):
        copies[1 + m].wait()
        for n in range(0, width, col_tile):
            part = jnp.dot(
                normed_ref[...], w_ref[m, :, n : n + col_tile], preferred_element_type=jnp.float32
            ).astype(jnp.bfloat16)
            if m == 0:
                part = part * jnp.bfloat16(HDIM ** (-0.5))
            qkv_ref[m, :, n : n + col_tile] = part

    out_ref[...] = jnp.zeros_like(out_ref)
    tile = 2 * clip_rows
    lane = lax.broadcasted_iota(jnp.int32, (tile, LANES), 1)
    low = lane < HDIM
    pairs = width // LANES
    ones = jnp.ones((tile, LANES), jnp.bfloat16)
    pick = (lax.broadcasted_iota(jnp.int32, (8, LANES), 1) == 0).astype(jnp.float32).astype(jnp.bfloat16)
    key_at = lax.broadcasted_iota(jnp.int32, (1, tile), 1)

    def two(ref, a, b, *at):
        return jnp.concatenate(
            [
                ref[(*at[:-1], pl.ds(pl.multiple_of(a * clip_rows, 16), clip_rows), at[-1])],
                ref[(*at[:-1], pl.ds(pl.multiple_of(b * clip_rows, 16), clip_rows), at[-1])],
            ],
            axis=0,
        )

    for s in range(SAMPLES):
        begin, size = starts[s], starts[s + 1] - starts[s]
        tiles = (size + 1) // 2

        def members(i):
            second = 2 * i + 1 < size
            return (
                order_ref[begin + 2 * i],
                order_ref[begin + 2 * i + second.astype(jnp.int32)],
                second,
            )

        def bias_of(a, b, second):
            label = lax.dot_general(
                pick,
                two(x_ref, a, b, slice(feats, feats + LANES)),
                (((1,), (1,)), ((), ())),
                preferred_element_type=jnp.float32,
            )[:1]
            limit = jnp.where(second, tile, clip_rows)
            good = jnp.logical_and(label == s + 1.0, key_at < limit)
            return jnp.where(good, 0.0, far_below)

        def scores_of(pair, half, query, a, b, bias):
            cols = slice(pair * LANES, (pair + 1) * LANES)
            keys = two(qkv_ref, a, b, 1, cols)
            one = jnp.where(low if half == 0 else jnp.logical_not(low), query, jnp.zeros_like(query))
            return (
                lax.dot_general(one, keys, (((1,), (1,)), ((), ())), preferred_element_type=jnp.float32)
                + bias
            )

        def mix(pair, shifted, a, b):
            cols = slice(pair * LANES, (pair + 1) * LANES)
            values = jnp.concatenate([two(qkv_ref, a, b, 2, cols), ones], axis=1)
            return jnp.dot(shifted.astype(jnp.bfloat16), values, preferred_element_type=jnp.float32)

        def store(pair, a, b, results):
            cols = slice(pair * LANES, (pair + 1) * LANES)
            heads = [r[:, :LANES] / r[:, LANES:] for r in results]
            mixed = jnp.where(low, heads[0], heads[1]).astype(jnp.bfloat16)
            out_ref[pl.ds(pl.multiple_of(b * clip_rows, 16), clip_rows), cols] = mixed[clip_rows:]
            out_ref[pl.ds(pl.multiple_of(a * clip_rows, 16), clip_rows), cols] = mixed[:clip_rows]

        def query_tile(i, carry):
            qa, qb, _ = members(i)

            @pl.when(tiles == 1)
            def _():
                ka, kb, second = members(0)
                bias = bias_of(ka, kb, second)
                for pair in range(pairs):
                    query = two(qkv_ref, qa, qb, 0, slice(pair * LANES, (pair + 1) * LANES))
                    results = []
                    for half in range(2):
                        scores = scores_of(pair, half, query, ka, kb, bias)
                        top = jnp.max(scores, axis=-1, keepdims=True)
                        results.append(mix(pair, jnp.exp(scores - top), ka, kb))
                    store(pair, qa, qb, results)

            @pl.when(tiles > 1)
            def _():
                for h in range(2 * pairs):
                    m_ref[h] = jnp.full((tile, LANES), far_below, jnp.float32)
                    r_ref[h] = jnp.zeros((tile, 2 * LANES), jnp.float32)

                def key_tile(j, inner):
                    ka, kb, second = members(j)
                    bias = bias_of(ka, kb, second)
                    for pair in range(pairs):
                        query = two(qkv_ref, qa, qb, 0, slice(pair * LANES, (pair + 1) * LANES))
                        for half in range(2):
                            h = 2 * pair + half
                            scores = scores_of(pair, half, query, ka, kb, bias)
                            old = m_ref[h][:, :1]
                            top = jnp.maximum(old, jnp.max(scores, axis=-1, keepdims=True))
                            r_ref[h] = r_ref[h] * jnp.exp(old - top) + mix(
                                pair, jnp.exp(scores - top), ka, kb
                            )
                            m_ref[h] = jnp.broadcast_to(top, (tile, LANES))
                    return inner

                lax.fori_loop(0, tiles, key_tile, 0)
                for pair in range(pairs):
                    store(pair, qa, qb, [r_ref[2 * pair], r_ref[2 * pair + 1]])

            return carry

        lax.fori_loop(0, tiles, query_tile, 0)


def collect_kernel(bags, cap, frames, heads, scal_ref, recv_ref, route_ref, out_ref):
    count, place = scal_ref[0], scal_ref[1]
    route_row = route_ref[pl.ds(place, 1), :]
    tokens = route_row.shape[1]
    per_frame = tokens // frames
    frame = place * frames + lax.broadcasted_iota(jnp.int32, (1, tokens), 1) // per_frame
    slot = slot_of(route_row, bags, cap, heads * cap)
    width = recv_ref.shape[1]
    for h in range(heads):
        onehot = onehot_of(jnp.where(frame < count, slot + h * cap, -1), recv_ref.shape[0])
        picked = lax.dot_general(
            onehot,
            recv_ref[...],
            (((0,), (0,)), ((), ())),
            preferred_element_type=jnp.float32,
        )
        out_ref[:, h * width : (h + 1) * width] = picked.astype(jnp.bfloat16)


def shards(latents, frame_counts, routes, samples, conv_weight, embed_weight, qkv_weight):
    frames_dev, rows, cols, depth = latents.shape[1:]
    heads_dev = lax.axis_size("head")
    bags = lax.axis_size("bag")
    place = lax.axis_index("head")
    frame_count = frame_counts[0]
    area = rows * cols
    tok_dev = frames_dev * area // 4
    cap = 3 * tok_dev // (2 * bags)
    slots = bags * cap
    local_width = qkv_weight.shape[2]
    chans = conv_weight.shape[2]

    tile = latents.reshape(frames_dev, area, depth)
    ends = heads_dev - 1
    prev_frame = lax.ppermute(tile[frames_dev - 1], "head", [(i, i + 1) for i in range(ends)])
    next_frame = lax.ppermute(tile[0], "head", [(i + 1, i) for i in range(ends)])

    route_rows = routes[:, 0].reshape(heads_dev, tok_dev)
    scal = jnp.stack([frame_count, place.astype(jnp.int32), samples[0]])
    row_width = 4 * chans + LANES
    outgoing = pl.pallas_call(
        functools.partial(conv_kernel, bags, cap, rows, cols, frames_dev),
        out_shape=jax.ShapeDtypeStruct((slots, row_width), jnp.bfloat16),
        in_specs=[SMEM, VMEM, VMEM, VMEM, VMEM, VMEM],
        out_specs=VMEM,
        scratch_shapes=[pltpu.VMEM((frames_dev * area, chans), jnp.float32)],
        name="conv",
    )(scal, tile.reshape(frames_dev * area, depth), prev_frame, next_frame, conv_weight, route_rows)

    arrived = lax.all_to_all(
        outgoing.reshape(bags, cap, row_width), "bag", split_axis=0, concat_axis=0, tiled=True
    )
    count_slots = heads_dev * slots
    gathered = lax.all_gather(arrived, "head", axis=1, tiled=True).reshape(count_slots, row_width)

    pair_rows = 2 * heads_dev * cap
    heads_here = local_width // HDIM
    attended = pl.pallas_call(
        functools.partial(bag_kernel, bags),
        out_shape=jax.ShapeDtypeStruct((count_slots, local_width), jnp.bfloat16),
        in_specs=[VMEM, pl.BlockSpec(memory_space=pl.ANY), pl.BlockSpec(memory_space=pl.ANY)],
        out_specs=VMEM,
        scratch_shapes=[
            pltpu.VMEM(embed_weight.shape, jnp.bfloat16),
            pltpu.VMEM(qkv_weight.shape, jnp.bfloat16),
            pltpu.VMEM((count_slots, embed_weight.shape[1]), jnp.bfloat16),
            pltpu.VMEM((3, count_slots, local_width), jnp.bfloat16),
            pltpu.VMEM((heads_here, pair_rows, LANES), jnp.float32),
            pltpu.VMEM((heads_here, pair_rows, 2 * LANES), jnp.float32),
            pltpu.SMEM((2 * bags,), jnp.int32),
            pltpu.SemaphoreType.DMA((4,)),
        ],
        name="bag",
    )(gathered, embed_weight, qkv_weight)

    returned = lax.all_to_all(
        attended.reshape(heads_dev * bags, cap, local_width),
        ("bag", "head"),
        split_axis=0,
        concat_axis=0,
        tiled=True,
    ).reshape(count_slots, local_width)
    return pl.pallas_call(
        functools.partial(collect_kernel, bags, cap, frames_dev, heads_dev),
        out_shape=jax.ShapeDtypeStruct((tok_dev, heads_dev * local_width), jnp.bfloat16),
        in_specs=[SMEM, VMEM, VMEM],
        out_specs=VMEM,
        name="collect",
    )(scal, returned, route_rows)


def solution(mesh):
    placed = (
        P("bag", "head", None, None, None),
        P("bag"),
        P("bag", None),
        P("bag"),
        P(),
        P(),
        P(None, None, "head"),
    )
    return jax.shard_map(
        shards, mesh=mesh, in_specs=placed, out_specs=P(("bag", "head"), None), check_vma=False
    )
```

time: 104 us -> 85 us (0.82)
  blocking collectives: 35.6 us -> 51 us
  starting transfers between devices: 16.3 us -> 3.7 us
  matrix products: 11.8 us -> 0 us
  waiting for transfers between devices: 6.57 us -> 1.08 us
  local copies, waits for them, and re-layouts: 6.36 us -> 2.95 us
    all_to_all x1 -> x2, blocking collectives: 25.2 us -> 37.8 us  [the longest x1 23.9 us: shards(): lax.all_to_all(attended.reshape(heads_dev * bags, cap, local_width), ('ba...]
    all_to_all x2 -> x0, starting transfers between devices: 12.6 us -> none  [the longest x1 6.62 us: shards(): lax.all_to_all(notes, 'bag', split_axis=0, concat_axis=0, tiled=True)]
    dot_general x4 -> x0, matrix products: 11.8 us -> none  [the longest x3 9.93 us: shards(): jnp.dot(normed, qkv_weight[m], preferred_element_type=jnp.float32)]
    all_to_all x2 -> x0, waiting for transfers between devices: 6.57 us -> none  [the longest x1 6.56 us: shards(): lax.all_to_all(outgoing.reshape(bags, cap, 4 * chans), 'bag', split_axis=...]
    all_gather x1, blocking collectives: 10.4 us -> 13.2 us  [shards(): lax.all_gather(arrived, 'head', axis=1, tiled=True)]
    select_n x2 -> x0, local copies, waits for them, and re-layouts: 1.59 us -> none  [shards(): jnp.where(jnp.arange(cap, dtype=jnp.int32)[None, None, :] < live_count[:,...]
    all_to_all x2 -> x0, local copies, waits for them, and re-layouts: 1.31 us -> none  [shards(): lax.all_to_all(notes, 'bag', split_axis=0, concat_axis=0, tiled=True)]
    ppermute x1, waiting for transfers between devices: 0.01 us -> 1.08 us  [shards(): lax.ppermute(tile[0], 'head', [(i + 1, i) for i in range(ends)])]
  transfers between devices with their start and end apart: 4 -> 2, of which waited for: 1 -> 1; matrix products, arithmetic and copies ran while one was open for 6% -> 3% of each run, Pallas kernels for 5% -> 0%
where the time goes in v2:
time: 85 us; the launch traced here: 84.5 us
  blocking collectives  51 us (60%)
  Pallas kernels  23.7 us (28%)
  starting transfers between devices  3.7 us (4%)
  local copies, waits for them, and re-layouts  2.95 us (3%)
  other arithmetic  1.31 us (2%)
  waiting for transfers between devices  1.08 us (1%)
    all_to_all x1, blocking collectives, shards(): lax.all_to_all(attended.reshape(heads_dev * bags, cap, local_width), ('ba...  23.9 us
    pallas_call x1, Pallas kernels, shards(): pl.pallas_call(functools.partial(bag_kernel, bags), out_shape=jax.ShapeDt...  15.5 us
    all_to_all x1, blocking collectives, shards(): lax.all_to_all(outgoing.reshape(bags, cap, row_width), 'bag', split_axis=...  13.9 us
    all_gather x1, blocking collectives, shards(): lax.all_gather(arrived, 'head', axis=1, tiled=True)  13.2 us
    pallas_call x1, Pallas kernels, shards(): pl.pallas_call(functools.partial(conv_kernel, bags, cap, rows, cols, fram...  5.53 us
    pallas_call x1, Pallas kernels, shards(): pl.pallas_call(functools.partial(collect_kernel, bags, cap, frames_dev, h...  2.7 us
    ppermute x1, starting transfers between devices, shards(): lax.ppermute(tile[frames_dev - 1], 'head', [(i, i + 1) for i in range(end...  2.41 us
  transfers between devices with their start and end apart: 2, of which 1 were waited for; matrix products, arithmetic and copies ran while one was open for 3% of the time, Pallas kernels for 0%

profile of v2, /device:TPU:0, one launch (start us, length us, event | category | flops | bytes accessed | tf_op | source)
XLA Modules:
  0.0 84.5 jit_solution(17866728978366262163)
XLA Ops:
  0.0 1.1 %fusion = (bf16[1,1,16,16,512]{4,3,2,1,0:T(8,128)(2,1)S(1)}, bf16[1,1,16,16,512]{4,3,2,1,0:T(8,128)(2,1)S(1)}) fusion(bf16[1,2,16,16,512]{4,3,2,1,0:T(8,128)(2,1)} %param.7), kind=kLoop, calls=%fused_computation.1 | loop fusion | bytes 1048576 | tf_op jit(solution)/shard_map/slice | solution.py:321
  1.1 2.4 %collective-permute-start = (bf16[256,512]{1,0:T(8,128)(2,1)S(1)}, bf16[256,512]{1,0:T(8,128)(2,1)S(1)}, u32[]{:S(2)}, u32[]{:S(2)}) collective-permute-start(bf16[256,512]{1,0:T(8,128)(2,1)S(1)} %bitcast.15), channel_id=1, source_target_pairs={{0,1},{1,2},{2,3},{4,5},{5,6},{6,7},{8,9},{9,10},{10,11},{12,13},{... | collective-permute-start | bytes 786440 | tf_op jit(solution)/shard_map/ppermute | solution.py:320
  3.5 1.3 %collective-permute-start.1 = (bf16[256,512]{1,0:T(8,128)(2,1)S(1)}, bf16[256,512]{1,0:T(8,128)(2,1)S(1)}, u32[]{:S(2)}, u32[]{:S(2)}) collective-permute-start(bf16[256,512]{1,0:T(8,128)(2,1)S(1)} %bitcast.14), channel_id=1, source_target_pairs={{1,0},{2,1},{3,2},{5,4},{6,5},{7,6},{9,8},{10,9},{11,10},{13,12},{... | collective-permute-start | bytes 786440 | tf_op jit(solution)/shard_map/ppermute | solution.py:321
  5.4 1.2 %slice.11 = s32[1]{0:T(128)} slice(s32[512]{0:T(512)} %param.10), slice={[0:1]} | slice | bytes 8 | tf_op jit(solution)/shard_map/slice | solution.py:324
  6.6 1.3 %pad_add_fusion.scal_ref = s32[3]{0:T(128)} fusion(s32[1]{0:T(128)} %slice.11, s32[1]{0:T(128)} %bitcast, s32[1]{0:T(128)S(6)} %copy.8), kind=kLoop, calls=%fused_computation | loop fusion | flops 6 | bytes 24 | tf_op jit(solution)/shard_map/stack | solution.py:324
  7.9 0.0 collective-permute-done.prev_ref
  7.9 0.0 copy-start
  7.9 1.1 %collective-permute-done.1.next_ref = bf16[256,512]{1,0:T(8,128)(2,1)S(1)} collective-permute-done((bf16[256,512]{1,0:T(8,128)(2,1)S(1)}, bf16[256,512]{1,0:T(8,128)(2,1)S(1)}, u32[]{:S(2)}, u32[]{:S(2)}) %collective-permute-start.1) | collective-permute-done | bytes 262176 | tf_op jit(solution)/shard_map/ppermute | solution.py:321
  9.0 0.0 copy-start.1
  9.0 0.0 copy-done
  9.0 0.7 copy-done.1
  9.7 5.5 %conv.1 = bf16[192,640]{1,0:T(8,128)(2,1)} custom-call(s32[3]{0:T(128)} %pad_add_fusion.scal_ref, bf16[512,512]{1,0:T(8,128)(2,1)} %bitcast.12, bf16[256,512]{1,0:T(8,128)(2,1)} %copy-done, bf16[256,512]{1,0:T(8,128)(2,1)} %copy-done.1, bf16[27,512,128]{2,1,0:T(8,128)(2,1)} %w_ref.1, s32[4,128]{1,0:T(4,128)} %bitcast.16), custom_call_target="tpu_custom_call" | custom-call | tf_op jit(solution)/shard_map/conv/pallas_call | solution.py:326
  15.2 13.9 %all_to_all.10 = bf16[8,24,640]{2,1,0:T(8,128)(2,1)S(1)} all-to-all(bf16[8,24,640]{2,1,0:T(8,128)(2,1)} %bitcast.13), channel_id=1, replica_groups=mesh['bag'=8,'head'=4] {'bag'}, dimensions={0} | all-to-all | bytes 491520 | tf_op jit(solution)/shard_map/all_to_all | solution.py:335
  29.2 13.2 %all_gather.3 = bf16[8,96,640]{2,1,0:T(8,128)(2,1)} all-gather(bf16[8,24,640]{2,1,0:T(8,128)(2,1)S(1)} %all_to_all.10), channel_id=1, replica_groups=mesh['bag'=8,'head'=4] {'head'}, dimensions={1}, use_global_device_ids=true | all-gather | bytes 1228800 | tf_op jit(solution)/shard_map/all_gather | solution.py:339
  42.4 15.5 %bag.1 = bf16[768,512]{1,0:T(8,128)(2,1)} custom-call(bf16[768,640]{1,0:T(8,128)(2,1)} %bitcast.9, bf16[512,2048]{1,0:T(8,128)(2,1)} %e_hbm.1, bf16[3,2048,512]{2,1,0:T(8,128)(2,1)} %w_hbm.1), custom_call_target="tpu_custom_call" | custom-call | tf_op jit(solution)/shard_map/bag/pallas_call | solution.py:343
  57.9 23.9 %all_to_all.11 = bf16[32,24,512]{2,1,0:T(8,128)(2,1)} all-to-all(bf16[32,24,512]{2,1,0:T(8,128)(2,1)} %bitcast.10), channel_id=1, replica_groups=mesh['bag'=8,'head'=4] {'bag','head'}, dimensions={0} | all-to-all | bytes 1572864 | tf_op jit(solution)/shard_map/all_to_all | solution.py:361
  81.8 2.7 %collect.1 = bf16[128,2048]{1,0:T(8,128)(2,1)} custom-call(s32[3]{0:T(128)} %pad_add_fusion.scal_ref, bf16[768,512]{1,0:T(8,128)(2,1)} %bitcast.11, s32[4,128]{1,0:T(4,128)} %bitcast.17), custom_call_target="tpu_custom_call" | custom-call | tf_op jit(solution)/shard_map/collect/pallas_call | solution.py:368
Async XLA Ops:
  1.1 6.9 %collective-permute-start = (bf16[256,512]{1,0:T(8,128)(2,1)S(1)}, bf16[256,512]{1,0:T(8,128)(2,1)S(1)}, u32[]{:S(2)}, u32[]{:S(2)}) collective-permute-start(bf16[256,512]{1,0:T(8,128)(2,1)S(1)} %bitcast.15), channel_id=1, source_target_pairs={{0,1},{1,2},{2,3},{4,5},{5,6},{6,7},{8,9},{9,10},{10,11},{12,13},{... | collective-permute-start | bytes 786440 | tf_op jit(solution)/shard_map/ppermute | solution.py:320
  3.5 5.5 %collective-permute-start.1 = (bf16[256,512]{1,0:T(8,128)(2,1)S(1)}, bf16[256,512]{1,0:T(8,128)(2,1)S(1)}, u32[]{:S(2)}, u32[]{:S(2)}) collective-permute-start(bf16[256,512]{1,0:T(8,128)(2,1)S(1)} %bitcast.14), channel_id=1, source_target_pairs={{1,0},{2,1},{3,2},{5,4},{6,5},{7,6},{9,8},{10,9},{11,10},{13,12},{... | collective-permute-start | bytes 786440 | tf_op jit(solution)/shard_map/ppermute | solution.py:321
  7.9 1.1 %copy-start = (bf16[256,512]{1,0:T(8,128)(2,1)}, bf16[256,512]{1,0:T(8,128)(2,1)S(1)}, u32[]{:S(2)}) copy-start(bf16[256,512]{1,0:T(8,128)(2,1)S(1)} %collective-permute-done.prev_ref) | copy-start | bytes 786436
  9.0 0.7 copy-start.1

commit v3 on v2

v3 whole, which is shorter than its diff:
```python
import functools
import jax
import jax.numpy as jnp
from jax import lax
from jax.experimental import pallas as pl
from jax.experimental.pallas import tpu as pltpu
from jax.sharding import PartitionSpec as P

HDIM = 64
TAPS = 3
SAMPLES = 4
LANES = 128

epsilon = 1e-06
far_below = -1e30

SMEM = pl.BlockSpec(memory_space=pltpu.SMEM)
VMEM = pl.BlockSpec(memory_space=pltpu.VMEM)
CHUNKS = 2


def limit(mib):
    return pltpu.CompilerParams(vmem_limit_bytes=mib << 20)


def slot_of(route_row, bags, cap, stride):
    tokens = route_row.shape[1]
    bag_ids = lax.broadcasted_iota(jnp.int32, (bags, tokens), 0)
    onehot = (bag_ids == route_row).astype(jnp.float32)
    before = (
        lax.broadcasted_iota(jnp.int32, (tokens, tokens), 0)
        < lax.broadcasted_iota(jnp.int32, (tokens, tokens), 1)
    )
    earlier = jnp.dot(
        onehot.astype(jnp.bfloat16),
        before.astype(jnp.float32).astype(jnp.bfloat16),
        preferred_element_type=jnp.float32,
    )
    rank = jnp.sum(earlier * onehot, axis=0, keepdims=True).astype(jnp.int32)
    return route_row * stride + rank


def onehot_of(slot, slots):
    slot_ids = lax.broadcasted_iota(jnp.int32, (slots, slot.shape[1]), 0)
    return (slot_ids == slot).astype(jnp.float32).astype(jnp.bfloat16)


def combine(products, rows, cols):
    chans = products[0].shape[1]
    blank = jnp.zeros((cols, chans), jnp.float32)
    area = rows * cols
    column = lax.broadcasted_iota(jnp.int32, (area, chans), 0) % cols
    total = None
    for e in range(TAPS):
        up, mid, down = products[e], products[TAPS + e], products[2 * TAPS + e]
        merged = (
            mid
            + jnp.concatenate([blank, up[: area - cols]], axis=0)
            + jnp.concatenate([down[cols:], blank], axis=0)
        )
        if e == 0:
            merged = jnp.where(column == 0, 0.0, pltpu.roll(merged, 1, axis=0))
        elif e == 2:
            merged = jnp.where(column == cols - 1, 0.0, pltpu.roll(merged, area - 1, axis=0))
        total = merged if total is None else total + merged
    return total


def plane_products(pieces, w_ref):
    plane = TAPS * TAPS
    chans = w_ref.shape[2]
    stacked = pieces[0][1] if len(pieces) == 1 else jnp.concatenate([x for _, x in pieces], axis=1)
    products = []
    for p in range(0, plane, 2):
        pair = []
        for q in range(p, min(p + 2, plane)):
            taps = [w_ref[plane * t + q] for t, _ in pieces]
            pair.append(taps[0] if len(taps) == 1 else jnp.concatenate(taps, axis=0))
        weight = pair[0] if len(pair) == 1 else jnp.concatenate(pair, axis=1)
        value = jnp.dot(stacked, weight, preferred_element_type=jnp.float32)
        for q in range(len(pair)):
            products.append(value[:, q * chans : (q + 1) * chans])
    return products


def own_kernel(bags, cap, rows, cols, frames, count_ref, x_ref, w_ref, route_ref, acc_ref, onehot_ref):
    count = count_ref[0]
    place = lax.axis_index("head")
    area = rows * cols
    first = place * frames
    inputs = []
    for f in range(frames):
        value = x_ref[f * area : (f + 1) * area, :]
        inputs.append(jnp.where(first + f < count, value, jnp.zeros_like(value)))
    for f in range(frames):
        pieces = [(t, inputs[f + t - 1]) for t in range(TAPS) if 0 <= f + t - 1 < frames]
        acc_ref[f * area : (f + 1) * area, :] = combine(plane_products(pieces, w_ref), rows, cols)
    route_row = route_ref[pl.ds(place, 1), :]
    onehot_ref[...] = onehot_of(slot_of(route_row, bags, cap, cap), bags * cap)


def halo_kernel(
    rows, cols, frames, count_ref, sample_ref, acc_ref, prev_ref, next_ref, w_ref, onehot_ref, out_ref, grid_ref
):
    count = count_ref[0]
    sample = sample_ref[0]
    place = lax.axis_index("head")
    area = rows * cols
    first = place * frames
    chans = w_ref.shape[2]

    def masked(value, frame):
        live = jnp.logical_and(frame >= 0, frame < count)
        return jnp.where(live, value, jnp.zeros_like(value))

    for f in range(frames):
        part = acc_ref[f * area : (f + 1) * area, :]
        pieces = []
        if f == 0:
            pieces.append((0, masked(prev_ref[...], first - 1)))
        if f == frames - 1:
            pieces.append((2, masked(next_ref[...], first + frames)))
        if pieces:
            part = part + combine(plane_products(pieces, w_ref), rows, cols)
        grid_ref[f * area : (f + 1) * area, :] = jnp.where(first + f < count, part, 0.0)
    pieces = [[None] * 2 for _ in range(2)]
    for odd in range(2):
        half = grid_ref[pl.ds(odd, frames * area // 2, stride=2), :]
        half = half.reshape(frames * rows // 2, 2, cols // 2, chans)
        for i in range(2):
            pieces[i][odd] = half[:, i].reshape(frames * area // 4, chans)
    tokens = frames * area // 4
    frame = first + lax.broadcasted_iota(jnp.int32, (tokens, LANES), 0) // (area // 4)
    label = jnp.where(frame < count, sample + 1, 0).astype(jnp.float32)
    patches = jnp.concatenate(
        [pieces[0][0], pieces[0][1], pieces[1][0], pieces[1][1], label], axis=1
    ).astype(jnp.bfloat16)
    out_ref[...] = jnp.dot(onehot_ref[...], patches, preferred_element_type=jnp.float32).astype(
        jnp.bfloat16
    )


def bag_kernel(clips, cap, chunk, x_ref, *refs):
    first = chunk == 0
    if first:
        e_hbm, w_hbm, out_ref, normed_ref, e_ref, w_ref, qkv_ref, m_ref, r_ref, order_ref, sems = refs
    else:
        normed_ref, w_hbm, out_ref, w_ref, qkv_ref, m_ref, r_ref, order_ref, sems = refs
    count_slots = x_ref.shape[0]
    feats = x_ref.shape[1] - LANES
    model = normed_ref.shape[1]
    width = w_ref.shape[2]
    clip_rows = count_slots // clips
    copies = []
    if first:
        copies.append(pltpu.make_async_copy(e_hbm, e_ref, sems.at[3]))
        copies[0].start()
    loads = [
        pltpu.make_async_copy(
            w_hbm.at[m, :, pl.ds(chunk * width, width)], w_ref.at[m], sems.at[m]
        )
        for m in range(3)
    ]
    for load in loads:
        load.start()

    for c in range(clips):
        note = x_ref[c * clip_rows : (c + 1) * clip_rows, feats:].astype(jnp.float32)
        order_ref[clips + c] = jnp.max(note).astype(jnp.int32)
    starts = [jnp.int32(0)]
    for s in range(SAMPLES):

        def keep_clip(c, at):
            hit = order_ref[clips + c] == s + 1

            @pl.when(hit)
            def _():
                order_ref[at] = c

            return at + hit.astype(jnp.int32)

        starts.append(lax.fori_loop(0, clips, keep_clip, starts[-1]))

    if first:
        row_tile = 256
        copies[0].wait()

        def embed(i, carry):
            at = pl.multiple_of(i * row_tile, row_tile)
            rows = pl.ds(at, row_tile)
            patch = x_ref[rows, :feats]
            total = jnp.zeros((row_tile, 1), jnp.float32)
            step = 512
            for n in range(0, model, step):
                part = jnp.dot(
                    patch, e_ref[:, n : n + step], preferred_element_type=jnp.float32
                ).astype(jnp.bfloat16)
                normed_ref[rows, n : n + step] = part
                wide = part.astype(jnp.float32)
                total = total + jnp.sum(wide * wide, axis=-1, keepdims=True)
            scale = lax.rsqrt(total * (1.0 / model) + epsilon)
            for n in range(0, model, step):
                wide = normed_ref[rows, n : n + step].astype(jnp.float32)
                normed_ref[rows, n : n + step] = (wide * scale).astype(jnp.bfloat16)
            return carry

        lax.fori_loop(0, count_slots // row_tile, embed, 0)

    col_tile = min(256, width)
    for m in range(3):
        loads[m].wait()
        for n in range(0, width, col_tile):
            part = jnp.dot(
                normed_ref[...], w_ref[m, :, n : n + col_tile], preferred_element_type=jnp.float32
            ).astype(jnp.bfloat16)
            if m == 0:
                part = part * jnp.bfloat16(HDIM ** (-0.5))
            qkv_ref[m, :, n : n + col_tile] = part

    out_ref[...] = jnp.zeros_like(out_ref)
    tile = 2 * clip_rows
    lane = lax.broadcasted_iota(jnp.int32, (tile, LANES), 1)
    low = lane < HDIM
    pairs = width // LANES
    ones = jnp.ones((tile, LANES), jnp.bfloat16)
    pick = (lax.broadcasted_iota(jnp.int32, (8, LANES), 1) == 0).astype(jnp.float32).astype(jnp.bfloat16)
    key_at = lax.broadcasted_iota(jnp.int32, (1, tile), 1)

    def two(ref, a, b, *at):
        return jnp.concatenate(
            [
                ref[(*at[:-1], pl.ds(pl.multiple_of(a * clip_rows, 16), clip_rows), at[-1])],
                ref[(*at[:-1], pl.ds(pl.multiple_of(b * clip_rows, 16), clip_rows), at[-1])],
            ],
            axis=0,
        )

    for s in range(SAMPLES):
        begin, size = starts[s], starts[s + 1] - starts[s]
        tiles = (size + 1) // 2

        def members(i):
            second = 2 * i + 1 < size
            return (
                order_ref[begin + 2 * i],
                order_ref[begin + 2 * i + second.astype(jnp.int32)],
                second,
            )

        def bias_of(a, b, second):
            label = lax.dot_general(
                pick,
                two(x_ref, a, b, slice(feats, feats + LANES)),
                (((1,), (1,)), ((), ())),
                preferred_element_type=jnp.float32,
            )[:1]
            limit = jnp.where(second, tile, clip_rows)
            good = jnp.logical_and(label == s + 1.0, key_at < limit)
            return jnp.where(good, 0.0, far_below)

        def scores_of(pair, half, query, a, b, bias):
            cols = slice(pair * LANES, (pair + 1) * LANES)
            keys = two(qkv_ref, a, b, 1, cols)
            one = jnp.where(low if half == 0 else jnp.logical_not(low), query, jnp.zeros_like(query))
            return (
                lax.dot_general(one, keys, (((1,), (1,)), ((), ())), preferred_element_type=jnp.float32)
                + bias
            )

        def mix(pair, shifted, a, b):
            cols = slice(pair * LANES, (pair + 1) * LANES)
            values = jnp.concatenate([two(qkv_ref, a, b, 2, cols), ones], axis=1)
            return jnp.dot(shifted.astype(jnp.bfloat16), values, preferred_element_type=jnp.float32)

        def store(pair, a, b, results):
            cols = slice(pair * LANES, (pair + 1) * LANES)
            heads = [r[:, :LANES] / r[:, LANES:] for r in results]
            mixed = jnp.where(low, heads[0], heads[1])
            for at, clip in ((clip_rows, b), (0, a)):
                for f in range(clip_rows // cap):
                    piece = mixed[at + f * cap : at + (f + 1) * cap]
                    out_ref[f * clips + clip, :, cols] = piece.astype(jnp.bfloat16)

        def query_tile(i, carry):
            qa, qb, _ = members(i)

            @pl.when(tiles == 1)
            def _():
                ka, kb, second = members(0)
                bias = bias_of(ka, kb, second)
                for pair in range(pairs):
                    query = two(qkv_ref, qa, qb, 0, slice(pair * LANES, (pair + 1) * LANES))
                    results = []
                    for half in range(2):
                        scores = scores_of(pair, half, query, ka, kb, bias)
                        top = jnp.max(scores, axis=-1, keepdims=True)
                        results.append(mix(pair, jnp.exp(scores - top), ka, kb))
                    store(pair, qa, qb, results)

            @pl.when(tiles > 1)
            def _():
                for h in range(2 * pairs):
                    m_ref[h] = jnp.full((tile, LANES), far_below, jnp.float32)
                    r_ref[h] = jnp.zeros((tile, 2 * LANES), jnp.float32)

                def key_tile(j, inner):
                    ka, kb, second = members(j)
                    bias = bias_of(ka, kb, second)
                    for pair in range(pairs):
                        query = two(qkv_ref, qa, qb, 0, slice(pair * LANES, (pair + 1) * LANES))
                        for half in range(2):
                            h = 2 * pair + half
                            scores = scores_of(pair, half, query, ka, kb, bias)
                            old = m_ref[h][:, :1]
                            top = jnp.maximum(old, jnp.max(scores, axis=-1, keepdims=True))
                            r_ref[h] = r_ref[h] * jnp.exp(old - top) + mix(
                                pair, jnp.exp(scores - top), ka, kb
                            )
                            m_ref[h] = jnp.broadcast_to(top, (tile, LANES))
                    return inner

                lax.fori_loop(0, tiles, key_tile, 0)
                for pair in range(pairs):
                    store(pair, qa, qb, [r_ref[2 * pair], r_ref[2 * pair + 1]])

            return carry

        lax.fori_loop(0, tiles, query_tile, 0)


def collect_kernel(frames, heads, chunks, count_ref, onehot_ref, *refs):
    recv_refs, out_ref = refs[:chunks], refs[chunks]
    count = count_ref[0]
    place = lax.axis_index("head")
    slots, tokens = onehot_ref.shape
    frame = place * frames + lax.broadcasted_iota(jnp.int32, (slots, tokens), 1) // (tokens // frames)
    onehot = jnp.where(frame < count, onehot_ref[...], jnp.zeros((), jnp.bfloat16))
    width = recv_refs[0].shape[1]
    for h in range(heads):
        for c in range(chunks):
            picked = lax.dot_general(
                onehot,
                recv_refs[c][h * slots : (h + 1) * slots, :],
                (((0,), (0,)), ((), ())),
                preferred_element_type=jnp.float32,
            )
            at = (h * chunks + c) * width
            out_ref[:, at : at + width] = picked.astype(jnp.bfloat16)


def shards(latents, frame_counts, routes, samples, conv_weight, embed_weight, qkv_weight):
    frames_dev, rows, cols, depth = latents.shape[1:]
    heads_dev = lax.axis_size("head")
    bags = lax.axis_size("bag")
    area = rows * cols
    tok_dev = frames_dev * area // 4
    cap = 3 * tok_dev // (2 * bags)
    slots = bags * cap
    local_width = qkv_weight.shape[2]
    chans = conv_weight.shape[2]

    tile = latents.reshape(frames_dev, area, depth)
    ends = heads_dev - 1
    prev_frame = lax.ppermute(tile[frames_dev - 1], "head", [(i, i + 1) for i in range(ends)])
    next_frame = lax.ppermute(tile[0], "head", [(i + 1, i) for i in range(ends)])

    route_rows = routes[:, 0].reshape(heads_dev, tok_dev)
    row_width = 4 * chans + LANES
    acc, onehot = pl.pallas_call(
        functools.partial(own_kernel, bags, cap, rows, cols, frames_dev),
        out_shape=(
            jax.ShapeDtypeStruct((frames_dev * area, chans), jnp.float32),
            jax.ShapeDtypeStruct((slots, tok_dev), jnp.bfloat16),
        ),
        in_specs=[SMEM, VMEM, VMEM, VMEM],
        out_specs=(VMEM, VMEM),
        compiler_params=limit(16),
        cost_estimate=pl.CostEstimate(flops=1200000000, bytes_accessed=4500000, transcendentals=0),
        name="own",
    )(frame_counts, tile.reshape(frames_dev * area, depth), conv_weight, route_rows)
    outgoing = pl.pallas_call(
        functools.partial(halo_kernel, rows, cols, frames_dev),
        out_shape=jax.ShapeDtypeStruct((slots, row_width), jnp.bfloat16),
        in_specs=[SMEM, SMEM, VMEM, VMEM, VMEM, VMEM, VMEM],
        out_specs=VMEM,
        scratch_shapes=[pltpu.VMEM((frames_dev * area, chans), jnp.float32)],
        compiler_params=limit(16),
        cost_estimate=pl.CostEstimate(flops=600000000, bytes_accessed=4500000, transcendentals=0),
        name="halo",
    )(frame_counts, samples, acc, prev_frame, next_frame, conv_weight, onehot)

    arrived = lax.all_to_all(
        outgoing.reshape(bags, cap, row_width), "bag", split_axis=0, concat_axis=0, tiled=True
    )
    count_slots = heads_dev * slots
    gathered = lax.all_gather(arrived, "head", axis=1, tiled=True).reshape(count_slots, row_width)

    pair_rows = 2 * heads_dev * cap
    model = embed_weight.shape[1]
    chunks = CHUNKS if local_width % (CHUNKS * LANES) == 0 else 1
    width = local_width // chunks
    heads_here = width // HDIM
    received = []
    normed = None
    for chunk in range(chunks):
        scratch = [
            pltpu.VMEM((3, model, width), jnp.bfloat16),
            pltpu.VMEM((3, count_slots, width), jnp.bfloat16),
            pltpu.VMEM((heads_here, pair_rows, LANES), jnp.float32),
            pltpu.VMEM((heads_here, pair_rows, 2 * LANES), jnp.float32),
            pltpu.SMEM((2 * bags,), jnp.int32),
            pltpu.SemaphoreType.DMA((4,)),
        ]
        out_shape = [jax.ShapeDtypeStruct((heads_dev * bags, cap, width), jnp.bfloat16)]
        if chunk == 0:
            out_shape.append(jax.ShapeDtypeStruct((count_slots, model), jnp.bfloat16))
            scratch.insert(0, pltpu.VMEM(embed_weight.shape, jnp.bfloat16))
            operands = (gathered, embed_weight, qkv_weight)
            in_specs = [VMEM, pl.BlockSpec(memory_space=pl.ANY), pl.BlockSpec(memory_space=pl.ANY)]
        else:
            operands = (gathered, normed, qkv_weight)
            in_specs = [VMEM, VMEM, pl.BlockSpec(memory_space=pl.ANY)]
        results = pl.pallas_call(
            functools.partial(bag_kernel, bags, cap, chunk),
            out_shape=out_shape,
            in_specs=in_specs,
            out_specs=[VMEM] * len(out_shape),
            scratch_shapes=scratch,
            compiler_params=limit(28),
            cost_estimate=pl.CostEstimate(
                flops=3000000000, bytes_accessed=8000000, transcendentals=600000
            ),
            name=f"bag{chunk}",
        )(*operands)
        if chunk == 0:
            normed = results[1]
        received.append(
            lax.all_to_all(results[0], ("head", "bag"), split_axis=0, concat_axis=0, tiled=True).reshape(
                count_slots, width
            )
        )
    return pl.pallas_call(
        functools.partial(collect_kernel, frames_dev, heads_dev, chunks),
        out_shape=jax.ShapeDtypeStruct((tok_dev, heads_dev * local_width), jnp.bfloat16),
        in_specs=[SMEM, VMEM] + [VMEM] * chunks,
        out_specs=VMEM,
        compiler_params=limit(16),
        name="collect",
    )(frame_counts, onehot, *received)


def solution(mesh):
    placed = (
        P("bag", "head", None, None, None),
        P("bag"),
        P("bag", None),
        P("bag"),
        P(),
        P(),
        P(None, None, "head"),
    )
    return jax.shard_map(
        shards, mesh=mesh, in_specs=placed, out_specs=P(("bag", "head"), None), check_vma=False
    )
```

time: 85 us -> 90.2 us (1.061)
  local copies, waits for them, and re-layouts: 2.95 us -> 13.1 us
  blocking collectives: 51 us -> 44.8 us
  starting transfers between devices: 3.7 us -> 6.3 us
  other arithmetic: 1.31 us -> 0 us
    unnamed x4 -> x20, local copies, waits for them, and re-layouts: 0.69 us -> 12 us
    all_to_all x1, blocking collectives: 23.9 us -> 18 us  [shards(): lax.all_to_all(results[0], ('head', 'bag'), split_axis=0, concat_axis=0,...]
    all_to_all x0 -> x1, starting transfers between devices: none -> 2.6 us  [shards(): lax.all_to_all(results[0], ('head', 'bag'), split_axis=0, concat_axis=0,...]
    all_gather x1, blocking collectives: 13.2 us -> 11.7 us  [shards(): lax.all_gather(arrived, 'head', axis=1, tiled=True)]
    another operation x1 -> x0, other arithmetic: 1.31 us -> none  [shards(): scal = jnp.stack([frame_count, place.astype(jnp.int32), samples[0]])]
    slice x1 -> x0, local copies, waits for them, and re-layouts: 1.19 us -> none  [shards(): scal = jnp.stack([frame_count, place.astype(jnp.int32), samples[0]])]
    all_to_all x1, blocking collectives: 13.9 us -> 15 us  [shards(): lax.all_to_all(outgoing.reshape(bags, cap, row_width), 'bag', split_axis=...]
    ppermute x1, waiting for transfers between devices: 1.08 us -> 0.01 us  [shards(): lax.ppermute(tile[0], 'head', [(i + 1, i) for i in range(ends)])]
  transfers between devices with their start and end apart: 2 -> 3, of which waited for: 1 -> 1; matrix products, arithmetic and copies ran while one was open for 3% -> 0% of each run, Pallas kernels for 0% -> 10%
where the time goes in v3:
time: 90.2 us; the launch traced here: 89.7 us
  blocking collectives  44.8 us (50%)
  Pallas kernels  23.7 us (26%)
  local copies, waits for them, and re-layouts  13.1 us (15%)
  starting transfers between devices  6.3 us (7%)
  waiting for transfers between devices  1.05 us (1%)
    pallas_call x2, Pallas kernels, shards(): pl.pallas_call(functools.partial(bag_kernel, bags, cap, chunk), out_shape...  19.4 us
    all_to_all x1, blocking collectives, shards(): lax.all_to_all(results[0], ('head', 'bag'), split_axis=0, concat_axis=0,...  18 us
    all_to_all x1, blocking collectives, shards(): lax.all_to_all(outgoing.reshape(bags, cap, row_width), 'bag', split_axis=...  15 us
    unnamed x20, local copies, waits for them, and re-layouts  12 us
    all_gather x1, blocking collectives, shards(): lax.all_gather(arrived, 'head', axis=1, tiled=True)  11.7 us
    all_to_all x1, starting transfers between devices, shards(): lax.all_to_all(results[0], ('head', 'bag'), split_axis=0, concat_axis=0,...  2.6 us
    ppermute x1, starting transfers between devices, shards(): lax.ppermute(tile[frames_dev - 1], 'head', [(i, i + 1) for i in range(end...  2.41 us
  transfers between devices with their start and end apart: 3, of which 1 were waited for; matrix products, arithmetic and copies ran while one was open for 0% of the time, Pallas kernels for 10%

profile of v3, /device:TPU:0, one launch (start us, length us, event | category | flops | bytes accessed | tf_op | source)
XLA Modules:
  0.0 89.7 jit_solution(8555522398048537708)
XLA Ops:
  0.0 0.0 copy-start.3
  0.0 1.1 %fusion = (bf16[1,1,16,16,512]{4,3,2,1,0:T(8,128)(2,1)S(1)}, bf16[1,1,16,16,512]{4,3,2,1,0:T(8,128)(2,1)S(1)}) fusion(bf16[1,2,16,16,512]{4,3,2,1,0:T(8,128)(2,1)} %param.7), kind=kLoop, calls=%fused_computation | loop fusion | bytes 1048576 | tf_op jit(solution)/shard_map/slice | solution.py:365
  1.1 2.4 %collective-permute-start = (bf16[256,512]{1,0:T(8,128)(2,1)S(1)}, bf16[256,512]{1,0:T(8,128)(2,1)S(1)}, u32[]{:S(2)}, u32[]{:S(2)}) collective-permute-start(bf16[256,512]{1,0:T(8,128)(2,1)S(1)} %bitcast.16), channel_id=1, source_target_pairs={{0,1},{1,2},{2,3},{4,5},{5,6},{6,7},{8,9},{9,10},{10,11},{12,13},{... | collective-permute-start | bytes 786440 | tf_op jit(solution)/shard_map/ppermute | solution.py:364
  3.5 1.3 %collective-permute-start.1 = (bf16[256,512]{1,0:T(8,128)(2,1)S(1)}, bf16[256,512]{1,0:T(8,128)(2,1)S(1)}, u32[]{:S(2)}, u32[]{:S(2)}) collective-permute-start(bf16[256,512]{1,0:T(8,128)(2,1)S(1)} %bitcast.15), channel_id=1, source_target_pairs={{1,0},{2,1},{3,2},{5,4},{6,5},{7,6},{9,8},{10,9},{11,10},{13,12},{... | collective-permute-start | bytes 786440 | tf_op jit(solution)/shard_map/ppermute | solution.py:365
  5.5 0.0 copy-start
  5.5 2.0 %copy-done = bf16[27,512,128]{2,1,0:T(8,128)(2,1)S(1)} copy-done((bf16[27,512,128]{2,1,0:T(8,128)(2,1)S(1)}, bf16[27,512,128]{2,1,0:T(8,128)(2,1)}, u32[]{:S(2)}) %copy-start) | copy-done | bytes 3538968
  7.5 0.0 copy-start.2
  7.5 1.0 %copy-done.2 = bf16[1,2,16,16,512]{4,3,2,1,0:T(8,128)(2,1)S(1)} copy-done((bf16[1,2,16,16,512]{4,3,2,1,0:T(8,128)(2,1)S(1)}, bf16[1,2,16,16,512]{4,3,2,1,0:T(8,128)(2,1)}, u32[]{:S(2)}) %copy-start.2) | copy-done | bytes 524312
  8.5 0.0 copy-start.7
  8.5 0.7 copy-done.7
  9.2 0.0 copy-start.1
  9.2 1.6 %own.1 = (f32[512,128]{1,0:T(8,128)S(1)}, bf16[192,128]{1,0:T(8,128)(2,1)S(1)}) custom-call(s32[1]{0:T(128)S(6)} %copy.8.count_ref, bf16[512,512]{1,0:T(8,128)(2,1)S(1)} %bitcast.13, bf16[27,512,128]{2,1,0:T(8,128)(2,1)S(1)} %copy-done, s32[4,128]{1,0:T(4,128)S(1)} %bitcast.14), custom_call_target="tpu_custom_call" | custom-call | flops 1200000000 | bytes 4500000 | tf_op jit(solution)/shard_map/own/pallas_call | solution.py:369
  10.7 0.0 copy-start.4
  10.8 0.0 collective-permute-done.prev_ref
  10.8 0.0 collective-permute-done.1.next_ref
  10.8 0.0 copy-done.3
  10.8 0.4 copy-done.1
  11.2 1.6 %halo.1 = bf16[192,640]{1,0:T(8,128)(2,1)S(1)} custom-call(s32[1]{0:T(128)S(6)} %copy.8.count_ref, s32[512]{0:T(512)S(1)} %copy-done.3, f32[512,128]{1,0:T(8,128)S(1)} %get-tuple-element.10.acc_ref, bf16[256,512]{1,0:T(8,128)(2,1)S(1)} %collective-permute-done.prev_ref, bf16[256,512]{1,0:T(8,128)(2,1)S(1)} %collective-permute-done.1.next_ref, ...), custom_call_target="tpu_custom_call" | custom-call | flops 600000000 | bytes 4500000 | tf_op jit(solution)/shard_map/halo/pallas_call | solution.py:381
  12.8 15.0 %all_to_all.15 = bf16[8,24,640]{2,1,0:T(8,128)(2,1)S(1)} all-to-all(bf16[8,24,640]{2,1,0:T(8,128)(2,1)S(1)} %bitcast.12), channel_id=1, replica_groups=mesh['bag'=8,'head'=4] {'bag'}, dimensions={0} | all-to-all | bytes 491520 | tf_op jit(solution)/shard_map/all_to_all | solution.py:392
  27.9 11.7 %all_gather.3 = bf16[8,96,640]{2,1,0:T(8,128)(2,1)S(1)} all-gather(bf16[8,24,640]{2,1,0:T(8,128)(2,1)S(1)} %all_to_all.15), channel_id=1, replica_groups=mesh['bag'=8,'head'=4] {'head'}, dimensions={1}, use_global_device_ids=true | all-gather | bytes 1228800 | tf_op jit(solution)/shard_map/all_gather | solution.py:396
  39.6 0.0 copy-done.4
  39.6 0.0 copy-start.6
  39.6 1.6 %copy-done.6 = bf16[512,2048]{1,0:T(8,128)(2,1)S(1)} copy-done((bf16[512,2048]{1,0:T(8,128)(2,1)S(1)}, bf16[512,2048]{1,0:T(8,128)(2,1)}, u32[]{:S(2)}) %copy-start.6) | copy-done | bytes 2097176
  41.2 11.7 %bag0.1 = (bf16[32,24,256]{2,1,0:T(8,128)(2,1)}, bf16[768,2048]{1,0:T(8,128)(2,1)S(1)}) custom-call(bf16[768,640]{1,0:T(8,128)(2,1)S(1)} %bitcast.10, bf16[512,2048]{1,0:T(8,128)(2,1)S(1)} %copy-done.6, bf16[3,2048,512]{2,1,0:T(8,128)(2,1)S(1)} %copy-done.4), custom_call_target="tpu_custom_call" | custom-call | flops 3000000000 | bytes 8000000 | tf_op jit(solution)/shard_map/bag0/pallas_call | solution.py:423
  52.9 0.0 copy-start.8
  52.9 1.6 %copy-done.8 = bf16[768,2048]{1,0:T(8,128)(2,1)} copy-done((bf16[768,2048]{1,0:T(8,128)(2,1)}, bf16[768,2048]{1,0:T(8,128)(2,1)S(1)}, u32[]{:S(2)}) %copy-start.8) | copy-done | bytes 3145752
  54.5 2.6 %all-to-all-start.1 = ((bf16[32,24,256]{2,1,0:T(8,128)(2,1)}), bf16[32,24,256]{2,1,0:T(8,128)(2,1)S(1)}, u32[]{:S(2)}, u32[]{:S(2)}) async-start(bf16[32,24,256]{2,1,0:T(8,128)(2,1)} %get-tuple-element.11), calls=%async_computation.1 | async-start | bytes 786432 | tf_op jit(solution)/shard_map/all_to_all | solution.py:438
  57.1 0.0 copy-start.5
  57.1 2.8 %copy-done.5 = bf16[3,2048,512]{2,1,0:T(8,128)(2,1)S(1)} copy-done((bf16[3,2048,512]{2,1,0:T(8,128)(2,1)S(1)}, bf16[3,2048,512]{2,1,0:T(8,128)(2,1)}, u32[]{:S(2)}) %copy-start.5) | copy-done | bytes 6291480
  59.9 0.0 copy-start.9
  59.9 1.9 %copy-done.9 = bf16[768,2048]{1,0:T(8,128)(2,1)S(1)} copy-done((bf16[768,2048]{1,0:T(8,128)(2,1)S(1)}, bf16[768,2048]{1,0:T(8,128)(2,1)}, u32[]{:S(2)}) %copy-start.9) | copy-done | bytes 3145752
  61.8 7.7 %bag1.1 = bf16[32,24,256]{2,1,0:T(8,128)(2,1)S(1)} custom-call(bf16[768,640]{1,0:T(8,128)(2,1)S(1)} %bitcast.11, bf16[768,2048]{1,0:T(8,128)(2,1)S(1)} %copy-done.9, bf16[3,2048,512]{2,1,0:T(8,128)(2,1)S(1)} %copy-done.5), custom_call_target="tpu_custom_call" | custom-call | flops 3000000000 | bytes 8000000 | tf_op jit(solution)/shard_map/bag1/pallas_call | solution.py:423
  69.5 1.0 %all-to-all-done.1 = bf16[32,24,256]{2,1,0:T(8,128)(2,1)S(1)} async-done(((bf16[32,24,256]{2,1,0:T(8,128)(2,1)}), bf16[32,24,256]{2,1,0:T(8,128)(2,1)S(1)}, u32[]{:S(2)}, u32[]{:S(2)}) %all-to-all-start.1) | async-done | bytes 393248 | tf_op jit(solution)/shard_map/all_to_all | solution.py:438
  70.5 18.0 %all_to_all.16 = bf16[32,24,256]{2,1,0:T(8,128)(2,1)S(1)} all-to-all(bf16[32,24,256]{2,1,0:T(8,128)(2,1)S(1)} %bag1.1), channel_id=1, replica_groups=mesh['bag'=8,'head'=4] {'head','bag'}, dimensions={0} | all-to-all | bytes 786432 | tf_op jit(solution)/shard_map/all_to_all | solution.py:438
  88.6 1.1 %collect.1 = bf16[128,2048]{1,0:T(8,128)(2,1)} custom-call(s32[1]{0:T(128)S(6)} %copy.8.count_ref, bf16[192,128]{1,0:T(8,128)(2,1)S(1)} %get-tuple-element.9.onehot_ref, bf16[768,256]{1,0:T(8,128)(2,1)S(1)} %bitcast.8, bf16[768,256]{1,0:T(8,128)(2,1)S(1)} %bitcast.9), custom_call_target="tpu_custom_call" | custom-call | tf_op jit(solution)/shard_map/collect/pallas_call | solution.py:442
Async XLA Ops:
  0.0 10.8 %copy-start.3 = (s32[512]{0:T(512)S(1)}, s32[512]{0:T(512)}, u32[]{:S(2)}) copy-start(s32[512]{0:T(512)} %sample_ref.1) | copy-start | bytes 6148
  1.1 9.7 %collective-permute-start = (bf16[256,512]{1,0:T(8,128)(2,1)S(1)}, bf16[256,512]{1,0:T(8,128)(2,1)S(1)}, u32[]{:S(2)}, u32[]{:S(2)}) collective-permute-start(bf16[256,512]{1,0:T(8,128)(2,1)S(1)} %bitcast.16), channel_id=1, source_target_pairs={{0,1},{1,2},{2,3},{4,5},{5,6},{6,7},{8,9},{9,10},{10,11},{12,13},{... | collective-permute-start | bytes 786440 | tf_op jit(solution)/shard_map/ppermute | solution.py:364
  3.5 7.3 %collective-permute-start.1 = (bf16[256,512]{1,0:T(8,128)(2,1)S(1)}, bf16[256,512]{1,0:T(8,128)(2,1)S(1)}, u32[]{:S(2)}, u32[]{:S(2)}) collective-permute-start(bf16[256,512]{1,0:T(8,128)(2,1)S(1)} %bitcast.15), channel_id=1, source_target_pairs={{1,0},{2,1},{3,2},{5,4},{6,5},{7,6},{9,8},{10,9},{11,10},{13,12},{... | collective-permute-start | bytes 786440 | tf_op jit(solution)/shard_map/ppermute | solution.py:365
  5.5 2.0 %copy-start = (bf16[27,512,128]{2,1,0:T(8,128)(2,1)S(1)}, bf16[27,512,128]{2,1,0:T(8,128)(2,1)}, u32[]{:S(2)}) copy-start(bf16[27,512,128]{2,1,0:T(8,128)(2,1)} %w_ref.3) | copy-start | bytes 10616836
  7.5 1.0 %copy-start.2 = (bf16[1,2,16,16,512]{4,3,2,1,0:T(8,128)(2,1)S(1)}, bf16[1,2,16,16,512]{4,3,2,1,0:T(8,128)(2,1)}, u32[]{:S(2)}) copy-start(bf16[1,2,16,16,512]{4,3,2,1,0:T(8,128)(2,1)} %param.7) | copy-start | bytes 1572868
  8.5 0.7 copy-start.7
  9.2 2.0 %copy-start.1 = (bf16[27,512,128]{2,1,0:T(8,128)(2,1)S(1)}, bf16[27,512,128]{2,1,0:T(8,128)(2,1)}, u32[]{:S(2)}) copy-start(bf16[27,512,128]{2,1,0:T(8,128)(2,1)} %w_ref.3) | copy-start | bytes 10616836
  10.7 28.8 %copy-start.4 = (bf16[3,2048,512]{2,1,0:T(8,128)(2,1)S(1)}, bf16[3,2048,512]{2,1,0:T(8,128)(2,1)}, u32[]{:S(2)}) copy-start(bf16[3,2048,512]{2,1,0:T(8,128)(2,1)} %refs_1_.3) | copy-start | bytes 18874372
  39.6 1.6 %copy-start.6 = (bf16[512,2048]{1,0:T(8,128)(2,1)S(1)}, bf16[512,2048]{1,0:T(8,128)(2,1)}, u32[]{:S(2)}) copy-start(bf16[512,2048]{1,0:T(8,128)(2,1)} %refs_0_.1) | copy-start | bytes 6291460
  52.9 1.7 %copy-start.8 = (bf16[768,2048]{1,0:T(8,128)(2,1)}, bf16[768,2048]{1,0:T(8,128)(2,1)S(1)}, u32[]{:S(2)}) copy-start(bf16[768,2048]{1,0:T(8,128)(2,1)S(1)} %get-tuple-element.12.refs_0_) | copy-start | bytes 9437188
  54.5 16.0 %all-to-all-start.1 = ((bf16[32,24,256]{2,1,0:T(8,128)(2,1)}), bf16[32,24,256]{2,1,0:T(8,128)(2,1)S(1)}, u32[]{:S(2)}, u32[]{:S(2)}) async-start(bf16[32,24,256]{2,1,0:T(8,128)(2,1)} %get-tuple-element.11), calls=%async_computation.1 | async-start | bytes 786432 | tf_op jit(solution)/shard_map/all_to_all | solution.py:438
  57.1 2.8 %copy-start.5 = (bf16[3,2048,512]{2,1,0:T(8,128)(2,1)S(1)}, bf16[3,2048,512]{2,1,0:T(8,128)(2,1)}, u32[]{:S(2)}) copy-start(bf16[3,2048,512]{2,1,0:T(8,128)(2,1)} %refs_1_.3) | copy-start | bytes 18874372
  59.9 1.9 %copy-start.9 = (bf16[768,2048]{1,0:T(8,128)(2,1)S(1)}, bf16[768,2048]{1,0:T(8,128)(2,1)}, u32[]{:S(2)}) copy-start(bf16[768,2048]{1,0:T(8,128)(2,1)} %copy-done.8) | copy-start | bytes 9437188

commit v4 on v3

--- a/solution.py
+++ b/solution.py
@@ -16,7 +16,7 @@
 
 SMEM = pl.BlockSpec(memory_space=pltpu.SMEM)
 VMEM = pl.BlockSpec(memory_space=pltpu.VMEM)
-CHUNKS = 2
+HBM = pl.BlockSpec(memory_space=pltpu.HBM)
 
 
 def limit(mib):
@@ -83,11 +83,23 @@
     return products
 
 
-def own_kernel(bags, cap, rows, cols, frames, count_ref, x_ref, w_ref, route_ref, acc_ref, onehot_ref):
+def own_kernel(
+    bags, cap, rows, cols, frames, count_ref, x_hbm, w_hbm, route_ref, acc_ref, onehot_ref, w_ref, x_ref, sems
+):
+    loads = [
+        pltpu.make_async_copy(x_hbm, x_ref, sems.at[0]),
+        pltpu.make_async_copy(w_hbm, w_ref, sems.at[1]),
+    ]
+    for load in loads:
+        load.start()
     count = count_ref[0]
     place = lax.axis_index("head")
     area = rows * cols
     first = place * frames
+    route_row = route_ref[pl.ds(place, 1), :]
+    onehot_ref[...] = onehot_of(slot_of(route_row, bags, cap, cap), bags * cap)
+    for load in loads:
+        load.wait()
     inputs = []
     for f in range(frames):
         value = x_ref[f * area : (f + 1) * area, :]
@@ -95,8 +107,6 @@
     for f in range(frames):
         pieces = [(t, inputs[f + t - 1]) for t in range(TAPS) if 0 <= f + t - 1 < frames]
         acc_ref[f * area : (f + 1) * area, :] = combine(plane_products(pieces, w_ref), rows, cols)
-    route_row = route_ref[pl.ds(place, 1), :]
-    onehot_ref[...] = onehot_of(slot_of(route_row, bags, cap, cap), bags * cap)
 
 
 def halo_kernel(
@@ -140,29 +150,35 @@
     )
 
 
-def bag_kernel(clips, cap, chunk, x_ref, *refs):
-    first = chunk == 0
-    if first:
-        e_hbm, w_hbm, out_ref, normed_ref, e_ref, w_ref, qkv_ref, m_ref, r_ref, order_ref, sems = refs
-    else:
-        normed_ref, w_hbm, out_ref, w_ref, qkv_ref, m_ref, r_ref, order_ref, sems = refs
-    count_slots = x_ref.shape[0]
-    feats = x_ref.shape[1] - LANES
-    model = normed_ref.shape[1]
+def fold_kernel(e_hbm, w_hbm, e_ref, fold_ref, w_ref, sems):
+    feats = e_ref.shape[0]
     width = w_ref.shape[2]
-    clip_rows = count_slots // clips
-    copies = []
-    if first:
-        copies.append(pltpu.make_async_copy(e_hbm, e_ref, sems.at[3]))
-        copies[0].start()
-    loads = [
-        pltpu.make_async_copy(
-            w_hbm.at[m, :, pl.ds(chunk * width, width)], w_ref.at[m], sems.at[m]
-        )
-        for m in range(3)
-    ]
+    loads = [pltpu.make_async_copy(e_hbm, e_ref, sems.at[3])]
+    for m in range(3):
+        loads.append(pltpu.make_async_copy(w_hbm.at[m], w_ref.at[m], sems.at[m]))
     for load in loads:
         load.start()
+    loads[0].wait()
+    col_tile = 256
+    for m in range(3):
+        loads[1 + m].wait()
+        for n in range(0, width, col_tile):
+            cols = slice(n, n + col_tile)
+            product = jnp.dot(e_ref[...], w_ref[m, :, cols], preferred_element_type=jnp.float32)
+            if m == 0:
+                product = product * HDIM ** (-0.5)
+            high = product.astype(jnp.bfloat16)
+            fold_ref[m, :feats, cols] = high
+            fold_ref[m, feats:, cols] = (product - high.astype(jnp.float32)).astype(jnp.bfloat16)
+
+
+def bag_kernel(
+    clips, cap, x_ref, e_ref, fold_ref, out_ref, qkv_ref, total_ref, m_ref, r_ref, order_ref
+):
+    count_slots = x_ref.shape[0]
+    feats, model = e_ref.shape
+    width = fold_ref.shape[2]
+    clip_rows = count_slots // clips
 
     for c in range(clips):
         note = x_ref[c * clip_rows : (c + 1) * clip_rows, feats:].astype(jnp.float32)
@@ -181,41 +197,23 @@
 
         starts.append(lax.fori_loop(0, clips, keep_clip, starts[-1]))
 
-    if first:
-        row_tile = 256
-        copies[0].wait()
-
-        def embed(i, carry):
-            at = pl.multiple_of(i * row_tile, row_tile)
-            rows = pl.ds(at, row_tile)
-            patch = x_ref[rows, :feats]
-            total = jnp.zeros((row_tile, 1), jnp.float32)
-            step = 512
-            for n in range(0, model, step):
-                part = jnp.dot(
-                    patch, e_ref[:, n : n + step], preferred_element_type=jnp.float32
-                ).astype(jnp.bfloat16)
-                normed_ref[rows, n : n + step] = part
-                wide = part.astype(jnp.float32)
-                total = total + jnp.sum(wide * wide, axis=-1, keepdims=True)
-            scale = lax.rsqrt(total * (1.0 / model) + epsilon)
-            for n in range(0, model, step):
-                wide = normed_ref[rows, n : n + step].astype(jnp.float32)
-                normed_ref[rows, n : n + step] = (wide * scale).astype(jnp.bfloat16)
-            return carry
-
-        lax.fori_loop(0, count_slots // row_tile, embed, 0)
-
-    col_tile = min(256, width)
+    col_tile = 256
+    patch = x_ref[:, :feats]
+    for n in range(0, model, col_tile):
+        part = jnp.dot(patch, e_ref[:, n : n + col_tile], preferred_element_type=jnp.float32)
+        squares = part * part
+        both = squares[:, :LANES] + squares[:, LANES:]
+        total_ref[...] = both if n == 0 else total_ref[...] + both
+    mean = jnp.sum(total_ref[...], axis=-1, keepdims=True) * (1.0 / model)
+    total_ref[...] = jnp.broadcast_to(lax.rsqrt(mean + epsilon), total_ref.shape)
+    twice = jnp.concatenate([patch, patch], axis=1)
     for m in range(3):
-        loads[m].wait()
         for n in range(0, width, col_tile):
-            part = jnp.dot(
-                normed_ref[...], w_ref[m, :, n : n + col_tile], preferred_element_type=jnp.float32
+            part = jnp.dot(twice, fold_ref[m, :, n : n + col_tile], preferred_element_type=jnp.float32)
+            scale = total_ref[...]
+            qkv_ref[m, :, n : n + col_tile] = (
+                part * jnp.concatenate([scale] * (col_tile // LANES), axis=1)
             ).astype(jnp.bfloat16)
-            if m == 0:
-                part = part * jnp.bfloat16(HDIM ** (-0.5))
-            qkv_ref[m, :, n : n + col_tile] = part
 
     out_ref[...] = jnp.zeros_like(out_ref)
     tile = 2 * clip_rows
@@ -328,24 +326,21 @@
         lax.fori_loop(0, tiles, query_tile, 0)
 
 
-def collect_kernel(frames, heads, chunks, count_ref, onehot_ref, *refs):
-    recv_refs, out_ref = refs[:chunks], refs[chunks]
+def collect_kernel(frames, heads, count_ref, onehot_ref, recv_ref, out_ref):
     count = count_ref[0]
     place = lax.axis_index("head")
     slots, tokens = onehot_ref.shape
     frame = place * frames + lax.broadcasted_iota(jnp.int32, (slots, tokens), 1) // (tokens // frames)
     onehot = jnp.where(frame < count, onehot_ref[...], jnp.zeros((), jnp.bfloat16))
-    width = recv_refs[0].shape[1]
+    width = recv_ref.shape[1]
     for h in range(heads):
-        for c in range(chunks):
-            picked = lax.dot_general(
-                onehot,
-                recv_refs[c][h * slots : (h + 1) * slots, :],
-                (((0,), (0,)), ((), ())),
-                preferred_element_type=jnp.float32,
-            )
-            at = (h * chunks + c) * width
-            out_ref[:, at : at + width] = picked.astype(jnp.bfloat16)
+        picked = lax.dot_general(
+            onehot,
+            recv_ref[h * slots : (h + 1) * slots, :],
+            (((0,), (0,)), ((), ())),
+            preferred_element_type=jnp.float32,
+        )
+        out_ref[:, h * width : (h + 1) * width] = picked.astype(jnp.bfloat16)
 
 
 def shards(latents, frame_counts, routes, samples, conv_weight, embed_weight, qkv_weight):
@@ -366,14 +361,20 @@
 
     route_rows = routes[:, 0].reshape(heads_dev, tok_dev)
     row_width = 4 * chans + LANES
-    acc, onehot = pl.pallas_call(
+    model = embed_weight.shape[1]
+    acc, onehot, conv_near = pl.pallas_call(
         functools.partial(own_kernel, bags, cap, rows, cols, frames_dev),
         out_shape=(
             jax.ShapeDtypeStruct((frames_dev * area, chans), jnp.float32),
             jax.ShapeDtypeStruct((slots, tok_dev), jnp.bfloat16),
+            jax.ShapeDtypeStruct(conv_weight.shape, jnp.bfloat16),
         ),
-        in_specs=[SMEM, VMEM, VMEM, VMEM],
-        out_specs=(VMEM, VMEM),
+        in_specs=[SMEM, HBM, HBM, VMEM],
+        out_specs=(VMEM, VMEM, VMEM),
+        scratch_shapes=[
+            pltpu.VMEM((frames_dev * area, depth), jnp.bfloat16),
+            pltpu.SemaphoreType.DMA((2,)),
+        ],
         compiler_params=limit(16),
         cost_estimate=pl.CostEstimate(flops=1200000000, bytes_accessed=4500000, transcendentals=0),
         name="own",
@@ -387,66 +388,57 @@
         compiler_params=limit(16),
         cost_estimate=pl.CostEstimate(flops=600000000, bytes_accessed=4500000, transcendentals=0),
         name="halo",
-    )(frame_counts, samples, acc, prev_frame, next_frame, conv_weight, onehot)
+    )(frame_counts, samples, acc, prev_frame, next_frame, conv_near, onehot)
 
     arrived = lax.all_to_all(
         outgoing.reshape(bags, cap, row_width), "bag", split_axis=0, concat_axis=0, tiled=True
     )
+    embed_near, folded = pl.pallas_call(
+        fold_kernel,
+        out_shape=(
+            jax.ShapeDtypeStruct(embed_weight.shape, jnp.bfloat16),
+            jax.ShapeDtypeStruct((3, 2 * embed_weight.shape[0], local_width), jnp.bfloat16),
+        ),
+        in_specs=[HBM, HBM],
+        out_specs=(VMEM, VMEM),
+        scratch_shapes=[
+            pltpu.VMEM(qkv_weight.shape, jnp.bfloat16),
+            pltpu.SemaphoreType.DMA((4,)),
+        ],
+        compiler_params=limit(24),
+        cost_estimate=pl.CostEstimate(flops=3300000000, bytes_accessed=14000000, transcendentals=0),
+        name="fold",
+    )(embed_weight, qkv_weight)
     count_slots = heads_dev * slots
     gathered = lax.all_gather(arrived, "head", axis=1, tiled=True).reshape(count_slots, row_width)
 
     pair_rows = 2 * heads_dev * cap
-    model = embed_weight.shape[1]
-    chunks = CHUNKS if local_width % (CHUNKS * LANES) == 0 else 1
-    width = local_width // chunks
-    heads_here = width // HDIM
-    received = []
-    normed = None
-    for chunk in range(chunks):
-        scratch = [
-            pltpu.VMEM((3, model, width), jnp.bfloat16),
-            pltpu.VMEM((3, count_slots, width), jnp.bfloat16),
+    heads_here = local_width // HDIM
+    attended = pl.pallas_call(
+        functools.partial(bag_kernel, bags, cap),
+        out_shape=jax.ShapeDtypeStruct((heads_dev * bags, cap, local_width), jnp.bfloat16),
+        in_specs=[VMEM, VMEM, VMEM],
+        out_specs=VMEM,
+        scratch_shapes=[
+            pltpu.VMEM((3, count_slots, local_width), jnp.bfloat16),
+            pltpu.VMEM((count_slots, LANES), jnp.float32),
             pltpu.VMEM((heads_here, pair_rows, LANES), jnp.float32),
             pltpu.VMEM((heads_here, pair_rows, 2 * LANES), jnp.float32),
             pltpu.SMEM((2 * bags,), jnp.int32),
-            pltpu.SemaphoreType.DMA((4,)),
-        ]
-        out_shape = [jax.ShapeDtypeStruct((heads_dev * bags, cap, width), jnp.bfloat16)]
-        if chunk == 0:
-            out_shape.append(jax.ShapeDtypeStruct((count_slots, model), jnp.bfloat16))
-            scratch.insert(0, pltpu.VMEM(embed_weight.shape, jnp.bfloat16))
-            operands = (gathered, embed_weight, qkv_weight)
-            in_specs = [VMEM, pl.BlockSpec(memory_space=pl.ANY), pl.BlockSpec(memory_space=pl.ANY)]
-        else:
-            operands = (gathered, normed, qkv_weight)
-            in_specs = [VMEM, VMEM, pl.BlockSpec(memory_space=pl.ANY)]
-        results = pl.pallas_call(
-            functools.partial(bag_kernel, bags, cap, chunk),
-            out_shape=out_shape,
-            in_specs=in_specs,
-            out_specs=[VMEM] * len(out_shape),
-            scratch_shapes=scratch,
-            compiler_params=limit(28),
-            cost_estimate=pl.CostEstimate(
-                flops=3000000000, bytes_accessed=8000000, transcendentals=600000
-            ),
-            name=f"bag{chunk}",
-        )(*operands)
-        if chunk == 0:
-            normed = results[1]
-        received.append(
-            lax.all_to_all(results[0], ("head", "bag"), split_axis=0, concat_axis=0, tiled=True).reshape(
-                count_slots, width
-            )
-        )
+        ],
+        compiler_params=limit(28),
+        cost_estimate=pl.CostEstimate(flops=5000000000, bytes_accessed=8000000, transcendentals=1200000),
+        name="bag",
+    )(gathered, embed_near, folded)
+    received = lax.all_to_all(attended, ("head", "bag"), split_axis=0, concat_axis=0, tiled=True)
     return pl.pallas_call(
-        functools.partial(collect_kernel, frames_dev, heads_dev, chunks),
+        functools.partial(collect_kernel, frames_dev, heads_dev),
         out_shape=jax.ShapeDtypeStruct((tok_dev, heads_dev * local_width), jnp.bfloat16),
-        in_specs=[SMEM, VMEM] + [VMEM] * chunks,
+        in_specs=[SMEM, VMEM, VMEM],
         out_specs=VMEM,
         compiler_params=limit(16),
         name="collect",
-    )(frame_counts, onehot, *received)
+    )(frame_counts, onehot, received.reshape(count_slots, local_width))
 
 
 def solution(mesh):

time: 90.2 us -> 82.8 us (0.918)
  blocking collectives: 44.8 us -> 38.9 us
  Pallas kernels: 23.7 us -> 18.3 us
  starting transfers between devices: 6.3 us -> 10.3 us
  waiting for transfers between devices: 1.05 us -> 0.01 us
  local copies, waits for them, and re-layouts: 13.1 us -> 14.1 us
    pallas_call x3, Pallas kernels: 20.5 us -> 13.7 us  [the longest x1 8.18 us: shards(): pl.pallas_call(functools.partial(bag_kernel, bags, cap), out_shape=jax.Sh...]
    all_to_all x2 -> x1, blocking collectives: 33 us -> 26.7 us  [shards(): lax.all_to_all(attended, ('head', 'bag'), split_axis=0, concat_axis=0, ti...]
    all_to_all x1, starting transfers between devices: 2.6 us -> 6.62 us  [shards(): lax.all_to_all(outgoing.reshape(bags, cap, row_width), 'bag', split_axis=...]
    all_to_all x1, waiting for transfers between devices: 1.05 us -> 0.01 us  [shards(): lax.all_to_all(outgoing.reshape(bags, cap, row_width), 'bag', split_axis=...]
    unnamed x20, local copies, waits for them, and re-layouts: 12 us -> 13 us
  transfers between devices with their start and end apart: 3 -> 3, of which waited for: 1 -> 0; matrix products, arithmetic and copies ran while one was open for 0% -> 0% of each run, Pallas kernels for 10% -> 8%
where the time goes in v4:
time: 82.8 us; the launch traced here: 82.4 us
  blocking collectives  38.9 us (47%)
  Pallas kernels  18.3 us (22%)
  local copies, waits for them, and re-layouts  14.1 us (17%)
  starting transfers between devices  10.3 us (12%)
    all_to_all x1, blocking collectives, shards(): lax.all_to_all(attended, ('head', 'bag'), split_axis=0, concat_axis=0, ti...  26.7 us
    unnamed x20, local copies, waits for them, and re-layouts  13 us
    all_gather x1, blocking collectives, shards(): lax.all_gather(arrived, 'head', axis=1, tiled=True)  12.2 us
    pallas_call x1, Pallas kernels, shards(): pl.pallas_call(functools.partial(bag_kernel, bags, cap), out_shape=jax.Sh...  8.18 us
    all_to_all x1, starting transfers between devices, shards(): lax.all_to_all(outgoing.reshape(bags, cap, row_width), 'bag', split_axis=...  6.62 us
    pallas_call x1, Pallas kernels, shards(): pl.pallas_call(fold_kernel, out_shape=(jax.ShapeDtypeStruct(embed_weight....  4.37 us
    ppermute x1, starting transfers between devices, shards(): lax.ppermute(tile[frames_dev - 1], 'head', [(i, i + 1) for i in range(end...  2.41 us
    pallas_call x1, Pallas kernels, shards(): pl.pallas_call(functools.partial(halo_kernel, rows, cols, frames_dev), ou...  2.35 us
  transfers between devices with their start and end apart: 3, of which 0 were waited for; matrix products, arithmetic and copies ran while one was open for 0% of the time, Pallas kernels for 8%

profile of v4, /device:TPU:0, one launch (start us, length us, event | category | flops | bytes accessed | tf_op | source)
XLA Modules:
  0.0 82.4 jit_solution(3972544145758265558)
XLA Ops:
  0.0 0.0 copy-start.1
  0.0 1.1 %fusion = (bf16[1,1,16,16,512]{4,3,2,1,0:T(8,128)(2,1)S(1)}, bf16[1,1,16,16,512]{4,3,2,1,0:T(8,128)(2,1)S(1)}) fusion(bf16[1,2,16,16,512]{4,3,2,1,0:T(8,128)(2,1)} %param.7), kind=kLoop, calls=%fused_computation | loop fusion | bytes 1048576 | tf_op jit(solution)/shard_map/slice | solution.py:360
  1.1 2.4 %collective-permute-start = (bf16[256,512]{1,0:T(8,128)(2,1)S(1)}, bf16[256,512]{1,0:T(8,128)(2,1)S(1)}, u32[]{:S(2)}, u32[]{:S(2)}) collective-permute-start(bf16[256,512]{1,0:T(8,128)(2,1)S(1)} %bitcast.12), channel_id=1, source_target_pairs={{0,1},{1,2},{2,3},{4,5},{5,6},{6,7},{8,9},{9,10},{10,11},{12,13},{... | collective-permute-start | bytes 786440 | tf_op jit(solution)/shard_map/ppermute | solution.py:359
  3.5 1.3 %collective-permute-start.1 = (bf16[256,512]{1,0:T(8,128)(2,1)S(1)}, bf16[256,512]{1,0:T(8,128)(2,1)S(1)}, u32[]{:S(2)}, u32[]{:S(2)}) collective-permute-start(bf16[256,512]{1,0:T(8,128)(2,1)S(1)} %bitcast.11), channel_id=1, source_target_pairs={{1,0},{2,1},{3,2},{5,4},{6,5},{7,6},{9,8},{10,9},{11,10},{13,12},{... | collective-permute-start | bytes 786440 | tf_op jit(solution)/shard_map/ppermute | solution.py:360
  5.5 0.0 copy-start
  5.5 1.0 %copy-done = bf16[1,2,16,16,512]{4,3,2,1,0:T(8,128)(2,1)S(1)} copy-done((bf16[1,2,16,16,512]{4,3,2,1,0:T(8,128)(2,1)S(1)}, bf16[1,2,16,16,512]{4,3,2,1,0:T(8,128)(2,1)}, u32[]{:S(2)}) %copy-start) | copy-done | bytes 524312
  6.5 0.0 copy-start.3
  6.5 2.0 %copy-done.3 = bf16[27,512,128]{2,1,0:T(8,128)(2,1)S(1)} copy-done((bf16[27,512,128]{2,1,0:T(8,128)(2,1)S(1)}, bf16[27,512,128]{2,1,0:T(8,128)(2,1)}, u32[]{:S(2)}) %copy-start.3) | copy-done | bytes 3538968
  8.5 0.0 copy-start.5
  8.5 0.7 copy-done.5
  9.2 2.2 %own.1 = (f32[512,128]{1,0:T(8,128)S(1)}, bf16[192,128]{1,0:T(8,128)(2,1)S(1)}, bf16[27,512,128]{2,1,0:T(8,128)(2,1)S(1)}) custom-call(s32[1]{0:T(128)S(6)} %copy.8.count_ref, bf16[512,512]{1,0:T(8,128)(2,1)S(1)} %bitcast.9, bf16[27,512,128]{2,1,0:T(8,128)(2,1)S(1)} %copy-done.3, s32[4,128]{1,0:T(4,128)S(1)} %bitcast.10), custom_call_target="tpu_custom_call" | custom-call | flops 1200000000 | bytes 4500000 | tf_op jit(solution)/shard_map/own/pallas_call | solution.py:365
  11.4 0.0 copy-start.4
  11.4 0.0 collective-permute-done.prev_ref
  11.4 0.0 collective-permute-done.1.next_ref
  11.4 0.0 copy-done.1
  11.5 2.3 %halo.1 = bf16[192,640]{1,0:T(8,128)(2,1)} custom-call(s32[1]{0:T(128)S(6)} %copy.8.count_ref, s32[512]{0:T(512)S(1)} %copy-done.1, f32[512,128]{1,0:T(8,128)S(1)} %get-tuple-element.11.acc_ref, bf16[256,512]{1,0:T(8,128)(2,1)S(1)} %collective-permute-done.prev_ref, bf16[256,512]{1,0:T(8,128)(2,1)S(1)} %collective-permute-done.1.next_ref, ...), custom_call_target="tpu_custom_call" | custom-call | flops 600000000 | bytes 4500000 | tf_op jit(solution)/shard_map/halo/pallas_call | solution.py:382
  13.8 6.6 %all-to-all-start = ((bf16[8,24,640]{2,1,0:T(8,128)(2,1)}), bf16[8,24,640]{2,1,0:T(8,128)(2,1)S(1)}, u32[]{:S(2)}, u32[]{:S(2)}) async-start(bf16[8,24,640]{2,1,0:T(8,128)(2,1)} %bitcast.4), calls=%async_computation | async-start | bytes 491520 | tf_op jit(solution)/shard_map/all_to_all | solution.py:393
  20.4 0.0 copy-done.4
  20.4 0.0 copy-start.2
  20.4 2.8 %copy-done.2 = bf16[3,2048,512]{2,1,0:T(8,128)(2,1)S(1)} copy-done((bf16[3,2048,512]{2,1,0:T(8,128)(2,1)S(1)}, bf16[3,2048,512]{2,1,0:T(8,128)(2,1)}, u32[]{:S(2)}) %copy-start.2) | copy-done | bytes 6291480
  23.2 4.4 %fold.1 = (bf16[512,2048]{1,0:T(8,128)(2,1)S(1)}, bf16[3,1024,512]{2,1,0:T(8,128)(2,1)S(1)}) custom-call(bf16[512,2048]{1,0:T(8,128)(2,1)S(1)} %copy-done.4, bf16[3,2048,512]{2,1,0:T(8,128)(2,1)S(1)} %copy-done.2), custom_call_target="tpu_custom_call" | custom-call | flops 3300000000 | bytes 14000000 | tf_op jit(solution)/shard_map/fold/pallas_call | solution.py:396
  27.6 0.0 copy-start.6
  27.6 1.6 %copy-done.6 = bf16[3,1024,512]{2,1,0:T(8,128)(2,1)} copy-done((bf16[3,1024,512]{2,1,0:T(8,128)(2,1)}, bf16[3,1024,512]{2,1,0:T(8,128)(2,1)S(1)}, u32[]{:S(2)}) %copy-start.6) | copy-done | bytes 3145752
  29.3 0.0 copy-start.8
  29.3 1.4 %copy-done.8 = bf16[512,2048]{1,0:T(8,128)(2,1)} copy-done((bf16[512,2048]{1,0:T(8,128)(2,1)}, bf16[512,2048]{1,0:T(8,128)(2,1)S(1)}, u32[]{:S(2)}) %copy-start.8) | copy-done | bytes 2097176
  30.6 0.0 all-to-all-done
  30.6 12.2 %all_gather.3 = bf16[8,96,640]{2,1,0:T(8,128)(2,1)S(1)} all-gather(bf16[8,24,640]{2,1,0:T(8,128)(2,1)S(1)} %all-to-all-done), channel_id=1, replica_groups=mesh['bag'=8,'head'=4] {'head'}, dimensions={1}, use_global_device_ids=true | all-gather | bytes 1228800 | tf_op jit(solution)/shard_map/all_gather | solution.py:413
  42.8 0.0 copy-start.7
  42.8 1.9 %copy-done.7 = bf16[3,1024,512]{2,1,0:T(8,128)(2,1)S(1)} copy-done((bf16[3,1024,512]{2,1,0:T(8,128)(2,1)S(1)}, bf16[3,1024,512]{2,1,0:T(8,128)(2,1)}, u32[]{:S(2)}) %copy-start.7) | copy-done | bytes 3145752
  44.7 0.0 copy-start.9
  44.7 1.6 %copy-done.9 = bf16[512,2048]{1,0:T(8,128)(2,1)S(1)} copy-done((bf16[512,2048]{1,0:T(8,128)(2,1)S(1)}, bf16[512,2048]{1,0:T(8,128)(2,1)}, u32[]{:S(2)}) %copy-start.9) | copy-done | bytes 2097176
  46.3 8.2 %bag.1 = bf16[32,24,512]{2,1,0:T(8,128)(2,1)S(1)} custom-call(bf16[768,640]{1,0:T(8,128)(2,1)S(1)} %bitcast.8, bf16[512,2048]{1,0:T(8,128)(2,1)S(1)} %copy-done.9, bf16[3,1024,512]{2,1,0:T(8,128)(2,1)S(1)} %copy-done.7), custom_call_target="tpu_custom_call" | custom-call | flops 5000000000 | bytes 8000000 | tf_op jit(solution)/shard_map/bag/pallas_call | solution.py:417
  54.5 26.7 %all_to_all.10 = bf16[32,24,512]{2,1,0:T(8,128)(2,1)S(1)} all-to-all(bf16[32,24,512]{2,1,0:T(8,128)(2,1)S(1)} %bag.1), channel_id=1, replica_groups=mesh['bag'=8,'head'=4] {'head','bag'}, dimensions={0} | all-to-all | bytes 1572864 | tf_op jit(solution)/shard_map/all_to_all | solution.py:433
  81.2 1.1 %collect.1 = bf16[128,2048]{1,0:T(8,128)(2,1)} custom-call(s32[1]{0:T(128)S(6)} %copy.8.count_ref, bf16[192,128]{1,0:T(8,128)(2,1)S(1)} %get-tuple-element.10.onehot_ref, bf16[768,512]{1,0:T(8,128)(2,1)S(1)} %bitcast.7), custom_call_target="tpu_custom_call" | custom-call | tf_op jit(solution)/shard_map/collect/pallas_call | solution.py:434
Async XLA Ops:
  0.0 11.4 %copy-start.1 = (s32[512]{0:T(512)S(1)}, s32[512]{0:T(512)}, u32[]{:S(2)}) copy-start(s32[512]{0:T(512)} %sample_ref.1) | copy-start | bytes 6148
  1.1 10.3 %collective-permute-start = (bf16[256,512]{1,0:T(8,128)(2,1)S(1)}, bf16[256,512]{1,0:T(8,128)(2,1)S(1)}, u32[]{:S(2)}, u32[]{:S(2)}) collective-permute-start(bf16[256,512]{1,0:T(8,128)(2,1)S(1)} %bitcast.12), channel_id=1, source_target_pairs={{0,1},{1,2},{2,3},{4,5},{5,6},{6,7},{8,9},{9,10},{10,11},{12,13},{... | collective-permute-start | bytes 786440 | tf_op jit(solution)/shard_map/ppermute | solution.py:359
  3.5 7.9 %collective-permute-start.1 = (bf16[256,512]{1,0:T(8,128)(2,1)S(1)}, bf16[256,512]{1,0:T(8,128)(2,1)S(1)}, u32[]{:S(2)}, u32[]{:S(2)}) collective-permute-start(bf16[256,512]{1,0:T(8,128)(2,1)S(1)} %bitcast.11), channel_id=1, source_target_pairs={{1,0},{2,1},{3,2},{5,4},{6,5},{7,6},{9,8},{10,9},{11,10},{13,12},{... | collective-permute-start | bytes 786440 | tf_op jit(solution)/shard_map/ppermute | solution.py:360
  5.5 1.0 %copy-start = (bf16[1,2,16,16,512]{4,3,2,1,0:T(8,128)(2,1)S(1)}, bf16[1,2,16,16,512]{4,3,2,1,0:T(8,128)(2,1)}, u32[]{:S(2)}) copy-start(bf16[1,2,16,16,512]{4,3,2,1,0:T(8,128)(2,1)} %param.7) | copy-start | bytes 1572868
  6.5 2.0 %copy-start.3 = (bf16[27,512,128]{2,1,0:T(8,128)(2,1)S(1)}, bf16[27,512,128]{2,1,0:T(8,128)(2,1)}, u32[]{:S(2)}) copy-start(bf16[27,512,128]{2,1,0:T(8,128)(2,1)} %w_hbm.2) | copy-start | bytes 10616836
  8.5 0.7 copy-start.5
  11.4 9.0 %copy-start.4 = (bf16[512,2048]{1,0:T(8,128)(2,1)S(1)}, bf16[512,2048]{1,0:T(8,128)(2,1)}, u32[]{:S(2)}) copy-start(bf16[512,2048]{1,0:T(8,128)(2,1)} %e_hbm.1) | copy-start | bytes 6291460
  13.8 16.8 %all-to-all-start = ((bf16[8,24,640]{2,1,0:T(8,128)(2,1)}), bf16[8,24,640]{2,1,0:T(8,128)(2,1)S(1)}, u32[]{:S(2)}, u32[]{:S(2)}) async-start(bf16[8,24,640]{2,1,0:T(8,128)(2,1)} %bitcast.4), calls=%async_computation | async-start | bytes 491520 | tf_op jit(solution)/shard_map/all_to_all | solution.py:393
  20.4 2.8 %copy-start.2 = (bf16[3,2048,512]{2,1,0:T(8,128)(2,1)S(1)}, bf16[3,2048,512]{2,1,0:T(8,128)(2,1)}, u32[]{:S(2)}) copy-start(bf16[3,2048,512]{2,1,0:T(8,128)(2,1)} %w_hbm.3) | copy-start | bytes 18874372
  27.6 1.7 %copy-start.6 = (bf16[3,1024,512]{2,1,0:T(8,128)(2,1)}, bf16[3,1024,512]{2,1,0:T(8,128)(2,1)S(1)}, u32[]{:S(2)}) copy-start(bf16[3,1024,512]{2,1,0:T(8,128)(2,1)S(1)} %get-tuple-element.14.fold_ref) | copy-start | bytes 9437188
  29.3 1.4 %copy-start.8 = (bf16[512,2048]{1,0:T(8,128)(2,1)}, bf16[512,2048]{1,0:T(8,128)(2,1)S(1)}, u32[]{:S(2)}) copy-start(bf16[512,2048]{1,0:T(8,128)(2,1)S(1)} %get-tuple-element.13.e_ref) | copy-start | bytes 6291460
  42.8 1.9 %copy-start.7 = (bf16[3,1024,512]{2,1,0:T(8,128)(2,1)S(1)}, bf16[3,1024,512]{2,1,0:T(8,128)(2,1)}, u32[]{:S(2)}) copy-start(bf16[3,1024,512]{2,1,0:T(8,128)(2,1)} %copy-done.6) | copy-start | bytes 9437188
  44.7 1.6 %copy-start.9 = (bf16[512,2048]{1,0:T(8,128)(2,1)S(1)}, bf16[512,2048]{1,0:T(8,128)(2,1)}, u32[]{:S(2)}) copy-start(bf16[512,2048]{1,0:T(8,128)(2,1)} %copy-done.8) | copy-start | bytes 6291460

commit v5 on v4

--- a/solution.py
+++ b/solution.py
@@ -16,7 +16,7 @@
 
 SMEM = pl.BlockSpec(memory_space=pltpu.SMEM)
 VMEM = pl.BlockSpec(memory_space=pltpu.VMEM)
-HBM = pl.BlockSpec(memory_space=pltpu.HBM)
+ANY = pl.BlockSpec(memory_space=pl.ANY)
 
 
 def limit(mib):
@@ -84,7 +84,7 @@
 
 
 def own_kernel(
-    bags, cap, rows, cols, frames, count_ref, x_hbm, w_hbm, route_ref, acc_ref, onehot_ref, w_ref, x_ref, sems
+    bags, cap, rows, cols, frames, count_ref, x_hbm, w_hbm, route_ref, acc_ref, onehot_ref, x_ref, w_ref, sems
 ):
     loads = [
         pltpu.make_async_copy(x_hbm, x_ref, sems.at[0]),
@@ -150,7 +150,7 @@
     )
 
 
-def fold_kernel(e_hbm, w_hbm, e_ref, fold_ref, w_ref, sems):
+def fold_kernel(e_hbm, w_hbm, fold_ref, e_ref, w_ref, sems):
     feats = e_ref.shape[0]
     width = w_ref.shape[2]
     loads = [pltpu.make_async_copy(e_hbm, e_ref, sems.at[3])]
@@ -173,8 +173,14 @@
 
 
 def bag_kernel(
-    clips, cap, x_ref, e_ref, fold_ref, out_ref, qkv_ref, total_ref, m_ref, r_ref, order_ref
+    clips, cap, x_ref, e_hbm, fold_hbm, out_ref, e_ref, fold_ref, qkv_ref, total_ref, m_ref, r_ref, order_ref, sems
 ):
+    loads = [
+        pltpu.make_async_copy(e_hbm, e_ref, sems.at[0]),
+        pltpu.make_async_copy(fold_hbm, fold_ref, sems.at[1]),
+    ]
+    for load in loads:
+        load.start()
     count_slots = x_ref.shape[0]
     feats, model = e_ref.shape
     width = fold_ref.shape[2]
@@ -199,6 +205,7 @@
 
     col_tile = 256
     patch = x_ref[:, :feats]
+    loads[0].wait()
     for n in range(0, model, col_tile):
         part = jnp.dot(patch, e_ref[:, n : n + col_tile], preferred_element_type=jnp.float32)
         squares = part * part
@@ -207,6 +214,7 @@
     mean = jnp.sum(total_ref[...], axis=-1, keepdims=True) * (1.0 / model)
     total_ref[...] = jnp.broadcast_to(lax.rsqrt(mean + epsilon), total_ref.shape)
     twice = jnp.concatenate([patch, patch], axis=1)
+    loads[1].wait()
     for m in range(3):
         for n in range(0, width, col_tile):
             part = jnp.dot(twice, fold_ref[m, :, n : n + col_tile], preferred_element_type=jnp.float32)
@@ -362,20 +370,19 @@
     route_rows = routes[:, 0].reshape(heads_dev, tok_dev)
     row_width = 4 * chans + LANES
     model = embed_weight.shape[1]
-    acc, onehot, conv_near = pl.pallas_call(
+    acc, onehot = pl.pallas_call(
         functools.partial(own_kernel, bags, cap, rows, cols, frames_dev),
         out_shape=(
             jax.ShapeDtypeStruct((frames_dev * area, chans), jnp.float32),
             jax.ShapeDtypeStruct((slots, tok_dev), jnp.bfloat16),
-            jax.ShapeDtypeStruct(conv_weight.shape, jnp.bfloat16),
         ),
-        in_specs=[SMEM, HBM, HBM, VMEM],
-        out_specs=(VMEM, VMEM, VMEM),
+        in_specs=[SMEM, ANY, ANY, VMEM],
+        out_specs=(VMEM, VMEM),
         scratch_shapes=[
             pltpu.VMEM((frames_dev * area, depth), jnp.bfloat16),
+            pltpu.VMEM(conv_weight.shape, jnp.bfloat16),
             pltpu.SemaphoreType.DMA((2,)),
         ],
-        compiler_params=limit(16),
         cost_estimate=pl.CostEstimate(flops=1200000000, bytes_accessed=4500000, transcendentals=0),
         name="own",
     )(frame_counts, tile.reshape(frames_dev * area, depth), conv_weight, route_rows)
@@ -388,24 +395,21 @@
         compiler_params=limit(16),
         cost_estimate=pl.CostEstimate(flops=600000000, bytes_accessed=4500000, transcendentals=0),
         name="halo",
-    )(frame_counts, samples, acc, prev_frame, next_frame, conv_near, onehot)
+    )(frame_counts, samples, acc, prev_frame, next_frame, conv_weight, onehot)
 
     arrived = lax.all_to_all(
         outgoing.reshape(bags, cap, row_width), "bag", split_axis=0, concat_axis=0, tiled=True
     )
-    embed_near, folded = pl.pallas_call(
+    folded = pl.pallas_call(
         fold_kernel,
-        out_shape=(
-            jax.ShapeDtypeStruct(embed_weight.shape, jnp.bfloat16),
-            jax.ShapeDtypeStruct((3, 2 * embed_weight.shape[0], local_width), jnp.bfloat16),
-        ),
-        in_specs=[HBM, HBM],
-        out_specs=(VMEM, VMEM),
+        out_shape=jax.ShapeDtypeStruct((3, 2 * embed_weight.shape[0], local_width), jnp.bfloat16),
+        in_specs=[ANY, ANY],
+        out_specs=VMEM,
         scratch_shapes=[
+            pltpu.VMEM(embed_weight.shape, jnp.bfloat16),
             pltpu.VMEM(qkv_weight.shape, jnp.bfloat16),
             pltpu.SemaphoreType.DMA((4,)),
         ],
-        compiler_params=limit(24),
         cost_estimate=pl.CostEstimate(flops=3300000000, bytes_accessed=14000000, transcendentals=0),
         name="fold",
     )(embed_weight, qkv_weight)
@@ -417,19 +421,21 @@
     attended = pl.pallas_call(
         functools.partial(bag_kernel, bags, cap),
         out_shape=jax.ShapeDtypeStruct((heads_dev * bags, cap, local_width), jnp.bfloat16),
-        in_specs=[VMEM, VMEM, VMEM],
+        in_specs=[VMEM, ANY, ANY],
         out_specs=VMEM,
         scratch_shapes=[
+            pltpu.VMEM(embed_weight.shape, jnp.bfloat16),
+            pltpu.VMEM(folded.shape, jnp.bfloat16),
             pltpu.VMEM((3, count_slots, local_width), jnp.bfloat16),
             pltpu.VMEM((count_slots, LANES), jnp.float32),
             pltpu.VMEM((heads_here, pair_rows, LANES), jnp.float32),
             pltpu.VMEM((heads_here, pair_rows, 2 * LANES), jnp.float32),
             pltpu.SMEM((2 * bags,), jnp.int32),
+            pltpu.SemaphoreType.DMA((2,)),
         ],
-        compiler_params=limit(28),
         cost_estimate=pl.CostEstimate(flops=5000000000, bytes_accessed=8000000, transcendentals=1200000),
         name="bag",
-    )(gathered, embed_near, folded)
+    )(gathered, embed_weight, folded)
     received = lax.all_to_all(attended, ("head", "bag"), split_axis=0, concat_axis=0, tiled=True)
     return pl.pallas_call(
         functools.partial(collect_kernel, frames_dev, heads_dev),

time: 82.8 us -> 83.4 us (level)
  local copies, waits for them, and re-layouts: 14.1 us -> 4.44 us
  Pallas kernels: 18.3 us -> 27.7 us
  waiting for transfers between devices: 0.01 us -> 1.44 us
  blocking collectives: 38.9 us -> 37.5 us
    unnamed x20 -> x12, local copies, waits for them, and re-layouts: 13 us -> 2.44 us
    pallas_call x1, Pallas kernels: 8.18 us -> 11.7 us  [shards(): pl.pallas_call(functools.partial(bag_kernel, bags, cap), out_shape=jax.Sh...]
    pallas_call x1, Pallas kernels: 4.37 us -> 7.66 us  [shards(): pl.pallas_call(fold_kernel, out_shape=jax.ShapeDtypeStruct((3, 2 * embed_...]
    pallas_call x1, Pallas kernels: 2.23 us -> 5.12 us  [shards(): pl.pallas_call(functools.partial(own_kernel, bags, cap, rows, cols, frame...]
    all_to_all x1, waiting for transfers between devices: 0.01 us -> 1.43 us  [shards(): lax.all_to_all(outgoing.reshape(bags, cap, row_width), 'bag', split_axis=...]
    all_gather x1, blocking collectives: 12.2 us -> 11.2 us  [shards(): lax.all_gather(arrived, 'head', axis=1, tiled=True)]
    slice x1, local copies, waits for them, and re-layouts: 1.08 us -> 2 us  [shards(): tile[0]]
  transfers between devices with their start and end apart: 3 -> 3, of which waited for: 0 -> 1; matrix products, arithmetic and copies ran while one was open for 0% -> 0% of each run, Pallas kernels for 8% -> 15%
where the time goes in v5:
time: 83.4 us; the launch traced here: 82.8 us
  blocking collectives  37.5 us (45%)
  Pallas kernels  27.7 us (33%)
  starting transfers between devices  11 us (13%)
  local copies, waits for them, and re-layouts  4.44 us (5%)
  waiting for transfers between devices  1.44 us (2%)
    all_to_all x1, blocking collectives, shards(): lax.all_to_all(attended, ('head', 'bag'), split_axis=0, concat_axis=0, ti...  26.3 us
    pallas_call x1, Pallas kernels, shards(): pl.pallas_call(functools.partial(bag_kernel, bags, cap), out_shape=jax.Sh...  11.7 us
    all_gather x1, blocking collectives, shards(): lax.all_gather(arrived, 'head', axis=1, tiled=True)  11.2 us
    pallas_call x1, Pallas kernels, shards(): pl.pallas_call(fold_kernel, out_shape=jax.ShapeDtypeStruct((3, 2 * embed_...  7.66 us
    all_to_all x1, starting transfers between devices, shards(): lax.all_to_all(outgoing.reshape(bags, cap, row_width), 'bag', split_axis=...  6.62 us
    pallas_call x1, Pallas kernels, shards(): pl.pallas_call(functools.partial(own_kernel, bags, cap, rows, cols, frame...  5.12 us
    ppermute x1, starting transfers between devices, shards(): lax.ppermute(tile[frames_dev - 1], 'head', [(i, i + 1) for i in range(end...  3.09 us
    unnamed x12, local copies, waits for them, and re-layouts  2.44 us
  transfers between devices with their start and end apart: 3, of which 1 were waited for; matrix products, arithmetic and copies ran while one was open for 0% of the time, Pallas kernels for 15%

profile of v5, /device:TPU:0, one launch (start us, length us, event | category | flops | bytes accessed | tf_op | source)
XLA Modules:
  0.0 82.8 jit_solution(4630303996469496891)
XLA Ops:
  0.0 0.0 copy-start
  0.0 0.0 copy-start.5
  0.0 2.0 %fusion = (bf16[1,1,16,16,512]{4,3,2,1,0:T(8,128)(2,1)}, bf16[1,1,16,16,512]{4,3,2,1,0:T(8,128)(2,1)}) fusion(bf16[1,2,16,16,512]{4,3,2,1,0:T(8,128)(2,1)} %param.7), kind=kLoop, calls=%fused_computation | loop fusion | bytes 1048576 | tf_op jit(solution)/shard_map/slice | solution.py:368
  2.0 3.1 %collective-permute-start = (bf16[256,512]{1,0:T(8,128)(2,1)}, bf16[256,512]{1,0:T(8,128)(2,1)}, u32[]{:S(2)}, u32[]{:S(2)}) collective-permute-start(bf16[256,512]{1,0:T(8,128)(2,1)} %bitcast.2), channel_id=1, source_target_pairs={{0,1},{1,2},{2,3},{4,5},{5,6},{6,7},{8,9},{9,10},{10,11},{12,13},{... | collective-permute-start | bytes 786440 | tf_op jit(solution)/shard_map/ppermute | solution.py:367
  5.1 1.3 %collective-permute-start.1 = (bf16[256,512]{1,0:T(8,128)(2,1)}, bf16[256,512]{1,0:T(8,128)(2,1)}, u32[]{:S(2)}, u32[]{:S(2)}) collective-permute-start(bf16[256,512]{1,0:T(8,128)(2,1)} %bitcast.3), channel_id=1, source_target_pairs={{1,0},{2,1},{3,2},{5,4},{6,5},{7,6},{9,8},{10,9},{11,10},{13,12},{... | collective-permute-start | bytes 786440 | tf_op jit(solution)/shard_map/ppermute | solution.py:368
  7.0 5.1 %own.1 = (f32[512,128]{1,0:T(8,128)}, bf16[192,128]{1,0:T(8,128)(2,1)}) custom-call(s32[1]{0:T(128)S(6)} %copy.8.count_ref, bf16[512,512]{1,0:T(8,128)(2,1)} %bitcast.10, bf16[27,512,128]{2,1,0:T(8,128)(2,1)} %w_ref.1, s32[4,128]{1,0:T(4,128)} %bitcast.11), custom_call_target="tpu_custom_call" | custom-call | flops 1200000000 | bytes 4500000 | tf_op jit(solution)/shard_map/own/pallas_call | solution.py:373
  12.2 0.0 collective-permute-done.prev_ref
  12.2 0.0 collective-permute-done.1.next_ref
  12.2 0.0 copy-done
  12.2 0.0 copy-done.5
  12.2 0.0 copy-start.2
  12.2 0.9 %copy-done.2 = f32[512,128]{1,0:T(8,128)S(1)} copy-done((f32[512,128]{1,0:T(8,128)S(1)}, f32[512,128]{1,0:T(8,128)}, u32[]{:S(2)}) %copy-start.2) | copy-done | bytes 262168
  13.2 0.0 copy-start.3
  13.2 0.8 copy-done.3
  14.0 2.1 %halo.1 = bf16[192,640]{1,0:T(8,128)(2,1)S(1)} custom-call(s32[1]{0:T(128)S(6)} %copy.8.count_ref, s32[512]{0:T(512)S(1)} %copy-done.5, f32[512,128]{1,0:T(8,128)S(1)} %copy-done.2, bf16[256,512]{1,0:T(8,128)(2,1)} %collective-permute-done.prev_ref, bf16[256,512]{1,0:T(8,128)(2,1)} %collective-permute-done.1.next_ref, bf16[27,512,128]{2,1,0:T(8,128)(2,1)S(1)} %copy-done, ...), custom_call_target="tpu_custom_call" | custom-call | flops 600000000 | bytes 4500000 | tf_op jit(solution)/shard_map/halo/pallas_call | solution.py:389
  16.1 0.0 copy-start.1
  16.1 0.7 copy-done.1
  16.8 6.6 %all-to-all-start = ((bf16[8,24,640]{2,1,0:T(8,128)(2,1)}), bf16[8,24,640]{2,1,0:T(8,128)(2,1)S(1)}, u32[]{:S(2)}, u32[]{:S(2)}) async-start(bf16[8,24,640]{2,1,0:T(8,128)(2,1)} %bitcast.8), calls=%async_computation | async-start | bytes 491520 | tf_op jit(solution)/shard_map/all_to_all | solution.py:400
  23.4 7.7 %fold.1.fold_hbm = bf16[3,1024,512]{2,1,0:T(8,128)(2,1)} custom-call(bf16[512,2048]{1,0:T(8,128)(2,1)} %e_hbm.3, bf16[3,2048,512]{2,1,0:T(8,128)(2,1)} %w_hbm.3), custom_call_target="tpu_custom_call" | custom-call | flops 3300000000 | bytes 14000000 | tf_op jit(solution)/shard_map/fold/pallas_call | solution.py:403
  31.1 1.4 %all-to-all-done = bf16[8,24,640]{2,1,0:T(8,128)(2,1)S(1)} async-done(((bf16[8,24,640]{2,1,0:T(8,128)(2,1)}), bf16[8,24,640]{2,1,0:T(8,128)(2,1)S(1)}, u32[]{:S(2)}, u32[]{:S(2)}) %all-to-all-start) | async-done | bytes 245792 | tf_op jit(solution)/shard_map/all_to_all | solution.py:400
  32.5 11.2 %all_gather.3 = bf16[8,96,640]{2,1,0:T(8,128)(2,1)} all-gather(bf16[8,24,640]{2,1,0:T(8,128)(2,1)S(1)} %all-to-all-done), channel_id=1, replica_groups=mesh['bag'=8,'head'=4] {'head'}, dimensions={1}, use_global_device_ids=true | all-gather | bytes 1228800 | tf_op jit(solution)/shard_map/all_gather | solution.py:417
  43.7 0.0 copy-start.4
  43.7 11.7 %bag.1 = bf16[32,24,512]{2,1,0:T(8,128)(2,1)} custom-call(bf16[768,640]{1,0:T(8,128)(2,1)} %bitcast.9, bf16[512,2048]{1,0:T(8,128)(2,1)} %e_hbm.3, bf16[3,1024,512]{2,1,0:T(8,128)(2,1)} %fold.1.fold_hbm), custom_call_target="tpu_custom_call" | custom-call | flops 5000000000 | bytes 8000000 | tf_op jit(solution)/shard_map/bag/pallas_call | solution.py:421
  55.4 26.3 %all_to_all.10 = bf16[32,24,512]{2,1,0:T(8,128)(2,1)S(1)} all-to-all(bf16[32,24,512]{2,1,0:T(8,128)(2,1)} %bag.1), channel_id=1, replica_groups=mesh['bag'=8,'head'=4] {'head','bag'}, dimensions={0} | all-to-all | bytes 1572864 | tf_op jit(solution)/shard_map/all_to_all | solution.py:439
  81.7 0.0 copy-done.4
  81.7 1.1 %collect.1 = bf16[128,2048]{1,0:T(8,128)(2,1)} custom-call(s32[1]{0:T(128)S(6)} %copy.8.count_ref, bf16[192,128]{1,0:T(8,128)(2,1)S(1)} %copy-done.4, bf16[768,512]{1,0:T(8,128)(2,1)S(1)} %bitcast.7), custom_call_target="tpu_custom_call" | custom-call | tf_op jit(solution)/shard_map/collect/pallas_call | solution.py:440
Async XLA Ops:
  0.0 12.2 %copy-start = (bf16[27,512,128]{2,1,0:T(8,128)(2,1)S(1)}, bf16[27,512,128]{2,1,0:T(8,128)(2,1)}, u32[]{:S(2)}) copy-start(bf16[27,512,128]{2,1,0:T(8,128)(2,1)} %w_ref.1) | copy-start | bytes 10616836
  0.0 12.2 %copy-start.5 = (s32[512]{0:T(512)S(1)}, s32[512]{0:T(512)}, u32[]{:S(2)}) copy-start(s32[512]{0:T(512)} %sample_ref.1) | copy-start | bytes 6148
  2.0 10.2 %collective-permute-start = (bf16[256,512]{1,0:T(8,128)(2,1)}, bf16[256,512]{1,0:T(8,128)(2,1)}, u32[]{:S(2)}, u32[]{:S(2)}) collective-permute-start(bf16[256,512]{1,0:T(8,128)(2,1)} %bitcast.2), channel_id=1, source_target_pairs={{0,1},{1,2},{2,3},{4,5},{5,6},{6,7},{8,9},{9,10},{10,11},{12,13},{... | collective-permute-start | bytes 786440 | tf_op jit(solution)/shard_map/ppermute | solution.py:367
  5.1 7.1 %collective-permute-start.1 = (bf16[256,512]{1,0:T(8,128)(2,1)}, bf16[256,512]{1,0:T(8,128)(2,1)}, u32[]{:S(2)}, u32[]{:S(2)}) collective-permute-start(bf16[256,512]{1,0:T(8,128)(2,1)} %bitcast.3), channel_id=1, source_target_pairs={{1,0},{2,1},{3,2},{5,4},{6,5},{7,6},{9,8},{10,9},{11,10},{13,12},{... | collective-permute-start | bytes 786440 | tf_op jit(solution)/shard_map/ppermute | solution.py:368
  12.2 1.0 %copy-start.2 = (f32[512,128]{1,0:T(8,128)S(1)}, f32[512,128]{1,0:T(8,128)}, u32[]{:S(2)}) copy-start(f32[512,128]{1,0:T(8,128)} %get-tuple-element.8.acc_ref) | copy-start | bytes 786436
  13.2 0.8 copy-start.3
  16.1 0.7 copy-start.1
  16.8 15.7 %all-to-all-start = ((bf16[8,24,640]{2,1,0:T(8,128)(2,1)}), bf16[8,24,640]{2,1,0:T(8,128)(2,1)S(1)}, u32[]{:S(2)}, u32[]{:S(2)}) async-start(bf16[8,24,640]{2,1,0:T(8,128)(2,1)} %bitcast.8), calls=%async_computation | async-start | bytes 491520 | tf_op jit(solution)/shard_map/all_to_all | solution.py:400
  43.7 38.0 %copy-start.4 = (bf16[192,128]{1,0:T(8,128)(2,1)S(1)}, bf16[192,128]{1,0:T(8,128)(2,1)}, u32[]{:S(2)}) copy-start(bf16[192,128]{1,0:T(8,128)(2,1)} %get-tuple-element.7.onehot_ref) | copy-start | bytes 147460

commit v6 on v5

--- a/solution.py
+++ b/solution.py
@@ -14,9 +14,9 @@
 epsilon = 1e-06
 far_below = -1e30
 
-SMEM = pl.BlockSpec(memory_space=pltpu.SMEM)
 VMEM = pl.BlockSpec(memory_space=pltpu.VMEM)
 ANY = pl.BlockSpec(memory_space=pl.ANY)
+FOLD_LIMIT = 24
 
 
 def limit(mib):
@@ -83,23 +83,33 @@
     return products
 
 
-def own_kernel(
-    bags, cap, rows, cols, frames, count_ref, x_hbm, w_hbm, route_ref, acc_ref, onehot_ref, x_ref, w_ref, sems
-):
+def scalar_of(ref):
+    return jnp.max(ref[...])
+
+
+def edge_kernel(rows, cols, frames, count_ref, x_hbm, w_hbm, up_ref, down_ref, x_ref, w_ref, sems):
     loads = [
         pltpu.make_async_copy(x_hbm, x_ref, sems.at[0]),
         pltpu.make_async_copy(w_hbm, w_ref, sems.at[1]),
     ]
     for load in loads:
         load.start()
-    count = count_ref[0]
+    count = scalar_of(count_ref)
+    area = rows * cols
+    first = lax.axis_index("head") * frames
+    for load in loads:
+        load.wait()
+    for out_ref, f, tap in ((up_ref, frames - 1, 0), (down_ref, 0, 2)):
+        value = x_ref[f * area : (f + 1) * area, :]
+        value = jnp.where(first + f < count, value, jnp.zeros_like(value))
+        out_ref[...] = combine(plane_products([(tap, value)], w_ref), rows, cols)
+
+
+def own_kernel(bags, cap, rows, cols, frames, count_ref, x_ref, w_ref, route_ref, acc_ref, onehot_ref):
+    count = scalar_of(count_ref)
     place = lax.axis_index("head")
     area = rows * cols
     first = place * frames
-    route_row = route_ref[pl.ds(place, 1), :]
-    onehot_ref[...] = onehot_of(slot_of(route_row, bags, cap, cap), bags * cap)
-    for load in loads:
-        load.wait()
     inputs = []
     for f in range(frames):
         value = x_ref[f * area : (f + 1) * area, :]
@@ -107,31 +117,24 @@
     for f in range(frames):
         pieces = [(t, inputs[f + t - 1]) for t in range(TAPS) if 0 <= f + t - 1 < frames]
         acc_ref[f * area : (f + 1) * area, :] = combine(plane_products(pieces, w_ref), rows, cols)
-
-
-def halo_kernel(
-    rows, cols, frames, count_ref, sample_ref, acc_ref, prev_ref, next_ref, w_ref, onehot_ref, out_ref, grid_ref
+    route_row = route_ref[pl.ds(place, 1), :]
+    onehot_ref[...] = onehot_of(slot_of(route_row, bags, cap, cap), bags * cap)
+
+
+def join_kernel(
+    rows, cols, frames, count_ref, sample_ref, acc_ref, prev_ref, next_ref, onehot_ref, e_ref, out_ref, grid_ref
 ):
-    count = count_ref[0]
-    sample = sample_ref[0]
-    place = lax.axis_index("head")
+    count = scalar_of(count_ref)
+    sample = scalar_of(sample_ref)
     area = rows * cols
-    first = place * frames
-    chans = w_ref.shape[2]
-
-    def masked(value, frame):
-        live = jnp.logical_and(frame >= 0, frame < count)
-        return jnp.where(live, value, jnp.zeros_like(value))
-
+    first = lax.axis_index("head") * frames
+    chans = acc_ref.shape[1]
     for f in range(frames):
         part = acc_ref[f * area : (f + 1) * area, :]
-        pieces = []
         if f == 0:
-            pieces.append((0, masked(prev_ref[...], first - 1)))
+            part = part + prev_ref[...]
         if f == frames - 1:
-            pieces.append((2, masked(next_ref[...], first + frames)))
-        if pieces:
-            part = part + combine(plane_products(pieces, w_ref), rows, cols)
+            part = part + next_ref[...]
         grid_ref[f * area : (f + 1) * area, :] = jnp.where(first + f < count, part, 0.0)
     pieces = [[None] * 2 for _ in range(2)]
     for odd in range(2):
@@ -140,11 +143,24 @@
         for i in range(2):
             pieces[i][odd] = half[:, i].reshape(frames * area // 4, chans)
     tokens = frames * area // 4
+    patches = jnp.concatenate(
+        [pieces[0][0], pieces[0][1], pieces[1][0], pieces[1][1]], axis=1
+    ).astype(jnp.bfloat16)
+    model = e_ref.shape[1]
+    col_tile = 256
+    total = None
+    for n in range(0, model, col_tile):
+        part = jnp.dot(patches, e_ref[:, n : n + col_tile], preferred_element_type=jnp.float32)
+        squares = part * part
+        both = squares[:, :LANES] + squares[:, LANES:]
+        total = both if total is None else total + both
+    scale = lax.rsqrt(jnp.sum(total, axis=-1, keepdims=True) * (1.0 / model) + epsilon)
+    high = scale.astype(jnp.bfloat16).astype(jnp.float32)
     frame = first + lax.broadcasted_iota(jnp.int32, (tokens, LANES), 0) // (area // 4)
+    lane = lax.broadcasted_iota(jnp.int32, (tokens, LANES), 1)
     label = jnp.where(frame < count, sample + 1, 0).astype(jnp.float32)
-    patches = jnp.concatenate(
-        [pieces[0][0], pieces[0][1], pieces[1][0], pieces[1][1], label], axis=1
-    ).astype(jnp.bfloat16)
+    notes = jnp.where(lane == 0, label, jnp.where(lane == 1, high, jnp.where(lane == 2, scale - high, 0.0)))
+    patches = jnp.concatenate([patches, notes.astype(jnp.bfloat16)], axis=1)
     out_ref[...] = jnp.dot(onehot_ref[...], patches, preferred_element_type=jnp.float32).astype(
         jnp.bfloat16
     )
@@ -172,23 +188,15 @@
             fold_ref[m, feats:, cols] = (product - high.astype(jnp.float32)).astype(jnp.bfloat16)
 
 
-def bag_kernel(
-    clips, cap, x_ref, e_hbm, fold_hbm, out_ref, e_ref, fold_ref, qkv_ref, total_ref, m_ref, r_ref, order_ref, sems
-):
-    loads = [
-        pltpu.make_async_copy(e_hbm, e_ref, sems.at[0]),
-        pltpu.make_async_copy(fold_hbm, fold_ref, sems.at[1]),
-    ]
-    for load in loads:
-        load.start()
+def bag_kernel(clips, cap, x_ref, fold_ref, out_ref, qkv_ref, m_ref, r_ref, order_ref):
     count_slots = x_ref.shape[0]
-    feats, model = e_ref.shape
+    feats = x_ref.shape[1] - LANES
     width = fold_ref.shape[2]
     clip_rows = count_slots // clips
 
     for c in range(clips):
-        note = x_ref[c * clip_rows : (c + 1) * clip_rows, feats:].astype(jnp.float32)
-        order_ref[clips + c] = jnp.max(note).astype(jnp.int32)
+        note = x_ref[c * clip_rows : (c + 1) * clip_rows, feats : feats + LANES].astype(jnp.float32)
+        order_ref[clips + c] = jnp.max(note[:, :1]).astype(jnp.int32)
     starts = [jnp.int32(0)]
     for s in range(SAMPLES):
 
@@ -205,23 +213,13 @@
 
     col_tile = 256
     patch = x_ref[:, :feats]
-    loads[0].wait()
-    for n in range(0, model, col_tile):
-        part = jnp.dot(patch, e_ref[:, n : n + col_tile], preferred_element_type=jnp.float32)
-        squares = part * part
-        both = squares[:, :LANES] + squares[:, LANES:]
-        total_ref[...] = both if n == 0 else total_ref[...] + both
-    mean = jnp.sum(total_ref[...], axis=-1, keepdims=True) * (1.0 / model)
-    total_ref[...] = jnp.broadcast_to(lax.rsqrt(mean + epsilon), total_ref.shape)
+    notes = x_ref[:, feats:].astype(jnp.float32)
+    scale = jnp.broadcast_to(notes[:, 1:2] + notes[:, 2:3], (count_slots, col_tile))
     twice = jnp.concatenate([patch, patch], axis=1)
-    loads[1].wait()
     for m in range(3):
         for n in range(0, width, col_tile):
             part = jnp.dot(twice, fold_ref[m, :, n : n + col_tile], preferred_element_type=jnp.float32)
-            scale = total_ref[...]
-            qkv_ref[m, :, n : n + col_tile] = (
-                part * jnp.concatenate([scale] * (col_tile // LANES), axis=1)
-            ).astype(jnp.bfloat16)
+            qkv_ref[m, :, n : n + col_tile] = (part * scale).astype(jnp.bfloat16)
 
     out_ref[...] = jnp.zeros_like(out_ref)
     tile = 2 * clip_rows
@@ -335,7 +333,7 @@
 
 
 def collect_kernel(frames, heads, count_ref, onehot_ref, recv_ref, out_ref):
-    count = count_ref[0]
+    count = scalar_of(count_ref)
     place = lax.axis_index("head")
     slots, tokens = onehot_ref.shape
     frame = place * frames + lax.broadcasted_iota(jnp.int32, (slots, tokens), 1) // (tokens // frames)
@@ -362,40 +360,50 @@
     local_width = qkv_weight.shape[2]
     chans = conv_weight.shape[2]
 
-    tile = latents.reshape(frames_dev, area, depth)
+    tile = latents.reshape(frames_dev * area, depth)
+    count = frame_counts.reshape(1, 1)
+    edge = jax.ShapeDtypeStruct((area, chans), jnp.float32)
+    upward, downward = pl.pallas_call(
+        functools.partial(edge_kernel, rows, cols, frames_dev),
+        out_shape=(edge, edge),
+        in_specs=[VMEM, ANY, ANY],
+        out_specs=(VMEM, VMEM),
+        scratch_shapes=[
+            pltpu.VMEM(tile.shape, jnp.bfloat16),
+            pltpu.VMEM(conv_weight.shape, jnp.bfloat16),
+            pltpu.SemaphoreType.DMA((2,)),
+        ],
+        cost_estimate=pl.CostEstimate(flops=600000000, bytes_accessed=4500000, transcendentals=0),
+        name="edge",
+    )(count, tile, conv_weight)
     ends = heads_dev - 1
-    prev_frame = lax.ppermute(tile[frames_dev - 1], "head", [(i, i + 1) for i in range(ends)])
-    next_frame = lax.ppermute(tile[0], "head", [(i + 1, i) for i in range(ends)])
+    from_prev = lax.ppermute(upward, "head", [(i, i + 1) for i in range(ends)])
+    from_next = lax.ppermute(downward, "head", [(i + 1, i) for i in range(ends)])
 
     route_rows = routes[:, 0].reshape(heads_dev, tok_dev)
     row_width = 4 * chans + LANES
-    model = embed_weight.shape[1]
     acc, onehot = pl.pallas_call(
         functools.partial(own_kernel, bags, cap, rows, cols, frames_dev),
         out_shape=(
             jax.ShapeDtypeStruct((frames_dev * area, chans), jnp.float32),
             jax.ShapeDtypeStruct((slots, tok_dev), jnp.bfloat16),
         ),
-        in_specs=[SMEM, ANY, ANY, VMEM],
+        in_specs=[VMEM, VMEM, VMEM, VMEM],
         out_specs=(VMEM, VMEM),
-        scratch_shapes=[
-            pltpu.VMEM((frames_dev * area, depth), jnp.bfloat16),
-            pltpu.VMEM(conv_weight.shape, jnp.bfloat16),
-            pltpu.SemaphoreType.DMA((2,)),
-        ],
+        compiler_params=limit(16),
         cost_estimate=pl.CostEstimate(flops=1200000000, bytes_accessed=4500000, transcendentals=0),
         name="own",
-    )(frame_counts, tile.reshape(frames_dev * area, depth), conv_weight, route_rows)
+    )(count, tile, conv_weight, route_rows)
     outgoing = pl.pallas_call(
-        functools.partial(halo_kernel, rows, cols, frames_dev),
+        functools.partial(join_kernel, rows, cols, frames_dev),
         out_shape=jax.ShapeDtypeStruct((slots, row_width), jnp.bfloat16),
-        in_specs=[SMEM, SMEM, VMEM, VMEM, VMEM, VMEM, VMEM],
+        in_specs=[VMEM] * 7,
         out_specs=VMEM,
         scratch_shapes=[pltpu.VMEM((frames_dev * area, chans), jnp.float32)],
         compiler_params=limit(16),
-        cost_estimate=pl.CostEstimate(flops=600000000, bytes_accessed=4500000, transcendentals=0),
-        name="halo",
-    )(frame_counts, samples, acc, prev_frame, next_frame, conv_weight, onehot)
+        cost_estimate=pl.CostEstimate(flops=300000000, bytes_accessed=3000000, transcendentals=0),
+        name="join",
+    )(count, samples.reshape(heads_dev, tok_dev), acc, from_prev, from_next, onehot, embed_weight)
 
     arrived = lax.all_to_all(
         outgoing.reshape(bags, cap, row_width), "bag", split_axis=0, concat_axis=0, tiled=True
@@ -410,6 +418,7 @@
             pltpu.VMEM(qkv_weight.shape, jnp.bfloat16),
             pltpu.SemaphoreType.DMA((4,)),
         ],
+        compiler_params=limit(FOLD_LIMIT),
         cost_estimate=pl.CostEstimate(flops=3300000000, bytes_accessed=14000000, transcendentals=0),
         name="fold",
     )(embed_weight, qkv_weight)
@@ -421,30 +430,27 @@
     attended = pl.pallas_call(
         functools.partial(bag_kernel, bags, cap),
         out_shape=jax.ShapeDtypeStruct((heads_dev * bags, cap, local_width), jnp.bfloat16),
-        in_specs=[VMEM, ANY, ANY],
+        in_specs=[VMEM, VMEM],
         out_specs=VMEM,
         scratch_shapes=[
-            pltpu.VMEM(embed_weight.shape, jnp.bfloat16),
-            pltpu.VMEM(folded.shape, jnp.bfloat16),
             pltpu.VMEM((3, count_slots, local_width), jnp.bfloat16),
-            pltpu.VMEM((count_slots, LANES), jnp.float32),
             pltpu.VMEM((heads_here, pair_rows, LANES), jnp.float32),
             pltpu.VMEM((heads_here, pair_rows, 2 * LANES), jnp.float32),
             pltpu.SMEM((2 * bags,), jnp.int32),
-            pltpu.SemaphoreType.DMA((2,)),
         ],
-        cost_estimate=pl.CostEstimate(flops=5000000000, bytes_accessed=8000000, transcendentals=1200000),
+        compiler_params=limit(28),
+        cost_estimate=pl.CostEstimate(flops=3000000000, bytes_accessed=5000000, transcendentals=1200000),
         name="bag",
-    )(gathered, embed_weight, folded)
+    )(gathered, folded)
     received = lax.all_to_all(attended, ("head", "bag"), split_axis=0, concat_axis=0, tiled=True)
     return pl.pallas_call(
         functools.partial(collect_kernel, frames_dev, heads_dev),
         out_shape=jax.ShapeDtypeStruct((tok_dev, heads_dev * local_width), jnp.bfloat16),
-        in_specs=[SMEM, VMEM, VMEM],
+        in_specs=[VMEM, VMEM, VMEM],
         out_specs=VMEM,
         compiler_params=limit(16),
         name="collect",
-    )(frame_counts, onehot, received.reshape(count_slots, local_width))
+    )(count, onehot, received.reshape(count_slots, local_width))
 
 
 def solution(mesh):

time: 83.4 us -> 75.9 us (0.910)
  Pallas kernels: 27.7 us -> 19 us
  blocking collectives: 37.5 us -> 38.9 us
  starting transfers between devices: 11 us -> 9.63 us
  local copies, waits for them, and re-layouts: 4.44 us -> 5.43 us
    pallas_call x1, Pallas kernels: 11.7 us -> 6.56 us  [shards(): pl.pallas_call(functools.partial(bag_kernel, bags, cap), out_shape=jax.Sh...]
    pallas_call x1, Pallas kernels: 5.12 us -> 1.56 us  [shards(): pl.pallas_call(functools.partial(own_kernel, bags, cap, rows, cols, frame...]
    pallas_call x1, Pallas kernels: 7.66 us -> 4.37 us  [shards(): pl.pallas_call(fold_kernel, out_shape=jax.ShapeDtypeStruct((3, 2 * embed_...]
    pallas_call x1 -> x2, Pallas kernels: 2.11 us -> 5.36 us  [the longest x1 3.98 us: shards(): pl.pallas_call(functools.partial(edge_kernel, rows, cols, frames_dev), ou...]
    unnamed x12 -> x18, local copies, waits for them, and re-layouts: 2.44 us -> 5.43 us
    slice x1 -> x0, local copies, waits for them, and re-layouts: 2 us -> none  [shards(): tile[0]]
    ppermute x2, waiting for transfers between devices: 0.01 us -> 1.62 us  [the longest x1 1.61 us: shards(): lax.ppermute(downward, 'head', [(i + 1, i) for i in range(ends)])]
    all_to_all x1, waiting for transfers between devices: 1.43 us -> 0.01 us  [shards(): lax.all_to_all(outgoing.reshape(bags, cap, row_width), 'bag', split_axis=...]
  transfers between devices with their start and end apart: 3 -> 3, of which waited for: 1 -> 1; matrix products, arithmetic and copies ran while one was open for 0% -> 0% of each run, Pallas kernels for 15% -> 8%
where the time goes in v6:
time: 75.9 us; the launch traced here: 75.5 us
  blocking collectives  38.9 us (51%)
  Pallas kernels  19 us (25%)
  starting transfers between devices  9.63 us (13%)
  local copies, waits for them, and re-layouts  5.43 us (7%)
  waiting for transfers between devices  1.62 us (2%)
  between operations  0.93 us (1%)
    all_to_all x1, blocking collectives, shards(): lax.all_to_all(attended, ('head', 'bag'), split_axis=0, concat_axis=0, ti...  27.4 us
    all_gather x1, blocking collectives, shards(): lax.all_gather(arrived, 'head', axis=1, tiled=True)  11.5 us
    pallas_call x1, Pallas kernels, shards(): pl.pallas_call(functools.partial(bag_kernel, bags, cap), out_shape=jax.Sh...  6.56 us
    all_to_all x1, starting transfers between devices, shards(): lax.all_to_all(outgoing.reshape(bags, cap, row_width), 'bag', split_axis=...  5.81 us
    unnamed x18, local copies, waits for them, and re-layouts  5.43 us
    pallas_call x1, Pallas kernels, shards(): pl.pallas_call(fold_kernel, out_shape=jax.ShapeDtypeStruct((3, 2 * embed_...  4.37 us
    pallas_call x1, Pallas kernels, shards(): pl.pallas_call(functools.partial(edge_kernel, rows, cols, frames_dev), ou...  3.98 us
    ppermute x1, starting transfers between devices, shards(): from_prev = lax.ppermute(upward, 'head', [(i, i + 1) for i in range(ends)])  2.53 us
  transfers between devices with their start and end apart: 3, of which 1 were waited for; matrix products, arithmetic and copies ran while one was open for 0% of the time, Pallas kernels for 8%

profile of v6, /device:TPU:0, one launch (start us, length us, event | category | flops | bytes accessed | tf_op | source)
XLA Modules:
  0.0 75.5 jit_solution(9847289318578335207)
XLA Ops:
  0.0 0.0 copy-start
  0.0 0.0 copy-start.8
  0.8 0.0 copy-start.6
  0.8 4.0 %edge.1 = (f32[256,128]{1,0:T(8,128)}, f32[256,128]{1,0:T(8,128)}) custom-call(s32[1,1]{1,0:T(1,128)} %bitcast.8.count_ref, bf16[512,512]{1,0:T(8,128)(2,1)} %bitcast.13, bf16[27,512,128]{2,1,0:T(8,128)(2,1)} %w_hbm.2), custom_call_target="tpu_custom_call" | custom-call | flops 600000000 | bytes 4500000 | tf_op jit(solution)/shard_map/edge/pallas_call | solution.py:366
  4.8 0.0 copy-start.1
  4.8 2.5 %collective-permute-start = (f32[256,128]{1,0:T(8,128)}, f32[256,128]{1,0:T(8,128)S(1)}, u32[]{:S(2)}, u32[]{:S(2)}) collective-permute-start(f32[256,128]{1,0:T(8,128)} %get-tuple-element.11), channel_id=1, source_target_pairs={{0,1},{1,2},{2,3},{4,5},{5,6},{6,7},{8,9},{9,10},{10,11},{12,13},{... | collective-permute-start | bytes 393224 | tf_op jit(solution)/shard_map/ppermute | solution.py:380
  7.4 1.3 %collective-permute-start.1 = (f32[256,128]{1,0:T(8,128)}, f32[256,128]{1,0:T(8,128)S(1)}, u32[]{:S(2)}, u32[]{:S(2)}) collective-permute-start(f32[256,128]{1,0:T(8,128)} %get-tuple-element.12), channel_id=1, source_target_pairs={{1,0},{2,1},{3,2},{5,4},{6,5},{7,6},{9,8},{10,9},{11,10},{13,12},{... | collective-permute-start | bytes 393224 | tf_op jit(solution)/shard_map/ppermute | solution.py:381
  8.7 0.0 copy-done
  8.7 0.0 copy-done.8
  8.7 0.0 copy-start.3
  8.7 1.0 %copy-done.3 = bf16[1,2,16,16,512]{4,3,2,1,0:T(8,128)(2,1)S(1)} copy-done((bf16[1,2,16,16,512]{4,3,2,1,0:T(8,128)(2,1)S(1)}, bf16[1,2,16,16,512]{4,3,2,1,0:T(8,128)(2,1)}, u32[]{:S(2)}) %copy-start.3) | copy-done | bytes 524312
  9.7 1.6 %own.1 = (f32[512,128]{1,0:T(8,128)S(1)}, bf16[192,128]{1,0:T(8,128)(2,1)S(1)}) custom-call(s32[1,1]{1,0:T(1,128)} %bitcast.7.count_ref, bf16[512,512]{1,0:T(8,128)(2,1)S(1)} %bitcast.14, bf16[27,512,128]{2,1,0:T(8,128)(2,1)S(1)} %copy-done, s32[4,128]{1,0:T(4,128)S(1)} %bitcast.16), custom_call_target="tpu_custom_call" | custom-call | flops 1200000000 | bytes 4500000 | tf_op jit(solution)/shard_map/own/pallas_call | solution.py:385
  11.3 0.0 copy-start.4
  11.3 0.0 collective-permute-done.prev_ref
  11.3 1.6 %collective-permute-done.1.next_ref = f32[256,128]{1,0:T(8,128)S(1)} collective-permute-done((f32[256,128]{1,0:T(8,128)}, f32[256,128]{1,0:T(8,128)S(1)}, u32[]{:S(2)}, u32[]{:S(2)}) %collective-permute-start.1) | collective-permute-done | bytes 131104 | tf_op jit(solution)/shard_map/ppermute | solution.py:381
  12.9 0.0 copy-done.6
  12.9 0.0 copy-done.1
  12.9 1.4 %join.1 = bf16[192,640]{1,0:T(8,128)(2,1)} custom-call(s32[1,1]{1,0:T(1,128)} %bitcast.9.count_ref, s32[4,128]{1,0:T(4,128)S(1)} %bitcast.15, f32[512,128]{1,0:T(8,128)S(1)} %get-tuple-element.10.acc_ref, f32[256,128]{1,0:T(8,128)S(1)} %collective-permute-done.prev_ref, f32[256,128]{1,0:T(8,128)S(1)} %collective-permute-done.1.next_ref, ...), custom_call_target="tpu_custom_call" | custom-call | flops 300000000 | bytes 3000000 | tf_op jit(solution)/shard_map/join/pallas_call | solution.py:397
  14.3 0.0 copy-done.4
  14.3 5.8 %all-to-all-start = ((bf16[8,24,640]{2,1,0:T(8,128)(2,1)}), bf16[8,24,640]{2,1,0:T(8,128)(2,1)S(1)}, u32[]{:S(2)}, u32[]{:S(2)}) async-start(bf16[8,24,640]{2,1,0:T(8,128)(2,1)} %bitcast.4), calls=%async_computation | async-start | bytes 491520 | tf_op jit(solution)/shard_map/all_to_all | solution.py:408
  20.1 0.0 copy-start.2
  20.1 1.6 %copy-done.2 = bf16[512,2048]{1,0:T(8,128)(2,1)S(1)} copy-done((bf16[512,2048]{1,0:T(8,128)(2,1)S(1)}, bf16[512,2048]{1,0:T(8,128)(2,1)}, u32[]{:S(2)}) %copy-start.2) | copy-done | bytes 2097176
  21.7 0.0 copy-start.7
  21.7 2.8 %copy-done.7 = bf16[3,2048,512]{2,1,0:T(8,128)(2,1)S(1)} copy-done((bf16[3,2048,512]{2,1,0:T(8,128)(2,1)S(1)}, bf16[3,2048,512]{2,1,0:T(8,128)(2,1)}, u32[]{:S(2)}) %copy-start.7) | copy-done | bytes 6291480
  24.5 4.4 %fold.1.fold_ref = bf16[3,1024,512]{2,1,0:T(8,128)(2,1)S(1)} custom-call(bf16[512,2048]{1,0:T(8,128)(2,1)S(1)} %copy-done.2, bf16[3,2048,512]{2,1,0:T(8,128)(2,1)S(1)} %copy-done.7), custom_call_target="tpu_custom_call" | custom-call | flops 3300000000 | bytes 14000000 | tf_op jit(solution)/shard_map/fold/pallas_call | solution.py:411
  28.9 0.0 all-to-all-done
  28.9 11.5 %all_gather.3 = bf16[8,96,640]{2,1,0:T(8,128)(2,1)S(1)} all-gather(bf16[8,24,640]{2,1,0:T(8,128)(2,1)S(1)} %all-to-all-done), channel_id=1, replica_groups=mesh['bag'=8,'head'=4] {'head'}, dimensions={1}, use_global_device_ids=true | all-gather | bytes 1228800 | tf_op jit(solution)/shard_map/all_gather | solution.py:426
  40.4 0.0 copy-start.5
  40.4 6.6 %bag.1 = bf16[32,24,512]{2,1,0:T(8,128)(2,1)S(1)} custom-call(bf16[768,640]{1,0:T(8,128)(2,1)S(1)} %bitcast.12, bf16[3,1024,512]{2,1,0:T(8,128)(2,1)S(1)} %fold.1.fold_ref), custom_call_target="tpu_custom_call" | custom-call | flops 3000000000 | bytes 5000000 | tf_op jit(solution)/shard_map/bag/pallas_call | solution.py:430
  46.9 27.4 %all_to_all.10 = bf16[32,24,512]{2,1,0:T(8,128)(2,1)S(1)} all-to-all(bf16[32,24,512]{2,1,0:T(8,128)(2,1)S(1)} %bag.1), channel_id=1, replica_groups=mesh['bag'=8,'head'=4] {'head','bag'}, dimensions={0} | all-to-all | bytes 1572864 | tf_op jit(solution)/shard_map/all_to_all | solution.py:445
  74.4 0.0 copy-done.5
  74.4 1.2 %collect.1 = bf16[128,2048]{1,0:T(8,128)(2,1)} custom-call(s32[1,1]{1,0:T(1,128)} %bitcast.10.count_ref, bf16[192,128]{1,0:T(8,128)(2,1)S(1)} %copy-done.5, bf16[768,512]{1,0:T(8,128)(2,1)S(1)} %bitcast.11), custom_call_target="tpu_custom_call" | custom-call | tf_op jit(solution)/shard_map/collect/pallas_call | solution.py:446
Async XLA Ops:
  0.0 8.7 %copy-start = (bf16[27,512,128]{2,1,0:T(8,128)(2,1)S(1)}, bf16[27,512,128]{2,1,0:T(8,128)(2,1)}, u32[]{:S(2)}) copy-start(bf16[27,512,128]{2,1,0:T(8,128)(2,1)} %w_hbm.2) | copy-start | bytes 10616836
  0.0 8.7 %copy-start.8 = (s32[512,1]{0,1:T(1,128)S(1)}, s32[512,1]{0,1:T(1,128)}, u32[]{:S(2)}) copy-start(s32[512,1]{0,1:T(1,128)} %param.9) | copy-start | bytes 6148
  0.8 12.1 %copy-start.6 = (s32[512]{0:T(512)S(1)}, s32[512]{0:T(512)}, u32[]{:S(2)}) copy-start(s32[512]{0:T(512)} %param.10) | copy-start | bytes 6148
  4.8 8.1 %copy-start.1 = (bf16[512,2048]{1,0:T(8,128)(2,1)S(1)}, bf16[512,2048]{1,0:T(8,128)(2,1)}, u32[]{:S(2)}) copy-start(bf16[512,2048]{1,0:T(8,128)(2,1)} %e_hbm.1) | copy-start | bytes 6291460
  4.8 6.5 %collective-permute-start = (f32[256,128]{1,0:T(8,128)}, f32[256,128]{1,0:T(8,128)S(1)}, u32[]{:S(2)}, u32[]{:S(2)}) collective-permute-start(f32[256,128]{1,0:T(8,128)} %get-tuple-element.11), channel_id=1, source_target_pairs={{0,1},{1,2},{2,3},{4,5},{5,6},{6,7},{8,9},{9,10},{10,11},{12,13},{... | collective-permute-start | bytes 393224 | tf_op jit(solution)/shard_map/ppermute | solution.py:380
  7.4 5.6 %collective-permute-start.1 = (f32[256,128]{1,0:T(8,128)}, f32[256,128]{1,0:T(8,128)S(1)}, u32[]{:S(2)}, u32[]{:S(2)}) collective-permute-start(f32[256,128]{1,0:T(8,128)} %get-tuple-element.12), channel_id=1, source_target_pairs={{1,0},{2,1},{3,2},{5,4},{6,5},{7,6},{9,8},{10,9},{11,10},{13,12},{... | collective-permute-start | bytes 393224 | tf_op jit(solution)/shard_map/ppermute | solution.py:381
  8.7 1.0 %copy-start.3 = (bf16[1,2,16,16,512]{4,3,2,1,0:T(8,128)(2,1)S(1)}, bf16[1,2,16,16,512]{4,3,2,1,0:T(8,128)(2,1)}, u32[]{:S(2)}) copy-start(bf16[1,2,16,16,512]{4,3,2,1,0:T(8,128)(2,1)} %param.7) | copy-start | bytes 1572868
  11.3 3.0 %copy-start.4 = (bf16[192,128]{1,0:T(8,128)(2,1)}, bf16[192,128]{1,0:T(8,128)(2,1)S(1)}, u32[]{:S(2)}) copy-start(bf16[192,128]{1,0:T(8,128)(2,1)S(1)} %get-tuple-element.9.onehot_ref) | copy-start | bytes 147460
  14.3 14.6 %all-to-all-start = ((bf16[8,24,640]{2,1,0:T(8,128)(2,1)}), bf16[8,24,640]{2,1,0:T(8,128)(2,1)S(1)}, u32[]{:S(2)}, u32[]{:S(2)}) async-start(bf16[8,24,640]{2,1,0:T(8,128)(2,1)} %bitcast.4), calls=%async_computation | async-start | bytes 491520 | tf_op jit(solution)/shard_map/all_to_all | solution.py:408
  20.1 1.6 %copy-start.2 = (bf16[512,2048]{1,0:T(8,128)(2,1)S(1)}, bf16[512,2048]{1,0:T(8,128)(2,1)}, u32[]{:S(2)}) copy-start(bf16[512,2048]{1,0:T(8,128)(2,1)} %e_hbm.1) | copy-start | bytes 6291460
  21.7 2.8 %copy-start.7 = (bf16[3,2048,512]{2,1,0:T(8,128)(2,1)S(1)}, bf16[3,2048,512]{2,1,0:T(8,128)(2,1)}, u32[]{:S(2)}) copy-start(bf16[3,2048,512]{2,1,0:T(8,128)(2,1)} %w_hbm.3) | copy-start | bytes 18874372
  40.4 34.0 %copy-start.5 = (bf16[192,128]{1,0:T(8,128)(2,1)S(1)}, bf16[192,128]{1,0:T(8,128)(2,1)}, u32[]{:S(2)}) copy-start(bf16[192,128]{1,0:T(8,128)(2,1)} %copy-done.4) | copy-start | bytes 147460

commit v7 on v6

--- a/solution.py
+++ b/solution.py
@@ -16,7 +16,7 @@
 
 VMEM = pl.BlockSpec(memory_space=pltpu.VMEM)
 ANY = pl.BlockSpec(memory_space=pl.ANY)
-FOLD_LIMIT = 24
+EDGE_LIMIT = 60
 
 
 def limit(mib):
@@ -88,21 +88,32 @@
 
 
 def edge_kernel(rows, cols, frames, count_ref, x_hbm, w_hbm, up_ref, down_ref, x_ref, w_ref, sems):
-    loads = [
-        pltpu.make_async_copy(x_hbm, x_ref, sems.at[0]),
-        pltpu.make_async_copy(w_hbm, w_ref, sems.at[1]),
-    ]
-    for load in loads:
-        load.start()
+    area = rows * cols
+    plane = TAPS * TAPS
+    jobs = ((up_ref, frames - 1, 0), (down_ref, 0, 2))
+    loads = []
+    for i, (_, f, tap) in enumerate(jobs):
+        loads.append(
+            (
+                pltpu.make_async_copy(
+                    x_hbm.at[pl.ds(f * area, area)], x_ref.at[pl.ds(i * area, area)], sems.at[2 * i]
+                ),
+                pltpu.make_async_copy(
+                    w_hbm.at[pl.ds(tap * plane, plane)], w_ref.at[pl.ds(i * plane, plane)], sems.at[2 * i + 1]
+                ),
+            )
+        )
+    for pair in loads:
+        for load in pair:
+            load.start()
     count = scalar_of(count_ref)
-    area = rows * cols
     first = lax.axis_index("head") * frames
-    for load in loads:
-        load.wait()
-    for out_ref, f, tap in ((up_ref, frames - 1, 0), (down_ref, 0, 2)):
-        value = x_ref[f * area : (f + 1) * area, :]
+    for i, (out_ref, f, _) in enumerate(jobs):
+        for load in loads[i]:
+            load.wait()
+        value = x_ref[i * area : (i + 1) * area, :]
         value = jnp.where(first + f < count, value, jnp.zeros_like(value))
-        out_ref[...] = combine(plane_products([(tap, value)], w_ref), rows, cols)
+        out_ref[...] = combine(plane_products([(i, value)], w_ref), rows, cols)
 
 
 def own_kernel(bags, cap, rows, cols, frames, count_ref, x_ref, w_ref, route_ref, acc_ref, onehot_ref):
@@ -166,18 +177,11 @@
     )
 
 
-def fold_kernel(e_hbm, w_hbm, fold_ref, e_ref, w_ref, sems):
+def fold_kernel(e_ref, w_ref, after_ref, fold_ref):
     feats = e_ref.shape[0]
     width = w_ref.shape[2]
-    loads = [pltpu.make_async_copy(e_hbm, e_ref, sems.at[3])]
-    for m in range(3):
-        loads.append(pltpu.make_async_copy(w_hbm.at[m], w_ref.at[m], sems.at[m]))
-    for load in loads:
-        load.start()
-    loads[0].wait()
     col_tile = 256
     for m in range(3):
-        loads[1 + m].wait()
         for n in range(0, width, col_tile):
             cols = slice(n, n + col_tile)
             product = jnp.dot(e_ref[...], w_ref[m, :, cols], preferred_element_type=jnp.float32)
@@ -188,14 +192,24 @@
             fold_ref[m, feats:, cols] = (product - high.astype(jnp.float32)).astype(jnp.bfloat16)
 
 
-def bag_kernel(clips, cap, x_ref, fold_ref, out_ref, qkv_ref, m_ref, r_ref, order_ref):
-    count_slots = x_ref.shape[0]
-    feats = x_ref.shape[1] - LANES
+def bag_kernel(clips, cap, masks, *refs):
+    pieces, (fold_ref, out_ref, qkv_ref, note_ref, m_ref, r_ref, order_ref) = refs[: len(masks)], refs[len(masks) :]
+    place = lax.axis_index("head")
+    slots = pieces[0].shape[0]
+    feats = pieces[0].shape[1] - LANES
     width = fold_ref.shape[2]
-    clip_rows = count_slots // clips
-
+    clip_rows = len(masks) * cap
+    count_slots = clips * clip_rows
+
+    def by_clip(value, c):
+        return jnp.concatenate(
+            [value[j * slots + c * cap : j * slots + (c + 1) * cap] for j in range(len(masks))], axis=0
+        )
+
+    notes = jnp.concatenate([ref[:, feats:].astype(jnp.float32) for ref in pieces], axis=0)
     for c in range(clips):
-        note = x_ref[c * clip_rows : (c + 1) * clip_rows, feats : feats + LANES].astype(jnp.float32)
+        note = by_clip(notes, c)
+        note_ref[c * clip_rows : (c + 1) * clip_rows, :] = note.astype(jnp.bfloat16)
         order_ref[clips + c] = jnp.max(note[:, :1]).astype(jnp.int32)
     starts = [jnp.int32(0)]
     for s in range(SAMPLES):
@@ -212,14 +226,17 @@
         starts.append(lax.fori_loop(0, clips, keep_clip, starts[-1]))
 
     col_tile = 256
-    patch = x_ref[:, :feats]
-    notes = x_ref[:, feats:].astype(jnp.float32)
+    patch = jnp.concatenate([ref[:, :feats] for ref in pieces], axis=0)
     scale = jnp.broadcast_to(notes[:, 1:2] + notes[:, 2:3], (count_slots, col_tile))
     twice = jnp.concatenate([patch, patch], axis=1)
     for m in range(3):
         for n in range(0, width, col_tile):
             part = jnp.dot(twice, fold_ref[m, :, n : n + col_tile], preferred_element_type=jnp.float32)
-            qkv_ref[m, :, n : n + col_tile] = (part * scale).astype(jnp.bfloat16)
+            part = part * scale
+            for c in range(clips):
+                qkv_ref[m, c * clip_rows : (c + 1) * clip_rows, n : n + col_tile] = by_clip(part, c).astype(
+                    jnp.bfloat16
+                )
 
     out_ref[...] = jnp.zeros_like(out_ref)
     tile = 2 * clip_rows
@@ -254,7 +271,7 @@
         def bias_of(a, b, second):
             label = lax.dot_general(
                 pick,
-                two(x_ref, a, b, slice(feats, feats + LANES)),
+                two(note_ref, a, b, slice(0, LANES)),
                 (((1,), (1,)), ((), ())),
                 preferred_element_type=jnp.float32,
             )[:1]
@@ -281,9 +298,9 @@
             heads = [r[:, :LANES] / r[:, LANES:] for r in results]
             mixed = jnp.where(low, heads[0], heads[1])
             for at, clip in ((clip_rows, b), (0, a)):
-                for f in range(clip_rows // cap):
-                    piece = mixed[at + f * cap : at + (f + 1) * cap]
-                    out_ref[f * clips + clip, :, cols] = piece.astype(jnp.bfloat16)
+                for j, mask in enumerate(masks):
+                    piece = mixed[at + j * cap : at + (j + 1) * cap]
+                    out_ref[jnp.bitwise_xor(place, mask) * clips + clip, :, cols] = piece.astype(jnp.bfloat16)
 
         def query_tile(i, carry):
             qa, qb, _ = members(i)
@@ -361,7 +378,7 @@
     chans = conv_weight.shape[2]
 
     tile = latents.reshape(frames_dev * area, depth)
-    count = frame_counts.reshape(1, 1)
+    count = frame_counts
     edge = jax.ShapeDtypeStruct((area, chans), jnp.float32)
     upward, downward = pl.pallas_call(
         functools.partial(edge_kernel, rows, cols, frames_dev),
@@ -369,10 +386,11 @@
         in_specs=[VMEM, ANY, ANY],
         out_specs=(VMEM, VMEM),
         scratch_shapes=[
-            pltpu.VMEM(tile.shape, jnp.bfloat16),
-            pltpu.VMEM(conv_weight.shape, jnp.bfloat16),
-            pltpu.SemaphoreType.DMA((2,)),
+            pltpu.VMEM((2 * area, depth), jnp.bfloat16),
+            pltpu.VMEM((2 * TAPS * TAPS, depth, chans), jnp.bfloat16),
+            pltpu.SemaphoreType.DMA((4,)),
         ],
+        compiler_params=limit(EDGE_LIMIT),
         cost_estimate=pl.CostEstimate(flops=600000000, bytes_accessed=4500000, transcendentals=0),
         name="edge",
     )(count, tile, conv_weight)
@@ -408,32 +426,39 @@
     arrived = lax.all_to_all(
         outgoing.reshape(bags, cap, row_width), "bag", split_axis=0, concat_axis=0, tiled=True
     )
+    arrived = arrived.reshape(slots, row_width)
+    pieces = {0: arrived}
+    bit = heads_dev // 2
+    swap = [(i, i ^ bit) for i in range(heads_dev)]
+    far = lax.ppermute(arrived, "head", swap)
     folded = pl.pallas_call(
         fold_kernel,
         out_shape=jax.ShapeDtypeStruct((3, 2 * embed_weight.shape[0], local_width), jnp.bfloat16),
-        in_specs=[ANY, ANY],
+        in_specs=[VMEM, VMEM, ANY],
         out_specs=VMEM,
-        scratch_shapes=[
-            pltpu.VMEM(embed_weight.shape, jnp.bfloat16),
-            pltpu.VMEM(qkv_weight.shape, jnp.bfloat16),
-            pltpu.SemaphoreType.DMA((4,)),
-        ],
-        compiler_params=limit(FOLD_LIMIT),
+        compiler_params=limit(16),
         cost_estimate=pl.CostEstimate(flops=3300000000, bytes_accessed=14000000, transcendentals=0),
         name="fold",
-    )(embed_weight, qkv_weight)
+    )(embed_weight, qkv_weight, arrived)
+    far, folded = lax.optimization_barrier((far, folded))
+    pieces = {0: arrived, bit: far}
+    while bit > 1:
+        bit //= 2
+        swap = [(i, i ^ bit) for i in range(heads_dev)]
+        pieces.update({mask | bit: lax.ppermute(piece, "head", swap) for mask, piece in pieces.items()})
     count_slots = heads_dev * slots
-    gathered = lax.all_gather(arrived, "head", axis=1, tiled=True).reshape(count_slots, row_width)
+    masks = tuple(pieces)
 
     pair_rows = 2 * heads_dev * cap
     heads_here = local_width // HDIM
     attended = pl.pallas_call(
-        functools.partial(bag_kernel, bags, cap),
+        functools.partial(bag_kernel, bags, cap, masks),
         out_shape=jax.ShapeDtypeStruct((heads_dev * bags, cap, local_width), jnp.bfloat16),
-        in_specs=[VMEM, VMEM],
+        in_specs=[VMEM] * (len(masks) + 1),
         out_specs=VMEM,
         scratch_shapes=[
             pltpu.VMEM((3, count_slots, local_width), jnp.bfloat16),
+            pltpu.VMEM((count_slots, LANES), jnp.bfloat16),
             pltpu.VMEM((heads_here, pair_rows, LANES), jnp.float32),
             pltpu.VMEM((heads_here, pair_rows, 2 * LANES), jnp.float32),
             pltpu.SMEM((2 * bags,), jnp.int32),
@@ -441,7 +466,7 @@
         compiler_params=limit(28),
         cost_estimate=pl.CostEstimate(flops=3000000000, bytes_accessed=5000000, transcendentals=1200000),
         name="bag",
-    )(gathered, folded)
+    )(*pieces.values(), folded)
     received = lax.all_to_all(attended, ("head", "bag"), split_axis=0, concat_axis=0, tiled=True)
     return pl.pallas_call(
         functools.partial(collect_kernel, frames_dev, heads_dev),

time: 75.9 us -> 71.2 us (0.938)
  waiting for transfers between devices: 1.62 us -> 4.54 us
  local copies, waits for them, and re-layouts: 5.43 us -> 2.81 us
  starting transfers between devices: 9.63 us -> 7.23 us
  Pallas kernels: 19 us -> 17 us
    all_to_all x0 -> x1, blocking collectives: none -> 13.7 us  [shards(): lax.all_to_all(outgoing.reshape(bags, cap, row_width), 'bag', split_axis=...]
    all_gather x1 -> x0, blocking collectives: 11.5 us -> none  [shards(): lax.all_gather(arrived, 'head', axis=1, tiled=True)]
    all_to_all x1 -> x0, starting transfers between devices: 5.81 us -> none  [shards(): lax.all_to_all(outgoing.reshape(bags, cap, row_width), 'bag', split_axis=...]
    ppermute x0 -> x3, starting transfers between devices: none -> 3.4 us  [the longest x2 2.12 us: shards(): lax.ppermute(piece, 'head', swap)]
    all_to_all x1, blocking collectives: 27.4 us -> 24.8 us  [shards(): lax.all_to_all(attended, ('head', 'bag'), split_axis=0, concat_axis=0, ti...]
    unnamed x18 -> x12, local copies, waits for them, and re-layouts: 5.43 us -> 2.81 us
    ppermute x0 -> x3, waiting for transfers between devices: none -> 1.88 us  [the longest x2 1.51 us: shards(): lax.ppermute(piece, 'head', swap)]
    ppermute x1, waiting for transfers between devices: 1.61 us -> 2.66 us  [shards(): lax.ppermute(downward, 'head', [(i + 1, i) for i in range(ends)])]
  transfers between devices with their start and end apart: 3 -> 5, of which waited for: 1 -> 3; matrix products, arithmetic and copies ran while one was open for 0% -> 0% of each run, Pallas kernels for 8% -> 7%
where the time goes in v7:
time: 71.2 us; the launch traced here: 71 us
  blocking collectives  38.5 us (54%)
  Pallas kernels  17 us (24%)
  starting transfers between devices  7.23 us (10%)
  waiting for transfers between devices  4.54 us (6%)
  local copies, waits for them, and re-layouts  2.81 us (4%)
  between operations  0.91 us (1%)
    all_to_all x1, blocking collectives, shards(): lax.all_to_all(attended, ('head', 'bag'), split_axis=0, concat_axis=0, ti...  24.8 us
    all_to_all x1, blocking collectives, shards(): lax.all_to_all(outgoing.reshape(bags, cap, row_width), 'bag', split_axis=...  13.7 us
    pallas_call x1, Pallas kernels, shards(): pl.pallas_call(functools.partial(bag_kernel, bags, cap, masks), out_shape...  6.59 us
    pallas_call x1, Pallas kernels, shards(): pl.pallas_call(functools.partial(edge_kernel, rows, cols, frames_dev), ou...  3.52 us
    pallas_call x1, Pallas kernels, shards(): pl.pallas_call(fold_kernel, out_shape=jax.ShapeDtypeStruct((3, 2 * embed_...  3.46 us
    unnamed x12, local copies, waits for them, and re-layouts  2.81 us
    ppermute x1, waiting for transfers between devices, shards(): lax.ppermute(downward, 'head', [(i + 1, i) for i in range(ends)])  2.66 us
    ppermute x1, starting transfers between devices, shards(): from_prev = lax.ppermute(upward, 'head', [(i, i + 1) for i in range(ends)])  2.54 us
  transfers between devices with their start and end apart: 5, of which 3 were waited for; matrix products, arithmetic and copies ran while one was open for 0% of the time, Pallas kernels for 7%

profile of v7, /device:TPU:0, one launch (start us, length us, event | category | flops | bytes accessed | tf_op | source)
XLA Modules:
  0.0 71.0 jit_solution(13774186902912803764)
XLA Ops:
  0.0 0.0 copy-start
  0.0 0.0 copy-start.2
  0.0 0.0 copy-start.5
  0.8 0.0 copy-start.3
  0.8 3.5 %edge.1 = (f32[256,128]{1,0:T(8,128)}, f32[256,128]{1,0:T(8,128)}) custom-call(s32[1]{0:T(128)S(6)} %copy.8.count_ref, bf16[512,512]{1,0:T(8,128)(2,1)} %bitcast.8, bf16[27,512,128]{2,1,0:T(8,128)(2,1)} %w_hbm.1), custom_call_target="tpu_custom_call" | custom-call | flops 600000000 | bytes 4500000 | tf_op jit(solution)/shard_map/edge/pallas_call | solution.py:383
  4.3 0.0 copy-start.1
  4.4 2.5 %collective-permute-start = (f32[256,128]{1,0:T(8,128)}, f32[256,128]{1,0:T(8,128)S(1)}, u32[]{:S(2)}, u32[]{:S(2)}) collective-permute-start(f32[256,128]{1,0:T(8,128)} %get-tuple-element.13), channel_id=1, source_target_pairs={{0,1},{1,2},{2,3},{4,5},{5,6},{6,7},{8,9},{9,10},{10,11},{12,13},{... | collective-permute-start | bytes 393224 | tf_op jit(solution)/shard_map/ppermute | solution.py:398
  6.9 1.3 %collective-permute-start.1 = (f32[256,128]{1,0:T(8,128)}, f32[256,128]{1,0:T(8,128)S(1)}, u32[]{:S(2)}, u32[]{:S(2)}) collective-permute-start(f32[256,128]{1,0:T(8,128)} %get-tuple-element.14), channel_id=1, source_target_pairs={{1,0},{2,1},{3,2},{5,4},{6,5},{7,6},{9,8},{10,9},{11,10},{13,12},{... | collective-permute-start | bytes 393224 | tf_op jit(solution)/shard_map/ppermute | solution.py:399
  8.2 0.0 copy-done
  8.2 0.0 copy-done.2
  8.2 0.0 copy-done.5
  8.2 1.6 %own.1 = (f32[512,128]{1,0:T(8,128)S(1)}, bf16[192,128]{1,0:T(8,128)(2,1)S(1)}) custom-call(s32[1]{0:T(128)S(6)} %copy.8.count_ref, bf16[512,512]{1,0:T(8,128)(2,1)S(1)} %bitcast.9, bf16[27,512,128]{2,1,0:T(8,128)(2,1)S(1)} %copy-done, s32[4,128]{1,0:T(4,128)S(1)} %bitcast.15), custom_call_target="tpu_custom_call" | custom-call | flops 1200000000 | bytes 4500000 | tf_op jit(solution)/shard_map/own/pallas_call | solution.py:403
  9.8 0.0 collective-permute-done.prev_ref
  9.8 2.7 %collective-permute-done.1.next_ref = f32[256,128]{1,0:T(8,128)S(1)} collective-permute-done((f32[256,128]{1,0:T(8,128)}, f32[256,128]{1,0:T(8,128)S(1)}, u32[]{:S(2)}, u32[]{:S(2)}) %collective-permute-start.1) | collective-permute-done | bytes 131104 | tf_op jit(solution)/shard_map/ppermute | solution.py:399
  12.5 0.0 copy-done.3
  12.5 0.0 copy-done.1
  12.5 0.7 %join.1 = bf16[192,640]{1,0:T(8,128)(2,1)S(1)} custom-call(s32[1]{0:T(128)S(6)} %copy.8.count_ref, s32[4,128]{1,0:T(4,128)S(1)} %bitcast.14, f32[512,128]{1,0:T(8,128)S(1)} %get-tuple-element.12.acc_ref, f32[256,128]{1,0:T(8,128)S(1)} %collective-permute-done.prev_ref, f32[256,128]{1,0:T(8,128)S(1)} %collective-permute-done.1.next_ref, ...), custom_call_target="tpu_custom_call" | custom-call | flops 300000000 | bytes 3000000 | tf_op jit(solution)/shard_map/join/pallas_call | solution.py:415
  13.2 13.7 %all_to_all.10 = bf16[8,24,640]{2,1,0:T(8,128)(2,1)S(1)} all-to-all(bf16[8,24,640]{2,1,0:T(8,128)(2,1)S(1)} %bitcast.7), channel_id=1, replica_groups=mesh['bag'=8,'head'=4] {'bag'}, dimensions={0} | all-to-all | bytes 491520 | tf_op jit(solution)/shard_map/all_to_all | solution.py:426
  26.9 2.1 %collective-permute-start.3 = (bf16[192,640]{1,0:T(8,128)(2,1)S(1)}, bf16[192,640]{1,0:T(8,128)(2,1)S(1)}, u32[]{:S(2)}, u32[]{:S(2)}) collective-permute-start(bf16[192,640]{1,0:T(8,128)(2,1)S(1)} %bitcast.10), channel_id=1, source_target_pairs={{0,1},{1,0},{2,3},{3,2},{4,5},{5,4},{6,7},{7,6},{8,9},{9,8},{10,11... | collective-permute-start | bytes 737288 | tf_op jit(solution)/shard_map/ppermute | solution.py:448
  29.0 1.3 %collective-permute-start.2 = (bf16[192,640]{1,0:T(8,128)(2,1)S(1)}, bf16[192,640]{1,0:T(8,128)(2,1)S(1)}, u32[]{:S(2)}, u32[]{:S(2)}) collective-permute-start(bf16[192,640]{1,0:T(8,128)(2,1)S(1)} %bitcast.11), channel_id=1, source_target_pairs={{0,2},{1,3},{2,0},{3,1},{4,6},{5,7},{6,4},{7,5},{8,10},{9,11},{10,... | collective-permute-start | bytes 737288 | tf_op jit(solution)/shard_map/ppermute | solution.py:433
  30.3 0.0 copy-start.4
  30.3 2.8 %copy-done.4 = bf16[3,2048,512]{2,1,0:T(8,128)(2,1)S(1)} copy-done((bf16[3,2048,512]{2,1,0:T(8,128)(2,1)S(1)}, bf16[3,2048,512]{2,1,0:T(8,128)(2,1)}, u32[]{:S(2)}) %copy-start.4) | copy-done | bytes 6291480
  33.1 3.5 %fold.1.refs_4_ = bf16[3,1024,512]{2,1,0:T(8,128)(2,1)S(1)} custom-call(bf16[512,2048]{1,0:T(8,128)(2,1)S(1)} %copy-done.1, bf16[3,2048,512]{2,1,0:T(8,128)(2,1)S(1)} %copy-done.4, bf16[192,640]{1,0:T(8,128)(2,1)S(1)} %bitcast.12), custom_call_target="tpu_custom_call" | custom-call | flops 3300000000 | bytes 14000000 | tf_op jit(solution)/shard_map/fold/pallas_call | solution.py:434
  36.6 0.4 collective-permute-done.2.refs_1_
  36.9 0.0 collective-permute-start.4
  36.9 0.0 collective-permute-done.3.refs_2_
  36.9 1.5 %collective-permute-done.4.refs_3_ = bf16[192,640]{1,0:T(8,128)(2,1)S(1)} collective-permute-done((bf16[192,640]{1,0:T(8,128)(2,1)S(1)}, bf16[192,640]{1,0:T(8,128)(2,1)S(1)}, u32[]{:S(2)}, u32[]{:S(2)}) %collective-permute-start.4) | collective-permute-done | bytes 245792 | tf_op jit(solution)/shard_map/ppermute | solution.py:448
  38.4 6.6 %bag.1 = bf16[32,24,512]{2,1,0:T(8,128)(2,1)S(1)} custom-call(bf16[192,640]{1,0:T(8,128)(2,1)S(1)} %bitcast.13, bf16[192,640]{1,0:T(8,128)(2,1)S(1)} %collective-permute-done.2.refs_1_, bf16[192,640]{1,0:T(8,128)(2,1)S(1)} %collective-permute-done.3.refs_2_, bf16[192,640]{1,0:T(8,128)(2,1)S(1)} %collective-permute-done.4.refs_3_, ...), custom_call_target="tpu_custom_call" | custom-call | flops 3000000000 | bytes 5000000 | tf_op jit(solution)/shard_map/bag/pallas_call | solution.py:454
  45.0 24.8 %all_to_all.11 = bf16[32,24,512]{2,1,0:T(8,128)(2,1)S(1)} all-to-all(bf16[32,24,512]{2,1,0:T(8,128)(2,1)S(1)} %bag.1), channel_id=1, replica_groups=mesh['bag'=8,'head'=4] {'head','bag'}, dimensions={0} | all-to-all | bytes 1572864 | tf_op jit(solution)/shard_map/all_to_all | solution.py:470
  69.8 1.2 %collect.1 = bf16[128,2048]{1,0:T(8,128)(2,1)} custom-call(s32[1]{0:T(128)S(6)} %copy.8.count_ref, bf16[192,128]{1,0:T(8,128)(2,1)S(1)} %get-tuple-element.11.onehot_ref, bf16[768,512]{1,0:T(8,128)(2,1)S(1)} %bitcast.6), custom_call_target="tpu_custom_call" | custom-call | tf_op jit(solution)/shard_map/collect/pallas_call | solution.py:471
Async XLA Ops:
  0.0 8.2 %copy-start = (bf16[27,512,128]{2,1,0:T(8,128)(2,1)S(1)}, bf16[27,512,128]{2,1,0:T(8,128)(2,1)}, u32[]{:S(2)}) copy-start(bf16[27,512,128]{2,1,0:T(8,128)(2,1)} %w_hbm.1) | copy-start | bytes 10616836
  0.0 8.2 %copy-start.2 = (bf16[1,2,16,16,512]{4,3,2,1,0:T(8,128)(2,1)S(1)}, bf16[1,2,16,16,512]{4,3,2,1,0:T(8,128)(2,1)}, u32[]{:S(2)}) copy-start(bf16[1,2,16,16,512]{4,3,2,1,0:T(8,128)(2,1)} %param.7) | copy-start | bytes 1572868
  0.0 8.2 %copy-start.5 = (s32[512,1]{0,1:T(1,128)S(1)}, s32[512,1]{0,1:T(1,128)}, u32[]{:S(2)}) copy-start(s32[512,1]{0,1:T(1,128)} %param.9) | copy-start | bytes 6148
  0.8 11.7 %copy-start.3 = (s32[512]{0:T(512)S(1)}, s32[512]{0:T(512)}, u32[]{:S(2)}) copy-start(s32[512]{0:T(512)} %param.10) | copy-start | bytes 6148
  4.3 8.1 %copy-start.1 = (bf16[512,2048]{1,0:T(8,128)(2,1)S(1)}, bf16[512,2048]{1,0:T(8,128)(2,1)}, u32[]{:S(2)}) copy-start(bf16[512,2048]{1,0:T(8,128)(2,1)} %e_ref.3) | copy-start | bytes 6291460
  4.4 5.4 %collective-permute-start = (f32[256,128]{1,0:T(8,128)}, f32[256,128]{1,0:T(8,128)S(1)}, u32[]{:S(2)}, u32[]{:S(2)}) collective-permute-start(f32[256,128]{1,0:T(8,128)} %get-tuple-element.13), channel_id=1, source_target_pairs={{0,1},{1,2},{2,3},{4,5},{5,6},{6,7},{8,9},{9,10},{10,11},{12,13},{... | collective-permute-start | bytes 393224 | tf_op jit(solution)/shard_map/ppermute | solution.py:398
  6.9 5.6 %collective-permute-start.1 = (f32[256,128]{1,0:T(8,128)}, f32[256,128]{1,0:T(8,128)S(1)}, u32[]{:S(2)}, u32[]{:S(2)}) collective-permute-start(f32[256,128]{1,0:T(8,128)} %get-tuple-element.14), channel_id=1, source_target_pairs={{1,0},{2,1},{3,2},{5,4},{6,5},{7,6},{9,8},{10,9},{11,10},{13,12},{... | collective-permute-start | bytes 393224 | tf_op jit(solution)/shard_map/ppermute | solution.py:399
  26.9 10.0 %collective-permute-start.3 = (bf16[192,640]{1,0:T(8,128)(2,1)S(1)}, bf16[192,640]{1,0:T(8,128)(2,1)S(1)}, u32[]{:S(2)}, u32[]{:S(2)}) collective-permute-start(bf16[192,640]{1,0:T(8,128)(2,1)S(1)} %bitcast.10), channel_id=1, source_target_pairs={{0,1},{1,0},{2,3},{3,2},{4,5},{5,4},{6,7},{7,6},{8,9},{9,8},{10,11... | collective-permute-start | bytes 737288 | tf_op jit(solution)/shard_map/ppermute | solution.py:448
  29.0 7.9 %collective-permute-start.2 = (bf16[192,640]{1,0:T(8,128)(2,1)S(1)}, bf16[192,640]{1,0:T(8,128)(2,1)S(1)}, u32[]{:S(2)}, u32[]{:S(2)}) collective-permute-start(bf16[192,640]{1,0:T(8,128)(2,1)S(1)} %bitcast.11), channel_id=1, source_target_pairs={{0,2},{1,3},{2,0},{3,1},{4,6},{5,7},{6,4},{7,5},{8,10},{9,11},{10,... | collective-permute-start | bytes 737288 | tf_op jit(solution)/shard_map/ppermute | solution.py:433
  30.3 2.8 %copy-start.4 = (bf16[3,2048,512]{2,1,0:T(8,128)(2,1)S(1)}, bf16[3,2048,512]{2,1,0:T(8,128)(2,1)}, u32[]{:S(2)}) copy-start(bf16[3,2048,512]{2,1,0:T(8,128)(2,1)} %w_ref.3) | copy-start | bytes 18874372
  36.9 1.5 %collective-permute-start.4 = (bf16[192,640]{1,0:T(8,128)(2,1)S(1)}, bf16[192,640]{1,0:T(8,128)(2,1)S(1)}, u32[]{:S(2)}, u32[]{:S(2)}) collective-permute-start(bf16[192,640]{1,0:T(8,128)(2,1)S(1)} %collective-permute-done.2.refs_1_), channel_id=1, source_target_pairs={{0,1},{1,0},{2,3},{3,2},{4,5},{5,4},{6,7},{7,6},{8,9},{9,8},{10,11... | collective-permute-start | bytes 737288 | tf_op jit(solution)/shard_map/ppermute | solution.py:448

commit v8 on v7

--- a/solution.py
+++ b/solution.py
@@ -87,12 +87,12 @@
     return jnp.max(ref[...])
 
 
-def edge_kernel(rows, cols, frames, count_ref, x_hbm, w_hbm, up_ref, down_ref, x_ref, w_ref, sems):
+def edge_kernel(rows, cols, frames, x_hbm, w_hbm, near_ref, far_ref, x_ref, w_ref, sems):
     area = rows * cols
     plane = TAPS * TAPS
-    jobs = ((up_ref, frames - 1, 0), (down_ref, 0, 2))
+    jobs = ((frames - 1, 0), (0, 2))
     loads = []
-    for i, (_, f, tap) in enumerate(jobs):
+    for i, (f, tap) in enumerate(jobs):
         loads.append(
             (
                 pltpu.make_async_copy(
@@ -106,14 +106,16 @@
     for pair in loads:
         for load in pair:
             load.start()
-    count = scalar_of(count_ref)
-    first = lax.axis_index("head") * frames
-    for i, (out_ref, f, _) in enumerate(jobs):
+    even = lax.axis_index("head") % 2 == 0
+    sums = []
+    for i in range(2):
         for load in loads[i]:
             load.wait()
         value = x_ref[i * area : (i + 1) * area, :]
-        value = jnp.where(first + f < count, value, jnp.zeros_like(value))
-        out_ref[...] = combine(plane_products([(i, value)], w_ref), rows, cols)
+        sums.append(combine(plane_products([(i, value)], w_ref), rows, cols))
+    up, down = sums
+    near_ref[...] = jnp.where(even, up, down)
+    far_ref[...] = jnp.where(even, down, up)
 
 
 def own_kernel(bags, cap, rows, cols, frames, count_ref, x_ref, w_ref, route_ref, acc_ref, onehot_ref):
@@ -133,19 +135,23 @@
 
 
 def join_kernel(
-    rows, cols, frames, count_ref, sample_ref, acc_ref, prev_ref, next_ref, onehot_ref, e_ref, out_ref, grid_ref
+    rows, cols, frames, count_ref, sample_ref, acc_ref, near_ref, far_ref, onehot_ref, e_ref, out_ref, grid_ref
 ):
     count = scalar_of(count_ref)
     sample = scalar_of(sample_ref)
     area = rows * cols
-    first = lax.axis_index("head") * frames
+    place = lax.axis_index("head")
+    even = place % 2 == 0
+    first = place * frames
     chans = acc_ref.shape[1]
+    near, far = near_ref[...], far_ref[...]
     for f in range(frames):
         part = acc_ref[f * area : (f + 1) * area, :]
         if f == 0:
-            part = part + prev_ref[...]
+            before = jnp.logical_and(first > 0, first - 1 < count)
+            part = part + jnp.where(before, jnp.where(even, far, near), 0.0)
         if f == frames - 1:
-            part = part + next_ref[...]
+            part = part + jnp.where(first + frames < count, jnp.where(even, near, far), 0.0)
         grid_ref[f * area : (f + 1) * area, :] = jnp.where(first + f < count, part, 0.0)
     pieces = [[None] * 2 for _ in range(2)]
     for odd in range(2):
@@ -380,10 +386,10 @@
     tile = latents.reshape(frames_dev * area, depth)
     count = frame_counts
     edge = jax.ShapeDtypeStruct((area, chans), jnp.float32)
-    upward, downward = pl.pallas_call(
+    near, far = pl.pallas_call(
         functools.partial(edge_kernel, rows, cols, frames_dev),
         out_shape=(edge, edge),
-        in_specs=[VMEM, ANY, ANY],
+        in_specs=[ANY, ANY],
         out_specs=(VMEM, VMEM),
         scratch_shapes=[
             pltpu.VMEM((2 * area, depth), jnp.bfloat16),
@@ -393,10 +399,10 @@
         compiler_params=limit(EDGE_LIMIT),
         cost_estimate=pl.CostEstimate(flops=600000000, bytes_accessed=4500000, transcendentals=0),
         name="edge",
-    )(count, tile, conv_weight)
-    ends = heads_dev - 1
-    from_prev = lax.ppermute(upward, "head", [(i, i + 1) for i in range(ends)])
-    from_next = lax.ppermute(downward, "head", [(i + 1, i) for i in range(ends)])
+    )(tile, conv_weight)
+    across = [(i, i + 1) for i in range(1, heads_dev - 1, 2)]
+    far = lax.ppermute(far, "head", across + [(j, i) for i, j in across])
+    near = lax.ppermute(near, "head", [(i, i ^ 1) for i in range(heads_dev)])
 
     route_rows = routes[:, 0].reshape(heads_dev, tok_dev)
     row_width = 4 * chans + LANES
@@ -421,7 +427,7 @@
         compiler_params=limit(16),
         cost_estimate=pl.CostEstimate(flops=300000000, bytes_accessed=3000000, transcendentals=0),
         name="join",
-    )(count, samples.reshape(heads_dev, tok_dev), acc, from_prev, from_next, onehot, embed_weight)
+    )(count, samples.reshape(heads_dev, tok_dev), acc, near, far, onehot, embed_weight)
 
     arrived = lax.all_to_all(
         outgoing.reshape(bags, cap, row_width), "bag", split_axis=0, concat_axis=0, tiled=True
@@ -430,7 +436,7 @@
     pieces = {0: arrived}
     bit = heads_dev // 2
     swap = [(i, i ^ bit) for i in range(heads_dev)]
-    far = lax.ppermute(arrived, "head", swap)
+    across = lax.ppermute(arrived, "head", swap)
     folded = pl.pallas_call(
         fold_kernel,
         out_shape=jax.ShapeDtypeStruct((3, 2 * embed_weight.shape[0], local_width), jnp.bfloat16),
@@ -440,8 +446,8 @@
         cost_estimate=pl.CostEstimate(flops=3300000000, bytes_accessed=14000000, transcendentals=0),
         name="fold",
     )(embed_weight, qkv_weight, arrived)
-    far, folded = lax.optimization_barrier((far, folded))
-    pieces = {0: arrived, bit: far}
+    across, folded = lax.optimization_barrier((across, folded))
+    pieces = {0: arrived, bit: across}
     while bit > 1:
         bit //= 2
         swap = [(i, i ^ bit) for i in range(heads_dev)]

time: 71.2 us -> 68.3 us (0.959)
  waiting for transfers between devices: 4.54 us -> 1.89 us
  blocking collectives: 38.5 us -> 39.5 us
  starting transfers between devices: 7.23 us -> 6.42 us
    ppermute x3, waiting for transfers between devices: 3.03 us -> 0.38 us  [the longest x1 0.37 us: shards(): across = lax.ppermute(arrived, 'head', swap)]
    ppermute x3, starting transfers between devices: 5.11 us -> 3.97 us  [the longest x1 2.61 us: shards(): across = lax.ppermute(arrived, 'head', swap)]
    all_to_all x1, blocking collectives: 13.7 us -> 14.7 us  [shards(): lax.all_to_all(outgoing.reshape(bags, cap, row_width), 'bag', split_axis=...]
  transfers between devices with their start and end apart: 5 -> 5, of which waited for: 3 -> 2; matrix products, arithmetic and copies ran while one was open for 0% -> 0% of each run, Pallas kernels for 7% -> 7%
where the time goes in v8:
time: 68.3 us; the launch traced here: 68.1 us
  blocking collectives  39.5 us (58%)
  Pallas kernels  16.7 us (24%)
  starting transfers between devices  6.42 us (9%)
  local copies, waits for them, and re-layouts  2.81 us (4%)
  waiting for transfers between devices  1.89 us (3%)
  between operations  0.77 us (1%)
    all_to_all x1, blocking collectives, shards(): lax.all_to_all(attended, ('head', 'bag'), split_axis=0, concat_axis=0, ti...  24.7 us
    all_to_all x1, blocking collectives, shards(): lax.all_to_all(outgoing.reshape(bags, cap, row_width), 'bag', split_axis=...  14.7 us
    pallas_call x1, Pallas kernels, shards(): pl.pallas_call(functools.partial(bag_kernel, bags, cap, masks), out_shape...  6.6 us
    pallas_call x1, Pallas kernels, shards(): pl.pallas_call(fold_kernel, out_shape=jax.ShapeDtypeStruct((3, 2 * embed_...  3.46 us
    pallas_call x1, Pallas kernels, shards(): pl.pallas_call(functools.partial(edge_kernel, rows, cols, frames_dev), ou...  3.26 us
    unnamed x12, local copies, waits for them, and re-layouts  2.81 us
    ppermute x1, starting transfers between devices, shards(): across = lax.ppermute(arrived, 'head', swap)  2.61 us
    ppermute x2, starting transfers between devices, shards(): lax.ppermute(piece, 'head', swap)  2.46 us
  transfers between devices with their start and end apart: 5, of which 2 were waited for; matrix products, arithmetic and copies ran while one was open for 0% of the time, Pallas kernels for 7%

profile of v8, /device:TPU:0, one launch (start us, length us, event | category | flops | bytes accessed | tf_op | source)
XLA Modules:
  0.0 68.1 jit_solution(13428741391296543222)
XLA Ops:
  0.0 0.0 copy-start
  0.0 0.0 copy-start.2
  0.0 0.0 copy-start.5
  0.0 0.0 copy-start.3
  0.0 3.3 %edge.1 = (f32[256,128]{1,0:T(8,128)}, f32[256,128]{1,0:T(8,128)}) custom-call(bf16[512,512]{1,0:T(8,128)(2,1)} %bitcast.8, bf16[27,512,128]{2,1,0:T(8,128)(2,1)} %w_hbm.1), custom_call_target="tpu_custom_call" | custom-call | flops 600000000 | bytes 4500000 | tf_op jit(solution)/shard_map/edge/pallas_call | solution.py:389
  3.3 0.0 copy-start.1
  3.3 0.6 collective-permute-start
  3.9 0.8 %collective-permute-start.1 = (f32[256,128]{1,0:T(8,128)}, f32[256,128]{1,0:T(8,128)S(1)}, u32[]{:S(2)}, u32[]{:S(2)}) collective-permute-start(f32[256,128]{1,0:T(8,128)} %get-tuple-element.14), channel_id=1, source_target_pairs={{1,2},{2,1},{5,6},{6,5},{9,10},{10,9},{13,14},{14,13},{17,18},{18,... | collective-permute-start | bytes 393224 | tf_op jit(solution)/shard_map/ppermute | solution.py:404
  5.3 0.0 copy-done
  5.3 0.0 copy-done.2
  5.3 0.0 copy-done.5
  5.3 1.6 %own.1 = (f32[512,128]{1,0:T(8,128)S(1)}, bf16[192,128]{1,0:T(8,128)(2,1)S(1)}) custom-call(s32[1]{0:T(128)S(6)} %copy.8.count_ref, bf16[512,512]{1,0:T(8,128)(2,1)S(1)} %bitcast.9, bf16[27,512,128]{2,1,0:T(8,128)(2,1)S(1)} %copy-done, s32[4,128]{1,0:T(4,128)S(1)} %bitcast.15), custom_call_target="tpu_custom_call" | custom-call | flops 1200000000 | bytes 4500000 | tf_op jit(solution)/shard_map/own/pallas_call | solution.py:409
  6.9 0.0 collective-permute-done.near_ref
  6.9 0.0 collective-permute-done.1.far_ref
  6.9 0.0 copy-done.3
  6.9 0.0 copy-done.1
  6.9 0.7 %join.1 = bf16[192,640]{1,0:T(8,128)(2,1)S(1)} custom-call(s32[1]{0:T(128)S(6)} %copy.8.count_ref, s32[4,128]{1,0:T(4,128)S(1)} %bitcast.14, f32[512,128]{1,0:T(8,128)S(1)} %get-tuple-element.12.acc_ref, f32[256,128]{1,0:T(8,128)S(1)} %collective-permute-done.near_ref, f32[256,128]{1,0:T(8,128)S(1)} %collective-permute-done.1.far_ref, ...), custom_call_target="tpu_custom_call" | custom-call | flops 300000000 | bytes 3000000 | tf_op jit(solution)/shard_map/join/pallas_call | solution.py:421
  7.7 14.7 %all_to_all.10 = bf16[8,24,640]{2,1,0:T(8,128)(2,1)S(1)} all-to-all(bf16[8,24,640]{2,1,0:T(8,128)(2,1)S(1)} %bitcast.7), channel_id=1, replica_groups=mesh['bag'=8,'head'=4] {'bag'}, dimensions={0} | all-to-all | bytes 491520 | tf_op jit(solution)/shard_map/all_to_all | solution.py:432
  22.4 2.5 %collective-permute-start.3 = (bf16[192,640]{1,0:T(8,128)(2,1)S(1)}, bf16[192,640]{1,0:T(8,128)(2,1)S(1)}, u32[]{:S(2)}, u32[]{:S(2)}) collective-permute-start(bf16[192,640]{1,0:T(8,128)(2,1)S(1)} %bitcast.10), channel_id=1, source_target_pairs={{0,1},{1,0},{2,3},{3,2},{4,5},{5,4},{6,7},{7,6},{8,9},{9,8},{10,11... | collective-permute-start | bytes 737288 | tf_op jit(solution)/shard_map/ppermute | solution.py:454
  24.9 2.6 %collective-permute-start.2 = (bf16[192,640]{1,0:T(8,128)(2,1)S(1)}, bf16[192,640]{1,0:T(8,128)(2,1)S(1)}, u32[]{:S(2)}, u32[]{:S(2)}) collective-permute-start(bf16[192,640]{1,0:T(8,128)(2,1)S(1)} %bitcast.11), channel_id=1, source_target_pairs={{0,2},{1,3},{2,0},{3,1},{4,6},{5,7},{6,4},{7,5},{8,10},{9,11},{10,... | collective-permute-start | bytes 737288 | tf_op jit(solution)/shard_map/ppermute | solution.py:439
  27.5 0.0 copy-start.4
  27.5 2.8 %copy-done.4 = bf16[3,2048,512]{2,1,0:T(8,128)(2,1)S(1)} copy-done((bf16[3,2048,512]{2,1,0:T(8,128)(2,1)S(1)}, bf16[3,2048,512]{2,1,0:T(8,128)(2,1)}, u32[]{:S(2)}) %copy-start.4) | copy-done | bytes 6291480
  30.2 3.5 %fold.1.refs_4_ = bf16[3,1024,512]{2,1,0:T(8,128)(2,1)S(1)} custom-call(bf16[512,2048]{1,0:T(8,128)(2,1)S(1)} %copy-done.1, bf16[3,2048,512]{2,1,0:T(8,128)(2,1)S(1)} %copy-done.4, bf16[192,640]{1,0:T(8,128)(2,1)S(1)} %bitcast.12), custom_call_target="tpu_custom_call" | custom-call | flops 3300000000 | bytes 14000000 | tf_op jit(solution)/shard_map/fold/pallas_call | solution.py:440
  33.7 0.4 collective-permute-done.2.refs_1_
  34.1 0.0 collective-permute-start.4
  34.1 0.0 collective-permute-done.3.refs_2_
  34.1 1.5 %collective-permute-done.4.refs_3_ = bf16[192,640]{1,0:T(8,128)(2,1)S(1)} collective-permute-done((bf16[192,640]{1,0:T(8,128)(2,1)S(1)}, bf16[192,640]{1,0:T(8,128)(2,1)S(1)}, u32[]{:S(2)}, u32[]{:S(2)}) %collective-permute-start.4) | collective-permute-done | bytes 245792 | tf_op jit(solution)/shard_map/ppermute | solution.py:454
  35.6 6.6 %bag.1 = bf16[32,24,512]{2,1,0:T(8,128)(2,1)S(1)} custom-call(bf16[192,640]{1,0:T(8,128)(2,1)S(1)} %bitcast.13, bf16[192,640]{1,0:T(8,128)(2,1)S(1)} %collective-permute-done.2.refs_1_, bf16[192,640]{1,0:T(8,128)(2,1)S(1)} %collective-permute-done.3.refs_2_, bf16[192,640]{1,0:T(8,128)(2,1)S(1)} %collective-permute-done.4.refs_3_, ...), custom_call_target="tpu_custom_call" | custom-call | flops 3000000000 | bytes 5000000 | tf_op jit(solution)/shard_map/bag/pallas_call | solution.py:460
  42.2 24.7 %all_to_all.11 = bf16[32,24,512]{2,1,0:T(8,128)(2,1)S(1)} all-to-all(bf16[32,24,512]{2,1,0:T(8,128)(2,1)S(1)} %bag.1), channel_id=1, replica_groups=mesh['bag'=8,'head'=4] {'head','bag'}, dimensions={0} | all-to-all | bytes 1572864 | tf_op jit(solution)/shard_map/all_to_all | solution.py:476
  66.9 1.2 %collect.1 = bf16[128,2048]{1,0:T(8,128)(2,1)} custom-call(s32[1]{0:T(128)S(6)} %copy.8.count_ref, bf16[192,128]{1,0:T(8,128)(2,1)S(1)} %get-tuple-element.11.onehot_ref, bf16[768,512]{1,0:T(8,128)(2,1)S(1)} %bitcast.6), custom_call_target="tpu_custom_call" | custom-call | tf_op jit(solution)/shard_map/collect/pallas_call | solution.py:477
Async XLA Ops:
  0.0 5.3 %copy-start = (bf16[27,512,128]{2,1,0:T(8,128)(2,1)S(1)}, bf16[27,512,128]{2,1,0:T(8,128)(2,1)}, u32[]{:S(2)}) copy-start(bf16[27,512,128]{2,1,0:T(8,128)(2,1)} %w_hbm.1) | copy-start | bytes 10616836
  0.0 5.3 %copy-start.2 = (bf16[1,2,16,16,512]{4,3,2,1,0:T(8,128)(2,1)S(1)}, bf16[1,2,16,16,512]{4,3,2,1,0:T(8,128)(2,1)}, u32[]{:S(2)}) copy-start(bf16[1,2,16,16,512]{4,3,2,1,0:T(8,128)(2,1)} %param.7) | copy-start | bytes 1572868
  0.0 5.3 %copy-start.5 = (s32[512,1]{0,1:T(1,128)S(1)}, s32[512,1]{0,1:T(1,128)}, u32[]{:S(2)}) copy-start(s32[512,1]{0,1:T(1,128)} %param.9) | copy-start | bytes 6148
  0.0 6.9 %copy-start.3 = (s32[512]{0:T(512)S(1)}, s32[512]{0:T(512)}, u32[]{:S(2)}) copy-start(s32[512]{0:T(512)} %param.10) | copy-start | bytes 6148
  3.3 3.7 %copy-start.1 = (bf16[512,2048]{1,0:T(8,128)(2,1)S(1)}, bf16[512,2048]{1,0:T(8,128)(2,1)}, u32[]{:S(2)}) copy-start(bf16[512,2048]{1,0:T(8,128)(2,1)} %e_ref.3) | copy-start | bytes 6291460
  3.3 3.6 %collective-permute-start = (f32[256,128]{1,0:T(8,128)}, f32[256,128]{1,0:T(8,128)S(1)}, u32[]{:S(2)}, u32[]{:S(2)}) collective-permute-start(f32[256,128]{1,0:T(8,128)} %get-tuple-element.13), channel_id=1, source_target_pairs={{0,1},{1,0},{2,3},{3,2},{4,5},{5,4},{6,7},{7,6},{8,9},{9,8},{10,11... | collective-permute-start | bytes 393224 | tf_op jit(solution)/shard_map/ppermute | solution.py:405
  3.9 3.1 %collective-permute-start.1 = (f32[256,128]{1,0:T(8,128)}, f32[256,128]{1,0:T(8,128)S(1)}, u32[]{:S(2)}, u32[]{:S(2)}) collective-permute-start(f32[256,128]{1,0:T(8,128)} %get-tuple-element.14), channel_id=1, source_target_pairs={{1,2},{2,1},{5,6},{6,5},{9,10},{10,9},{13,14},{14,13},{17,18},{18,... | collective-permute-start | bytes 393224 | tf_op jit(solution)/shard_map/ppermute | solution.py:404
  22.4 11.7 %collective-permute-start.3 = (bf16[192,640]{1,0:T(8,128)(2,1)S(1)}, bf16[192,640]{1,0:T(8,128)(2,1)S(1)}, u32[]{:S(2)}, u32[]{:S(2)}) collective-permute-start(bf16[192,640]{1,0:T(8,128)(2,1)S(1)} %bitcast.10), channel_id=1, source_target_pairs={{0,1},{1,0},{2,3},{3,2},{4,5},{5,4},{6,7},{7,6},{8,9},{9,8},{10,11... | collective-permute-start | bytes 737288 | tf_op jit(solution)/shard_map/ppermute | solution.py:454
  24.9 9.2 %collective-permute-start.2 = (bf16[192,640]{1,0:T(8,128)(2,1)S(1)}, bf16[192,640]{1,0:T(8,128)(2,1)S(1)}, u32[]{:S(2)}, u32[]{:S(2)}) collective-permute-start(bf16[192,640]{1,0:T(8,128)(2,1)S(1)} %bitcast.11), channel_id=1, source_target_pairs={{0,2},{1,3},{2,0},{3,1},{4,6},{5,7},{6,4},{7,5},{8,10},{9,11},{10,... | collective-permute-start | bytes 737288 | tf_op jit(solution)/shard_map/ppermute | solution.py:439
  27.5 2.8 %copy-start.4 = (bf16[3,2048,512]{2,1,0:T(8,128)(2,1)S(1)}, bf16[3,2048,512]{2,1,0:T(8,128)(2,1)}, u32[]{:S(2)}) copy-start(bf16[3,2048,512]{2,1,0:T(8,128)(2,1)} %w_ref.3) | copy-start | bytes 18874372
  34.1 1.5 %collective-permute-start.4 = (bf16[192,640]{1,0:T(8,128)(2,1)S(1)}, bf16[192,640]{1,0:T(8,128)(2,1)S(1)}, u32[]{:S(2)}, u32[]{:S(2)}) collective-permute-start(bf16[192,640]{1,0:T(8,128)(2,1)S(1)} %collective-permute-done.2.refs_1_), channel_id=1, source_target_pairs={{0,1},{1,0},{2,3},{3,2},{4,5},{5,4},{6,7},{7,6},{8,9},{9,8},{10,11... | collective-permute-start | bytes 737288 | tf_op jit(solution)/shard_map/ppermute | solution.py:454

commit v9 on v8

--- a/solution.py
+++ b/solution.py
@@ -198,21 +198,44 @@
             fold_ref[m, feats:, cols] = (product - high.astype(jnp.float32)).astype(jnp.bfloat16)
 
 
+def qkv_kernel(*refs):
+    pieces, fold_ref, out_ref = refs[:-2], refs[-2], refs[-1]
+    for m, at, part in qkv_parts(pieces, fold_ref):
+        out_ref[m, :, at : at + part.shape[1]] = part
+
+
+def qkv_parts(pieces, fold_ref):
+    feats = pieces[0].shape[1] - LANES
+    col_tile = 256
+    patch = jnp.concatenate([ref[:, :feats] for ref in pieces], axis=0)
+    notes = jnp.concatenate([ref[:, feats:].astype(jnp.float32) for ref in pieces], axis=0)
+    scale = jnp.broadcast_to(notes[:, 1:2] + notes[:, 2:3], (notes.shape[0], col_tile))
+    twice = jnp.concatenate([patch, patch], axis=1)
+    for m in range(3):
+        for n in range(0, fold_ref.shape[2], col_tile):
+            part = jnp.dot(twice, fold_ref[m, :, n : n + col_tile], preferred_element_type=jnp.float32)
+            yield m, n, part * scale
+
+
 def bag_kernel(clips, cap, masks, *refs):
-    pieces, (fold_ref, out_ref, qkv_ref, note_ref, m_ref, r_ref, order_ref) = refs[: len(masks)], refs[len(masks) :]
+    count = len(masks)
+    pieces, (near_ref, fold_ref, out_ref, qkv_ref, note_ref, m_ref, r_ref, order_ref) = refs[:count], refs[count:]
     place = lax.axis_index("head")
     slots = pieces[0].shape[0]
     feats = pieces[0].shape[1] - LANES
     width = fold_ref.shape[2]
-    clip_rows = len(masks) * cap
-    count_slots = clips * clip_rows
-
-    def by_clip(value, c):
+    clip_rows = count * cap
+    half = count // 2
+
+    def by_clip(values, c):
         return jnp.concatenate(
-            [value[j * slots + c * cap : j * slots + (c + 1) * cap] for j in range(len(masks))], axis=0
+            [value[j * slots + c * cap : j * slots + (c + 1) * cap] for value in values for j in range(half)], axis=0
         )
 
-    notes = jnp.concatenate([ref[:, feats:].astype(jnp.float32) for ref in pieces], axis=0)
+    notes = [
+        jnp.concatenate([ref[:, feats:].astype(jnp.float32) for ref in group], axis=0)
+        for group in (pieces[:half], pieces[half:])
+    ]
     for c in range(clips):
         note = by_clip(notes, c)
         note_ref[c * clip_rows : (c + 1) * clip_rows, :] = note.astype(jnp.bfloat16)
@@ -231,18 +254,11 @@
 
         starts.append(lax.fori_loop(0, clips, keep_clip, starts[-1]))
 
-    col_tile = 256
-    patch = jnp.concatenate([ref[:, :feats] for ref in pieces], axis=0)
-    scale = jnp.broadcast_to(notes[:, 1:2] + notes[:, 2:3], (count_slots, col_tile))
-    twice = jnp.concatenate([patch, patch], axis=1)
-    for m in range(3):
-        for n in range(0, width, col_tile):
-            part = jnp.dot(twice, fold_ref[m, :, n : n + col_tile], preferred_element_type=jnp.float32)
-            part = part * scale
-            for c in range(clips):
-                qkv_ref[m, c * clip_rows : (c + 1) * clip_rows, n : n + col_tile] = by_clip(part, c).astype(
-                    jnp.bfloat16
-                )
+    for m, at, part in qkv_parts(pieces[half:], fold_ref):
+        cols = slice(at, at + part.shape[1])
+        both = (near_ref[m, :, cols], part)
+        for c in range(clips):
+            qkv_ref[m, c * clip_rows : (c + 1) * clip_rows, cols] = by_clip(both, c).astype(jnp.bfloat16)
 
     out_ref[...] = jnp.zeros_like(out_ref)
     tile = 2 * clip_rows
@@ -446,12 +462,27 @@
         cost_estimate=pl.CostEstimate(flops=3300000000, bytes_accessed=14000000, transcendentals=0),
         name="fold",
     )(embed_weight, qkv_weight, arrived)
-    across, folded = lax.optimization_barrier((across, folded))
-    pieces = {0: arrived, bit: across}
-    while bit > 1:
-        bit //= 2
-        swap = [(i, i ^ bit) for i in range(heads_dev)]
-        pieces.update({mask | bit: lax.ppermute(piece, "head", swap) for mask, piece in pieces.items()})
+    def spread(start, bits):
+        found = dict(start)
+        for lower in bits:
+            pairs = [(i, i ^ lower) for i in range(heads_dev)]
+            found.update({mask | lower: lax.ppermute(piece, "head", pairs) for mask, piece in found.items()})
+        return found
+
+    lower_bits = [1 << i for i in reversed(range(bit.bit_length() - 1))]
+    close = spread({0: arrived}, lower_bits)
+    near_qkv = pl.pallas_call(
+        qkv_kernel,
+        out_shape=jax.ShapeDtypeStruct((3, len(close) * slots, local_width), jnp.float32),
+        in_specs=[VMEM] * (len(close) + 1),
+        out_specs=VMEM,
+        compiler_params=limit(16),
+        cost_estimate=pl.CostEstimate(flops=1200000000, bytes_accessed=6000000, transcendentals=0),
+        name="near_qkv",
+    )(*close.values(), folded)
+    across, near_qkv = lax.optimization_barrier((across, near_qkv))
+    pieces = dict(close)
+    pieces.update(spread({bit: across}, lower_bits))
     count_slots = heads_dev * slots
     masks = tuple(pieces)
 
@@ -460,7 +491,7 @@
     attended = pl.pallas_call(
         functools.partial(bag_kernel, bags, cap, masks),
         out_shape=jax.ShapeDtypeStruct((heads_dev * bags, cap, local_width), jnp.bfloat16),
-        in_specs=[VMEM] * (len(masks) + 1),
+        in_specs=[VMEM] * (len(masks) + 2),
         out_specs=VMEM,
         scratch_shapes=[
             pltpu.VMEM((3, count_slots, local_width), jnp.bfloat16),
@@ -472,7 +503,7 @@
         compiler_params=limit(28),
         cost_estimate=pl.CostEstimate(flops=3000000000, bytes_accessed=5000000, transcendentals=1200000),
         name="bag",
-    )(*pieces.values(), folded)
+    )(*pieces.values(), near_qkv, folded)
     received = lax.all_to_all(attended, ("head", "bag"), split_axis=0, concat_axis=0, tiled=True)
     return pl.pallas_call(
         functools.partial(collect_kernel, frames_dev, heads_dev),

time: 68.3 us -> 67.3 us (0.985)
  blocking collectives: 39.5 us -> 38.3 us
  waiting for transfers between devices: 1.89 us -> 1.15 us
    ppermute x1, starting transfers between devices: 2.61 us -> 5.06 us  [shards(): across = lax.ppermute(arrived, 'head', swap)]
    ppermute x2, starting transfers between devices: 2.46 us -> 0.58 us  [spread(): lax.ppermute(piece, 'head', pairs)]
    pallas_call x0 -> x1, Pallas kernels: none -> 1.38 us  [shards(): pl.pallas_call(qkv_kernel, out_shape=jax.ShapeDtypeStruct((3, len(close)...]
    pallas_call x1, Pallas kernels: 6.6 us -> 5.44 us  [shards(): pl.pallas_call(functools.partial(bag_kernel, bags, cap, masks), out_shape...]
    all_to_all x1, blocking collectives: 24.7 us -> 23.6 us  [shards(): lax.all_to_all(attended, ('head', 'bag'), split_axis=0, concat_axis=0, ti...]
  transfers between devices with their start and end apart: 5 -> 5, of which waited for: 2 -> 1; matrix products, arithmetic and copies ran while one was open for 0% -> 0% of each run, Pallas kernels for 7% -> 10%
where the time goes in v9:
time: 67.3 us; the launch traced here: 67 us
  blocking collectives  38.3 us (57%)
  Pallas kernels  17 us (25%)
  starting transfers between devices  6.98 us (10%)
  local copies, waits for them, and re-layouts  2.81 us (4%)
  waiting for transfers between devices  1.15 us (2%)
  between operations  0.8 us (1%)
    all_to_all x1, blocking collectives, shards(): lax.all_to_all(attended, ('head', 'bag'), split_axis=0, concat_axis=0, ti...  23.6 us
    all_to_all x1, blocking collectives, shards(): lax.all_to_all(outgoing.reshape(bags, cap, row_width), 'bag', split_axis=...  14.7 us
    pallas_call x1, Pallas kernels, shards(): pl.pallas_call(functools.partial(bag_kernel, bags, cap, masks), out_shape...  5.44 us
    ppermute x1, starting transfers between devices, shards(): across = lax.ppermute(arrived, 'head', swap)  5.06 us
    pallas_call x1, Pallas kernels, shards(): pl.pallas_call(fold_kernel, out_shape=jax.ShapeDtypeStruct((3, 2 * embed_...  3.46 us
    pallas_call x1, Pallas kernels, shards(): pl.pallas_call(functools.partial(edge_kernel, rows, cols, frames_dev), ou...  3.26 us
    unnamed x12, local copies, waits for them, and re-layouts  2.81 us
    pallas_call x1, Pallas kernels, shards(): pl.pallas_call(functools.partial(own_kernel, bags, cap, rows, cols, frame...  1.56 us
  transfers between devices with their start and end apart: 5, of which 1 were waited for; matrix products, arithmetic and copies ran while one was open for 0% of the time, Pallas kernels for 10%

profile of v9, /device:TPU:0, one launch (start us, length us, event | category | flops | bytes accessed | tf_op | source)
XLA Modules:
  0.0 67.0 jit_solution(10157125989504505465)
XLA Ops:
  0.0 0.0 copy-start
  0.0 0.0 copy-start.2
  0.0 0.0 copy-start.5
  0.0 3.3 %edge.1 = (f32[256,128]{1,0:T(8,128)}, f32[256,128]{1,0:T(8,128)}) custom-call(bf16[512,512]{1,0:T(8,128)(2,1)} %bitcast.13, bf16[27,512,128]{2,1,0:T(8,128)(2,1)} %w_hbm.1), custom_call_target="tpu_custom_call" | custom-call | flops 600000000 | bytes 4500000 | tf_op jit(solution)/shard_map/edge/pallas_call | solution.py:405
  3.3 0.0 copy-start.1
  3.3 0.0 copy-start.3
  3.3 0.6 collective-permute-start
  3.9 0.8 %collective-permute-start.1 = (f32[256,128]{1,0:T(8,128)}, f32[256,128]{1,0:T(8,128)S(1)}, u32[]{:S(2)}, u32[]{:S(2)}) collective-permute-start(f32[256,128]{1,0:T(8,128)} %get-tuple-element.14), channel_id=1, source_target_pairs={{1,2},{2,1},{5,6},{6,5},{9,10},{10,9},{13,14},{14,13},{17,18},{18,... | collective-permute-start | bytes 393224 | tf_op jit(solution)/shard_map/ppermute | solution.py:420
  5.3 0.0 copy-done
  5.3 0.0 copy-done.2
  5.3 0.0 copy-done.5
  5.3 1.6 %own.1 = (f32[512,128]{1,0:T(8,128)S(1)}, bf16[192,128]{1,0:T(8,128)(2,1)S(1)}) custom-call(s32[1]{0:T(128)S(6)} %copy.8.count_ref, bf16[512,512]{1,0:T(8,128)(2,1)S(1)} %bitcast.14, bf16[27,512,128]{2,1,0:T(8,128)(2,1)S(1)} %copy-done, s32[4,128]{1,0:T(4,128)S(1)} %bitcast.16), custom_call_target="tpu_custom_call" | custom-call | flops 1200000000 | bytes 4500000 | tf_op jit(solution)/shard_map/own/pallas_call | solution.py:425
  6.9 0.0 collective-permute-done.near_ref
  6.9 0.0 collective-permute-done.1.far_ref
  6.9 0.0 copy-done.1
  6.9 0.0 copy-done.3
  6.9 0.7 %join.1 = bf16[192,640]{1,0:T(8,128)(2,1)S(1)} custom-call(s32[1]{0:T(128)S(6)} %copy.8.count_ref, s32[4,128]{1,0:T(4,128)S(1)} %bitcast.15, f32[512,128]{1,0:T(8,128)S(1)} %get-tuple-element.12.acc_ref, f32[256,128]{1,0:T(8,128)S(1)} %collective-permute-done.near_ref, f32[256,128]{1,0:T(8,128)S(1)} %collective-permute-done.1.far_ref, ...), custom_call_target="tpu_custom_call" | custom-call | flops 300000000 | bytes 3000000 | tf_op jit(solution)/shard_map/join/pallas_call | solution.py:437
  7.7 14.7 %all_to_all.10 = bf16[8,24,640]{2,1,0:T(8,128)(2,1)S(1)} all-to-all(bf16[8,24,640]{2,1,0:T(8,128)(2,1)S(1)} %bitcast.12), channel_id=1, replica_groups=mesh['bag'=8,'head'=4] {'bag'}, dimensions={0} | all-to-all | bytes 491520 | tf_op jit(solution)/shard_map/all_to_all | solution.py:448
  22.4 5.1 %collective-permute-start.3 = (bf16[192,640]{1,0:T(8,128)(2,1)S(1)}, bf16[192,640]{1,0:T(8,128)(2,1)S(1)}, u32[]{:S(2)}, u32[]{:S(2)}) collective-permute-start(bf16[192,640]{1,0:T(8,128)(2,1)S(1)} %bitcast.7), channel_id=1, source_target_pairs={{0,2},{1,3},{2,0},{3,1},{4,6},{5,7},{6,4},{7,5},{8,10},{9,11},{10,... | collective-permute-start | bytes 737288 | tf_op jit(solution)/shard_map/ppermute | solution.py:455
  27.5 0.0 collective-permute-start.2
  27.5 0.0 copy-start.4
  27.5 2.8 %copy-done.4 = bf16[3,2048,512]{2,1,0:T(8,128)(2,1)S(1)} copy-done((bf16[3,2048,512]{2,1,0:T(8,128)(2,1)S(1)}, bf16[3,2048,512]{2,1,0:T(8,128)(2,1)}, u32[]{:S(2)}) %copy-start.4) | copy-done | bytes 6291480
  30.2 3.5 %fold.1.refs_2_.refs_5_ = bf16[3,1024,512]{2,1,0:T(8,128)(2,1)S(1)} custom-call(bf16[512,2048]{1,0:T(8,128)(2,1)S(1)} %copy-done.1, bf16[3,2048,512]{2,1,0:T(8,128)(2,1)S(1)} %copy-done.4, bf16[192,640]{1,0:T(8,128)(2,1)S(1)} %bitcast.9), custom_call_target="tpu_custom_call" | custom-call | flops 3300000000 | bytes 14000000 | tf_op jit(solution)/shard_map/fold/pallas_call | solution.py:456
  33.7 0.0 collective-permute-done.2.refs_1_
  33.7 1.4 %near_qkv.1.refs_4_ = f32[3,384,512]{2,1,0:T(8,128)S(1)} custom-call(bf16[192,640]{1,0:T(8,128)(2,1)S(1)} %bitcast.10, bf16[192,640]{1,0:T(8,128)(2,1)S(1)} %collective-permute-done.2.refs_1_, bf16[3,1024,512]{2,1,0:T(8,128)(2,1)S(1)} %fold.1.refs_2_.refs_5_), custom_call_target="tpu_custom_call" | custom-call | flops 1200000000 | bytes 6000000 | tf_op jit(solution)/shard_map/near_qkv/pallas_call | solution.py:474
  35.1 0.0 collective-permute-done.3.refs_2_
  35.1 0.6 collective-permute-start.4
  35.7 1.1 %collective-permute-done.4.refs_3_ = bf16[192,640]{1,0:T(8,128)(2,1)S(1)} collective-permute-done((bf16[192,640]{1,0:T(8,128)(2,1)S(1)}, bf16[192,640]{1,0:T(8,128)(2,1)S(1)}, u32[]{:S(2)}, u32[]{:S(2)}) %collective-permute-start.4) | collective-permute-done | bytes 245792 | tf_op jit(solution)/shard_map/ppermute | solution.py:469
  36.8 5.4 %bag.1 = bf16[32,24,512]{2,1,0:T(8,128)(2,1)S(1)} custom-call(bf16[192,640]{1,0:T(8,128)(2,1)S(1)} %bitcast.11, bf16[192,640]{1,0:T(8,128)(2,1)S(1)} %collective-permute-done.2.refs_1_, bf16[192,640]{1,0:T(8,128)(2,1)S(1)} %collective-permute-done.3.refs_2_, bf16[192,640]{1,0:T(8,128)(2,1)S(1)} %collective-permute-done.4.refs_3_, ...), custom_call_target="tpu_custom_call" | custom-call | flops 3000000000 | bytes 5000000 | tf_op jit(solution)/shard_map/bag/pallas_call | solution.py:491
  42.3 23.6 %all_to_all.11 = bf16[32,24,512]{2,1,0:T(8,128)(2,1)S(1)} all-to-all(bf16[32,24,512]{2,1,0:T(8,128)(2,1)S(1)} %bag.1), channel_id=1, replica_groups=mesh['bag'=8,'head'=4] {'head','bag'}, dimensions={0} | all-to-all | bytes 1572864 | tf_op jit(solution)/shard_map/all_to_all | solution.py:507
  65.9 1.2 %collect.1 = bf16[128,2048]{1,0:T(8,128)(2,1)} custom-call(s32[1]{0:T(128)S(6)} %copy.8.count_ref, bf16[192,128]{1,0:T(8,128)(2,1)S(1)} %get-tuple-element.11.onehot_ref, bf16[768,512]{1,0:T(8,128)(2,1)S(1)} %bitcast.6), custom_call_target="tpu_custom_call" | custom-call | tf_op jit(solution)/shard_map/collect/pallas_call | solution.py:508
Async XLA Ops:
  0.0 5.3 %copy-start = (bf16[27,512,128]{2,1,0:T(8,128)(2,1)S(1)}, bf16[27,512,128]{2,1,0:T(8,128)(2,1)}, u32[]{:S(2)}) copy-start(bf16[27,512,128]{2,1,0:T(8,128)(2,1)} %w_hbm.1) | copy-start | bytes 10616836
  0.0 5.3 %copy-start.2 = (bf16[1,2,16,16,512]{4,3,2,1,0:T(8,128)(2,1)S(1)}, bf16[1,2,16,16,512]{4,3,2,1,0:T(8,128)(2,1)}, u32[]{:S(2)}) copy-start(bf16[1,2,16,16,512]{4,3,2,1,0:T(8,128)(2,1)} %param.7) | copy-start | bytes 1572868
  0.0 5.3 %copy-start.5 = (s32[512,1]{0,1:T(1,128)S(1)}, s32[512,1]{0,1:T(1,128)}, u32[]{:S(2)}) copy-start(s32[512,1]{0,1:T(1,128)} %param.9) | copy-start | bytes 6148
  3.3 3.7 %copy-start.1 = (bf16[512,2048]{1,0:T(8,128)(2,1)S(1)}, bf16[512,2048]{1,0:T(8,128)(2,1)}, u32[]{:S(2)}) copy-start(bf16[512,2048]{1,0:T(8,128)(2,1)} %e_ref.3) | copy-start | bytes 6291460
  3.3 3.7 %copy-start.3 = (s32[512]{0:T(512)S(1)}, s32[512]{0:T(512)}, u32[]{:S(2)}) copy-start(s32[512]{0:T(512)} %param.10) | copy-start | bytes 6148
  3.3 3.6 %collective-permute-start = (f32[256,128]{1,0:T(8,128)}, f32[256,128]{1,0:T(8,128)S(1)}, u32[]{:S(2)}, u32[]{:S(2)}) collective-permute-start(f32[256,128]{1,0:T(8,128)} %get-tuple-element.13), channel_id=1, source_target_pairs={{0,1},{1,0},{2,3},{3,2},{4,5},{5,4},{6,7},{7,6},{8,9},{9,8},{10,11... | collective-permute-start | bytes 393224 | tf_op jit(solution)/shard_map/ppermute | solution.py:421
  3.9 3.1 %collective-permute-start.1 = (f32[256,128]{1,0:T(8,128)}, f32[256,128]{1,0:T(8,128)S(1)}, u32[]{:S(2)}, u32[]{:S(2)}) collective-permute-start(f32[256,128]{1,0:T(8,128)} %get-tuple-element.14), channel_id=1, source_target_pairs={{1,2},{2,1},{5,6},{6,5},{9,10},{10,9},{13,14},{14,13},{17,18},{18,... | collective-permute-start | bytes 393224 | tf_op jit(solution)/shard_map/ppermute | solution.py:420
  22.4 12.7 %collective-permute-start.3 = (bf16[192,640]{1,0:T(8,128)(2,1)S(1)}, bf16[192,640]{1,0:T(8,128)(2,1)S(1)}, u32[]{:S(2)}, u32[]{:S(2)}) collective-permute-start(bf16[192,640]{1,0:T(8,128)(2,1)S(1)} %bitcast.7), channel_id=1, source_target_pairs={{0,2},{1,3},{2,0},{3,1},{4,6},{5,7},{6,4},{7,5},{8,10},{9,11},{10,... | collective-permute-start | bytes 737288 | tf_op jit(solution)/shard_map/ppermute | solution.py:455
  27.5 6.3 %collective-permute-start.2 = (bf16[192,640]{1,0:T(8,128)(2,1)S(1)}, bf16[192,640]{1,0:T(8,128)(2,1)S(1)}, u32[]{:S(2)}, u32[]{:S(2)}) collective-permute-start(bf16[192,640]{1,0:T(8,128)(2,1)S(1)} %bitcast.8), channel_id=1, source_target_pairs={{0,1},{1,0},{2,3},{3,2},{4,5},{5,4},{6,7},{7,6},{8,9},{9,8},{10,11... | collective-permute-start | bytes 737288 | tf_op jit(solution)/shard_map/ppermute | solution.py:469
  27.5 2.8 %copy-start.4 = (bf16[3,2048,512]{2,1,0:T(8,128)(2,1)S(1)}, bf16[3,2048,512]{2,1,0:T(8,128)(2,1)}, u32[]{:S(2)}) copy-start(bf16[3,2048,512]{2,1,0:T(8,128)(2,1)} %w_ref.3) | copy-start | bytes 18874372
  35.1 1.7 %collective-permute-start.4 = (bf16[192,640]{1,0:T(8,128)(2,1)S(1)}, bf16[192,640]{1,0:T(8,128)(2,1)S(1)}, u32[]{:S(2)}, u32[]{:S(2)}) collective-permute-start(bf16[192,640]{1,0:T(8,128)(2,1)S(1)} %collective-permute-done.3.refs_2_), channel_id=1, source_target_pairs={{0,1},{1,0},{2,3},{3,2},{4,5},{5,4},{6,7},{7,6},{8,9},{9,8},{10,11... | collective-permute-start | bytes 737288 | tf_op jit(solution)/shard_map/ppermute | solution.py:469

commit v10 on v9

--- a/solution.py
+++ b/solution.py
@@ -87,42 +87,40 @@
     return jnp.max(ref[...])
 
 
-def edge_kernel(rows, cols, frames, x_hbm, w_hbm, near_ref, far_ref, x_ref, w_ref, sems):
+def edge_jobs(frames):
+    even = lax.axis_index("head") % 2 == 0
+    last, zero, two = jnp.int32(frames - 1), jnp.int32(0), jnp.int32(2)
+    up, down = (last, zero), (zero, two)
+    near = tuple(jnp.where(even, a, b) for a, b in zip(up, down))
+    far = tuple(jnp.where(even, b, a) for a, b in zip(up, down))
+    return near, far
+
+
+def edge_kernel(rows, cols, frames, x_hbm, w_hbm, far_ref, x_ref, w_ref, sems):
     area = rows * cols
     plane = TAPS * TAPS
-    jobs = ((frames - 1, 0), (0, 2))
-    loads = []
-    for i, (f, tap) in enumerate(jobs):
-        loads.append(
-            (
-                pltpu.make_async_copy(
-                    x_hbm.at[pl.ds(f * area, area)], x_ref.at[pl.ds(i * area, area)], sems.at[2 * i]
-                ),
-                pltpu.make_async_copy(
-                    w_hbm.at[pl.ds(tap * plane, plane)], w_ref.at[pl.ds(i * plane, plane)], sems.at[2 * i + 1]
-                ),
-            )
-        )
-    for pair in loads:
-        for load in pair:
-            load.start()
-    even = lax.axis_index("head") % 2 == 0
-    sums = []
-    for i in range(2):
-        for load in loads[i]:
-            load.wait()
-        value = x_ref[i * area : (i + 1) * area, :]
-        sums.append(combine(plane_products([(i, value)], w_ref), rows, cols))
-    up, down = sums
-    near_ref[...] = jnp.where(even, up, down)
-    far_ref[...] = jnp.where(even, down, up)
-
-
-def own_kernel(bags, cap, rows, cols, frames, count_ref, x_ref, w_ref, route_ref, acc_ref, onehot_ref):
+    _, (frame, tap) = edge_jobs(frames)
+    loads = [
+        pltpu.make_async_copy(x_hbm.at[pl.ds(pl.multiple_of(frame * area, area), area)], x_ref, sems.at[0]),
+        pltpu.make_async_copy(w_hbm.at[pl.ds(tap * plane, plane)], w_ref, sems.at[1]),
+    ]
+    for load in loads:
+        load.start()
+    for load in loads:
+        load.wait()
+    far_ref[...] = combine(plane_products([(0, x_ref[...])], w_ref), rows, cols)
+
+
+def own_kernel(
+    bags, cap, rows, cols, frames, count_ref, x_ref, w_ref, route_ref, near_ref, acc_ref, onehot_ref
+):
     count = scalar_of(count_ref)
     place = lax.axis_index("head")
     area = rows * cols
     first = place * frames
+    (frame, tap), _ = edge_jobs(frames)
+    value = x_ref[pl.ds(pl.multiple_of(frame * area, area), area), :]
+    near_ref[...] = combine(plane_products([(tap, value)], w_ref), rows, cols)
     inputs = []
     for f in range(frames):
         value = x_ref[f * area : (f + 1) * area, :]
@@ -301,12 +299,15 @@
             good = jnp.logical_and(label == s + 1.0, key_at < limit)
             return jnp.where(good, 0.0, far_below)
 
-        def scores_of(pair, half, query, a, b, bias):
-            cols = slice(pair * LANES, (pair + 1) * LANES)
-            keys = two(qkv_ref, a, b, 1, cols)
-            one = jnp.where(low if half == 0 else jnp.logical_not(low), query, jnp.zeros_like(query))
+        def stacked(pair, a, b):
+            query = two(qkv_ref, a, b, 0, slice(pair * LANES, (pair + 1) * LANES))
+            blank = jnp.zeros_like(query)
+            return jnp.concatenate([jnp.where(low, query, blank), jnp.where(low, blank, query)], axis=0)
+
+        def scores_of(pair, query, a, b, bias):
+            keys = two(qkv_ref, a, b, 1, slice(pair * LANES, (pair + 1) * LANES))
             return (
-                lax.dot_general(one, keys, (((1,), (1,)), ((), ())), preferred_element_type=jnp.float32)
+                lax.dot_general(query, keys, (((1,), (1,)), ((), ())), preferred_element_type=jnp.float32)
                 + bias
             )
 
@@ -315,10 +316,10 @@
             values = jnp.concatenate([two(qkv_ref, a, b, 2, cols), ones], axis=1)
             return jnp.dot(shifted.astype(jnp.bfloat16), values, preferred_element_type=jnp.float32)
 
-        def store(pair, a, b, results):
+        def store(pair, a, b, result):
             cols = slice(pair * LANES, (pair + 1) * LANES)
-            heads = [r[:, :LANES] / r[:, LANES:] for r in results]
-            mixed = jnp.where(low, heads[0], heads[1])
+            shares = result[:, :LANES] / result[:, LANES:]
+            mixed = jnp.where(low, shares[:tile], shares[tile:])
             for at, clip in ((clip_rows, b), (0, a)):
                 for j, mask in enumerate(masks):
                     piece = mixed[at + j * cap : at + (j + 1) * cap]
@@ -332,39 +333,32 @@
                 ka, kb, second = members(0)
                 bias = bias_of(ka, kb, second)
                 for pair in range(pairs):
-                    query = two(qkv_ref, qa, qb, 0, slice(pair * LANES, (pair + 1) * LANES))
-                    results = []
-                    for half in range(2):
-                        scores = scores_of(pair, half, query, ka, kb, bias)
-                        top = jnp.max(scores, axis=-1, keepdims=True)
-                        results.append(mix(pair, jnp.exp(scores - top), ka, kb))
-                    store(pair, qa, qb, results)
+                    scores = scores_of(pair, stacked(pair, qa, qb), ka, kb, bias)
+                    top = jnp.max(scores, axis=-1, keepdims=True)
+                    store(pair, qa, qb, mix(pair, jnp.exp(scores - top), ka, kb))
 
             @pl.when(tiles > 1)
             def _():
-                for h in range(2 * pairs):
-                    m_ref[h] = jnp.full((tile, LANES), far_below, jnp.float32)
-                    r_ref[h] = jnp.zeros((tile, 2 * LANES), jnp.float32)
+                for pair in range(pairs):
+                    m_ref[pair] = jnp.full((2 * tile, LANES), far_below, jnp.float32)
+                    r_ref[pair] = jnp.zeros((2 * tile, 2 * LANES), jnp.float32)
 
                 def key_tile(j, inner):
                     ka, kb, second = members(j)
                     bias = bias_of(ka, kb, second)
                     for pair in range(pairs):
-                        query = two(qkv_ref, qa, qb, 0, slice(pair * LANES, (pair + 1) * LANES))
-                        for half in range(2):
-                            h = 2 * pair + half
-                            scores = scores_of(pair, half, query, ka, kb, bias)
-                            old = m_ref[h][:, :1]
-                            top = jnp.maximum(old, jnp.max(scores, axis=-1, keepdims=True))
-                            r_ref[h] = r_ref[h] * jnp.exp(old - top) + mix(
-                                pair, jnp.exp(scores - top), ka, kb
-                            )
-                            m_ref[h] = jnp.broadcast_to(top, (tile, LANES))
+                        scores = scores_of(pair, stacked(pair, qa, qb), ka, kb, bias)
+                        old = m_ref[pair][:, :1]
+                        top = jnp.maximum(old, jnp.max(scores, axis=-1, keepdims=True))
+                        r_ref[pair] = r_ref[pair] * jnp.exp(old - top) + mix(
+                            pair, jnp.exp(scores - top), ka, kb
+                        )
+                        m_ref[pair] = jnp.broadcast_to(top, (2 * tile, LANES))
                     return inner
 
                 lax.fori_loop(0, tiles, key_tile, 0)
                 for pair in range(pairs):
-                    store(pair, qa, qb, [r_ref[2 * pair], r_ref[2 * pair + 1]])
+                    store(pair, qa, qb, r_ref[pair])
 
             return carry
 
@@ -402,38 +396,39 @@
     tile = latents.reshape(frames_dev * area, depth)
     count = frame_counts
     edge = jax.ShapeDtypeStruct((area, chans), jnp.float32)
-    near, far = pl.pallas_call(
+    far = pl.pallas_call(
         functools.partial(edge_kernel, rows, cols, frames_dev),
-        out_shape=(edge, edge),
+        out_shape=edge,
         in_specs=[ANY, ANY],
-        out_specs=(VMEM, VMEM),
+        out_specs=VMEM,
         scratch_shapes=[
-            pltpu.VMEM((2 * area, depth), jnp.bfloat16),
-            pltpu.VMEM((2 * TAPS * TAPS, depth, chans), jnp.bfloat16),
-            pltpu.SemaphoreType.DMA((4,)),
+            pltpu.VMEM((area, depth), jnp.bfloat16),
+            pltpu.VMEM((TAPS * TAPS, depth, chans), jnp.bfloat16),
+            pltpu.SemaphoreType.DMA((2,)),
         ],
         compiler_params=limit(EDGE_LIMIT),
-        cost_estimate=pl.CostEstimate(flops=600000000, bytes_accessed=4500000, transcendentals=0),
+        cost_estimate=pl.CostEstimate(flops=300000000, bytes_accessed=2000000, transcendentals=0),
         name="edge",
     )(tile, conv_weight)
     across = [(i, i + 1) for i in range(1, heads_dev - 1, 2)]
     far = lax.ppermute(far, "head", across + [(j, i) for i, j in across])
-    near = lax.ppermute(near, "head", [(i, i ^ 1) for i in range(heads_dev)])
 
     route_rows = routes[:, 0].reshape(heads_dev, tok_dev)
     row_width = 4 * chans + LANES
-    acc, onehot = pl.pallas_call(
+    near, acc, onehot = pl.pallas_call(
         functools.partial(own_kernel, bags, cap, rows, cols, frames_dev),
         out_shape=(
+            edge,
             jax.ShapeDtypeStruct((frames_dev * area, chans), jnp.float32),
             jax.ShapeDtypeStruct((slots, tok_dev), jnp.bfloat16),
         ),
         in_specs=[VMEM, VMEM, VMEM, VMEM],
-        out_specs=(VMEM, VMEM),
+        out_specs=(VMEM, VMEM, VMEM),
         compiler_params=limit(16),
-        cost_estimate=pl.CostEstimate(flops=1200000000, bytes_accessed=4500000, transcendentals=0),
+        cost_estimate=pl.CostEstimate(flops=1500000000, bytes_accessed=4500000, transcendentals=0),
         name="own",
     )(count, tile, conv_weight, route_rows)
+    near = lax.ppermute(near, "head", [(i, i ^ 1) for i in range(heads_dev)])
     outgoing = pl.pallas_call(
         functools.partial(join_kernel, rows, cols, frames_dev),
         out_shape=jax.ShapeDtypeStruct((slots, row_width), jnp.bfloat16),
@@ -487,7 +482,6 @@
     masks = tuple(pieces)
 
     pair_rows = 2 * heads_dev * cap
-    heads_here = local_width // HDIM
     attended = pl.pallas_call(
         functools.partial(bag_kernel, bags, cap, masks),
         out_shape=jax.ShapeDtypeStruct((heads_dev * bags, cap, local_width), jnp.bfloat16),
@@ -496,8 +490,8 @@
         scratch_shapes=[
             pltpu.VMEM((3, count_slots, local_width), jnp.bfloat16),
             pltpu.VMEM((count_slots, LANES), jnp.bfloat16),
-            pltpu.VMEM((heads_here, pair_rows, LANES), jnp.float32),
-            pltpu.VMEM((heads_here, pair_rows, 2 * LANES), jnp.float32),
+            pltpu.VMEM((local_width // LANES, 2 * pair_rows, LANES), jnp.float32),
+            pltpu.VMEM((local_width // LANES, 2 * pair_rows, 2 * LANES), jnp.float32),
             pltpu.SMEM((2 * bags,), jnp.int32),
         ],
         compiler_params=limit(28),

time: 67.3 us -> 67.4 us (level)
  waiting for transfers between devices: 1.15 us -> 4.05 us
  local copies, waits for them, and re-layouts: 2.81 us -> 0.03 us
  blocking collectives: 38.3 us -> 40.3 us
  starting transfers between devices: 6.98 us -> 5.28 us
    ppermute x1, starting transfers between devices: 5.06 us -> 0.04 us  [shards(): across = lax.ppermute(arrived, 'head', swap)]
    ppermute x1, starting transfers between devices: 0.56 us -> 4.43 us  [shards(): near = lax.ppermute(near, 'head', [(i, i ^ 1) for i in range(heads_dev)])]
    unnamed x12, local copies, waits for them, and re-layouts: 2.81 us -> 0.03 us
    all_to_all x1, blocking collectives: 23.6 us -> 25.5 us  [shards(): lax.all_to_all(attended, ('head', 'bag'), split_axis=0, concat_axis=0, ti...]
    ppermute x1, waiting for transfers between devices: 0.01 us -> 1.55 us  [shards(): across = lax.ppermute(arrived, 'head', swap)]
    ppermute x1, waiting for transfers between devices: 0.01 us -> 0.98 us  [shards(): near = lax.ppermute(near, 'head', [(i, i ^ 1) for i in range(heads_dev)])]
  transfers between devices with their start and end apart: 5 -> 5, of which waited for: 1 -> 3; matrix products, arithmetic and copies ran while one was open for 0% -> 0% of each run, Pallas kernels for 10% -> 10%
where the time goes in v10:
time: 67.4 us; the launch traced here: 67.2 us
  blocking collectives  40.3 us (60%)
  Pallas kernels  16.8 us (25%)
  starting transfers between devices  5.28 us (8%)
  waiting for transfers between devices  4.05 us (6%)
  between operations  0.77 us (1%)
    all_to_all x1, blocking collectives, shards(): lax.all_to_all(attended, ('head', 'bag'), split_axis=0, concat_axis=0, ti...  25.5 us
    all_to_all x1, blocking collectives, shards(): lax.all_to_all(outgoing.reshape(bags, cap, row_width), 'bag', split_axis=...  14.8 us
    pallas_call x1, Pallas kernels, shards(): pl.pallas_call(functools.partial(bag_kernel, bags, cap, masks), out_shape...  5.44 us
    ppermute x1, starting transfers between devices, shards(): near = lax.ppermute(near, 'head', [(i, i ^ 1) for i in range(heads_dev)])  4.43 us
    pallas_call x1, Pallas kernels, shards(): pl.pallas_call(fold_kernel, out_shape=jax.ShapeDtypeStruct((3, 2 * embed_...  3.46 us
    pallas_call x1, Pallas kernels, shards(): pl.pallas_call(functools.partial(edge_kernel, rows, cols, frames_dev), ou...  2.68 us
    pallas_call x1, Pallas kernels, shards(): pl.pallas_call(functools.partial(own_kernel, bags, cap, rows, cols, frame...  1.92 us
    ppermute x1, waiting for transfers between devices, shards(): across = lax.ppermute(arrived, 'head', swap)  1.55 us
  transfers between devices with their start and end apart: 5, of which 3 were waited for; matrix products, arithmetic and copies ran while one was open for 0% of the time, Pallas kernels for 10%

profile of v10, /device:TPU:0, one launch (start us, length us, event | category | flops | bytes accessed | tf_op | source)
XLA Modules:
  0.0 67.2 jit_solution(15408916887031756428)
XLA Ops:
  0.0 0.0 copy-start
  0.0 0.0 copy-start.2
  0.0 0.0 copy-start.5
  0.0 2.7 %edge.1 = f32[256,128]{1,0:T(8,128)} custom-call(bf16[512,512]{1,0:T(8,128)(2,1)} %bitcast.13, bf16[27,512,128]{2,1,0:T(8,128)(2,1)} %w_hbm.1), custom_call_target="tpu_custom_call" | custom-call | flops 300000000 | bytes 2000000 | tf_op jit(solution)/shard_map/edge/pallas_call | solution.py:399
  2.7 0.0 copy-start.1
  2.7 0.0 copy-start.3
  2.7 0.8 %collective-permute-start.1 = (f32[256,128]{1,0:T(8,128)}, f32[256,128]{1,0:T(8,128)S(1)}, u32[]{:S(2)}, u32[]{:S(2)}) collective-permute-start(f32[256,128]{1,0:T(8,128)} %edge.1), channel_id=1, source_target_pairs={{1,2},{2,1},{5,6},{6,5},{9,10},{10,9},{13,14},{14,13},{17,18},{18,... | collective-permute-start | bytes 393224 | tf_op jit(solution)/shard_map/ppermute | solution.py:414
  4.2 0.0 copy-done
  4.2 0.0 copy-done.2
  4.2 0.0 copy-done.5
  4.2 0.0 copy-start.4
  4.2 1.9 %own.1 = (f32[256,128]{1,0:T(8,128)S(1)}, f32[512,128]{1,0:T(8,128)S(1)}, bf16[192,128]{1,0:T(8,128)(2,1)S(1)}) custom-call(s32[1]{0:T(128)S(6)} %copy.8.count_ref, bf16[512,512]{1,0:T(8,128)(2,1)S(1)} %bitcast.14, bf16[27,512,128]{2,1,0:T(8,128)(2,1)S(1)} %copy-done, s32[4,128]{1,0:T(4,128)S(1)} %bitcast.16), custom_call_target="tpu_custom_call" | custom-call | flops 1500000000 | bytes 4500000 | tf_op jit(solution)/shard_map/own/pallas_call | solution.py:418
  6.2 4.4 %collective-permute-start = (f32[256,128]{1,0:T(8,128)S(1)}, f32[256,128]{1,0:T(8,128)S(1)}, u32[]{:S(2)}, u32[]{:S(2)}) collective-permute-start(f32[256,128]{1,0:T(8,128)S(1)} %get-tuple-element.12), channel_id=1, source_target_pairs={{0,1},{1,0},{2,3},{3,2},{4,5},{5,4},{6,7},{7,6},{8,9},{9,8},{10,11... | collective-permute-start | bytes 393224 | tf_op jit(solution)/shard_map/ppermute | solution.py:431
  10.6 0.0 collective-permute-done.1.far_ref
  10.6 1.0 %collective-permute-done.near_ref = f32[256,128]{1,0:T(8,128)S(1)} collective-permute-done((f32[256,128]{1,0:T(8,128)S(1)}, f32[256,128]{1,0:T(8,128)S(1)}, u32[]{:S(2)}, u32[]{:S(2)}) %collective-permute-start) | collective-permute-done | bytes 131104 | tf_op jit(solution)/shard_map/ppermute | solution.py:431
  11.6 0.0 copy-done.1
  11.6 0.0 copy-done.3
  11.6 0.7 %join.1 = bf16[192,640]{1,0:T(8,128)(2,1)S(1)} custom-call(s32[1]{0:T(128)S(6)} %copy.8.count_ref, s32[4,128]{1,0:T(4,128)S(1)} %bitcast.15, f32[512,128]{1,0:T(8,128)S(1)} %get-tuple-element.11.acc_ref, f32[256,128]{1,0:T(8,128)S(1)} %collective-permute-done.near_ref, f32[256,128]{1,0:T(8,128)S(1)} %collective-permute-done.1.far_ref, ...), custom_call_target="tpu_custom_call" | custom-call | flops 300000000 | bytes 3000000 | tf_op jit(solution)/shard_map/join/pallas_call | solution.py:432
  12.3 14.8 %all_to_all.10 = bf16[8,24,640]{2,1,0:T(8,128)(2,1)S(1)} all-to-all(bf16[8,24,640]{2,1,0:T(8,128)(2,1)S(1)} %bitcast.12), channel_id=1, replica_groups=mesh['bag'=8,'head'=4] {'bag'}, dimensions={0} | all-to-all | bytes 491520 | tf_op jit(solution)/shard_map/all_to_all | solution.py:443
  27.1 0.0 collective-permute-start.3
  27.2 0.0 collective-permute-start.2
  27.2 0.0 copy-done.4
  27.2 3.5 %fold.1.refs_2_.refs_5_ = bf16[3,1024,512]{2,1,0:T(8,128)(2,1)S(1)} custom-call(bf16[512,2048]{1,0:T(8,128)(2,1)S(1)} %copy-done.1, bf16[3,2048,512]{2,1,0:T(8,128)(2,1)S(1)} %copy-done.4, bf16[192,640]{1,0:T(8,128)(2,1)S(1)} %bitcast.9), custom_call_target="tpu_custom_call" | custom-call | flops 3300000000 | bytes 14000000 | tf_op jit(solution)/shard_map/fold/pallas_call | solution.py:451
  30.6 0.0 collective-permute-done.2.refs_1_
  30.6 1.4 %near_qkv.1.refs_4_ = f32[3,384,512]{2,1,0:T(8,128)S(1)} custom-call(bf16[192,640]{1,0:T(8,128)(2,1)S(1)} %bitcast.10, bf16[192,640]{1,0:T(8,128)(2,1)S(1)} %collective-permute-done.2.refs_1_, bf16[3,1024,512]{2,1,0:T(8,128)(2,1)S(1)} %fold.1.refs_2_.refs_5_), custom_call_target="tpu_custom_call" | custom-call | flops 1200000000 | bytes 6000000 | tf_op jit(solution)/shard_map/near_qkv/pallas_call | solution.py:469
  32.0 1.6 %collective-permute-done.3.refs_2_ = bf16[192,640]{1,0:T(8,128)(2,1)S(1)} collective-permute-done((bf16[192,640]{1,0:T(8,128)(2,1)S(1)}, bf16[192,640]{1,0:T(8,128)(2,1)S(1)}, u32[]{:S(2)}, u32[]{:S(2)}) %collective-permute-start.3) | collective-permute-done | bytes 245792 | tf_op jit(solution)/shard_map/ppermute | solution.py:450
  33.6 0.0 collective-permute-start.4
  33.6 1.5 %collective-permute-done.4.refs_3_ = bf16[192,640]{1,0:T(8,128)(2,1)S(1)} collective-permute-done((bf16[192,640]{1,0:T(8,128)(2,1)S(1)}, bf16[192,640]{1,0:T(8,128)(2,1)S(1)}, u32[]{:S(2)}, u32[]{:S(2)}) %collective-permute-start.4) | collective-permute-done | bytes 245792 | tf_op jit(solution)/shard_map/ppermute | solution.py:464
  35.1 5.4 %bag.1 = bf16[32,24,512]{2,1,0:T(8,128)(2,1)S(1)} custom-call(bf16[192,640]{1,0:T(8,128)(2,1)S(1)} %bitcast.11, bf16[192,640]{1,0:T(8,128)(2,1)S(1)} %collective-permute-done.2.refs_1_, bf16[192,640]{1,0:T(8,128)(2,1)S(1)} %collective-permute-done.3.refs_2_, bf16[192,640]{1,0:T(8,128)(2,1)S(1)} %collective-permute-done.4.refs_3_, ...), custom_call_target="tpu_custom_call" | custom-call | flops 3000000000 | bytes 5000000 | tf_op jit(solution)/shard_map/bag/pallas_call | solution.py:485
  40.5 25.5 %all_to_all.11 = bf16[32,24,512]{2,1,0:T(8,128)(2,1)S(1)} all-to-all(bf16[32,24,512]{2,1,0:T(8,128)(2,1)S(1)} %bag.1), channel_id=1, replica_groups=mesh['bag'=8,'head'=4] {'head','bag'}, dimensions={0} | all-to-all | bytes 1572864 | tf_op jit(solution)/shard_map/all_to_all | solution.py:501
  66.1 1.2 %collect.1 = bf16[128,2048]{1,0:T(8,128)(2,1)} custom-call(s32[1]{0:T(128)S(6)} %copy.8.count_ref, bf16[192,128]{1,0:T(8,128)(2,1)S(1)} %get-tuple-element.10.onehot_ref, bf16[768,512]{1,0:T(8,128)(2,1)S(1)} %bitcast.6), custom_call_target="tpu_custom_call" | custom-call | tf_op jit(solution)/shard_map/collect/pallas_call | solution.py:502
Async XLA Ops:
  0.0 4.2 %copy-start = (bf16[27,512,128]{2,1,0:T(8,128)(2,1)S(1)}, bf16[27,512,128]{2,1,0:T(8,128)(2,1)}, u32[]{:S(2)}) copy-start(bf16[27,512,128]{2,1,0:T(8,128)(2,1)} %w_hbm.1) | copy-start | bytes 10616836
  0.0 4.2 %copy-start.2 = (bf16[1,2,16,16,512]{4,3,2,1,0:T(8,128)(2,1)S(1)}, bf16[1,2,16,16,512]{4,3,2,1,0:T(8,128)(2,1)}, u32[]{:S(2)}) copy-start(bf16[1,2,16,16,512]{4,3,2,1,0:T(8,128)(2,1)} %param.7) | copy-start | bytes 1572868
  0.0 4.2 %copy-start.5 = (s32[512,1]{0,1:T(1,128)S(1)}, s32[512,1]{0,1:T(1,128)}, u32[]{:S(2)}) copy-start(s32[512,1]{0,1:T(1,128)} %param.9) | copy-start | bytes 6148
  2.7 8.9 %copy-start.1 = (bf16[512,2048]{1,0:T(8,128)(2,1)S(1)}, bf16[512,2048]{1,0:T(8,128)(2,1)}, u32[]{:S(2)}) copy-start(bf16[512,2048]{1,0:T(8,128)(2,1)} %e_ref.3) | copy-start | bytes 6291460
  2.7 8.9 %copy-start.3 = (s32[512]{0:T(512)S(1)}, s32[512]{0:T(512)}, u32[]{:S(2)}) copy-start(s32[512]{0:T(512)} %param.10) | copy-start | bytes 6148
  2.7 7.9 %collective-permute-start.1 = (f32[256,128]{1,0:T(8,128)}, f32[256,128]{1,0:T(8,128)S(1)}, u32[]{:S(2)}, u32[]{:S(2)}) collective-permute-start(f32[256,128]{1,0:T(8,128)} %edge.1), channel_id=1, source_target_pairs={{1,2},{2,1},{5,6},{6,5},{9,10},{10,9},{13,14},{14,13},{17,18},{18,... | collective-permute-start | bytes 393224 | tf_op jit(solution)/shard_map/ppermute | solution.py:414
  4.2 23.0 %copy-start.4 = (bf16[3,2048,512]{2,1,0:T(8,128)(2,1)S(1)}, bf16[3,2048,512]{2,1,0:T(8,128)(2,1)}, u32[]{:S(2)}) copy-start(bf16[3,2048,512]{2,1,0:T(8,128)(2,1)} %w_ref.3) | copy-start | bytes 18874372
  6.2 5.4 %collective-permute-start = (f32[256,128]{1,0:T(8,128)S(1)}, f32[256,128]{1,0:T(8,128)S(1)}, u32[]{:S(2)}, u32[]{:S(2)}) collective-permute-start(f32[256,128]{1,0:T(8,128)S(1)} %get-tuple-element.12), channel_id=1, source_target_pairs={{0,1},{1,0},{2,3},{3,2},{4,5},{5,4},{6,7},{7,6},{8,9},{9,8},{10,11... | collective-permute-start | bytes 393224 | tf_op jit(solution)/shard_map/ppermute | solution.py:431
  27.1 6.5 %collective-permute-start.3 = (bf16[192,640]{1,0:T(8,128)(2,1)S(1)}, bf16[192,640]{1,0:T(8,128)(2,1)S(1)}, u32[]{:S(2)}, u32[]{:S(2)}) collective-permute-start(bf16[192,640]{1,0:T(8,128)(2,1)S(1)} %bitcast.7), channel_id=1, source_target_pairs={{0,2},{1,3},{2,0},{3,1},{4,6},{5,7},{6,4},{7,5},{8,10},{9,11},{10,... | collective-permute-start | bytes 737288 | tf_op jit(solution)/shard_map/ppermute | solution.py:450
  27.2 3.5 %collective-permute-start.2 = (bf16[192,640]{1,0:T(8,128)(2,1)S(1)}, bf16[192,640]{1,0:T(8,128)(2,1)S(1)}, u32[]{:S(2)}, u32[]{:S(2)}) collective-permute-start(bf16[192,640]{1,0:T(8,128)(2,1)S(1)} %bitcast.8), channel_id=1, source_target_pairs={{0,1},{1,0},{2,3},{3,2},{4,5},{5,4},{6,7},{7,6},{8,9},{9,8},{10,11... | collective-permute-start | bytes 737288 | tf_op jit(solution)/shard_map/ppermute | solution.py:464
  33.6 1.5 %collective-permute-start.4 = (bf16[192,640]{1,0:T(8,128)(2,1)S(1)}, bf16[192,640]{1,0:T(8,128)(2,1)S(1)}, u32[]{:S(2)}, u32[]{:S(2)}) collective-permute-start(bf16[192,640]{1,0:T(8,128)(2,1)S(1)} %collective-permute-done.3.refs_2_), channel_id=1, source_target_pairs={{0,1},{1,0},{2,3},{3,2},{4,5},{5,4},{6,7},{7,6},{8,9},{9,8},{10,11... | collective-permute-start | bytes 737288 | tf_op jit(solution)/shard_map/ppermute | solution.py:464

commit v11 on v9

--- a/solution.py
+++ b/solution.py
@@ -1,4 +1,5 @@
 import functools
+import math
 import jax
 import jax.numpy as jnp
 from jax import lax
@@ -16,7 +17,7 @@
 
 VMEM = pl.BlockSpec(memory_space=pltpu.VMEM)
 ANY = pl.BlockSpec(memory_space=pl.ANY)
-EDGE_LIMIT = 60
+EDGE_LIMIT = 62
 
 
 def limit(mib):
@@ -192,7 +193,7 @@
             cols = slice(n, n + col_tile)
             product = jnp.dot(e_ref[...], w_ref[m, :, cols], preferred_element_type=jnp.float32)
             if m == 0:
-                product = product * HDIM ** (-0.5)
+                product = product * (HDIM ** (-0.5) * math.log2(math.e))
             high = product.astype(jnp.bfloat16)
             fold_ref[m, :feats, cols] = high
             fold_ref[m, feats:, cols] = (product - high.astype(jnp.float32)).astype(jnp.bfloat16)
@@ -266,8 +267,9 @@
     low = lane < HDIM
     pairs = width // LANES
     ones = jnp.ones((tile, LANES), jnp.bfloat16)
-    pick = (lax.broadcasted_iota(jnp.int32, (8, LANES), 1) == 0).astype(jnp.float32).astype(jnp.bfloat16)
-    key_at = lax.broadcasted_iota(jnp.int32, (1, tile), 1)
+    unit = lax.broadcasted_iota(jnp.int32, (2 * tile, LANES), 1) == 0
+    unit = unit.astype(jnp.float32).astype(jnp.bfloat16)
+    key_at = lax.broadcasted_iota(jnp.int32, (tile, LANES), 0)
 
     def two(ref, a, b, *at):
         return jnp.concatenate(
@@ -291,34 +293,31 @@
             )
 
         def bias_of(a, b, second):
-            label = lax.dot_general(
-                pick,
-                two(note_ref, a, b, slice(0, LANES)),
-                (((1,), (1,)), ((), ())),
-                preferred_element_type=jnp.float32,
-            )[:1]
+            label = two(note_ref, a, b, slice(0, LANES)).astype(jnp.float32)
             limit = jnp.where(second, tile, clip_rows)
             good = jnp.logical_and(label == s + 1.0, key_at < limit)
-            return jnp.where(good, 0.0, far_below)
-
-        def scores_of(pair, half, query, a, b, bias):
-            cols = slice(pair * LANES, (pair + 1) * LANES)
-            keys = two(qkv_ref, a, b, 1, cols)
-            one = jnp.where(low if half == 0 else jnp.logical_not(low), query, jnp.zeros_like(query))
-            return (
-                lax.dot_general(one, keys, (((1,), (1,)), ((), ())), preferred_element_type=jnp.float32)
-                + bias
-            )
+            return jnp.where(good, 0.0, far_below).astype(jnp.bfloat16)
+
+        def stacked(pair, a, b):
+            query = two(qkv_ref, a, b, 0, slice(pair * LANES, (pair + 1) * LANES))
+            blank = jnp.zeros_like(query)
+            both = jnp.concatenate([jnp.where(low, query, blank), jnp.where(low, blank, query)], axis=0)
+            return jnp.concatenate([both, unit], axis=1)
+
+        def scores_of(pair, query, a, b, bias):
+            keys = two(qkv_ref, a, b, 1, slice(pair * LANES, (pair + 1) * LANES))
+            keys = jnp.concatenate([keys, bias], axis=1)
+            return lax.dot_general(query, keys, (((1,), (1,)), ((), ())), preferred_element_type=jnp.float32)
 
         def mix(pair, shifted, a, b):
             cols = slice(pair * LANES, (pair + 1) * LANES)
             values = jnp.concatenate([two(qkv_ref, a, b, 2, cols), ones], axis=1)
             return jnp.dot(shifted.astype(jnp.bfloat16), values, preferred_element_type=jnp.float32)
 
-        def store(pair, a, b, results):
+        def store(pair, a, b, result):
             cols = slice(pair * LANES, (pair + 1) * LANES)
-            heads = [r[:, :LANES] / r[:, LANES:] for r in results]
-            mixed = jnp.where(low, heads[0], heads[1])
+            shares = result[:, :LANES] / result[:, LANES:]
+            mixed = jnp.where(low, shares[:tile], shares[tile:])
             for at, clip in ((clip_rows, b), (0, a)):
                 for j, mask in enumerate(masks):
                     piece = mixed[at + j * cap : at + (j + 1) * cap]
@@ -332,39 +331,32 @@
                 ka, kb, second = members(0)
                 bias = bias_of(ka, kb, second)
                 for pair in range(pairs):
-                    query = two(qkv_ref, qa, qb, 0, slice(pair * LANES, (pair + 1) * LANES))
-                    results = []
-                    for half in range(2):
-                        scores = scores_of(pair, half, query, ka, kb, bias)
-                        top = jnp.max(scores, axis=-1, keepdims=True)
-                        results.append(mix(pair, jnp.exp(scores - top), ka, kb))
-                    store(pair, qa, qb, results)
+                    scores = scores_of(pair, stacked(pair, qa, qb), ka, kb, bias)
+                    top = jnp.max(scores, axis=-1, keepdims=True)
+                    store(pair, qa, qb, mix(pair, jnp.exp2(scores - top), ka, kb))
 
             @pl.when(tiles > 1)
             def _():
-                for h in range(2 * pairs):
-                    m_ref[h] = jnp.full((tile, LANES), far_below, jnp.float32)
-                    r_ref[h] = jnp.zeros((tile, 2 * LANES), jnp.float32)
+                for pair in range(pairs):
+                    m_ref[pair] = jnp.full((2 * tile, LANES), far_below, jnp.float32)
+                    r_ref[pair] = jnp.zeros((2 * tile, 2 * LANES), jnp.float32)
 
                 def key_tile(j, inner):
                     ka, kb, second = members(j)
                     bias = bias_of(ka, kb, second)
                     for pair in range(pairs):
-                        query = two(qkv_ref, qa, qb, 0, slice(pair * LANES, (pair + 1) * LANES))
-                        for half in range(2):
-                            h = 2 * pair + half
-                            scores = scores_of(pair, half, query, ka, kb, bias)
-                            old = m_ref[h][:, :1]
-                            top = jnp.maximum(old, jnp.max(scores, axis=-1, keepdims=True))
-                            r_ref[h] = r_ref[h] * jnp.exp(old - top) + mix(
-                                pair, jnp.exp(scores - top), ka, kb
-                            )
-                            m_ref[h] = jnp.broadcast_to(top, (tile, LANES))
+                        scores = scores_of(pair, stacked(pair, qa, qb), ka, kb, bias)
+                        old = m_ref[pair][:, :1]
+                        top = jnp.maximum(old, jnp.max(scores, axis=-1, keepdims=True))
+                        r_ref[pair] = r_ref[pair] * jnp.exp2(old - top) + mix(
+                            pair, jnp.exp2(scores - top), ka, kb
+                        )
+                        m_ref[pair] = jnp.broadcast_to(top, (2 * tile, LANES))
                     return inner
 
                 lax.fori_loop(0, tiles, key_tile, 0)
                 for pair in range(pairs):
-                    store(pair, qa, qb, [r_ref[2 * pair], r_ref[2 * pair + 1]])
+                    store(pair, qa, qb, r_ref[pair])
 
             return carry
 
@@ -487,7 +479,6 @@
     masks = tuple(pieces)
 
     pair_rows = 2 * heads_dev * cap
-    heads_here = local_width // HDIM
     attended = pl.pallas_call(
         functools.partial(bag_kernel, bags, cap, masks),
         out_shape=jax.ShapeDtypeStruct((heads_dev * bags, cap, local_width), jnp.bfloat16),
@@ -496,8 +487,8 @@
         scratch_shapes=[
             pltpu.VMEM((3, count_slots, local_width), jnp.bfloat16),
             pltpu.VMEM((count_slots, LANES), jnp.bfloat16),
-            pltpu.VMEM((heads_here, pair_rows, LANES), jnp.float32),
-            pltpu.VMEM((heads_here, pair_rows, 2 * LANES), jnp.float32),
+            pltpu.VMEM((local_width // LANES, 2 * pair_rows, LANES), jnp.float32),
+            pltpu.VMEM((local_width // LANES, 2 * pair_rows, 2 * LANES), jnp.float32),
             pltpu.SMEM((2 * bags,), jnp.int32),
         ],
         compiler_params=limit(28),

time: 67.3 us -> 68.3 us (1.015)
  local copies, waits for them, and re-layouts: 2.81 us -> 4.8 us
  starting transfers between devices: 6.98 us -> 5.13 us
  Pallas kernels: 17 us -> 17.7 us
    unnamed x12, local copies, waits for them, and re-layouts: 2.81 us -> 4.8 us
    ppermute x1, starting transfers between devices: 5.06 us -> 3.34 us  [shards(): across = lax.ppermute(arrived, 'head', swap)]
    pallas_call x1, Pallas kernels: 5.44 us -> 6.24 us  [shards(): pl.pallas_call(functools.partial(bag_kernel, bags, cap, masks), out_shape...]
  transfers between devices with their start and end apart: 5 -> 5, of which waited for: 1 -> 1; matrix products, arithmetic and copies ran while one was open for 0% -> 0% of each run, Pallas kernels for 10% -> 9%
where the time goes in v11:
time: 68.3 us; the launch traced here: 68 us
  blocking collectives  38.5 us (56%)
  Pallas kernels  17.7 us (26%)
  starting transfers between devices  5.13 us (8%)
  local copies, waits for them, and re-layouts  4.8 us (7%)
  waiting for transfers between devices  1.15 us (2%)
  between operations  0.79 us (1%)
    all_to_all x1, blocking collectives, shards(): lax.all_to_all(attended, ('head', 'bag'), split_axis=0, concat_axis=0, ti...  23.7 us
    all_to_all x1, blocking collectives, shards(): lax.all_to_all(outgoing.reshape(bags, cap, row_width), 'bag', split_axis=...  14.7 us
    pallas_call x1, Pallas kernels, shards(): pl.pallas_call(functools.partial(bag_kernel, bags, cap, masks), out_shape...  6.24 us
    unnamed x12, local copies, waits for them, and re-layouts  4.8 us
    pallas_call x1, Pallas kernels, shards(): pl.pallas_call(fold_kernel, out_shape=jax.ShapeDtypeStruct((3, 2 * embed_...  3.43 us
    ppermute x1, starting transfers between devices, shards(): across = lax.ppermute(arrived, 'head', swap)  3.34 us
    pallas_call x1, Pallas kernels, shards(): pl.pallas_call(functools.partial(edge_kernel, rows, cols, frames_dev), ou...  3.17 us
    pallas_call x1, Pallas kernels, shards(): pl.pallas_call(functools.partial(own_kernel, bags, cap, rows, cols, frame...  1.56 us
  transfers between devices with their start and end apart: 5, of which 1 were waited for; matrix products, arithmetic and copies ran while one was open for 0% of the time, Pallas kernels for 9%

profile of v11, /device:TPU:0, one launch (start us, length us, event | category | flops | bytes accessed | tf_op | source)
XLA Modules:
  0.0 68.0 jit_solution(10318510576325621017)
XLA Ops:
  0.0 0.0 copy-start.2
  0.0 0.0 copy-start.5
  0.0 3.2 %edge.1 = (f32[256,128]{1,0:T(8,128)}, f32[256,128]{1,0:T(8,128)}) custom-call(bf16[512,512]{1,0:T(8,128)(2,1)} %bitcast.13, bf16[27,512,128]{2,1,0:T(8,128)(2,1)} %w_hbm.1), custom_call_target="tpu_custom_call" | custom-call | flops 600000000 | bytes 4500000 | tf_op jit(solution)/shard_map/edge/pallas_call | solution.py:397
  3.2 0.0 copy-start.3
  3.2 0.6 collective-permute-start
  3.7 0.7 collective-permute-start.1
  5.1 0.0 copy-done.2
  5.1 0.0 copy-done.5
  5.1 0.0 copy-start
  5.1 2.0 %copy-done = bf16[27,512,128]{2,1,0:T(8,128)(2,1)S(1)} copy-done((bf16[27,512,128]{2,1,0:T(8,128)(2,1)S(1)}, bf16[27,512,128]{2,1,0:T(8,128)(2,1)}, u32[]{:S(2)}) %copy-start) | copy-done | bytes 3538968
  7.1 0.0 copy-start.1
  7.1 1.6 %own.1 = (f32[512,128]{1,0:T(8,128)S(1)}, bf16[192,128]{1,0:T(8,128)(2,1)S(1)}) custom-call(s32[1]{0:T(128)S(6)} %copy.8.count_ref, bf16[512,512]{1,0:T(8,128)(2,1)S(1)} %bitcast.14, bf16[27,512,128]{2,1,0:T(8,128)(2,1)S(1)} %copy-done, s32[4,128]{1,0:T(4,128)S(1)} %bitcast.16), custom_call_target="tpu_custom_call" | custom-call | flops 1200000000 | bytes 4500000 | tf_op jit(solution)/shard_map/own/pallas_call | solution.py:417
  8.7 0.0 collective-permute-done.near_ref
  8.7 0.0 collective-permute-done.1.far_ref
  8.7 0.0 copy-done.3
  8.7 0.0 copy-done.1
  8.7 0.7 %join.1 = bf16[192,640]{1,0:T(8,128)(2,1)S(1)} custom-call(s32[1]{0:T(128)S(6)} %copy.8.count_ref, s32[4,128]{1,0:T(4,128)S(1)} %bitcast.15, f32[512,128]{1,0:T(8,128)S(1)} %get-tuple-element.12.acc_ref, f32[256,128]{1,0:T(8,128)S(1)} %collective-permute-done.near_ref, f32[256,128]{1,0:T(8,128)S(1)} %collective-permute-done.1.far_ref, ...), custom_call_target="tpu_custom_call" | custom-call | flops 300000000 | bytes 3000000 | tf_op jit(solution)/shard_map/join/pallas_call | solution.py:429
  9.4 14.7 %all_to_all.10 = bf16[8,24,640]{2,1,0:T(8,128)(2,1)S(1)} all-to-all(bf16[8,24,640]{2,1,0:T(8,128)(2,1)S(1)} %bitcast.12), channel_id=1, replica_groups=mesh['bag'=8,'head'=4] {'bag'}, dimensions={0} | all-to-all | bytes 491520 | tf_op jit(solution)/shard_map/all_to_all | solution.py:440
  24.2 3.3 %collective-permute-start.3 = (bf16[192,640]{1,0:T(8,128)(2,1)S(1)}, bf16[192,640]{1,0:T(8,128)(2,1)S(1)}, u32[]{:S(2)}, u32[]{:S(2)}) collective-permute-start(bf16[192,640]{1,0:T(8,128)(2,1)S(1)} %bitcast.7), channel_id=1, source_target_pairs={{0,2},{1,3},{2,0},{3,1},{4,6},{5,7},{6,4},{7,5},{8,10},{9,11},{10,... | collective-permute-start | bytes 737288 | tf_op jit(solution)/shard_map/ppermute | solution.py:447
  27.5 0.0 collective-permute-start.2
  27.5 0.0 copy-start.4
  27.5 2.8 %copy-done.4 = bf16[3,2048,512]{2,1,0:T(8,128)(2,1)S(1)} copy-done((bf16[3,2048,512]{2,1,0:T(8,128)(2,1)S(1)}, bf16[3,2048,512]{2,1,0:T(8,128)(2,1)}, u32[]{:S(2)}) %copy-start.4) | copy-done | bytes 6291480
  30.3 3.4 %fold.1.refs_2_.refs_5_ = bf16[3,1024,512]{2,1,0:T(8,128)(2,1)S(1)} custom-call(bf16[512,2048]{1,0:T(8,128)(2,1)S(1)} %copy-done.1, bf16[3,2048,512]{2,1,0:T(8,128)(2,1)S(1)} %copy-done.4, bf16[192,640]{1,0:T(8,128)(2,1)S(1)} %bitcast.9), custom_call_target="tpu_custom_call" | custom-call | flops 3300000000 | bytes 14000000 | tf_op jit(solution)/shard_map/fold/pallas_call | solution.py:448
  33.7 0.0 collective-permute-done.2.refs_1_
  33.7 1.4 %near_qkv.1.refs_4_ = f32[3,384,512]{2,1,0:T(8,128)S(1)} custom-call(bf16[192,640]{1,0:T(8,128)(2,1)S(1)} %bitcast.10, bf16[192,640]{1,0:T(8,128)(2,1)S(1)} %collective-permute-done.2.refs_1_, bf16[3,1024,512]{2,1,0:T(8,128)(2,1)S(1)} %fold.1.refs_2_.refs_5_), custom_call_target="tpu_custom_call" | custom-call | flops 1200000000 | bytes 6000000 | tf_op jit(solution)/shard_map/near_qkv/pallas_call | solution.py:466
  35.1 0.0 collective-permute-done.3.refs_2_
  35.1 0.6 collective-permute-start.4
  35.7 1.1 %collective-permute-done.4.refs_3_ = bf16[192,640]{1,0:T(8,128)(2,1)S(1)} collective-permute-done((bf16[192,640]{1,0:T(8,128)(2,1)S(1)}, bf16[192,640]{1,0:T(8,128)(2,1)S(1)}, u32[]{:S(2)}, u32[]{:S(2)}) %collective-permute-start.4) | collective-permute-done | bytes 245792 | tf_op jit(solution)/shard_map/ppermute | solution.py:461
  36.9 6.2 %bag.1 = bf16[32,24,512]{2,1,0:T(8,128)(2,1)S(1)} custom-call(bf16[192,640]{1,0:T(8,128)(2,1)S(1)} %bitcast.11, bf16[192,640]{1,0:T(8,128)(2,1)S(1)} %collective-permute-done.2.refs_1_, bf16[192,640]{1,0:T(8,128)(2,1)S(1)} %collective-permute-done.3.refs_2_, bf16[192,640]{1,0:T(8,128)(2,1)S(1)} %collective-permute-done.4.refs_3_, ...), custom_call_target="tpu_custom_call" | custom-call | flops 3000000000 | bytes 5000000 | tf_op jit(solution)/shard_map/bag/pallas_call | solution.py:482
  43.1 23.7 %all_to_all.11 = bf16[32,24,512]{2,1,0:T(8,128)(2,1)S(1)} all-to-all(bf16[32,24,512]{2,1,0:T(8,128)(2,1)S(1)} %bag.1), channel_id=1, replica_groups=mesh['bag'=8,'head'=4] {'head','bag'}, dimensions={0} | all-to-all | bytes 1572864 | tf_op jit(solution)/shard_map/all_to_all | solution.py:498
  66.8 1.2 %collect.1 = bf16[128,2048]{1,0:T(8,128)(2,1)} custom-call(s32[1]{0:T(128)S(6)} %copy.8.count_ref, bf16[192,128]{1,0:T(8,128)(2,1)S(1)} %get-tuple-element.11.onehot_ref, bf16[768,512]{1,0:T(8,128)(2,1)S(1)} %bitcast.6), custom_call_target="tpu_custom_call" | custom-call | tf_op jit(solution)/shard_map/collect/pallas_call | solution.py:499
Async XLA Ops:
  0.0 5.1 %copy-start.2 = (bf16[1,2,16,16,512]{4,3,2,1,0:T(8,128)(2,1)S(1)}, bf16[1,2,16,16,512]{4,3,2,1,0:T(8,128)(2,1)}, u32[]{:S(2)}) copy-start(bf16[1,2,16,16,512]{4,3,2,1,0:T(8,128)(2,1)} %param.7) | copy-start | bytes 1572868
  0.0 5.1 %copy-start.5 = (s32[512,1]{0,1:T(1,128)S(1)}, s32[512,1]{0,1:T(1,128)}, u32[]{:S(2)}) copy-start(s32[512,1]{0,1:T(1,128)} %param.9) | copy-start | bytes 6148
  3.2 5.5 %copy-start.3 = (s32[512]{0:T(512)S(1)}, s32[512]{0:T(512)}, u32[]{:S(2)}) copy-start(s32[512]{0:T(512)} %param.10) | copy-start | bytes 6148
  3.2 5.5 %collective-permute-start = (f32[256,128]{1,0:T(8,128)}, f32[256,128]{1,0:T(8,128)S(1)}, u32[]{:S(2)}, u32[]{:S(2)}) collective-permute-start(f32[256,128]{1,0:T(8,128)} %get-tuple-element.13), channel_id=1, source_target_pairs={{0,1},{1,0},{2,3},{3,2},{4,5},{5,4},{6,7},{7,6},{8,9},{9,8},{10,11... | collective-permute-start | bytes 393224 | tf_op jit(solution)/shard_map/ppermute | solution.py:413
  3.7 4.9 %collective-permute-start.1 = (f32[256,128]{1,0:T(8,128)}, f32[256,128]{1,0:T(8,128)S(1)}, u32[]{:S(2)}, u32[]{:S(2)}) collective-permute-start(f32[256,128]{1,0:T(8,128)} %get-tuple-element.14), channel_id=1, source_target_pairs={{1,2},{2,1},{5,6},{6,5},{9,10},{10,9},{13,14},{14,13},{17,18},{18,... | collective-permute-start | bytes 393224 | tf_op jit(solution)/shard_map/ppermute | solution.py:412
  5.1 2.0 %copy-start = (bf16[27,512,128]{2,1,0:T(8,128)(2,1)S(1)}, bf16[27,512,128]{2,1,0:T(8,128)(2,1)}, u32[]{:S(2)}) copy-start(bf16[27,512,128]{2,1,0:T(8,128)(2,1)} %w_hbm.1) | copy-start | bytes 10616836
  7.1 1.6 %copy-start.1 = (bf16[512,2048]{1,0:T(8,128)(2,1)S(1)}, bf16[512,2048]{1,0:T(8,128)(2,1)}, u32[]{:S(2)}) copy-start(bf16[512,2048]{1,0:T(8,128)(2,1)} %e_ref.3) | copy-start | bytes 6291460
  24.2 11.0 %collective-permute-start.3 = (bf16[192,640]{1,0:T(8,128)(2,1)S(1)}, bf16[192,640]{1,0:T(8,128)(2,1)S(1)}, u32[]{:S(2)}, u32[]{:S(2)}) collective-permute-start(bf16[192,640]{1,0:T(8,128)(2,1)S(1)} %bitcast.7), channel_id=1, source_target_pairs={{0,2},{1,3},{2,0},{3,1},{4,6},{5,7},{6,4},{7,5},{8,10},{9,11},{10,... | collective-permute-start | bytes 737288 | tf_op jit(solution)/shard_map/ppermute | solution.py:447
  27.5 6.2 %collective-permute-start.2 = (bf16[192,640]{1,0:T(8,128)(2,1)S(1)}, bf16[192,640]{1,0:T(8,128)(2,1)S(1)}, u32[]{:S(2)}, u32[]{:S(2)}) collective-permute-start(bf16[192,640]{1,0:T(8,128)(2,1)S(1)} %bitcast.8), channel_id=1, source_target_pairs={{0,1},{1,0},{2,3},{3,2},{4,5},{5,4},{6,7},{7,6},{8,9},{9,8},{10,11... | collective-permute-start | bytes 737288 | tf_op jit(solution)/shard_map/ppermute | solution.py:461
  27.5 2.8 %copy-start.4 = (bf16[3,2048,512]{2,1,0:T(8,128)(2,1)S(1)}, bf16[3,2048,512]{2,1,0:T(8,128)(2,1)}, u32[]{:S(2)}) copy-start(bf16[3,2048,512]{2,1,0:T(8,128)(2,1)} %w_ref.3) | copy-start | bytes 18874372
  35.1 1.7 %collective-permute-start.4 = (bf16[192,640]{1,0:T(8,128)(2,1)S(1)}, bf16[192,640]{1,0:T(8,128)(2,1)S(1)}, u32[]{:S(2)}, u32[]{:S(2)}) collective-permute-start(bf16[192,640]{1,0:T(8,128)(2,1)S(1)} %collective-permute-done.3.refs_2_), channel_id=1, source_target_pairs={{0,1},{1,0},{2,3},{3,2},{4,5},{5,4},{6,7},{7,6},{8,9},{9,8},{10,11... | collective-permute-start | bytes 737288 | tf_op jit(solution)/shard_map/ppermute | solution.py:461

commit v12 on v11

--- a/solution.py
+++ b/solution.py
@@ -17,7 +17,7 @@
 
 VMEM = pl.BlockSpec(memory_space=pltpu.VMEM)
 ANY = pl.BlockSpec(memory_space=pl.ANY)
-EDGE_LIMIT = 62
+EDGE_LIMIT = 60
 
 
 def limit(mib):
@@ -94,18 +94,22 @@
     jobs = ((frames - 1, 0), (0, 2))
     loads = []
     for i, (f, tap) in enumerate(jobs):
-        loads.append(
-            (
+        group = [
+            pltpu.make_async_copy(
+                x_hbm.at[pl.ds(f * area, area)], x_ref.at[pl.ds(i * area, area)], sems.at[i, TAPS]
+            )
+        ]
+        for row in range(TAPS):
+            group.append(
                 pltpu.make_async_copy(
-                    x_hbm.at[pl.ds(f * area, area)], x_ref.at[pl.ds(i * area, area)], sems.at[2 * i]
-                ),
-                pltpu.make_async_copy(
-                    w_hbm.at[pl.ds(tap * plane, plane)], w_ref.at[pl.ds(i * plane, plane)], sems.at[2 * i + 1]
-                ),
+                    w_hbm.at[pl.ds(tap * plane + row * TAPS, TAPS)],
+                    w_ref.at[pl.ds(i * plane + row * TAPS, TAPS)],
+                    sems.at[i, row],
+                )
             )
-        )
-    for pair in loads:
-        for load in pair:
+        loads.append(group)
+    for group in loads:
+        for load in group:
             load.start()
     even = lax.axis_index("head") % 2 == 0
     sums = []
@@ -218,25 +222,29 @@
             yield m, n, part * scale
 
 
-def bag_kernel(clips, cap, masks, *refs):
+def bag_kernel(clips, cap, masks, groups, *refs):
     count = len(masks)
-    pieces, (near_ref, fold_ref, out_ref, qkv_ref, note_ref, m_ref, r_ref, order_ref) = refs[:count], refs[count:]
+    pieces, rest = refs[:count], refs[count:]
+    early, rest = rest[: len(groups)], rest[len(groups) :]
+    fold_ref, out_ref, qkv_ref, note_ref, m_ref, r_ref, order_ref = rest
     place = lax.axis_index("head")
     slots = pieces[0].shape[0]
     feats = pieces[0].shape[1] - LANES
     width = fold_ref.shape[2]
     clip_rows = count * cap
-    half = count // 2
+    done = sum(groups)
 
     def by_clip(values, c):
         return jnp.concatenate(
-            [value[j * slots + c * cap : j * slots + (c + 1) * cap] for value in values for j in range(half)], axis=0
+            [
+                value[j * slots + c * cap : j * slots + (c + 1) * cap]
+                for value in values
+                for j in range(value.shape[0] // slots)
+            ],
+            axis=0,
         )
 
-    notes = [
-        jnp.concatenate([ref[:, feats:].astype(jnp.float32) for ref in group], axis=0)
-        for group in (pieces[:half], pieces[half:])
-    ]
+    notes = [ref[:, feats:].astype(jnp.float32) for ref in pieces]
     for c in range(clips):
         note = by_clip(notes, c)
         note_ref[c * clip_rows : (c + 1) * clip_rows, :] = note.astype(jnp.bfloat16)
@@ -255,11 +263,11 @@
 
         starts.append(lax.fori_loop(0, clips, keep_clip, starts[-1]))
 
-    for m, at, part in qkv_parts(pieces[half:], fold_ref):
+    for m, at, part in qkv_parts(pieces[done:], fold_ref):
         cols = slice(at, at + part.shape[1])
-        both = (near_ref[m, :, cols], part)
+        parts = [ref[m, :, cols] for ref in early] + [part]
         for c in range(clips):
-            qkv_ref[m, c * clip_rows : (c + 1) * clip_rows, cols] = by_clip(both, c).astype(jnp.bfloat16)
+            qkv_ref[m, c * clip_rows : (c + 1) * clip_rows, cols] = by_clip(parts, c).astype(jnp.bfloat16)
 
     out_ref[...] = jnp.zeros_like(out_ref)
     tile = 2 * clip_rows
@@ -267,9 +275,8 @@
     low = lane < HDIM
     pairs = width // LANES
     ones = jnp.ones((tile, LANES), jnp.bfloat16)
-    unit = lax.broadcasted_iota(jnp.int32, (2 * tile, LANES), 1) == 0
-    unit = unit.astype(jnp.float32).astype(jnp.bfloat16)
-    key_at = lax.broadcasted_iota(jnp.int32, (tile, LANES), 0)
+    pick = (lax.broadcasted_iota(jnp.int32, (8, LANES), 1) == 0).astype(jnp.float32).astype(jnp.bfloat16)
+    key_at = lax.broadcasted_iota(jnp.int32, (1, tile), 1)
 
     def two(ref, a, b, *at):
         return jnp.concatenate(
@@ -293,21 +300,27 @@
             )
 
         def bias_of(a, b, second):
-            label = two(note_ref, a, b, slice(0, LANES)).astype(jnp.float32)
+            label = lax.dot_general(
+                pick,
+                two(note_ref, a, b, slice(0, LANES)),
+                (((1,), (1,)), ((), ())),
+                preferred_element_type=jnp.float32,
+            )[:1]
             limit = jnp.where(second, tile, clip_rows)
             good = jnp.logical_and(label == s + 1.0, key_at < limit)
-            return jnp.where(good, 0.0, far_below).astype(jnp.bfloat16)
+            return jnp.where(good, 0.0, far_below)
 
         def stacked(pair, a, b):
             query = two(qkv_ref, a, b, 0, slice(pair * LANES, (pair + 1) * LANES))
             blank = jnp.zeros_like(query)
-            both = jnp.concatenate([jnp.where(low, query, blank), jnp.where(low, blank, query)], axis=0)
-            return jnp.concatenate([both, unit], axis=1)
+            return jnp.concatenate([jnp.where(low, query, blank), jnp.where(low, blank, query)], axis=0)
 
         def scores_of(pair, query, a, b, bias):
             keys = two(qkv_ref, a, b, 1, slice(pair * LANES, (pair + 1) * LANES))
-            keys = jnp.concatenate([keys, bias], axis=1)
-            return lax.dot_general(query, keys, (((1,), (1,)), ((), ())), preferred_element_type=jnp.float32)
+            return (
+                lax.dot_general(query, keys, (((1,), (1,)), ((), ())), preferred_element_type=jnp.float32)
+                + bias
+            )
 
         def mix(pair, shifted, a, b):
             cols = slice(pair * LANES, (pair + 1) * LANES)
@@ -402,7 +415,7 @@
         scratch_shapes=[
             pltpu.VMEM((2 * area, depth), jnp.bfloat16),
             pltpu.VMEM((2 * TAPS * TAPS, depth, chans), jnp.bfloat16),
-            pltpu.SemaphoreType.DMA((4,)),
+            pltpu.SemaphoreType.DMA((2, TAPS + 1)),
         ],
         compiler_params=limit(EDGE_LIMIT),
         cost_estimate=pl.CostEstimate(flops=600000000, bytes_accessed=4500000, transcendentals=0),
@@ -463,26 +476,34 @@
 
     lower_bits = [1 << i for i in reversed(range(bit.bit_length() - 1))]
     close = spread({0: arrived}, lower_bits)
-    near_qkv = pl.pallas_call(
-        qkv_kernel,
-        out_shape=jax.ShapeDtypeStruct((3, len(close) * slots, local_width), jnp.float32),
-        in_specs=[VMEM] * (len(close) + 1),
-        out_specs=VMEM,
-        compiler_params=limit(16),
-        cost_estimate=pl.CostEstimate(flops=1200000000, bytes_accessed=6000000, transcendentals=0),
-        name="near_qkv",
-    )(*close.values(), folded)
+
+    def project(group, name):
+        return pl.pallas_call(
+            qkv_kernel,
+            out_shape=jax.ShapeDtypeStruct((3, len(group) * slots, local_width), jnp.float32),
+            in_specs=[VMEM] * (len(group) + 1),
+            out_specs=VMEM,
+            compiler_params=limit(16),
+            cost_estimate=pl.CostEstimate(
+                flops=600000000 * len(group), bytes_accessed=3000000 * len(group), transcendentals=0
+            ),
+            name=name,
+        )(*group, folded)
+
+    near_qkv = project(list(close.values()), "near_qkv")
     across, near_qkv = lax.optimization_barrier((across, near_qkv))
     pieces = dict(close)
     pieces.update(spread({bit: across}, lower_bits))
+    across_qkv = project([across], "across_qkv")
+    groups = (len(close), 1)
     count_slots = heads_dev * slots
     masks = tuple(pieces)
 
     pair_rows = 2 * heads_dev * cap
     attended = pl.pallas_call(
-        functools.partial(bag_kernel, bags, cap, masks),
+        functools.partial(bag_kernel, bags, cap, masks, groups),
         out_shape=jax.ShapeDtypeStruct((heads_dev * bags, cap, local_width), jnp.bfloat16),
-        in_specs=[VMEM] * (len(masks) + 2),
+        in_specs=[VMEM] * (len(masks) + 3),
         out_specs=VMEM,
         scratch_shapes=[
             pltpu.VMEM((3, count_slots, local_width), jnp.bfloat16),
@@ -494,7 +515,7 @@
         compiler_params=limit(28),
         cost_estimate=pl.CostEstimate(flops=3000000000, bytes_accessed=5000000, transcendentals=1200000),
         name="bag",
-    )(*pieces.values(), near_qkv, folded)
+    )(*pieces.values(), near_qkv, across_qkv, folded)
     received = lax.all_to_all(attended, ("head", "bag"), split_axis=0, concat_axis=0, tiled=True)
     return pl.pallas_call(
         functools.partial(collect_kernel, frames_dev, heads_dev),

time: 68.3 us -> 66.7 us (0.977)
  local copies, waits for them, and re-layouts: 4.8 us -> 2.81 us
  starting transfers between devices: 5.13 us -> 6.98 us
  waiting for transfers between devices: 1.15 us -> 0.37 us
    unnamed x12, local copies, waits for them, and re-layouts: 4.8 us -> 2.81 us
    ppermute x1, starting transfers between devices: 3.34 us -> 5.06 us  [shards(): across = lax.ppermute(arrived, 'head', swap)]
    ppermute x2, waiting for transfers between devices: 1.14 us -> 0.36 us  [spread(): lax.ppermute(piece, 'head', pairs)]
    pallas_call x2 -> x3, Pallas kernels: 7.62 us -> 7.04 us  [the longest x1 4.88 us: shards(): pl.pallas_call(functools.partial(bag_kernel, bags, cap, masks, groups), o...]
  transfers between devices with their start and end apart: 5 -> 5, of which waited for: 1 -> 1; matrix products, arithmetic and copies ran while one was open for 0% -> 0% of each run, Pallas kernels for 9% -> 11%
where the time goes in v12:
time: 66.7 us; the launch traced here: 66.4 us
  blocking collectives  38.3 us (57%)
  Pallas kernels  17.2 us (26%)
  starting transfers between devices  6.98 us (10%)
  local copies, waits for them, and re-layouts  2.81 us (4%)
  between operations  0.8 us (1%)
    all_to_all x1, blocking collectives, shards(): lax.all_to_all(attended, ('head', 'bag'), split_axis=0, concat_axis=0, ti...  23.6 us
    all_to_all x1, blocking collectives, shards(): lax.all_to_all(outgoing.reshape(bags, cap, row_width), 'bag', split_axis=...  14.7 us
    ppermute x1, starting transfers between devices, shards(): across = lax.ppermute(arrived, 'head', swap)  5.06 us
    pallas_call x1, Pallas kernels, shards(): pl.pallas_call(functools.partial(bag_kernel, bags, cap, masks, groups), o...  4.88 us
    pallas_call x1, Pallas kernels, shards(): pl.pallas_call(fold_kernel, out_shape=jax.ShapeDtypeStruct((3, 2 * embed_...  3.43 us
    pallas_call x1, Pallas kernels, shards(): pl.pallas_call(functools.partial(edge_kernel, rows, cols, frames_dev), ou...  3.26 us
    unnamed x12, local copies, waits for them, and re-layouts  2.81 us
    pallas_call x2, Pallas kernels, project(): pl.pallas_call(qkv_kernel, out_shape=jax.ShapeDtypeStruct((3, len(group)...  2.16 us
  transfers between devices with their start and end apart: 5, of which 1 were waited for; matrix products, arithmetic and copies ran while one was open for 0% of the time, Pallas kernels for 11%

profile of v12, /device:TPU:0, one launch (start us, length us, event | category | flops | bytes accessed | tf_op | source)
XLA Modules:
  0.0 66.4 jit_solution(7422692361591605545)
XLA Ops:
  0.0 0.0 copy-start
  0.0 0.0 copy-start.2
  0.0 0.0 copy-start.5
  0.0 3.3 %edge.1 = (f32[256,128]{1,0:T(8,128)}, f32[256,128]{1,0:T(8,128)}) custom-call(bf16[512,512]{1,0:T(8,128)(2,1)} %bitcast.13, bf16[27,512,128]{2,1,0:T(8,128)(2,1)} %w_hbm.1), custom_call_target="tpu_custom_call" | custom-call | flops 600000000 | bytes 4500000 | tf_op jit(solution)/shard_map/edge/pallas_call | solution.py:410
  3.3 0.0 copy-start.1
  3.3 0.0 copy-start.3
  3.3 0.6 collective-permute-start
  3.9 0.8 %collective-permute-start.1 = (f32[256,128]{1,0:T(8,128)}, f32[256,128]{1,0:T(8,128)S(1)}, u32[]{:S(2)}, u32[]{:S(2)}) collective-permute-start(f32[256,128]{1,0:T(8,128)} %get-tuple-element.14), channel_id=1, source_target_pairs={{1,2},{2,1},{5,6},{6,5},{9,10},{10,9},{13,14},{14,13},{17,18},{18,... | collective-permute-start | bytes 393224 | tf_op jit(solution)/shard_map/ppermute | solution.py:425
  5.3 0.0 copy-done
  5.3 0.0 copy-done.2
  5.3 0.0 copy-done.5
  5.3 1.6 %own.1 = (f32[512,128]{1,0:T(8,128)S(1)}, bf16[192,128]{1,0:T(8,128)(2,1)S(1)}) custom-call(s32[1]{0:T(128)S(6)} %copy.8.count_ref, bf16[512,512]{1,0:T(8,128)(2,1)S(1)} %bitcast.14, bf16[27,512,128]{2,1,0:T(8,128)(2,1)S(1)} %copy-done, s32[4,128]{1,0:T(4,128)S(1)} %bitcast.16), custom_call_target="tpu_custom_call" | custom-call | flops 1200000000 | bytes 4500000 | tf_op jit(solution)/shard_map/own/pallas_call | solution.py:430
  6.9 0.0 collective-permute-done.near_ref
  6.9 0.0 collective-permute-done.1.far_ref
  6.9 0.0 copy-done.1
  6.9 0.0 copy-done.3
  6.9 0.7 %join.1 = bf16[192,640]{1,0:T(8,128)(2,1)S(1)} custom-call(s32[1]{0:T(128)S(6)} %copy.8.count_ref, s32[4,128]{1,0:T(4,128)S(1)} %bitcast.15, f32[512,128]{1,0:T(8,128)S(1)} %get-tuple-element.12.acc_ref, f32[256,128]{1,0:T(8,128)S(1)} %collective-permute-done.near_ref, f32[256,128]{1,0:T(8,128)S(1)} %collective-permute-done.1.far_ref, ...), custom_call_target="tpu_custom_call" | custom-call | flops 300000000 | bytes 3000000 | tf_op jit(solution)/shard_map/join/pallas_call | solution.py:442
  7.7 14.7 %all_to_all.10 = bf16[8,24,640]{2,1,0:T(8,128)(2,1)S(1)} all-to-all(bf16[8,24,640]{2,1,0:T(8,128)(2,1)S(1)} %bitcast.12), channel_id=1, replica_groups=mesh['bag'=8,'head'=4] {'bag'}, dimensions={0} | all-to-all | bytes 491520 | tf_op jit(solution)/shard_map/all_to_all | solution.py:453
  22.4 5.1 %collective-permute-start.3 = (bf16[192,640]{1,0:T(8,128)(2,1)S(1)}, bf16[192,640]{1,0:T(8,128)(2,1)S(1)}, u32[]{:S(2)}, u32[]{:S(2)}) collective-permute-start(bf16[192,640]{1,0:T(8,128)(2,1)S(1)} %bitcast.7), channel_id=1, source_target_pairs={{0,2},{1,3},{2,0},{3,1},{4,6},{5,7},{6,4},{7,5},{8,10},{9,11},{10,... | collective-permute-start | bytes 737288 | tf_op jit(solution)/shard_map/ppermute | solution.py:460
  27.5 0.0 collective-permute-start.2
  27.5 0.0 copy-start.4
  27.5 2.8 %copy-done.4 = bf16[3,2048,512]{2,1,0:T(8,128)(2,1)S(1)} copy-done((bf16[3,2048,512]{2,1,0:T(8,128)(2,1)S(1)}, bf16[3,2048,512]{2,1,0:T(8,128)(2,1)}, u32[]{:S(2)}) %copy-start.4) | copy-done | bytes 6291480
  30.2 3.4 %fold.1.refs_2_.refs_1_.refs_6_ = bf16[3,1024,512]{2,1,0:T(8,128)(2,1)S(1)} custom-call(bf16[512,2048]{1,0:T(8,128)(2,1)S(1)} %copy-done.1, bf16[3,2048,512]{2,1,0:T(8,128)(2,1)S(1)} %copy-done.4, bf16[192,640]{1,0:T(8,128)(2,1)S(1)} %bitcast.9), custom_call_target="tpu_custom_call" | custom-call | flops 3300000000 | bytes 14000000 | tf_op jit(solution)/shard_map/fold/pallas_call | solution.py:461
  33.7 0.0 collective-permute-done.2.refs_1_
  33.7 1.4 %near_qkv.1.refs_4_ = f32[3,384,512]{2,1,0:T(8,128)S(1)} custom-call(bf16[192,640]{1,0:T(8,128)(2,1)S(1)} %bitcast.10, bf16[192,640]{1,0:T(8,128)(2,1)S(1)} %collective-permute-done.2.refs_1_, bf16[3,1024,512]{2,1,0:T(8,128)(2,1)S(1)} %fold.1.refs_2_.refs_1_.refs_6_), custom_call_target="tpu_custom_call" | custom-call | flops 1200000000 | bytes 6000000 | tf_op jit(solution)/shard_map/near_qkv/pallas_call | solution.py:481
  35.1 0.0 collective-permute-done.3.refs_0_.refs_2_
  35.1 0.6 collective-permute-start.4
  35.7 0.8 %across_qkv.1.refs_5_ = f32[3,192,512]{2,1,0:T(8,128)S(1)} custom-call(bf16[192,640]{1,0:T(8,128)(2,1)S(1)} %collective-permute-done.3.refs_0_.refs_2_, bf16[3,1024,512]{2,1,0:T(8,128)(2,1)S(1)} %fold.1.refs_2_.refs_1_.refs_6_), custom_call_target="tpu_custom_call" | custom-call | flops 600000000 | bytes 3000000 | tf_op jit(solution)/shard_map/across_qkv/pallas_call | solution.py:481
  36.5 0.4 collective-permute-done.4.refs_3_
  36.8 4.9 %bag.1 = bf16[32,24,512]{2,1,0:T(8,128)(2,1)S(1)} custom-call(bf16[192,640]{1,0:T(8,128)(2,1)S(1)} %bitcast.11, bf16[192,640]{1,0:T(8,128)(2,1)S(1)} %collective-permute-done.2.refs_1_, bf16[192,640]{1,0:T(8,128)(2,1)S(1)} %collective-permute-done.3.refs_0_.refs_2_, bf16[192,640]{1,0:T(8,128)(2,1)S(1)} %collective-permute-done.4.refs_3_, ...), custom_call_target="tpu_custom_call" | custom-call | flops 3000000000 | bytes 5000000 | tf_op jit(solution)/shard_map/bag/pallas_call | solution.py:503
  41.7 23.6 %all_to_all.11 = bf16[32,24,512]{2,1,0:T(8,128)(2,1)S(1)} all-to-all(bf16[32,24,512]{2,1,0:T(8,128)(2,1)S(1)} %bag.1), channel_id=1, replica_groups=mesh['bag'=8,'head'=4] {'head','bag'}, dimensions={0} | all-to-all | bytes 1572864 | tf_op jit(solution)/shard_map/all_to_all | solution.py:519
  65.3 1.2 %collect.1 = bf16[128,2048]{1,0:T(8,128)(2,1)} custom-call(s32[1]{0:T(128)S(6)} %copy.8.count_ref, bf16[192,128]{1,0:T(8,128)(2,1)S(1)} %get-tuple-element.11.onehot_ref, bf16[768,512]{1,0:T(8,128)(2,1)S(1)} %bitcast.6), custom_call_target="tpu_custom_call" | custom-call | tf_op jit(solution)/shard_map/collect/pallas_call | solution.py:520
Async XLA Ops:
  0.0 5.3 %copy-start = (bf16[27,512,128]{2,1,0:T(8,128)(2,1)S(1)}, bf16[27,512,128]{2,1,0:T(8,128)(2,1)}, u32[]{:S(2)}) copy-start(bf16[27,512,128]{2,1,0:T(8,128)(2,1)} %w_hbm.1) | copy-start | bytes 10616836
  0.0 5.3 %copy-start.2 = (bf16[1,2,16,16,512]{4,3,2,1,0:T(8,128)(2,1)S(1)}, bf16[1,2,16,16,512]{4,3,2,1,0:T(8,128)(2,1)}, u32[]{:S(2)}) copy-start(bf16[1,2,16,16,512]{4,3,2,1,0:T(8,128)(2,1)} %param.7) | copy-start | bytes 1572868
  0.0 5.3 %copy-start.5 = (s32[512,1]{0,1:T(1,128)S(1)}, s32[512,1]{0,1:T(1,128)}, u32[]{:S(2)}) copy-start(s32[512,1]{0,1:T(1,128)} %param.9) | copy-start | bytes 6148
  3.3 3.7 %copy-start.1 = (bf16[512,2048]{1,0:T(8,128)(2,1)S(1)}, bf16[512,2048]{1,0:T(8,128)(2,1)}, u32[]{:S(2)}) copy-start(bf16[512,2048]{1,0:T(8,128)(2,1)} %e_ref.3) | copy-start | bytes 6291460
  3.3 3.7 %copy-start.3 = (s32[512]{0:T(512)S(1)}, s32[512]{0:T(512)}, u32[]{:S(2)}) copy-start(s32[512]{0:T(512)} %param.10) | copy-start | bytes 6148
  3.3 3.6 %collective-permute-start = (f32[256,128]{1,0:T(8,128)}, f32[256,128]{1,0:T(8,128)S(1)}, u32[]{:S(2)}, u32[]{:S(2)}) collective-permute-start(f32[256,128]{1,0:T(8,128)} %get-tuple-element.13), channel_id=1, source_target_pairs={{0,1},{1,0},{2,3},{3,2},{4,5},{5,4},{6,7},{7,6},{8,9},{9,8},{10,11... | collective-permute-start | bytes 393224 | tf_op jit(solution)/shard_map/ppermute | solution.py:426
  3.9 3.1 %collective-permute-start.1 = (f32[256,128]{1,0:T(8,128)}, f32[256,128]{1,0:T(8,128)S(1)}, u32[]{:S(2)}, u32[]{:S(2)}) collective-permute-start(f32[256,128]{1,0:T(8,128)} %get-tuple-element.14), channel_id=1, source_target_pairs={{1,2},{2,1},{5,6},{6,5},{9,10},{10,9},{13,14},{14,13},{17,18},{18,... | collective-permute-start | bytes 393224 | tf_op jit(solution)/shard_map/ppermute | solution.py:425
  22.4 12.7 %collective-permute-start.3 = (bf16[192,640]{1,0:T(8,128)(2,1)S(1)}, bf16[192,640]{1,0:T(8,128)(2,1)S(1)}, u32[]{:S(2)}, u32[]{:S(2)}) collective-permute-start(bf16[192,640]{1,0:T(8,128)(2,1)S(1)} %bitcast.7), channel_id=1, source_target_pairs={{0,2},{1,3},{2,0},{3,1},{4,6},{5,7},{6,4},{7,5},{8,10},{9,11},{10,... | collective-permute-start | bytes 737288 | tf_op jit(solution)/shard_map/ppermute | solution.py:460
  27.5 6.2 %collective-permute-start.2 = (bf16[192,640]{1,0:T(8,128)(2,1)S(1)}, bf16[192,640]{1,0:T(8,128)(2,1)S(1)}, u32[]{:S(2)}, u32[]{:S(2)}) collective-permute-start(bf16[192,640]{1,0:T(8,128)(2,1)S(1)} %bitcast.8), channel_id=1, source_target_pairs={{0,1},{1,0},{2,3},{3,2},{4,5},{5,4},{6,7},{7,6},{8,9},{9,8},{10,11... | collective-permute-start | bytes 737288 | tf_op jit(solution)/shard_map/ppermute | solution.py:474
  27.5 2.8 %copy-start.4 = (bf16[3,2048,512]{2,1,0:T(8,128)(2,1)S(1)}, bf16[3,2048,512]{2,1,0:T(8,128)(2,1)}, u32[]{:S(2)}) copy-start(bf16[3,2048,512]{2,1,0:T(8,128)(2,1)} %w_ref.3) | copy-start | bytes 18874372
  35.1 1.7 %collective-permute-start.4 = (bf16[192,640]{1,0:T(8,128)(2,1)S(1)}, bf16[192,640]{1,0:T(8,128)(2,1)S(1)}, u32[]{:S(2)}, u32[]{:S(2)}) collective-permute-start(bf16[192,640]{1,0:T(8,128)(2,1)S(1)} %collective-permute-done.3.refs_0_.refs_2_), channel_id=1, source_target_pairs={{0,1},{1,0},{2,3},{3,2},{4,5},{5,4},{6,7},{7,6},{8,9},{9,8},{10,11... | collective-permute-start | bytes 737288 | tf_op jit(solution)/shard_map/ppermute | solution.py:474

commit v13 on v12

--- a/solution.py
+++ b/solution.py
@@ -323,14 +323,21 @@
             )
 
         def mix(pair, shifted, a, b):
-            cols = slice(pair * LANES, (pair + 1) * LANES)
-            values = jnp.concatenate([two(qkv_ref, a, b, 2, cols), ones], axis=1)
-            return jnp.dot(shifted.astype(jnp.bfloat16), values, preferred_element_type=jnp.float32)
+            values = two(qkv_ref, a, b, 2, slice(pair * LANES, (pair + 1) * LANES))
+            weights = shifted.astype(jnp.bfloat16)
+            sides = (jnp.where(low, values, ones), jnp.where(low, ones, values))
+            return jnp.concatenate(
+                [
+                    jnp.dot(weights[i * tile : (i + 1) * tile], side, preferred_element_type=jnp.float32)
+                    for i, side in enumerate(sides)
+                ],
+                axis=0,
+            )
 
         def store(pair, a, b, result):
             cols = slice(pair * LANES, (pair + 1) * LANES)
-            shares = result[:, :LANES] / result[:, LANES:]
-            mixed = jnp.where(low, shares[:tile], shares[tile:])
+            sums = pltpu.roll(jnp.where(low, result[tile:], result[:tile]), HDIM, axis=1)
+            mixed = jnp.where(low, result[:tile], result[tile:]) / sums
             for at, clip in ((clip_rows, b), (0, a)):
                 for j, mask in enumerate(masks):
                     piece = mixed[at + j * cap : at + (j + 1) * cap]
@@ -352,7 +359,7 @@
             def _():
                 for pair in range(pairs):
                     m_ref[pair] = jnp.full((2 * tile, LANES), far_below, jnp.float32)
-                    r_ref[pair] = jnp.zeros((2 * tile, 2 * LANES), jnp.float32)
+                    r_ref[pair] = jnp.zeros((2 * tile, LANES), jnp.float32)
 
                 def key_tile(j, inner):
                     ka, kb, second = members(j)
@@ -509,7 +516,7 @@
             pltpu.VMEM((3, count_slots, local_width), jnp.bfloat16),
             pltpu.VMEM((count_slots, LANES), jnp.bfloat16),
             pltpu.VMEM((local_width // LANES, 2 * pair_rows, LANES), jnp.float32),
-            pltpu.VMEM((local_width // LANES, 2 * pair_rows, 2 * LANES), jnp.float32),
+            pltpu.VMEM((local_width // LANES, 2 * pair_rows, LANES), jnp.float32),
             pltpu.SMEM((2 * bags,), jnp.int32),
         ],
         compiler_params=limit(28),

time: 66.7 us -> 66.9 us (level)
  no operation moved by 1% of the time
where the time goes in v13:
time: 66.9 us; the launch traced here: 66.7 us
  blocking collectives  38.3 us (57%)
  Pallas kernels  17.4 us (26%)
  starting transfers between devices  6.98 us (10%)
  local copies, waits for them, and re-layouts  2.81 us (4%)
  between operations  0.8 us (1%)
    all_to_all x1, blocking collectives, shards(): lax.all_to_all(attended, ('head', 'bag'), split_axis=0, concat_axis=0, ti...  23.6 us
    all_to_all x1, blocking collectives, shards(): lax.all_to_all(outgoing.reshape(bags, cap, row_width), 'bag', split_axis=...  14.7 us
    pallas_call x1, Pallas kernels, shards(): pl.pallas_call(functools.partial(bag_kernel, bags, cap, masks, groups), o...  5.13 us
    ppermute x1, starting transfers between devices, shards(): across = lax.ppermute(arrived, 'head', swap)  5.06 us
    pallas_call x1, Pallas kernels, shards(): pl.pallas_call(fold_kernel, out_shape=jax.ShapeDtypeStruct((3, 2 * embed_...  3.43 us
    pallas_call x1, Pallas kernels, shards(): pl.pallas_call(functools.partial(edge_kernel, rows, cols, frames_dev), ou...  3.26 us
    unnamed x12, local copies, waits for them, and re-layouts  2.81 us
    pallas_call x2, Pallas kernels, project(): pl.pallas_call(qkv_kernel, out_shape=jax.ShapeDtypeStruct((3, len(group)...  2.16 us
  transfers between devices with their start and end apart: 5, of which 1 were waited for; matrix products, arithmetic and copies ran while one was open for 0% of the time, Pallas kernels for 11%

profile of v13, /device:TPU:0, one launch (start us, length us, event | category | flops | bytes accessed | tf_op | source)
XLA Modules:
  0.0 66.7 jit_solution(14708609395913935041)
XLA Ops:
  0.0 0.0 copy-start
  0.0 0.0 copy-start.2
  0.0 0.0 copy-start.5
  0.0 3.3 %edge.1 = (f32[256,128]{1,0:T(8,128)}, f32[256,128]{1,0:T(8,128)}) custom-call(bf16[512,512]{1,0:T(8,128)(2,1)} %bitcast.13, bf16[27,512,128]{2,1,0:T(8,128)(2,1)} %w_hbm.1), custom_call_target="tpu_custom_call" | custom-call | flops 600000000 | bytes 4500000 | tf_op jit(solution)/shard_map/edge/pallas_call | solution.py:417
  3.3 0.0 copy-start.1
  3.3 0.0 copy-start.3
  3.3 0.6 collective-permute-start
  3.9 0.8 %collective-permute-start.1 = (f32[256,128]{1,0:T(8,128)}, f32[256,128]{1,0:T(8,128)S(1)}, u32[]{:S(2)}, u32[]{:S(2)}) collective-permute-start(f32[256,128]{1,0:T(8,128)} %get-tuple-element.14), channel_id=1, source_target_pairs={{1,2},{2,1},{5,6},{6,5},{9,10},{10,9},{13,14},{14,13},{17,18},{18,... | collective-permute-start | bytes 393224 | tf_op jit(solution)/shard_map/ppermute | solution.py:432
  5.3 0.0 copy-done
  5.3 0.0 copy-done.2
  5.3 0.0 copy-done.5
  5.3 1.6 %own.1 = (f32[512,128]{1,0:T(8,128)S(1)}, bf16[192,128]{1,0:T(8,128)(2,1)S(1)}) custom-call(s32[1]{0:T(128)S(6)} %copy.8.count_ref, bf16[512,512]{1,0:T(8,128)(2,1)S(1)} %bitcast.14, bf16[27,512,128]{2,1,0:T(8,128)(2,1)S(1)} %copy-done, s32[4,128]{1,0:T(4,128)S(1)} %bitcast.16), custom_call_target="tpu_custom_call" | custom-call | flops 1200000000 | bytes 4500000 | tf_op jit(solution)/shard_map/own/pallas_call | solution.py:437
  6.9 0.0 collective-permute-done.near_ref
  6.9 0.0 collective-permute-done.1.far_ref
  6.9 0.0 copy-done.1
  6.9 0.0 copy-done.3
  6.9 0.7 %join.1 = bf16[192,640]{1,0:T(8,128)(2,1)S(1)} custom-call(s32[1]{0:T(128)S(6)} %copy.8.count_ref, s32[4,128]{1,0:T(4,128)S(1)} %bitcast.15, f32[512,128]{1,0:T(8,128)S(1)} %get-tuple-element.12.acc_ref, f32[256,128]{1,0:T(8,128)S(1)} %collective-permute-done.near_ref, f32[256,128]{1,0:T(8,128)S(1)} %collective-permute-done.1.far_ref, ...), custom_call_target="tpu_custom_call" | custom-call | flops 300000000 | bytes 3000000 | tf_op jit(solution)/shard_map/join/pallas_call | solution.py:449
  7.7 14.7 %all_to_all.10 = bf16[8,24,640]{2,1,0:T(8,128)(2,1)S(1)} all-to-all(bf16[8,24,640]{2,1,0:T(8,128)(2,1)S(1)} %bitcast.12), channel_id=1, replica_groups=mesh['bag'=8,'head'=4] {'bag'}, dimensions={0} | all-to-all | bytes 491520 | tf_op jit(solution)/shard_map/all_to_all | solution.py:460
  22.4 5.1 %collective-permute-start.3 = (bf16[192,640]{1,0:T(8,128)(2,1)S(1)}, bf16[192,640]{1,0:T(8,128)(2,1)S(1)}, u32[]{:S(2)}, u32[]{:S(2)}) collective-permute-start(bf16[192,640]{1,0:T(8,128)(2,1)S(1)} %bitcast.7), channel_id=1, source_target_pairs={{0,2},{1,3},{2,0},{3,1},{4,6},{5,7},{6,4},{7,5},{8,10},{9,11},{10,... | collective-permute-start | bytes 737288 | tf_op jit(solution)/shard_map/ppermute | solution.py:467
  27.5 0.0 collective-permute-start.2
  27.5 0.0 copy-start.4
  27.5 2.8 %copy-done.4 = bf16[3,2048,512]{2,1,0:T(8,128)(2,1)S(1)} copy-done((bf16[3,2048,512]{2,1,0:T(8,128)(2,1)S(1)}, bf16[3,2048,512]{2,1,0:T(8,128)(2,1)}, u32[]{:S(2)}) %copy-start.4) | copy-done | bytes 6291480
  30.2 3.4 %fold.1.refs_2_.refs_1_.refs_6_ = bf16[3,1024,512]{2,1,0:T(8,128)(2,1)S(1)} custom-call(bf16[512,2048]{1,0:T(8,128)(2,1)S(1)} %copy-done.1, bf16[3,2048,512]{2,1,0:T(8,128)(2,1)S(1)} %copy-done.4, bf16[192,640]{1,0:T(8,128)(2,1)S(1)} %bitcast.9), custom_call_target="tpu_custom_call" | custom-call | flops 3300000000 | bytes 14000000 | tf_op jit(solution)/shard_map/fold/pallas_call | solution.py:468
  33.7 0.0 collective-permute-done.2.refs_1_
  33.7 1.4 %near_qkv.1.refs_4_ = f32[3,384,512]{2,1,0:T(8,128)S(1)} custom-call(bf16[192,640]{1,0:T(8,128)(2,1)S(1)} %bitcast.10, bf16[192,640]{1,0:T(8,128)(2,1)S(1)} %collective-permute-done.2.refs_1_, bf16[3,1024,512]{2,1,0:T(8,128)(2,1)S(1)} %fold.1.refs_2_.refs_1_.refs_6_), custom_call_target="tpu_custom_call" | custom-call | flops 1200000000 | bytes 6000000 | tf_op jit(solution)/shard_map/near_qkv/pallas_call | solution.py:488
  35.1 0.0 collective-permute-done.3.refs_0_.refs_2_
  35.1 0.6 collective-permute-start.4
  35.7 0.8 %across_qkv.1.refs_5_ = f32[3,192,512]{2,1,0:T(8,128)S(1)} custom-call(bf16[192,640]{1,0:T(8,128)(2,1)S(1)} %collective-permute-done.3.refs_0_.refs_2_, bf16[3,1024,512]{2,1,0:T(8,128)(2,1)S(1)} %fold.1.refs_2_.refs_1_.refs_6_), custom_call_target="tpu_custom_call" | custom-call | flops 600000000 | bytes 3000000 | tf_op jit(solution)/shard_map/across_qkv/pallas_call | solution.py:488
  36.5 0.4 collective-permute-done.4.refs_3_
  36.8 5.1 %bag.1 = bf16[32,24,512]{2,1,0:T(8,128)(2,1)S(1)} custom-call(bf16[192,640]{1,0:T(8,128)(2,1)S(1)} %bitcast.11, bf16[192,640]{1,0:T(8,128)(2,1)S(1)} %collective-permute-done.2.refs_1_, bf16[192,640]{1,0:T(8,128)(2,1)S(1)} %collective-permute-done.3.refs_0_.refs_2_, bf16[192,640]{1,0:T(8,128)(2,1)S(1)} %collective-permute-done.4.refs_3_, ...), custom_call_target="tpu_custom_call" | custom-call | flops 3000000000 | bytes 5000000 | tf_op jit(solution)/shard_map/bag/pallas_call | solution.py:510
  41.9 23.6 %all_to_all.11 = bf16[32,24,512]{2,1,0:T(8,128)(2,1)S(1)} all-to-all(bf16[32,24,512]{2,1,0:T(8,128)(2,1)S(1)} %bag.1), channel_id=1, replica_groups=mesh['bag'=8,'head'=4] {'head','bag'}, dimensions={0} | all-to-all | bytes 1572864 | tf_op jit(solution)/shard_map/all_to_all | solution.py:526
  65.5 1.2 %collect.1 = bf16[128,2048]{1,0:T(8,128)(2,1)} custom-call(s32[1]{0:T(128)S(6)} %copy.8.count_ref, bf16[192,128]{1,0:T(8,128)(2,1)S(1)} %get-tuple-element.11.onehot_ref, bf16[768,512]{1,0:T(8,128)(2,1)S(1)} %bitcast.6), custom_call_target="tpu_custom_call" | custom-call | tf_op jit(solution)/shard_map/collect/pallas_call | solution.py:527
Async XLA Ops:
  0.0 5.3 %copy-start = (bf16[27,512,128]{2,1,0:T(8,128)(2,1)S(1)}, bf16[27,512,128]{2,1,0:T(8,128)(2,1)}, u32[]{:S(2)}) copy-start(bf16[27,512,128]{2,1,0:T(8,128)(2,1)} %w_hbm.1) | copy-start | bytes 10616836
  0.0 5.3 %copy-start.2 = (bf16[1,2,16,16,512]{4,3,2,1,0:T(8,128)(2,1)S(1)}, bf16[1,2,16,16,512]{4,3,2,1,0:T(8,128)(2,1)}, u32[]{:S(2)}) copy-start(bf16[1,2,16,16,512]{4,3,2,1,0:T(8,128)(2,1)} %param.7) | copy-start | bytes 1572868
  0.0 5.3 %copy-start.5 = (s32[512,1]{0,1:T(1,128)S(1)}, s32[512,1]{0,1:T(1,128)}, u32[]{:S(2)}) copy-start(s32[512,1]{0,1:T(1,128)} %param.9) | copy-start | bytes 6148
  3.3 3.7 %copy-start.1 = (bf16[512,2048]{1,0:T(8,128)(2,1)S(1)}, bf16[512,2048]{1,0:T(8,128)(2,1)}, u32[]{:S(2)}) copy-start(bf16[512,2048]{1,0:T(8,128)(2,1)} %e_ref.3) | copy-start | bytes 6291460
  3.3 3.7 %copy-start.3 = (s32[512]{0:T(512)S(1)}, s32[512]{0:T(512)}, u32[]{:S(2)}) copy-start(s32[512]{0:T(512)} %param.10) | copy-start | bytes 6148
  3.3 3.6 %collective-permute-start = (f32[256,128]{1,0:T(8,128)}, f32[256,128]{1,0:T(8,128)S(1)}, u32[]{:S(2)}, u32[]{:S(2)}) collective-permute-start(f32[256,128]{1,0:T(8,128)} %get-tuple-element.13), channel_id=1, source_target_pairs={{0,1},{1,0},{2,3},{3,2},{4,5},{5,4},{6,7},{7,6},{8,9},{9,8},{10,11... | collective-permute-start | bytes 393224 | tf_op jit(solution)/shard_map/ppermute | solution.py:433
  3.9 3.1 %collective-permute-start.1 = (f32[256,128]{1,0:T(8,128)}, f32[256,128]{1,0:T(8,128)S(1)}, u32[]{:S(2)}, u32[]{:S(2)}) collective-permute-start(f32[256,128]{1,0:T(8,128)} %get-tuple-element.14), channel_id=1, source_target_pairs={{1,2},{2,1},{5,6},{6,5},{9,10},{10,9},{13,14},{14,13},{17,18},{18,... | collective-permute-start | bytes 393224 | tf_op jit(solution)/shard_map/ppermute | solution.py:432
  22.4 12.7 %collective-permute-start.3 = (bf16[192,640]{1,0:T(8,128)(2,1)S(1)}, bf16[192,640]{1,0:T(8,128)(2,1)S(1)}, u32[]{:S(2)}, u32[]{:S(2)}) collective-permute-start(bf16[192,640]{1,0:T(8,128)(2,1)S(1)} %bitcast.7), channel_id=1, source_target_pairs={{0,2},{1,3},{2,0},{3,1},{4,6},{5,7},{6,4},{7,5},{8,10},{9,11},{10,... | collective-permute-start | bytes 737288 | tf_op jit(solution)/shard_map/ppermute | solution.py:467
  27.5 6.2 %collective-permute-start.2 = (bf16[192,640]{1,0:T(8,128)(2,1)S(1)}, bf16[192,640]{1,0:T(8,128)(2,1)S(1)}, u32[]{:S(2)}, u32[]{:S(2)}) collective-permute-start(bf16[192,640]{1,0:T(8,128)(2,1)S(1)} %bitcast.8), channel_id=1, source_target_pairs={{0,1},{1,0},{2,3},{3,2},{4,5},{5,4},{6,7},{7,6},{8,9},{9,8},{10,11... | collective-permute-start | bytes 737288 | tf_op jit(solution)/shard_map/ppermute | solution.py:481
  27.5 2.8 %copy-start.4 = (bf16[3,2048,512]{2,1,0:T(8,128)(2,1)S(1)}, bf16[3,2048,512]{2,1,0:T(8,128)(2,1)}, u32[]{:S(2)}) copy-start(bf16[3,2048,512]{2,1,0:T(8,128)(2,1)} %w_ref.3) | copy-start | bytes 18874372
  35.1 1.7 %collective-permute-start.4 = (bf16[192,640]{1,0:T(8,128)(2,1)S(1)}, bf16[192,640]{1,0:T(8,128)(2,1)S(1)}, u32[]{:S(2)}, u32[]{:S(2)}) collective-permute-start(bf16[192,640]{1,0:T(8,128)(2,1)S(1)} %collective-permute-done.3.refs_0_.refs_2_), channel_id=1, source_target_pairs={{0,1},{1,0},{2,3},{3,2},{4,5},{5,4},{6,7},{7,6},{8,9},{9,8},{10,11... | collective-permute-start | bytes 737288 | tf_op jit(solution)/shard_map/ppermute | solution.py:481

commit v14 on v12

--- a/solution.py
+++ b/solution.py
@@ -269,7 +269,13 @@
         for c in range(clips):
             qkv_ref[m, c * clip_rows : (c + 1) * clip_rows, cols] = by_clip(parts, c).astype(jnp.bfloat16)
 
-    out_ref[...] = jnp.zeros_like(out_ref)
+    for c in range(clips):
+
+        @pl.when(order_ref[clips + c] == 0)
+        def _():
+            for j in range(count):
+                out_ref[j * clips + c] = jnp.zeros(out_ref.shape[1:], out_ref.dtype)
+
     tile = 2 * clip_rows
     lane = lax.broadcasted_iota(jnp.int32, (tile, LANES), 1)
     low = lane < HDIM
@@ -436,7 +442,7 @@
         in_specs=[VMEM, VMEM, VMEM, VMEM],
         out_specs=(VMEM, VMEM),
         compiler_params=limit(16),
-        cost_estimate=pl.CostEstimate(flops=1200000000, bytes_accessed=4500000, transcendentals=0),
+        cost_estimate=pl.CostEstimate(flops=4000000000, bytes_accessed=4500000, transcendentals=0),
         name="own",
     )(count, tile, conv_weight, route_rows)
     outgoing = pl.pallas_call(

time: 66.7 us -> 64.3 us (0.964)
  local copies, waits for them, and re-layouts: 2.81 us -> 0.15 us
  waiting for transfers between devices: 0.37 us -> 1.25 us
  starting transfers between devices: 6.98 us -> 6.16 us
    unnamed x12 -> x14, local copies, waits for them, and re-layouts: 2.81 us -> 0.15 us
  transfers between devices with their start and end apart: 5 -> 5, of which waited for: 1 -> 2; matrix products, arithmetic and copies ran while one was open for 0% -> 0% of each run, Pallas kernels for 11% -> 11%
where the time goes in v14:
time: 64.3 us; the launch traced here: 64.1 us
  blocking collectives  38.5 us (60%)
  Pallas kernels  17.2 us (27%)
  starting transfers between devices  6.16 us (10%)
  waiting for transfers between devices  1.25 us (2%)
  between operations  0.81 us (1%)
    all_to_all x1, blocking collectives, shards(): lax.all_to_all(attended, ('head', 'bag'), split_axis=0, concat_axis=0, ti...  23.8 us
    all_to_all x1, blocking collectives, shards(): lax.all_to_all(outgoing.reshape(bags, cap, row_width), 'bag', split_axis=...  14.7 us
    pallas_call x1, Pallas kernels, shards(): pl.pallas_call(functools.partial(bag_kernel, bags, cap, masks, groups), o...  4.94 us
    ppermute x1, starting transfers between devices, shards(): across = lax.ppermute(arrived, 'head', swap)  4.91 us
    pallas_call x1, Pallas kernels, shards(): pl.pallas_call(fold_kernel, out_shape=jax.ShapeDtypeStruct((3, 2 * embed_...  3.43 us
    pallas_call x1, Pallas kernels, shards(): pl.pallas_call(functools.partial(edge_kernel, rows, cols, frames_dev), ou...  3.27 us
    pallas_call x2, Pallas kernels, project(): pl.pallas_call(qkv_kernel, out_shape=jax.ShapeDtypeStruct((3, len(group)...  2.16 us
    pallas_call x1, Pallas kernels, shards(): pl.pallas_call(functools.partial(own_kernel, bags, cap, rows, cols, frame...  1.56 us
  transfers between devices with their start and end apart: 5, of which 2 were waited for; matrix products, arithmetic and copies ran while one was open for 0% of the time, Pallas kernels for 11%

profile of v14, /device:TPU:0, one launch (start us, length us, event | category | flops | bytes accessed | tf_op | source)
XLA Modules:
  0.0 64.1 jit_solution(16821539786271531949)
XLA Ops:
  0.0 0.0 copy-start
  0.0 0.0 copy-start.2
  0.0 0.0 copy-start.4
  0.0 3.3 %edge.1 = (f32[256,128]{1,0:T(8,128)}, f32[256,128]{1,0:T(8,128)}) custom-call(bf16[512,512]{1,0:T(8,128)(2,1)} %bitcast.13, bf16[27,512,128]{2,1,0:T(8,128)(2,1)} %w_hbm.1), custom_call_target="tpu_custom_call" | custom-call | flops 600000000 | bytes 4500000 | tf_op jit(solution)/shard_map/edge/pallas_call | solution.py:416
  3.3 0.6 collective-permute-start
  3.8 0.7 %collective-permute-start.1 = (f32[256,128]{1,0:T(8,128)}, f32[256,128]{1,0:T(8,128)S(1)}, u32[]{:S(2)}, u32[]{:S(2)}) collective-permute-start(f32[256,128]{1,0:T(8,128)} %get-tuple-element.14), channel_id=1, source_target_pairs={{1,2},{2,1},{5,6},{6,5},{9,10},{10,9},{13,14},{14,13},{17,18},{18,... | collective-permute-start | bytes 393224 | tf_op jit(solution)/shard_map/ppermute | solution.py:431
  5.2 0.0 slice-start
  5.2 0.0 copy-done
  5.2 0.0 copy-done.2
  5.2 0.0 copy-done.4
  5.2 0.0 copy-start.1
  5.2 0.0 copy-start.3
  5.2 0.0 slice-start.1
  5.2 1.6 %own.1 = (f32[512,128]{1,0:T(8,128)S(1)}, bf16[192,128]{1,0:T(8,128)(2,1)S(1)}) custom-call(s32[1]{0:T(128)S(6)} %copy.8.count_ref, bf16[512,512]{1,0:T(8,128)(2,1)S(1)} %bitcast.14, bf16[27,512,128]{2,1,0:T(8,128)(2,1)S(1)} %copy-done, s32[4,128]{1,0:T(4,128)S(1)} %bitcast.18), custom_call_target="tpu_custom_call" | custom-call | flops 4000000000 | bytes 4500000 | tf_op jit(solution)/shard_map/own/pallas_call | solution.py:436
  6.8 0.0 collective-permute-done.near_ref
  6.8 0.0 collective-permute-done.1.far_ref
  6.8 0.1 copy-done.1
  6.9 0.0 copy-done.3
  6.9 0.7 %join.1 = bf16[192,640]{1,0:T(8,128)(2,1)S(1)} custom-call(s32[1]{0:T(128)S(6)} %copy.8.count_ref, s32[4,128]{1,0:T(4,128)S(1)} %bitcast.15, f32[512,128]{1,0:T(8,128)S(1)} %get-tuple-element.12.acc_ref, f32[256,128]{1,0:T(8,128)S(1)} %collective-permute-done.near_ref, f32[256,128]{1,0:T(8,128)S(1)} %collective-permute-done.1.far_ref, ...), custom_call_target="tpu_custom_call" | custom-call | flops 300000000 | bytes 3000000 | tf_op jit(solution)/shard_map/join/pallas_call | solution.py:448
  7.7 14.7 %all_to_all.10 = bf16[8,24,640]{2,1,0:T(8,128)(2,1)S(1)} all-to-all(bf16[8,24,640]{2,1,0:T(8,128)(2,1)S(1)} %bitcast.12), channel_id=1, replica_groups=mesh['bag'=8,'head'=4] {'bag'}, dimensions={0} | all-to-all | bytes 491520 | tf_op jit(solution)/shard_map/all_to_all | solution.py:459
  22.4 4.9 %collective-permute-start.3 = (bf16[192,640]{1,0:T(8,128)(2,1)S(1)}, bf16[192,640]{1,0:T(8,128)(2,1)S(1)}, u32[]{:S(2)}, u32[]{:S(2)}) collective-permute-start(bf16[192,640]{1,0:T(8,128)(2,1)S(1)} %bitcast.7), channel_id=1, source_target_pairs={{0,2},{1,3},{2,0},{3,1},{4,6},{5,7},{6,4},{7,5},{8,10},{9,11},{10,... | collective-permute-start | bytes 737288 | tf_op jit(solution)/shard_map/ppermute | solution.py:466
  27.3 0.0 collective-permute-start.2
  27.3 0.0 slice-done
  27.3 0.0 slice-done.1
  27.3 3.4 %fold.1.refs_2_.refs_1_.refs_6_ = bf16[3,1024,512]{2,1,0:T(8,128)(2,1)S(1)} custom-call(bf16[512,2048]{1,0:T(8,128)(2,1)S(1)} %copy-done.1, bf16[3,2048,512]{2,1,0:T(8,128)(2,1)S(1)} %bitcast.17, bf16[192,640]{1,0:T(8,128)(2,1)S(1)} %bitcast.9), custom_call_target="tpu_custom_call" | custom-call | flops 3300000000 | bytes 14000000 | tf_op jit(solution)/shard_map/fold/pallas_call | solution.py:467
  30.8 0.0 collective-permute-done.2.refs_1_
  30.8 1.4 %near_qkv.1.refs_4_ = f32[3,384,512]{2,1,0:T(8,128)S(1)} custom-call(bf16[192,640]{1,0:T(8,128)(2,1)S(1)} %bitcast.10, bf16[192,640]{1,0:T(8,128)(2,1)S(1)} %collective-permute-done.2.refs_1_, bf16[3,1024,512]{2,1,0:T(8,128)(2,1)S(1)} %fold.1.refs_2_.refs_1_.refs_6_), custom_call_target="tpu_custom_call" | custom-call | flops 1200000000 | bytes 6000000 | tf_op jit(solution)/shard_map/near_qkv/pallas_call | solution.py:487
  32.2 0.5 collective-permute-done.3.refs_0_.refs_2_
  32.7 0.0 collective-permute-start.4
  32.7 0.8 %across_qkv.1.refs_5_ = f32[3,192,512]{2,1,0:T(8,128)S(1)} custom-call(bf16[192,640]{1,0:T(8,128)(2,1)S(1)} %collective-permute-done.3.refs_0_.refs_2_, bf16[3,1024,512]{2,1,0:T(8,128)(2,1)S(1)} %fold.1.refs_2_.refs_1_.refs_6_), custom_call_target="tpu_custom_call" | custom-call | flops 600000000 | bytes 3000000 | tf_op jit(solution)/shard_map/across_qkv/pallas_call | solution.py:487
  33.5 0.7 %collective-permute-done.4.refs_3_ = bf16[192,640]{1,0:T(8,128)(2,1)S(1)} collective-permute-done((bf16[192,640]{1,0:T(8,128)(2,1)S(1)}, bf16[192,640]{1,0:T(8,128)(2,1)S(1)}, u32[]{:S(2)}, u32[]{:S(2)}) %collective-permute-start.4) | collective-permute-done | bytes 245792 | tf_op jit(solution)/shard_map/ppermute | solution.py:480
  34.2 4.9 %bag.1 = bf16[32,24,512]{2,1,0:T(8,128)(2,1)S(1)} custom-call(bf16[192,640]{1,0:T(8,128)(2,1)S(1)} %bitcast.11, bf16[192,640]{1,0:T(8,128)(2,1)S(1)} %collective-permute-done.2.refs_1_, bf16[192,640]{1,0:T(8,128)(2,1)S(1)} %collective-permute-done.3.refs_0_.refs_2_, bf16[192,640]{1,0:T(8,128)(2,1)S(1)} %collective-permute-done.4.refs_3_, ...), custom_call_target="tpu_custom_call" | custom-call | flops 3000000000 | bytes 5000000 | tf_op jit(solution)/shard_map/bag/pallas_call | solution.py:509
  39.2 23.8 %all_to_all.11 = bf16[32,24,512]{2,1,0:T(8,128)(2,1)S(1)} all-to-all(bf16[32,24,512]{2,1,0:T(8,128)(2,1)S(1)} %bag.1), channel_id=1, replica_groups=mesh['bag'=8,'head'=4] {'head','bag'}, dimensions={0} | all-to-all | bytes 1572864 | tf_op jit(solution)/shard_map/all_to_all | solution.py:525
  63.0 1.2 %collect.1 = bf16[128,2048]{1,0:T(8,128)(2,1)} custom-call(s32[1]{0:T(128)S(6)} %copy.8.count_ref, bf16[192,128]{1,0:T(8,128)(2,1)S(1)} %get-tuple-element.11.onehot_ref, bf16[768,512]{1,0:T(8,128)(2,1)S(1)} %bitcast.6), custom_call_target="tpu_custom_call" | custom-call | tf_op jit(solution)/shard_map/collect/pallas_call | solution.py:526
  (1 shorter events, 0.0 us)
Async XLA Ops:
  0.0 5.2 %copy-start = (bf16[27,512,128]{2,1,0:T(8,128)(2,1)S(1)}, bf16[27,512,128]{2,1,0:T(8,128)(2,1)}, u32[]{:S(2)}) copy-start(bf16[27,512,128]{2,1,0:T(8,128)(2,1)} %w_hbm.1) | copy-start | bytes 10616836
  0.0 5.2 %copy-start.2 = (bf16[1,2,16,16,512]{4,3,2,1,0:T(8,128)(2,1)S(1)}, bf16[1,2,16,16,512]{4,3,2,1,0:T(8,128)(2,1)}, u32[]{:S(2)}) copy-start(bf16[1,2,16,16,512]{4,3,2,1,0:T(8,128)(2,1)} %param.7) | copy-start | bytes 1572868
  0.0 5.2 %copy-start.4 = (s32[512,1]{0,1:T(1,128)S(1)}, s32[512,1]{0,1:T(1,128)}, u32[]{:S(2)}) copy-start(s32[512,1]{0,1:T(1,128)} %param.9) | copy-start | bytes 6148
  3.3 3.5 %collective-permute-start = (f32[256,128]{1,0:T(8,128)}, f32[256,128]{1,0:T(8,128)S(1)}, u32[]{:S(2)}, u32[]{:S(2)}) collective-permute-start(f32[256,128]{1,0:T(8,128)} %get-tuple-element.13), channel_id=1, source_target_pairs={{0,1},{1,0},{2,3},{3,2},{4,5},{5,4},{6,7},{7,6},{8,9},{9,8},{10,11... | collective-permute-start | bytes 393224 | tf_op jit(solution)/shard_map/ppermute | solution.py:432
  3.8 3.0 %collective-permute-start.1 = (f32[256,128]{1,0:T(8,128)}, f32[256,128]{1,0:T(8,128)S(1)}, u32[]{:S(2)}, u32[]{:S(2)}) collective-permute-start(f32[256,128]{1,0:T(8,128)} %get-tuple-element.14), channel_id=1, source_target_pairs={{1,2},{2,1},{5,6},{6,5},{9,10},{10,9},{13,14},{14,13},{17,18},{18,... | collective-permute-start | bytes 393224 | tf_op jit(solution)/shard_map/ppermute | solution.py:431
  5.2 22.1 %slice-start = ((s8[6291456]{0:T(1024)(128)(4,1)}), s8[4194304]{0:T(1024)(128)(4,1)S(1)}, s32[]{:S(2)}) async-start(s8[6291456]{0:T(1024)(128)(4,1)} %bitcast.16), calls=%async_computation.2 | async-start | bytes 8388608
  5.2 1.7 %copy-start.1 = (bf16[512,2048]{1,0:T(8,128)(2,1)S(1)}, bf16[512,2048]{1,0:T(8,128)(2,1)}, u32[]{:S(2)}) copy-start(bf16[512,2048]{1,0:T(8,128)(2,1)} %e_ref.3) | copy-start | bytes 6291460
  5.2 1.7 %copy-start.3 = (s32[512]{0:T(512)S(1)}, s32[512]{0:T(512)}, u32[]{:S(2)}) copy-start(s32[512]{0:T(512)} %param.10) | copy-start | bytes 6148
  5.2 22.1 %slice-start.1 = ((s8[6291456]{0:T(1024)(128)(4,1)}), s8[2097152]{0:T(1024)(128)(4,1)S(1)}, s32[]{:S(2)}) async-start(s8[6291456]{0:T(1024)(128)(4,1)} %bitcast.16), calls=%async_computation.3 | async-start | bytes 4194304
  22.4 10.3 %collective-permute-start.3 = (bf16[192,640]{1,0:T(8,128)(2,1)S(1)}, bf16[192,640]{1,0:T(8,128)(2,1)S(1)}, u32[]{:S(2)}, u32[]{:S(2)}) collective-permute-start(bf16[192,640]{1,0:T(8,128)(2,1)S(1)} %bitcast.7), channel_id=1, source_target_pairs={{0,2},{1,3},{2,0},{3,1},{4,6},{5,7},{6,4},{7,5},{8,10},{9,11},{10,... | collective-permute-start | bytes 737288 | tf_op jit(solution)/shard_map/ppermute | solution.py:466
  27.3 3.5 %collective-permute-start.2 = (bf16[192,640]{1,0:T(8,128)(2,1)S(1)}, bf16[192,640]{1,0:T(8,128)(2,1)S(1)}, u32[]{:S(2)}, u32[]{:S(2)}) collective-permute-start(bf16[192,640]{1,0:T(8,128)(2,1)S(1)} %bitcast.8), channel_id=1, source_target_pairs={{0,1},{1,0},{2,3},{3,2},{4,5},{5,4},{6,7},{7,6},{8,9},{9,8},{10,11... | collective-permute-start | bytes 737288 | tf_op jit(solution)/shard_map/ppermute | solution.py:480
  32.7 1.5 %collective-permute-start.4 = (bf16[192,640]{1,0:T(8,128)(2,1)S(1)}, bf16[192,640]{1,0:T(8,128)(2,1)S(1)}, u32[]{:S(2)}, u32[]{:S(2)}) collective-permute-start(bf16[192,640]{1,0:T(8,128)(2,1)S(1)} %collective-permute-done.3.refs_0_.refs_2_), channel_id=1, source_target_pairs={{0,1},{1,0},{2,3},{3,2},{4,5},{5,4},{6,7},{7,6},{8,9},{9,8},{10,11... | collective-permute-start | bytes 737288 | tf_op jit(solution)/shard_map/ppermute | solution.py:480

commit v15 on v12

--- a/solution.py
+++ b/solution.py
@@ -7,6 +7,7 @@
 from jax.experimental.pallas import tpu as pltpu
 from jax.sharding import PartitionSpec as P
 
+
 HDIM = 64
 TAPS = 3
 SAMPLES = 4
@@ -24,7 +25,7 @@
     return pltpu.CompilerParams(vmem_limit_bytes=mib << 20)
 
 
-def slot_of(route_row, bags, cap, stride):
+def slot_of(route_row, bags, stride):
     tokens = route_row.shape[1]
     bag_ids = lax.broadcasted_iota(jnp.int32, (bags, tokens), 0)
     onehot = (bag_ids == route_row).astype(jnp.float32)
@@ -136,7 +137,7 @@
         pieces = [(t, inputs[f + t - 1]) for t in range(TAPS) if 0 <= f + t - 1 < frames]
         acc_ref[f * area : (f + 1) * area, :] = combine(plane_products(pieces, w_ref), rows, cols)
     route_row = route_ref[pl.ds(place, 1), :]
-    onehot_ref[...] = onehot_of(slot_of(route_row, bags, cap, cap), bags * cap)
+    onehot_ref[...] = onehot_of(slot_of(route_row, bags, cap), bags * cap)
 
 
 def join_kernel(
@@ -436,7 +437,7 @@
         in_specs=[VMEM, VMEM, VMEM, VMEM],
         out_specs=(VMEM, VMEM),
         compiler_params=limit(16),
-        cost_estimate=pl.CostEstimate(flops=1200000000, bytes_accessed=4500000, transcendentals=0),
+        cost_estimate=pl.CostEstimate(flops=4000000000, bytes_accessed=4500000, transcendentals=0),
         name="own",
     )(count, tile, conv_weight, route_rows)
     outgoing = pl.pallas_call(
@@ -467,6 +468,7 @@
         cost_estimate=pl.CostEstimate(flops=3300000000, bytes_accessed=14000000, transcendentals=0),
         name="fold",
     )(embed_weight, qkv_weight, arrived)
+
     def spread(start, bits):
         found = dict(start)
         for lower in bits:
@@ -477,7 +479,7 @@
     lower_bits = [1 << i for i in reversed(range(bit.bit_length() - 1))]
     close = spread({0: arrived}, lower_bits)
 
-    def project(group, name):
+    def project(group):
         return pl.pallas_call(
             qkv_kernel,
             out_shape=jax.ShapeDtypeStruct((3, len(group) * slots, local_width), jnp.float32),
@@ -487,14 +489,13 @@
             cost_estimate=pl.CostEstimate(
                 flops=600000000 * len(group), bytes_accessed=3000000 * len(group), transcendentals=0
             ),
-            name=name,
         )(*group, folded)
 
-    near_qkv = project(list(close.values()), "near_qkv")
+    near_qkv = project(list(close.values()))
     across, near_qkv = lax.optimization_barrier((across, near_qkv))
     pieces = dict(close)
     pieces.update(spread({bit: across}, lower_bits))
-    across_qkv = project([across], "across_qkv")
+    across_qkv = project([across])
     groups = (len(close), 1)
     count_slots = heads_dev * slots
     masks = tuple(pieces)
@@ -537,6 +538,5 @@
         P(),
         P(None, None, "head"),
     )
-    return jax.shard_map(
-        shards, mesh=mesh, in_specs=placed, out_specs=P(("bag", "head"), None), check_vma=False
-    )
+
+    return jax.shard_map(shards, mesh=mesh, in_specs=placed, out_specs=P(("bag", "head"), None), check_vma=False)

time: 66.7 us -> 64.3 us (0.964)
  local copies, waits for them, and re-layouts: 2.81 us -> 0.15 us
  waiting for transfers between devices: 0.37 us -> 1.25 us
  starting transfers between devices: 6.98 us -> 6.16 us
    unnamed x12 -> x14, local copies, waits for them, and re-layouts: 2.81 us -> 0.15 us
  transfers between devices with their start and end apart: 5 -> 5, of which waited for: 1 -> 2; matrix products, arithmetic and copies ran while one was open for 0% -> 0% of each run, Pallas kernels for 11% -> 11%
where the time goes in v15:
time: 64.3 us; the launch traced here: 64.1 us
  blocking collectives  38.5 us (60%)
  Pallas kernels  17.2 us (27%)
  starting transfers between devices  6.16 us (10%)
  waiting for transfers between devices  1.25 us (2%)
  between operations  0.81 us (1%)
    all_to_all x1, blocking collectives, shards(): lax.all_to_all(attended, ('head', 'bag'), split_axis=0, concat_axis=0, ti...  23.8 us
    all_to_all x1, blocking collectives, shards(): lax.all_to_all(outgoing.reshape(bags, cap, row_width), 'bag', split_axis=...  14.7 us
    ppermute x1, starting transfers between devices, shards(): across = lax.ppermute(arrived, 'head', swap)  4.91 us
    pallas_call x1, Pallas kernels, shards(): pl.pallas_call(functools.partial(bag_kernel, bags, cap, masks, groups), o...  4.88 us
    pallas_call x1, Pallas kernels, shards(): pl.pallas_call(fold_kernel, out_shape=jax.ShapeDtypeStruct((3, 2 * embed_...  3.43 us
    pallas_call x1, Pallas kernels, shards(): pl.pallas_call(functools.partial(edge_kernel, rows, cols, frames_dev), ou...  3.27 us
    pallas_call x2, Pallas kernels, project(): pl.pallas_call(qkv_kernel, out_shape=jax.ShapeDtypeStruct((3, len(group)...  2.16 us
    pallas_call x1, Pallas kernels, shards(): pl.pallas_call(functools.partial(own_kernel, bags, cap, rows, cols, frame...  1.56 us
  transfers between devices with their start and end apart: 5, of which 2 were waited for; matrix products, arithmetic and copies ran while one was open for 0% of the time, Pallas kernels for 11%

profile of v15, /device:TPU:0, one launch (start us, length us, event | category | flops | bytes accessed | tf_op | source)
XLA Modules:
  0.0 64.1 jit_solution(6263227206083843792)
XLA Ops:
  0.0 0.0 copy-start
  0.0 0.0 copy-start.2
  0.0 0.0 copy-start.4
  0.0 3.3 %edge.1 = (f32[256,128]{1,0:T(8,128)}, f32[256,128]{1,0:T(8,128)}) custom-call(bf16[512,512]{1,0:T(8,128)(2,1)} %bitcast.13, bf16[27,512,128]{2,1,0:T(8,128)(2,1)} %w_hbm.1), custom_call_target="tpu_custom_call" | custom-call | flops 600000000 | bytes 4500000 | tf_op jit(solution)/shard_map/edge/pallas_call | solution.py:411
  3.3 0.6 collective-permute-start
  3.8 0.7 %collective-permute-start.1 = (f32[256,128]{1,0:T(8,128)}, f32[256,128]{1,0:T(8,128)S(1)}, u32[]{:S(2)}, u32[]{:S(2)}) collective-permute-start(f32[256,128]{1,0:T(8,128)} %get-tuple-element.14), channel_id=1, source_target_pairs={{1,2},{2,1},{5,6},{6,5},{9,10},{10,9},{13,14},{14,13},{17,18},{18,... | collective-permute-start | bytes 393224 | tf_op jit(solution)/shard_map/ppermute | solution.py:426
  5.2 0.0 slice-start
  5.2 0.0 copy-done
  5.2 0.0 copy-done.2
  5.2 0.0 copy-done.4
  5.2 0.0 copy-start.1
  5.2 0.0 copy-start.3
  5.2 0.0 slice-start.1
  5.2 1.6 %own.1 = (f32[512,128]{1,0:T(8,128)S(1)}, bf16[192,128]{1,0:T(8,128)(2,1)S(1)}) custom-call(s32[1]{0:T(128)S(6)} %copy.8.count_ref, bf16[512,512]{1,0:T(8,128)(2,1)S(1)} %bitcast.14, bf16[27,512,128]{2,1,0:T(8,128)(2,1)S(1)} %copy-done, s32[4,128]{1,0:T(4,128)S(1)} %bitcast.18), custom_call_target="tpu_custom_call" | custom-call | flops 4000000000 | bytes 4500000 | tf_op jit(solution)/shard_map/own/pallas_call | solution.py:431
  6.8 0.0 collective-permute-done.near_ref
  6.8 0.0 collective-permute-done.1.far_ref
  6.8 0.1 copy-done.1
  6.9 0.0 copy-done.3
  6.9 0.7 %join.1 = bf16[192,640]{1,0:T(8,128)(2,1)S(1)} custom-call(s32[1]{0:T(128)S(6)} %copy.8.count_ref, s32[4,128]{1,0:T(4,128)S(1)} %bitcast.15, f32[512,128]{1,0:T(8,128)S(1)} %get-tuple-element.12.acc_ref, f32[256,128]{1,0:T(8,128)S(1)} %collective-permute-done.near_ref, f32[256,128]{1,0:T(8,128)S(1)} %collective-permute-done.1.far_ref, ...), custom_call_target="tpu_custom_call" | custom-call | flops 300000000 | bytes 3000000 | tf_op jit(solution)/shard_map/join/pallas_call | solution.py:443
  7.7 14.7 %all_to_all.10 = bf16[8,24,640]{2,1,0:T(8,128)(2,1)S(1)} all-to-all(bf16[8,24,640]{2,1,0:T(8,128)(2,1)S(1)} %bitcast.12), channel_id=1, replica_groups=mesh['bag'=8,'head'=4] {'bag'}, dimensions={0} | all-to-all | bytes 491520 | tf_op jit(solution)/shard_map/all_to_all | solution.py:454
  22.4 4.9 %collective-permute-start.3 = (bf16[192,640]{1,0:T(8,128)(2,1)S(1)}, bf16[192,640]{1,0:T(8,128)(2,1)S(1)}, u32[]{:S(2)}, u32[]{:S(2)}) collective-permute-start(bf16[192,640]{1,0:T(8,128)(2,1)S(1)} %bitcast.7), channel_id=1, source_target_pairs={{0,2},{1,3},{2,0},{3,1},{4,6},{5,7},{6,4},{7,5},{8,10},{9,11},{10,... | collective-permute-start | bytes 737288 | tf_op jit(solution)/shard_map/ppermute | solution.py:461
  27.3 0.0 collective-permute-start.2
  27.3 0.0 slice-done
  27.3 0.0 slice-done.1
  27.3 3.4 %fold.1.refs_2_.refs_1_.refs_6_ = bf16[3,1024,512]{2,1,0:T(8,128)(2,1)S(1)} custom-call(bf16[512,2048]{1,0:T(8,128)(2,1)S(1)} %copy-done.1, bf16[3,2048,512]{2,1,0:T(8,128)(2,1)S(1)} %bitcast.17, bf16[192,640]{1,0:T(8,128)(2,1)S(1)} %bitcast.9), custom_call_target="tpu_custom_call" | custom-call | flops 3300000000 | bytes 14000000 | tf_op jit(solution)/shard_map/fold/pallas_call | solution.py:462
  30.8 0.0 collective-permute-done.2.refs_1_
  30.8 1.4 %shard_map.73.refs_4_ = f32[3,384,512]{2,1,0:T(8,128)S(1)} custom-call(bf16[192,640]{1,0:T(8,128)(2,1)S(1)} %bitcast.10, bf16[192,640]{1,0:T(8,128)(2,1)S(1)} %collective-permute-done.2.refs_1_, bf16[3,1024,512]{2,1,0:T(8,128)(2,1)S(1)} %fold.1.refs_2_.refs_1_.refs_6_), custom_call_target="tpu_custom_call" | custom-call | flops 1200000000 | bytes 6000000 | tf_op jit(solution)/shard_map/pallas_call | solution.py:483
  32.2 0.5 collective-permute-done.3.refs_0_.refs_2_
  32.7 0.0 collective-permute-start.4
  32.7 0.8 %shard_map.74.refs_5_ = f32[3,192,512]{2,1,0:T(8,128)S(1)} custom-call(bf16[192,640]{1,0:T(8,128)(2,1)S(1)} %collective-permute-done.3.refs_0_.refs_2_, bf16[3,1024,512]{2,1,0:T(8,128)(2,1)S(1)} %fold.1.refs_2_.refs_1_.refs_6_), custom_call_target="tpu_custom_call" | custom-call | flops 600000000 | bytes 3000000 | tf_op jit(solution)/shard_map/pallas_call | solution.py:483
  33.5 0.7 %collective-permute-done.4.refs_3_ = bf16[192,640]{1,0:T(8,128)(2,1)S(1)} collective-permute-done((bf16[192,640]{1,0:T(8,128)(2,1)S(1)}, bf16[192,640]{1,0:T(8,128)(2,1)S(1)}, u32[]{:S(2)}, u32[]{:S(2)}) %collective-permute-start.4) | collective-permute-done | bytes 245792 | tf_op jit(solution)/shard_map/ppermute | solution.py:476
  34.2 4.9 %bag.1 = bf16[32,24,512]{2,1,0:T(8,128)(2,1)S(1)} custom-call(bf16[192,640]{1,0:T(8,128)(2,1)S(1)} %bitcast.11, bf16[192,640]{1,0:T(8,128)(2,1)S(1)} %collective-permute-done.2.refs_1_, bf16[192,640]{1,0:T(8,128)(2,1)S(1)} %collective-permute-done.3.refs_0_.refs_2_, bf16[192,640]{1,0:T(8,128)(2,1)S(1)} %collective-permute-done.4.refs_3_, ...), custom_call_target="tpu_custom_call" | custom-call | flops 3000000000 | bytes 5000000 | tf_op jit(solution)/shard_map/bag/pallas_call | solution.py:504
  39.1 23.8 %all_to_all.11 = bf16[32,24,512]{2,1,0:T(8,128)(2,1)S(1)} all-to-all(bf16[32,24,512]{2,1,0:T(8,128)(2,1)S(1)} %bag.1), channel_id=1, replica_groups=mesh['bag'=8,'head'=4] {'head','bag'}, dimensions={0} | all-to-all | bytes 1572864 | tf_op jit(solution)/shard_map/all_to_all | solution.py:520
  62.9 1.2 %collect.1 = bf16[128,2048]{1,0:T(8,128)(2,1)} custom-call(s32[1]{0:T(128)S(6)} %copy.8.count_ref, bf16[192,128]{1,0:T(8,128)(2,1)S(1)} %get-tuple-element.11.onehot_ref, bf16[768,512]{1,0:T(8,128)(2,1)S(1)} %bitcast.6), custom_call_target="tpu_custom_call" | custom-call | tf_op jit(solution)/shard_map/collect/pallas_call | solution.py:521
  (1 shorter events, 0.0 us)
Async XLA Ops:
  0.0 5.2 %copy-start = (bf16[27,512,128]{2,1,0:T(8,128)(2,1)S(1)}, bf16[27,512,128]{2,1,0:T(8,128)(2,1)}, u32[]{:S(2)}) copy-start(bf16[27,512,128]{2,1,0:T(8,128)(2,1)} %w_hbm.1) | copy-start | bytes 10616836
  0.0 5.2 %copy-start.2 = (bf16[1,2,16,16,512]{4,3,2,1,0:T(8,128)(2,1)S(1)}, bf16[1,2,16,16,512]{4,3,2,1,0:T(8,128)(2,1)}, u32[]{:S(2)}) copy-start(bf16[1,2,16,16,512]{4,3,2,1,0:T(8,128)(2,1)} %param.7) | copy-start | bytes 1572868
  0.0 5.2 %copy-start.4 = (s32[512,1]{0,1:T(1,128)S(1)}, s32[512,1]{0,1:T(1,128)}, u32[]{:S(2)}) copy-start(s32[512,1]{0,1:T(1,128)} %param.9) | copy-start | bytes 6148
  3.3 3.5 %collective-permute-start = (f32[256,128]{1,0:T(8,128)}, f32[256,128]{1,0:T(8,128)S(1)}, u32[]{:S(2)}, u32[]{:S(2)}) collective-permute-start(f32[256,128]{1,0:T(8,128)} %get-tuple-element.13), channel_id=1, source_target_pairs={{0,1},{1,0},{2,3},{3,2},{4,5},{5,4},{6,7},{7,6},{8,9},{9,8},{10,11... | collective-permute-start | bytes 393224 | tf_op jit(solution)/shard_map/ppermute | solution.py:427
  3.8 3.0 %collective-permute-start.1 = (f32[256,128]{1,0:T(8,128)}, f32[256,128]{1,0:T(8,128)S(1)}, u32[]{:S(2)}, u32[]{:S(2)}) collective-permute-start(f32[256,128]{1,0:T(8,128)} %get-tuple-element.14), channel_id=1, source_target_pairs={{1,2},{2,1},{5,6},{6,5},{9,10},{10,9},{13,14},{14,13},{17,18},{18,... | collective-permute-start | bytes 393224 | tf_op jit(solution)/shard_map/ppermute | solution.py:426
  5.2 22.1 %slice-start = ((s8[6291456]{0:T(1024)(128)(4,1)}), s8[4194304]{0:T(1024)(128)(4,1)S(1)}, s32[]{:S(2)}) async-start(s8[6291456]{0:T(1024)(128)(4,1)} %bitcast.16), calls=%async_computation.2 | async-start | bytes 8388608
  5.2 1.7 %copy-start.1 = (bf16[512,2048]{1,0:T(8,128)(2,1)S(1)}, bf16[512,2048]{1,0:T(8,128)(2,1)}, u32[]{:S(2)}) copy-start(bf16[512,2048]{1,0:T(8,128)(2,1)} %e_ref.3) | copy-start | bytes 6291460
  5.2 1.7 %copy-start.3 = (s32[512]{0:T(512)S(1)}, s32[512]{0:T(512)}, u32[]{:S(2)}) copy-start(s32[512]{0:T(512)} %param.10) | copy-start | bytes 6148
  5.2 22.1 %slice-start.1 = ((s8[6291456]{0:T(1024)(128)(4,1)}), s8[2097152]{0:T(1024)(128)(4,1)S(1)}, s32[]{:S(2)}) async-start(s8[6291456]{0:T(1024)(128)(4,1)} %bitcast.16), calls=%async_computation.3 | async-start | bytes 4194304
  22.4 10.3 %collective-permute-start.3 = (bf16[192,640]{1,0:T(8,128)(2,1)S(1)}, bf16[192,640]{1,0:T(8,128)(2,1)S(1)}, u32[]{:S(2)}, u32[]{:S(2)}) collective-permute-start(bf16[192,640]{1,0:T(8,128)(2,1)S(1)} %bitcast.7), channel_id=1, source_target_pairs={{0,2},{1,3},{2,0},{3,1},{4,6},{5,7},{6,4},{7,5},{8,10},{9,11},{10,... | collective-permute-start | bytes 737288 | tf_op jit(solution)/shard_map/ppermute | solution.py:461
  27.3 3.5 %collective-permute-start.2 = (bf16[192,640]{1,0:T(8,128)(2,1)S(1)}, bf16[192,640]{1,0:T(8,128)(2,1)S(1)}, u32[]{:S(2)}, u32[]{:S(2)}) collective-permute-start(bf16[192,640]{1,0:T(8,128)(2,1)S(1)} %bitcast.8), channel_id=1, source_target_pairs={{0,1},{1,0},{2,3},{3,2},{4,5},{5,4},{6,7},{7,6},{8,9},{9,8},{10,11... | collective-permute-start | bytes 737288 | tf_op jit(solution)/shard_map/ppermute | solution.py:476
  32.7 1.5 %collective-permute-start.4 = (bf16[192,640]{1,0:T(8,128)(2,1)S(1)}, bf16[192,640]{1,0:T(8,128)(2,1)S(1)}, u32[]{:S(2)}, u32[]{:S(2)}) collective-permute-start(bf16[192,640]{1,0:T(8,128)(2,1)S(1)} %collective-permute-done.3.refs_0_.refs_2_), channel_id=1, source_target_pairs={{0,1},{1,0},{2,3},{3,2},{4,5},{5,4},{6,7},{7,6},{8,9},{9,8},{10,11... | collective-permute-start | bytes 737288 | tf_op jit(solution)/shard_map/ppermute | solution.py:476

commit v16 on v12

--- a/solution.py
+++ b/solution.py
@@ -381,14 +381,11 @@
     place = lax.axis_index("head")
     slots, tokens = onehot_ref.shape
     frame = place * frames + lax.broadcasted_iota(jnp.int32, (slots, tokens), 1) // (tokens // frames)
-    onehot = jnp.where(frame < count, onehot_ref[...], jnp.zeros((), jnp.bfloat16))
+    onehot = jnp.where(frame < count, onehot_ref[...].astype(jnp.float32), 0.0).T.astype(jnp.bfloat16)
     width = recv_ref.shape[1]
     for h in range(heads):
-        picked = lax.dot_general(
-            onehot,
-            recv_ref[h * slots : (h + 1) * slots, :],
-            (((0,), (0,)), ((), ())),
-            preferred_element_type=jnp.float32,
+        picked = jnp.dot(
+            onehot, recv_ref[h * slots : (h + 1) * slots, :], preferred_element_type=jnp.float32
         )
         out_ref[:, h * width : (h + 1) * width] = picked.astype(jnp.bfloat16)
 
@@ -436,7 +433,7 @@
         in_specs=[VMEM, VMEM, VMEM, VMEM],
         out_specs=(VMEM, VMEM),
         compiler_params=limit(16),
-        cost_estimate=pl.CostEstimate(flops=1200000000, bytes_accessed=4500000, transcendentals=0),
+        cost_estimate=pl.CostEstimate(flops=4000000000, bytes_accessed=4500000, transcendentals=0),
         name="own",
     )(count, tile, conv_weight, route_rows)
     outgoing = pl.pallas_call(

time: 66.7 us -> 64.3 us (0.964)
  local copies, waits for them, and re-layouts: 2.81 us -> 0.15 us
  waiting for transfers between devices: 0.37 us -> 1.25 us
  starting transfers between devices: 6.98 us -> 6.16 us
    unnamed x12 -> x14, local copies, waits for them, and re-layouts: 2.81 us -> 0.15 us
  transfers between devices with their start and end apart: 5 -> 5, of which waited for: 1 -> 2; matrix products, arithmetic and copies ran while one was open for 0% -> 0% of each run, Pallas kernels for 11% -> 11%
where the time goes in v16:
time: 64.3 us; the launch traced here: 64.1 us
  blocking collectives  38.5 us (60%)
  Pallas kernels  17.2 us (27%)
  starting transfers between devices  6.16 us (10%)
  waiting for transfers between devices  1.25 us (2%)
  between operations  0.81 us (1%)
    all_to_all x1, blocking collectives, shards(): lax.all_to_all(attended, ('head', 'bag'), split_axis=0, concat_axis=0, ti...  23.8 us
    all_to_all x1, blocking collectives, shards(): lax.all_to_all(outgoing.reshape(bags, cap, row_width), 'bag', split_axis=...  14.7 us
    ppermute x1, starting transfers between devices, shards(): across = lax.ppermute(arrived, 'head', swap)  4.91 us
    pallas_call x1, Pallas kernels, shards(): pl.pallas_call(functools.partial(bag_kernel, bags, cap, masks, groups), o...  4.88 us
    pallas_call x1, Pallas kernels, shards(): pl.pallas_call(fold_kernel, out_shape=jax.ShapeDtypeStruct((3, 2 * embed_...  3.43 us
    pallas_call x1, Pallas kernels, shards(): pl.pallas_call(functools.partial(edge_kernel, rows, cols, frames_dev), ou...  3.27 us
    pallas_call x2, Pallas kernels, project(): pl.pallas_call(qkv_kernel, out_shape=jax.ShapeDtypeStruct((3, len(group)...  2.16 us
    pallas_call x1, Pallas kernels, shards(): pl.pallas_call(functools.partial(own_kernel, bags, cap, rows, cols, frame...  1.56 us
  transfers between devices with their start and end apart: 5, of which 2 were waited for; matrix products, arithmetic and copies ran while one was open for 0% of the time, Pallas kernels for 11%

profile of v16, /device:TPU:0, one launch (start us, length us, event | category | flops | bytes accessed | tf_op | source)
XLA Modules:
  0.0 64.1 jit_solution(2665203337515096054)
XLA Ops:
  0.0 0.0 copy-start
  0.0 0.0 copy-start.2
  0.0 0.0 copy-start.4
  0.0 3.3 %edge.1 = (f32[256,128]{1,0:T(8,128)}, f32[256,128]{1,0:T(8,128)}) custom-call(bf16[512,512]{1,0:T(8,128)(2,1)} %bitcast.13, bf16[27,512,128]{2,1,0:T(8,128)(2,1)} %w_hbm.1), custom_call_target="tpu_custom_call" | custom-call | flops 600000000 | bytes 4500000 | tf_op jit(solution)/shard_map/edge/pallas_call | solution.py:407
  3.3 0.6 collective-permute-start
  3.8 0.7 %collective-permute-start.1 = (f32[256,128]{1,0:T(8,128)}, f32[256,128]{1,0:T(8,128)S(1)}, u32[]{:S(2)}, u32[]{:S(2)}) collective-permute-start(f32[256,128]{1,0:T(8,128)} %get-tuple-element.14), channel_id=1, source_target_pairs={{1,2},{2,1},{5,6},{6,5},{9,10},{10,9},{13,14},{14,13},{17,18},{18,... | collective-permute-start | bytes 393224 | tf_op jit(solution)/shard_map/ppermute | solution.py:422
  5.2 0.0 slice-start
  5.2 0.0 copy-done
  5.2 0.0 copy-done.2
  5.2 0.0 copy-done.4
  5.2 0.0 copy-start.1
  5.2 0.0 copy-start.3
  5.2 0.0 slice-start.1
  5.2 1.6 %own.1 = (f32[512,128]{1,0:T(8,128)S(1)}, bf16[192,128]{1,0:T(8,128)(2,1)S(1)}) custom-call(s32[1]{0:T(128)S(6)} %copy.8.count_ref, bf16[512,512]{1,0:T(8,128)(2,1)S(1)} %bitcast.14, bf16[27,512,128]{2,1,0:T(8,128)(2,1)S(1)} %copy-done, s32[4,128]{1,0:T(4,128)S(1)} %bitcast.18), custom_call_target="tpu_custom_call" | custom-call | flops 4000000000 | bytes 4500000 | tf_op jit(solution)/shard_map/own/pallas_call | solution.py:427
  6.8 0.0 collective-permute-done.near_ref
  6.8 0.0 collective-permute-done.1.far_ref
  6.8 0.1 copy-done.1
  6.9 0.0 copy-done.3
  6.9 0.7 %join.1 = bf16[192,640]{1,0:T(8,128)(2,1)S(1)} custom-call(s32[1]{0:T(128)S(6)} %copy.8.count_ref, s32[4,128]{1,0:T(4,128)S(1)} %bitcast.15, f32[512,128]{1,0:T(8,128)S(1)} %get-tuple-element.12.acc_ref, f32[256,128]{1,0:T(8,128)S(1)} %collective-permute-done.near_ref, f32[256,128]{1,0:T(8,128)S(1)} %collective-permute-done.1.far_ref, ...), custom_call_target="tpu_custom_call" | custom-call | flops 300000000 | bytes 3000000 | tf_op jit(solution)/shard_map/join/pallas_call | solution.py:439
  7.7 14.7 %all_to_all.10 = bf16[8,24,640]{2,1,0:T(8,128)(2,1)S(1)} all-to-all(bf16[8,24,640]{2,1,0:T(8,128)(2,1)S(1)} %bitcast.12), channel_id=1, replica_groups=mesh['bag'=8,'head'=4] {'bag'}, dimensions={0} | all-to-all | bytes 491520 | tf_op jit(solution)/shard_map/all_to_all | solution.py:450
  22.4 4.9 %collective-permute-start.3 = (bf16[192,640]{1,0:T(8,128)(2,1)S(1)}, bf16[192,640]{1,0:T(8,128)(2,1)S(1)}, u32[]{:S(2)}, u32[]{:S(2)}) collective-permute-start(bf16[192,640]{1,0:T(8,128)(2,1)S(1)} %bitcast.7), channel_id=1, source_target_pairs={{0,2},{1,3},{2,0},{3,1},{4,6},{5,7},{6,4},{7,5},{8,10},{9,11},{10,... | collective-permute-start | bytes 737288 | tf_op jit(solution)/shard_map/ppermute | solution.py:457
  27.3 0.0 collective-permute-start.2
  27.3 0.0 slice-done
  27.3 0.0 slice-done.1
  27.3 3.4 %fold.1.refs_2_.refs_1_.refs_6_ = bf16[3,1024,512]{2,1,0:T(8,128)(2,1)S(1)} custom-call(bf16[512,2048]{1,0:T(8,128)(2,1)S(1)} %copy-done.1, bf16[3,2048,512]{2,1,0:T(8,128)(2,1)S(1)} %bitcast.17, bf16[192,640]{1,0:T(8,128)(2,1)S(1)} %bitcast.9), custom_call_target="tpu_custom_call" | custom-call | flops 3300000000 | bytes 14000000 | tf_op jit(solution)/shard_map/fold/pallas_call | solution.py:458
  30.8 0.0 collective-permute-done.2.refs_1_
  30.8 1.4 %near_qkv.1.refs_4_ = f32[3,384,512]{2,1,0:T(8,128)S(1)} custom-call(bf16[192,640]{1,0:T(8,128)(2,1)S(1)} %bitcast.10, bf16[192,640]{1,0:T(8,128)(2,1)S(1)} %collective-permute-done.2.refs_1_, bf16[3,1024,512]{2,1,0:T(8,128)(2,1)S(1)} %fold.1.refs_2_.refs_1_.refs_6_), custom_call_target="tpu_custom_call" | custom-call | flops 1200000000 | bytes 6000000 | tf_op jit(solution)/shard_map/near_qkv/pallas_call | solution.py:478
  32.2 0.5 collective-permute-done.3.refs_0_.refs_2_
  32.7 0.0 collective-permute-start.4
  32.7 0.8 %across_qkv.1.refs_5_ = f32[3,192,512]{2,1,0:T(8,128)S(1)} custom-call(bf16[192,640]{1,0:T(8,128)(2,1)S(1)} %collective-permute-done.3.refs_0_.refs_2_, bf16[3,1024,512]{2,1,0:T(8,128)(2,1)S(1)} %fold.1.refs_2_.refs_1_.refs_6_), custom_call_target="tpu_custom_call" | custom-call | flops 600000000 | bytes 3000000 | tf_op jit(solution)/shard_map/across_qkv/pallas_call | solution.py:478
  33.5 0.7 %collective-permute-done.4.refs_3_ = bf16[192,640]{1,0:T(8,128)(2,1)S(1)} collective-permute-done((bf16[192,640]{1,0:T(8,128)(2,1)S(1)}, bf16[192,640]{1,0:T(8,128)(2,1)S(1)}, u32[]{:S(2)}, u32[]{:S(2)}) %collective-permute-start.4) | collective-permute-done | bytes 245792 | tf_op jit(solution)/shard_map/ppermute | solution.py:471
  34.2 4.9 %bag.1 = bf16[32,24,512]{2,1,0:T(8,128)(2,1)S(1)} custom-call(bf16[192,640]{1,0:T(8,128)(2,1)S(1)} %bitcast.11, bf16[192,640]{1,0:T(8,128)(2,1)S(1)} %collective-permute-done.2.refs_1_, bf16[192,640]{1,0:T(8,128)(2,1)S(1)} %collective-permute-done.3.refs_0_.refs_2_, bf16[192,640]{1,0:T(8,128)(2,1)S(1)} %collective-permute-done.4.refs_3_, ...), custom_call_target="tpu_custom_call" | custom-call | flops 3000000000 | bytes 5000000 | tf_op jit(solution)/shard_map/bag/pallas_call | solution.py:500
  39.1 23.8 %all_to_all.11 = bf16[32,24,512]{2,1,0:T(8,128)(2,1)S(1)} all-to-all(bf16[32,24,512]{2,1,0:T(8,128)(2,1)S(1)} %bag.1), channel_id=1, replica_groups=mesh['bag'=8,'head'=4] {'head','bag'}, dimensions={0} | all-to-all | bytes 1572864 | tf_op jit(solution)/shard_map/all_to_all | solution.py:516
  62.9 1.2 %collect.1 = bf16[128,2048]{1,0:T(8,128)(2,1)} custom-call(s32[1]{0:T(128)S(6)} %copy.8.count_ref, bf16[192,128]{1,0:T(8,128)(2,1)S(1)} %get-tuple-element.11.onehot_ref, bf16[768,512]{1,0:T(8,128)(2,1)S(1)} %bitcast.6), custom_call_target="tpu_custom_call" | custom-call | tf_op jit(solution)/shard_map/collect/pallas_call | solution.py:517
  (1 shorter events, 0.0 us)
Async XLA Ops:
  0.0 5.2 %copy-start = (bf16[27,512,128]{2,1,0:T(8,128)(2,1)S(1)}, bf16[27,512,128]{2,1,0:T(8,128)(2,1)}, u32[]{:S(2)}) copy-start(bf16[27,512,128]{2,1,0:T(8,128)(2,1)} %w_hbm.1) | copy-start | bytes 10616836
  0.0 5.2 %copy-start.2 = (bf16[1,2,16,16,512]{4,3,2,1,0:T(8,128)(2,1)S(1)}, bf16[1,2,16,16,512]{4,3,2,1,0:T(8,128)(2,1)}, u32[]{:S(2)}) copy-start(bf16[1,2,16,16,512]{4,3,2,1,0:T(8,128)(2,1)} %param.7) | copy-start | bytes 1572868
  0.0 5.2 %copy-start.4 = (s32[512,1]{0,1:T(1,128)S(1)}, s32[512,1]{0,1:T(1,128)}, u32[]{:S(2)}) copy-start(s32[512,1]{0,1:T(1,128)} %param.9) | copy-start | bytes 6148
  3.3 3.5 %collective-permute-start = (f32[256,128]{1,0:T(8,128)}, f32[256,128]{1,0:T(8,128)S(1)}, u32[]{:S(2)}, u32[]{:S(2)}) collective-permute-start(f32[256,128]{1,0:T(8,128)} %get-tuple-element.13), channel_id=1, source_target_pairs={{0,1},{1,0},{2,3},{3,2},{4,5},{5,4},{6,7},{7,6},{8,9},{9,8},{10,11... | collective-permute-start | bytes 393224 | tf_op jit(solution)/shard_map/ppermute | solution.py:423
  3.8 3.0 %collective-permute-start.1 = (f32[256,128]{1,0:T(8,128)}, f32[256,128]{1,0:T(8,128)S(1)}, u32[]{:S(2)}, u32[]{:S(2)}) collective-permute-start(f32[256,128]{1,0:T(8,128)} %get-tuple-element.14), channel_id=1, source_target_pairs={{1,2},{2,1},{5,6},{6,5},{9,10},{10,9},{13,14},{14,13},{17,18},{18,... | collective-permute-start | bytes 393224 | tf_op jit(solution)/shard_map/ppermute | solution.py:422
  5.2 22.1 %slice-start = ((s8[6291456]{0:T(1024)(128)(4,1)}), s8[4194304]{0:T(1024)(128)(4,1)S(1)}, s32[]{:S(2)}) async-start(s8[6291456]{0:T(1024)(128)(4,1)} %bitcast.16), calls=%async_computation.2 | async-start | bytes 8388608
  5.2 1.7 %copy-start.1 = (bf16[512,2048]{1,0:T(8,128)(2,1)S(1)}, bf16[512,2048]{1,0:T(8,128)(2,1)}, u32[]{:S(2)}) copy-start(bf16[512,2048]{1,0:T(8,128)(2,1)} %e_ref.3) | copy-start | bytes 6291460
  5.2 1.7 %copy-start.3 = (s32[512]{0:T(512)S(1)}, s32[512]{0:T(512)}, u32[]{:S(2)}) copy-start(s32[512]{0:T(512)} %param.10) | copy-start | bytes 6148
  5.2 22.1 %slice-start.1 = ((s8[6291456]{0:T(1024)(128)(4,1)}), s8[2097152]{0:T(1024)(128)(4,1)S(1)}, s32[]{:S(2)}) async-start(s8[6291456]{0:T(1024)(128)(4,1)} %bitcast.16), calls=%async_computation.3 | async-start | bytes 4194304
  22.4 10.3 %collective-permute-start.3 = (bf16[192,640]{1,0:T(8,128)(2,1)S(1)}, bf16[192,640]{1,0:T(8,128)(2,1)S(1)}, u32[]{:S(2)}, u32[]{:S(2)}) collective-permute-start(bf16[192,640]{1,0:T(8,128)(2,1)S(1)} %bitcast.7), channel_id=1, source_target_pairs={{0,2},{1,3},{2,0},{3,1},{4,6},{5,7},{6,4},{7,5},{8,10},{9,11},{10,... | collective-permute-start | bytes 737288 | tf_op jit(solution)/shard_map/ppermute | solution.py:457
  27.3 3.5 %collective-permute-start.2 = (bf16[192,640]{1,0:T(8,128)(2,1)S(1)}, bf16[192,640]{1,0:T(8,128)(2,1)S(1)}, u32[]{:S(2)}, u32[]{:S(2)}) collective-permute-start(bf16[192,640]{1,0:T(8,128)(2,1)S(1)} %bitcast.8), channel_id=1, source_target_pairs={{0,1},{1,0},{2,3},{3,2},{4,5},{5,4},{6,7},{7,6},{8,9},{9,8},{10,11... | collective-permute-start | bytes 737288 | tf_op jit(solution)/shard_map/ppermute | solution.py:471
  32.7 1.5 %collective-permute-start.4 = (bf16[192,640]{1,0:T(8,128)(2,1)S(1)}, bf16[192,640]{1,0:T(8,128)(2,1)S(1)}, u32[]{:S(2)}, u32[]{:S(2)}) collective-permute-start(bf16[192,640]{1,0:T(8,128)(2,1)S(1)} %collective-permute-done.3.refs_0_.refs_2_), channel_id=1, source_target_pairs={{0,1},{1,0},{2,3},{3,2},{4,5},{5,4},{6,7},{7,6},{8,9},{9,8},{10,11... | collective-permute-start | bytes 737288 | tf_op jit(solution)/shard_map/ppermute | solution.py:471

commit v17 on v16

--- a/solution.py
+++ b/solution.py
@@ -441,7 +441,7 @@
         out_shape=jax.ShapeDtypeStruct((slots, row_width), jnp.bfloat16),
         in_specs=[VMEM] * 7,
         out_specs=VMEM,
-        scratch_shapes=[pltpu.VMEM((frames_dev * area, chans), jnp.float32)],
+        scratch_shapes=[pltpu.VMEM((frames_dev * area + 8, chans), jnp.float32)],
         compiler_params=limit(16),
         cost_estimate=pl.CostEstimate(flops=300000000, bytes_accessed=3000000, transcendentals=0),
         name="join",

time: 64.3 us -> 64.3 us (level)
  no operation moved by 1% of the time
where the time goes in v17:
time: 64.3 us; the launch traced here: 64.1 us
  blocking collectives  38.7 us (60%)
  Pallas kernels  17.2 us (27%)
  starting transfers between devices  6.03 us (9%)
  waiting for transfers between devices  1.24 us (2%)
  between operations  0.81 us (1%)
    all_to_all x1, blocking collectives, shards(): lax.all_to_all(attended, ('head', 'bag'), split_axis=0, concat_axis=0, ti...  23.8 us
    all_to_all x1, blocking collectives, shards(): lax.all_to_all(outgoing.reshape(bags, cap, row_width), 'bag', split_axis=...  14.9 us
    pallas_call x1, Pallas kernels, shards(): pl.pallas_call(functools.partial(bag_kernel, bags, cap, masks, groups), o...  4.88 us
    ppermute x1, starting transfers between devices, shards(): across = lax.ppermute(arrived, 'head', swap)  4.77 us
    pallas_call x1, Pallas kernels, shards(): pl.pallas_call(fold_kernel, out_shape=jax.ShapeDtypeStruct((3, 2 * embed_...  3.43 us
    pallas_call x1, Pallas kernels, shards(): pl.pallas_call(functools.partial(edge_kernel, rows, cols, frames_dev), ou...  3.27 us
    pallas_call x2, Pallas kernels, project(): pl.pallas_call(qkv_kernel, out_shape=jax.ShapeDtypeStruct((3, len(group)...  2.16 us
    pallas_call x1, Pallas kernels, shards(): pl.pallas_call(functools.partial(own_kernel, bags, cap, rows, cols, frame...  1.56 us
  transfers between devices with their start and end apart: 5, of which 2 were waited for; matrix products, arithmetic and copies ran while one was open for 0% of the time, Pallas kernels for 11%

profile of v17, /device:TPU:0, one launch (start us, length us, event | category | flops | bytes accessed | tf_op | source)
XLA Modules:
  0.0 64.1 jit_solution(2891019185851183830)
XLA Ops:
  0.0 0.0 copy-start
  0.0 0.0 copy-start.2
  0.0 0.0 copy-start.4
  0.0 3.3 %edge.1 = (f32[256,128]{1,0:T(8,128)}, f32[256,128]{1,0:T(8,128)}) custom-call(bf16[512,512]{1,0:T(8,128)(2,1)} %bitcast.13, bf16[27,512,128]{2,1,0:T(8,128)(2,1)} %w_hbm.1), custom_call_target="tpu_custom_call" | custom-call | flops 600000000 | bytes 4500000 | tf_op jit(solution)/shard_map/edge/pallas_call | solution.py:407
  3.3 0.6 collective-permute-start
  3.8 0.7 %collective-permute-start.1 = (f32[256,128]{1,0:T(8,128)}, f32[256,128]{1,0:T(8,128)S(1)}, u32[]{:S(2)}, u32[]{:S(2)}) collective-permute-start(f32[256,128]{1,0:T(8,128)} %get-tuple-element.14), channel_id=1, source_target_pairs={{1,2},{2,1},{5,6},{6,5},{9,10},{10,9},{13,14},{14,13},{17,18},{18,... | collective-permute-start | bytes 393224 | tf_op jit(solution)/shard_map/ppermute | solution.py:422
  5.2 0.0 slice-start
  5.2 0.0 copy-done
  5.2 0.0 copy-done.2
  5.2 0.0 copy-done.4
  5.2 0.0 copy-start.1
  5.2 0.0 copy-start.3
  5.2 0.0 slice-start.1
  5.2 1.6 %own.1 = (f32[512,128]{1,0:T(8,128)S(1)}, bf16[192,128]{1,0:T(8,128)(2,1)S(1)}) custom-call(s32[1]{0:T(128)S(6)} %copy.8.count_ref, bf16[512,512]{1,0:T(8,128)(2,1)S(1)} %bitcast.14, bf16[27,512,128]{2,1,0:T(8,128)(2,1)S(1)} %copy-done, s32[4,128]{1,0:T(4,128)S(1)} %bitcast.18), custom_call_target="tpu_custom_call" | custom-call | flops 4000000000 | bytes 4500000 | tf_op jit(solution)/shard_map/own/pallas_call | solution.py:427
  6.8 0.0 collective-permute-done.near_ref
  6.8 0.0 collective-permute-done.1.far_ref
  6.8 0.1 copy-done.1
  6.9 0.0 copy-done.3
  6.9 0.7 %join.1 = bf16[192,640]{1,0:T(8,128)(2,1)S(1)} custom-call(s32[1]{0:T(128)S(6)} %copy.8.count_ref, s32[4,128]{1,0:T(4,128)S(1)} %bitcast.15, f32[512,128]{1,0:T(8,128)S(1)} %get-tuple-element.12.acc_ref, f32[256,128]{1,0:T(8,128)S(1)} %collective-permute-done.near_ref, f32[256,128]{1,0:T(8,128)S(1)} %collective-permute-done.1.far_ref, ...), custom_call_target="tpu_custom_call" | custom-call | flops 300000000 | bytes 3000000 | tf_op jit(solution)/shard_map/join/pallas_call | solution.py:439
  7.7 14.9 %all_to_all.10 = bf16[8,24,640]{2,1,0:T(8,128)(2,1)S(1)} all-to-all(bf16[8,24,640]{2,1,0:T(8,128)(2,1)S(1)} %bitcast.12), channel_id=1, replica_groups=mesh['bag'=8,'head'=4] {'bag'}, dimensions={0} | all-to-all | bytes 491520 | tf_op jit(solution)/shard_map/all_to_all | solution.py:450
  22.5 4.8 %collective-permute-start.3 = (bf16[192,640]{1,0:T(8,128)(2,1)S(1)}, bf16[192,640]{1,0:T(8,128)(2,1)S(1)}, u32[]{:S(2)}, u32[]{:S(2)}) collective-permute-start(bf16[192,640]{1,0:T(8,128)(2,1)S(1)} %bitcast.7), channel_id=1, source_target_pairs={{0,2},{1,3},{2,0},{3,1},{4,6},{5,7},{6,4},{7,5},{8,10},{9,11},{10,... | collective-permute-start | bytes 737288 | tf_op jit(solution)/shard_map/ppermute | solution.py:457
  27.3 0.0 collective-permute-start.2
  27.3 0.0 slice-done
  27.3 0.0 slice-done.1
  27.3 3.4 %fold.1.refs_2_.refs_1_.refs_6_ = bf16[3,1024,512]{2,1,0:T(8,128)(2,1)S(1)} custom-call(bf16[512,2048]{1,0:T(8,128)(2,1)S(1)} %copy-done.1, bf16[3,2048,512]{2,1,0:T(8,128)(2,1)S(1)} %bitcast.17, bf16[192,640]{1,0:T(8,128)(2,1)S(1)} %bitcast.9), custom_call_target="tpu_custom_call" | custom-call | flops 3300000000 | bytes 14000000 | tf_op jit(solution)/shard_map/fold/pallas_call | solution.py:458
  30.7 0.0 collective-permute-done.2.refs_1_
  30.8 1.4 %near_qkv.1.refs_4_ = f32[3,384,512]{2,1,0:T(8,128)S(1)} custom-call(bf16[192,640]{1,0:T(8,128)(2,1)S(1)} %bitcast.10, bf16[192,640]{1,0:T(8,128)(2,1)S(1)} %collective-permute-done.2.refs_1_, bf16[3,1024,512]{2,1,0:T(8,128)(2,1)S(1)} %fold.1.refs_2_.refs_1_.refs_6_), custom_call_target="tpu_custom_call" | custom-call | flops 1200000000 | bytes 6000000 | tf_op jit(solution)/shard_map/near_qkv/pallas_call | solution.py:478
  32.1 0.5 collective-permute-done.3.refs_0_.refs_2_
  32.7 0.0 collective-permute-start.4
  32.7 0.8 %across_qkv.1.refs_5_ = f32[3,192,512]{2,1,0:T(8,128)S(1)} custom-call(bf16[192,640]{1,0:T(8,128)(2,1)S(1)} %collective-permute-done.3.refs_0_.refs_2_, bf16[3,1024,512]{2,1,0:T(8,128)(2,1)S(1)} %fold.1.refs_2_.refs_1_.refs_6_), custom_call_target="tpu_custom_call" | custom-call | flops 600000000 | bytes 3000000 | tf_op jit(solution)/shard_map/across_qkv/pallas_call | solution.py:478
  33.5 0.7 %collective-permute-done.4.refs_3_ = bf16[192,640]{1,0:T(8,128)(2,1)S(1)} collective-permute-done((bf16[192,640]{1,0:T(8,128)(2,1)S(1)}, bf16[192,640]{1,0:T(8,128)(2,1)S(1)}, u32[]{:S(2)}, u32[]{:S(2)}) %collective-permute-start.4) | collective-permute-done | bytes 245792 | tf_op jit(solution)/shard_map/ppermute | solution.py:471
  34.2 4.9 %bag.1 = bf16[32,24,512]{2,1,0:T(8,128)(2,1)S(1)} custom-call(bf16[192,640]{1,0:T(8,128)(2,1)S(1)} %bitcast.11, bf16[192,640]{1,0:T(8,128)(2,1)S(1)} %collective-permute-done.2.refs_1_, bf16[192,640]{1,0:T(8,128)(2,1)S(1)} %collective-permute-done.3.refs_0_.refs_2_, bf16[192,640]{1,0:T(8,128)(2,1)S(1)} %collective-permute-done.4.refs_3_, ...), custom_call_target="tpu_custom_call" | custom-call | flops 3000000000 | bytes 5000000 | tf_op jit(solution)/shard_map/bag/pallas_call | solution.py:500
  39.1 23.8 %all_to_all.11 = bf16[32,24,512]{2,1,0:T(8,128)(2,1)S(1)} all-to-all(bf16[32,24,512]{2,1,0:T(8,128)(2,1)S(1)} %bag.1), channel_id=1, replica_groups=mesh['bag'=8,'head'=4] {'head','bag'}, dimensions={0} | all-to-all | bytes 1572864 | tf_op jit(solution)/shard_map/all_to_all | solution.py:516
  62.9 1.2 %collect.1 = bf16[128,2048]{1,0:T(8,128)(2,1)} custom-call(s32[1]{0:T(128)S(6)} %copy.8.count_ref, bf16[192,128]{1,0:T(8,128)(2,1)S(1)} %get-tuple-element.11.onehot_ref, bf16[768,512]{1,0:T(8,128)(2,1)S(1)} %bitcast.6), custom_call_target="tpu_custom_call" | custom-call | tf_op jit(solution)/shard_map/collect/pallas_call | solution.py:517
  (1 shorter events, 0.0 us)
Async XLA Ops:
  0.0 5.2 %copy-start = (bf16[27,512,128]{2,1,0:T(8,128)(2,1)S(1)}, bf16[27,512,128]{2,1,0:T(8,128)(2,1)}, u32[]{:S(2)}) copy-start(bf16[27,512,128]{2,1,0:T(8,128)(2,1)} %w_hbm.1) | copy-start | bytes 10616836
  0.0 5.2 %copy-start.2 = (bf16[1,2,16,16,512]{4,3,2,1,0:T(8,128)(2,1)S(1)}, bf16[1,2,16,16,512]{4,3,2,1,0:T(8,128)(2,1)}, u32[]{:S(2)}) copy-start(bf16[1,2,16,16,512]{4,3,2,1,0:T(8,128)(2,1)} %param.7) | copy-start | bytes 1572868
  0.0 5.2 %copy-start.4 = (s32[512,1]{0,1:T(1,128)S(1)}, s32[512,1]{0,1:T(1,128)}, u32[]{:S(2)}) copy-start(s32[512,1]{0,1:T(1,128)} %param.9) | copy-start | bytes 6148
  3.3 3.5 %collective-permute-start = (f32[256,128]{1,0:T(8,128)}, f32[256,128]{1,0:T(8,128)S(1)}, u32[]{:S(2)}, u32[]{:S(2)}) collective-permute-start(f32[256,128]{1,0:T(8,128)} %get-tuple-element.13), channel_id=1, source_target_pairs={{0,1},{1,0},{2,3},{3,2},{4,5},{5,4},{6,7},{7,6},{8,9},{9,8},{10,11... | collective-permute-start | bytes 393224 | tf_op jit(solution)/shard_map/ppermute | solution.py:423
  3.8 3.0 %collective-permute-start.1 = (f32[256,128]{1,0:T(8,128)}, f32[256,128]{1,0:T(8,128)S(1)}, u32[]{:S(2)}, u32[]{:S(2)}) collective-permute-start(f32[256,128]{1,0:T(8,128)} %get-tuple-element.14), channel_id=1, source_target_pairs={{1,2},{2,1},{5,6},{6,5},{9,10},{10,9},{13,14},{14,13},{17,18},{18,... | collective-permute-start | bytes 393224 | tf_op jit(solution)/shard_map/ppermute | solution.py:422
  5.2 22.1 %slice-start = ((s8[6291456]{0:T(1024)(128)(4,1)}), s8[4194304]{0:T(1024)(128)(4,1)S(1)}, s32[]{:S(2)}) async-start(s8[6291456]{0:T(1024)(128)(4,1)} %bitcast.16), calls=%async_computation.2 | async-start | bytes 8388608
  5.2 1.7 %copy-start.1 = (bf16[512,2048]{1,0:T(8,128)(2,1)S(1)}, bf16[512,2048]{1,0:T(8,128)(2,1)}, u32[]{:S(2)}) copy-start(bf16[512,2048]{1,0:T(8,128)(2,1)} %e_ref.3) | copy-start | bytes 6291460
  5.2 1.7 %copy-start.3 = (s32[512]{0:T(512)S(1)}, s32[512]{0:T(512)}, u32[]{:S(2)}) copy-start(s32[512]{0:T(512)} %param.10) | copy-start | bytes 6148
  5.2 22.1 %slice-start.1 = ((s8[6291456]{0:T(1024)(128)(4,1)}), s8[2097152]{0:T(1024)(128)(4,1)S(1)}, s32[]{:S(2)}) async-start(s8[6291456]{0:T(1024)(128)(4,1)} %bitcast.16), calls=%async_computation.3 | async-start | bytes 4194304
  22.5 10.2 %collective-permute-start.3 = (bf16[192,640]{1,0:T(8,128)(2,1)S(1)}, bf16[192,640]{1,0:T(8,128)(2,1)S(1)}, u32[]{:S(2)}, u32[]{:S(2)}) collective-permute-start(bf16[192,640]{1,0:T(8,128)(2,1)S(1)} %bitcast.7), channel_id=1, source_target_pairs={{0,2},{1,3},{2,0},{3,1},{4,6},{5,7},{6,4},{7,5},{8,10},{9,11},{10,... | collective-permute-start | bytes 737288 | tf_op jit(solution)/shard_map/ppermute | solution.py:457
  27.3 3.5 %collective-permute-start.2 = (bf16[192,640]{1,0:T(8,128)(2,1)S(1)}, bf16[192,640]{1,0:T(8,128)(2,1)S(1)}, u32[]{:S(2)}, u32[]{:S(2)}) collective-permute-start(bf16[192,640]{1,0:T(8,128)(2,1)S(1)} %bitcast.8), channel_id=1, source_target_pairs={{0,1},{1,0},{2,3},{3,2},{4,5},{5,4},{6,7},{7,6},{8,9},{9,8},{10,11... | collective-permute-start | bytes 737288 | tf_op jit(solution)/shard_map/ppermute | solution.py:471
  32.7 1.5 %collective-permute-start.4 = (bf16[192,640]{1,0:T(8,128)(2,1)S(1)}, bf16[192,640]{1,0:T(8,128)(2,1)S(1)}, u32[]{:S(2)}, u32[]{:S(2)}) collective-permute-start(bf16[192,640]{1,0:T(8,128)(2,1)S(1)} %collective-permute-done.3.refs_0_.refs_2_), channel_id=1, source_target_pairs={{0,1},{1,0},{2,3},{3,2},{4,5},{5,4},{6,7},{7,6},{8,9},{9,8},{10,11... | collective-permute-start | bytes 737288 | tf_op jit(solution)/shard_map/ppermute | solution.py:471
